TPU v7x, 32 devices: a whole 2x2x4 slice. The times are simulated.
32 devices in a mesh: groups: 2 (over x), chan: 16 (over z, y, core).
Axes of the slice: x: 2, y: 2, z: 4, core: 2. Of those that a mesh axis runs over, the one named last changes fastest.
Arguments:
- psi_prev: float32 [1024, 32, 128], P(('groups', 'chan')), parts along dimension 0, may hold values from -6 to 6
- psi_cur: float32 [1024, 32, 128], P(('groups', 'chan')), parts along dimension 0, may hold values from -6 to 6
- kin_stretch: float32 [32, 32], replicated, may hold values from -0.75 to 0.75
- kin_radius: float32 [128, 128], replicated, may hold values from -0.375 to 0.375
- potential: float32 [3, 32, 128], replicated, may hold values from -4 to 4
- angular: float32 [6, 512, 512], P('groups'), parts along dimension 0, may hold values from -0.4375 to 0.4375
- pattern: int32 [16, 8], P('groups'), parts along dimension 0, may hold values 0 or 1
- quanta: int32 [1024, 2], P(('groups', 'chan')), parts along dimension 0, may hold values from 0 to 39
Outputs:
- prev_out: float32 [1024, 32, 128], P(('groups', 'chan')), parts along dimension 0
- cur_out: float32 [1024, 32, 128], P(('groups', 'chan')), parts along dimension 0
- norms: float32 [6], P('groups'), parts along dimension 0
There are 2 independent parts, one for each index of `groups`. A program takes and returns all parts, laid end to end along the dimension named above; an argument that names none is the same for every part. Nothing has to cross between parts.
All inputs are finite; a program needn't handle non-finite values.
Results may differ from a plain program's by a relative error of at most 0.00085.
Values sent between devices are 32-bit elements; how exact they have to be, the bound alone decides.
No kernel may reach another device: no remote copies, remote signals or barrier semaphores. Data moves between devices by JAX's collectives and lax.ppermute only.
A program may use at most 64 MiB of HBM per device.

v0:
```python
import functools

import jax
import jax.numpy as jnp
import numpy as np
from jax import lax
from jax.experimental import pallas as pl
from jax.experimental.pallas import tpu as pltpu
from jax.sharding import PartitionSpec as P

JL_MAX = 40
ITERS = 3
TEAM = 4
F32 = jnp.float32
BF16 = jnp.bfloat16
HP = lax.Precision.HIGHEST
VM = pl.BlockSpec(memory_space=pltpu.VMEM)
SM = pl.BlockSpec(memory_space=pltpu.SMEM)
ANY = pl.BlockSpec(memory_space=pl.ANY)


def place(me_ref):
    return me_ref[0] // TEAM, me_ref[0] % TEAM


def rows_of(spot, s, q, na, nk):
    return pl.ds(pl.multiple_of((spot ^ s) * na + q * nk, nk), nk)


def to_pieces_kernel(na, nc, n, n_chunk, me_ref, x_ref, *outs):
    spot, _ = place(me_ref)
    nk = na // n_chunk
    for q in range(n_chunk):
        for s in range(n):
            out = outs[q * n + s]
            for c in range(nc):
                out[pl.ds(c, nk, stride=nc), :] = x_ref[c, rows_of(spot, s, q, na, nk), :]


def pack_kernel(n, me_ref, *refs):
    spot, _ = place(me_ref)
    for s in range(n):
        refs[n][spot ^ s] = refs[s][...]


def kinetic_kernel(na, nc, n, n_chunk, from_pieces, to_pieces, me_ref, quanta, ks, kr, prev, *refs):
    spot, _ = place(me_ref)
    nk = na // n_chunk
    refs = list(refs)
    take = lambda k: [refs.pop(0) for _ in range(k)]
    pieces = take(n * n_chunk) if from_pieces else ()
    cur = None if from_pieces else take(1)[0]
    u_refs = take(n * n_chunk if to_pieces else 1)
    cur = take(1)[0] if from_pieces else cur
    y_ref = refs.pop(0) if to_pieces else u_refs[0]
    nr, nb = prev.shape[1:]
    kstr = 2.0 * ks[...]
    krad = 2.0 * kr[...]
    stretch = 1.0 + lax.broadcasted_iota(jnp.int32, (nr, nb), 0).astype(F32) / nr
    radius = 1.0 + 3.0 * lax.broadcasted_iota(jnp.int32, (nr, nb), 1).astype(F32) / nb
    rotation = 1.0 / (stretch * stretch)
    orbital = 1.0 / (radius * radius)
    scale = np.float32(0.3 / (JL_MAX * (JL_MAX - 1)))
    group = min(8, nc)
    for start in range(0, nc, group):
        chans = range(start, start + group)
        if from_pieces:
            for q in range(n_chunk):
                for s in range(n):
                    for c in chans:
                        cur[c, rows_of(spot, s, q, na, nk), :] = pieces[q * n + s][pl.ds(c, nk, stride=nc), :]
        tiles = [cur[c] for c in chans]
        mixed_a = jnp.dot(kstr, jnp.concatenate(tiles, 1), precision=HP, preferred_element_type=F32)
        mixed_b = jnp.dot(jnp.concatenate(tiles, 0), krad, precision=HP, preferred_element_type=F32)
        for i, c in enumerate(chans):
            j = quanta[c, 0].astype(F32)
            l = quanta[c, 1].astype(F32)
            barrier = orbital * (scale * (l * (l + 1.0))) + rotation * (scale * (j * (j + 1.0))) - 0.2
            y = mixed_a[:, i * nb : (i + 1) * nb] + mixed_b[i * nr : (i + 1) * nr]
            y_ref[i if to_pieces else c] = y + barrier * tiles[i] - prev[c]
        if to_pieces:
            for q in range(n_chunk):
                for s in range(n):
                    for i, c in enumerate(chans):
                        u_refs[q * n + s][pl.ds(c, nk, stride=nc), :] = y_ref[i, rows_of(spot, s, q, na, nk), :]


def coupling_kernel(cb, nc, n, me_ref, pat_ref, ang_ref, out_ref, buf, sems):
    _, seat = place(me_ref)
    lam, _, tot = ang_ref.shape

    def row(z):
        return (z * TEAM + seat) * nc

    copies = [
        pltpu.make_async_copy(
            ang_ref.at[m, pl.ds(pl.multiple_of(row(z), nc), nc), :], buf.at[m, z], sems.at[m * n + z]
        )
        for m in range(lam)
        for z in range(n)
    ]
    for copy in copies:
        copy.start()
    lane = lax.broadcasted_iota(jnp.int32, (nc, tot), 1) // cb
    for copy in copies:
        copy.wait()
    for z in range(n):
        factor = jnp.zeros((nc, tot), F32)
        for k in range(tot // cb):
            factor = jnp.where(lane == k, pat_ref[row(z) // cb, k].astype(F32), factor)
        for m in range(lam):
            val = buf[m, z] * factor
            hi = val.astype(BF16)
            out_ref[m, 0, z] = hi
            out_ref[m, 1, z] = (val - hi.astype(F32)).astype(BF16)


def mix_kernel(nc, q, n, mode, me_ref, coup, pot, *refs):
    spot, seat = place(me_ref)
    sources, refs = refs[:TEAM], list(refs[TEAM:])
    take = lambda k: [refs.pop(0) for _ in range(k)]
    us = take(n) if mode == "next" else ()
    pieces = take(n)
    out, sq = take(2) if mode == "next" else (None, None)
    tmp = out if mode == "next" else refs.pop(0)
    xs_hi, xs_lo = refs
    _, rows, nb = sources[0].shape
    nk, ch = rows // nc, n * nc
    lam, tot = coup.shape[0], coup.shape[-1]
    for m, src in enumerate(sources):
        for z in range(n):
            x = jnp.concatenate([src[z, k * nc : (k + 1) * nc] for k in range(nk)], 1)
            hi = x.astype(BF16)
            xs_hi[z * TEAM + (seat ^ m)] = hi
            xs_lo[z * TEAM + (seat ^ m)] = (x - hi.astype(F32)).astype(BF16)
    for s, u in enumerate(us):
        tmp[spot ^ s] = u[...]
    x_hi = xs_hi[...].reshape(tot, nk * nb)
    x_lo = xs_lo[...].reshape(tot, nk * nb)
    na = pot.shape[1] // n
    acc = None
    for m in range(lam):
        both = coup[m].reshape(2 * ch, tot)
        p = jnp.dot(both, x_hi, preferred_element_type=F32)
        p = p[:ch] + p[ch:] + jnp.dot(both[:ch], x_lo, preferred_element_type=F32)
        w = jnp.concatenate([pot[m, pl.ds(spot * na + q * nk + k, 1), :] for k in range(nk)], 1)
        p = p * (2.0 * w)
        acc = p if acc is None else acc + p
    total = jnp.zeros((8, nb), F32)
    for k in range(nk):
        y = acc[:, k * nb : (k + 1) * nb].reshape(n, nc, nb)
        if mode == "next":
            y = y + tmp[:, k * nc : (k + 1) * nc]
            total = total + jnp.sum((y * y).reshape(ch // 8, 8, nb), axis=0)
        tmp[:, k * nc : (k + 1) * nc] = y
    for s, piece in enumerate(pieces):
        piece[...] = tmp[spot ^ s]
    if mode == "next":
        sq[...] = total


def finish_kernel(na, nc, n, n_chunk, me_ref, u_ref, *refs):
    spot, _ = place(me_ref)
    nk = na // n_chunk
    pieces, squares, (out, sums) = refs[: n * n_chunk], refs[n * n_chunk : -2], refs[-2:]
    nb = u_ref.shape[-1]
    total = jnp.zeros((nk, nb), F32)
    for q in range(n_chunk):
        for s in range(n):
            at = rows_of(spot, s, q, na, nk)
            for c in range(nc):
                y = u_ref[c, at, :] + pieces[q * n + s][pl.ds(c, nk, stride=nc), :]
                out[c, at, :] = y
                total = total + y * y
    tiles = [sum((r[...] for r in squares[k + 1 : k + n_chunk]), squares[k][...]) for k in (0, n_chunk)]
    tiles = [jnp.sum(t, axis=0, keepdims=True) for t in (*tiles, total)]
    sums[...] = jnp.concatenate([*tiles, jnp.zeros((8 - ITERS, nb), F32)], 0)


def local(x):
    return pltpu.with_memory_space_constraint(x, pltpu.VMEM)


def call(kernel, outs, scalars, arrays, scratch=(), specs=None):
    return pl.pallas_call(
        kernel,
        out_shape=outs,
        in_specs=[SM] * len(scalars) + (specs or [VM] * len(arrays)),
        out_specs=[VM] * len(outs),
        scratch_shapes=list(scratch),
        compiler_params=pltpu.CompilerParams(vmem_limit_bytes=20 << 20),
        cost_estimate=pl.CostEstimate(flops=0, bytes_accessed=1 << 16, transcendentals=0),
    )(*scalars, *arrays)


def per_device(psi_prev, psi_cur, kin_stretch, kin_radius, potential, angular, pattern, quanta):
    nc, nr, nb = psi_cur.shape
    lam = potential.shape[0]
    nd = lax.axis_size("chan")
    n = nd // TEAM
    na = nr // n
    total_ch = nc * nd
    cb = total_ch // pattern.shape[1]
    n_chunk = 2 if na % 2 == 0 else 1
    nk = na // n_chunk
    me = lax.axis_index("chan").astype(jnp.int32).reshape(1)
    sds = jax.ShapeDtypeStruct

    def swap(x, bits):
        return lax.ppermute(x, "chan", [(i, i ^ bits) for i in range(nd)])

    def across(x, bits):
        return local(swap(x, bits))

    def exchange(pieces):
        return [across(x, i % n * TEAM) if i % n else x for i, x in enumerate(pieces)]

    def gather(x):
        over = across(x, 2)
        return [x, across(x, 1), over, across(over, 1)]

    piece = pltpu.VMEM((nk * nc, nb), F32)
    packed = pltpu.VMEM((n, nk * nc, nb), F32)
    square = pltpu.VMEM((8, nb), F32)
    on_chip = pltpu.VMEM((nc, nr, nb), F32)
    natural = sds((nc, nr, nb), F32)
    shape = (na, nc, n, n_chunk)

    (coup,) = call(
        functools.partial(coupling_kernel, cb, nc, n),
        [pltpu.VMEM((lam, 2, n, nc, total_ch), BF16)],
        [me, pattern],
        [angular],
        [pltpu.VMEM((lam, n, nc, total_ch), F32), pltpu.SemaphoreType.DMA((lam * n,))],
        [ANY],
    )

    def kinetic(prev, cur, from_pieces, to_pieces, out=None):
        outs = ([piece] * (n * n_chunk) if to_pieces else [on_chip]) + ([out] if from_pieces else [])
        scratch = [pltpu.VMEM((min(8, nc), nr, nb), F32)] if to_pieces else []
        kernel = functools.partial(kinetic_kernel, *shape, from_pieces, to_pieces)
        return call(kernel, outs, [me, quanta], [kin_stretch, kin_radius, prev, *cur], scratch)

    def mix(q, sources, u=()):
        keep = bool(u)
        outs = [piece] * n + ([packed, square] if keep else [])
        split = pltpu.VMEM((nd, nc, nk * nb), BF16)
        return call(
            functools.partial(mix_kernel, nc, q, n, "next" if keep else "last"),
            outs,
            [me],
            [coup, potential, *sources, *u],
            ([] if keep else [packed]) + [split, split],
        )

    def step(v, u):
        pieces, chunks, squares = [], [], []
        for q in range(n_chunk):
            *part, chunk, square_sum = mix(q, gather(v[q]), u[q * n : (q + 1) * n])
            pieces += part
            chunks.append(chunk)
            squares.append(square_sum)
        return exchange(pieces), chunks, squares

    pieces = exchange(
        call(functools.partial(to_pieces_kernel, *shape), [piece] * (n * n_chunk), [me], [psi_cur])
    )
    v1 = [
        call(functools.partial(pack_kernel, n), [packed], [me], pieces[q * n : (q + 1) * n])[0]
        for q in range(n_chunk)
    ]
    u1 = exchange(kinetic(psi_prev, [psi_cur], False, True))
    pieces, v2, s2 = step(v1, u1)
    *u2, v2_nat = kinetic(psi_cur, pieces, True, True, on_chip)
    pieces, v3, s3 = step(v2, exchange(u2))
    u3, prev_out = kinetic(v2_nat, pieces, True, False, natural)
    pieces = exchange([p for q in range(n_chunk) for p in mix(q, gather(v3[q]))])
    cur_out, sums = call(
        functools.partial(finish_kernel, *shape), [natural, sds((8, nb), F32)], [me], [u3, *pieces, *s2, *s3]
    )
    bit = 1
    while bit < nd:
        sums = (sums + swap(sums, bit)) + (swap(sums, 2 * bit) + swap(sums, 3 * bit))
        bit *= 4
    norms = jnp.sum(sums[:ITERS], axis=1) / (total_ch * nr * nb)
    return prev_out, cur_out, norms


def solution(mesh):
    return jax.shard_map(
        per_device,
        mesh=mesh,
        in_specs=(
            P(("groups", "chan"), None, None),
            P(("groups", "chan"), None, None),
            P(),
            P(),
            P(),
            P("groups", None, None),
            P("groups", None),
            P(("groups", "chan"), None),
        ),
        out_specs=(
            P(("groups", "chan"), None, None),
            P(("groups", "chan"), None, None),
            P("groups"),
        ),
        check_vma=False,
    )
```

profile of v0, /device:TPU:0, one launch (start us, length us, event | category | flops | bytes accessed | tf_op | source)
XLA Modules:
  0.0 150.1 jit_solution(10758586189059319915)
XLA Ops:
  2.0 3.1 %collective-permute-start = (f32[128,128]{1,0:T(8,128)S(1)}, f32[128,128]{1,0:T(8,128)S(1)}, u32[]{:S(2)}, u32[]{:S(2)}) collective-permute-start(f32[128,128]{1,0:T(8,128)S(1)} %get-tuple-element.65), channel_id=1, source_target_pairs={{0,4},{1,5},{2,6},{3,7},{4,0},{5,1},{6,2},{7,3},{8,12},{9,13},{10,... | collective-permute-start | bytes 196616 | tf_op jit(solution)/shard_map/ppermute | solution.py:210
  5.1 2.6 %collective-permute-start.1 = (f32[128,128]{1,0:T(8,128)S(1)}, f32[128,128]{1,0:T(8,128)S(1)}, u32[]{:S(2)}, u32[]{:S(2)}) collective-permute-start(f32[128,128]{1,0:T(8,128)S(1)} %get-tuple-element.66), channel_id=1, source_target_pairs={{0,8},{1,9},{2,10},{3,11},{4,12},{5,13},{6,14},{7,15},{8,0},{9,1},... | collective-permute-start | bytes 196616 | tf_op jit(solution)/shard_map/ppermute | solution.py:210
  7.7 4.7 %collective-permute-done.1.refs_2_ = f32[128,128]{1,0:T(8,128)S(1)} collective-permute-done((f32[128,128]{1,0:T(8,128)S(1)}, f32[128,128]{1,0:T(8,128)S(1)}, u32[]{:S(2)}, u32[]{:S(2)}) %collective-permute-start.1) | collective-permute-done | bytes 65568 | tf_op jit(solution)/shard_map/ppermute | solution.py:210
  15.4 2.3 %collective-permute-start.13 = (f32[128,128]{1,0:T(8,128)S(1)}, f32[128,128]{1,0:T(8,128)S(1)}, u32[]{:S(2)}, u32[]{:S(2)}) collective-permute-start(f32[128,128]{1,0:T(8,128)S(1)} %get-tuple-element.78), channel_id=1, source_target_pairs={{0,8},{1,9},{2,10},{3,11},{4,12},{5,13},{6,14},{7,15},{8,0},{9,1},... | collective-permute-start | bytes 196616 | tf_op jit(solution)/shard_map/ppermute | solution.py:210
  21.1 2.7 %collective-permute-done.14.refs_3_ = f32[128,128]{1,0:T(8,128)S(1)} collective-permute-done((f32[128,128]{1,0:T(8,128)S(1)}, f32[128,128]{1,0:T(8,128)S(1)}, u32[]{:S(2)}, u32[]{:S(2)}) %collective-permute-start.14) | collective-permute-done | bytes 65568 | tf_op jit(solution)/shard_map/ppermute | solution.py:210
  31.5 2.6 %collective-permute-start.7 = (f32[128,128]{1,0:T(8,128)S(1)}, f32[128,128]{1,0:T(8,128)S(1)}, u32[]{:S(2)}, u32[]{:S(2)}) collective-permute-start(f32[128,128]{1,0:T(8,128)S(1)} %get-tuple-element.70), channel_id=1, source_target_pairs={{0,8},{1,9},{2,10},{3,11},{4,12},{5,13},{6,14},{7,15},{8,0},{9,1},... | collective-permute-start | bytes 196616 | tf_op jit(solution)/shard_map/ppermute | solution.py:210
  34.1 2.7 %collective-permute-done.6.refs_5_ = f32[128,128]{1,0:T(8,128)S(1)} collective-permute-done((f32[128,128]{1,0:T(8,128)S(1)}, f32[128,128]{1,0:T(8,128)S(1)}, u32[]{:S(2)}, u32[]{:S(2)}) %collective-permute-start.6) | collective-permute-done | bytes 65568 | tf_op jit(solution)/shard_map/ppermute | solution.py:210
  40.2 4.0 %collective-permute-done.8.refs_7_ = f32[128,128]{1,0:T(8,128)S(1)} collective-permute-done((f32[128,128]{1,0:T(8,128)S(1)}, f32[128,128]{1,0:T(8,128)S(1)}, u32[]{:S(2)}, u32[]{:S(2)}) %collective-permute-start.8) | collective-permute-done | bytes 65568 | tf_op jit(solution)/shard_map/ppermute | solution.py:210
  49.0 2.6 %collective-permute-start.19 = (f32[128,128]{1,0:T(8,128)S(1)}, f32[128,128]{1,0:T(8,128)S(1)}, u32[]{:S(2)}, u32[]{:S(2)}) collective-permute-start(f32[128,128]{1,0:T(8,128)S(1)} %get-tuple-element.82), channel_id=1, source_target_pairs={{0,8},{1,9},{2,10},{3,11},{4,12},{5,13},{6,14},{7,15},{8,0},{9,1},... | collective-permute-start | bytes 196616 | tf_op jit(solution)/shard_map/ppermute | solution.py:210
  60.2 2.3 %collective-permute-start.10 = (f32[128,128]{1,0:T(8,128)S(1)}, f32[128,128]{1,0:T(8,128)S(1)}, u32[]{:S(2)}, u32[]{:S(2)}) collective-permute-start(f32[128,128]{1,0:T(8,128)S(1)} %get-tuple-element.74), channel_id=1, source_target_pairs={{0,8},{1,9},{2,10},{3,11},{4,12},{5,13},{6,14},{7,15},{8,0},{9,1},... | collective-permute-start | bytes 196616 | tf_op jit(solution)/shard_map/ppermute | solution.py:210
  75.2 2.3 %shard_map.110 = (f32[128,128]{1,0:T(8,128)S(1)}, f32[128,128]{1,0:T(8,128)S(1)}, f32[128,128]{1,0:T(8,128)S(1)}, f32[128,128]{1,0:T(8,128)S(1)}, f32[128,128]{1...) custom-call(s32[1]{0:T(128)} %bitcast.me_ref, ...), custom_call_target="tpu_custom_call" | custom-call | bytes 65536 | tf_op jit(solution)/shard_map/pallas_call | solution.py:185
  78.2 3.7 %collective-permute-done.27.refs_5_ = f32[128,128]{1,0:T(8,128)S(1)} collective-permute-done((f32[128,128]{1,0:T(8,128)S(1)}, f32[128,128]{1,0:T(8,128)S(1)}, u32[]{:S(2)}, u32[]{:S(2)}) %collective-permute-start.27) | collective-permute-done | bytes 65568 | tf_op jit(solution)/shard_map/ppermute | solution.py:210
  82.5 6.0 %collective-permute-done.28.refs_6_ = f32[128,128]{1,0:T(8,128)S(1)} collective-permute-done((f32[128,128]{1,0:T(8,128)S(1)}, f32[128,128]{1,0:T(8,128)S(1)}, u32[]{:S(2)}, u32[]{:S(2)}) %collective-permute-start.28) | collective-permute-done | bytes 65568 | tf_op jit(solution)/shard_map/ppermute | solution.py:210
  90.7 4.6 %collective-permute-done.29.refs_7_ = f32[128,128]{1,0:T(8,128)S(1)} collective-permute-done((f32[128,128]{1,0:T(8,128)S(1)}, f32[128,128]{1,0:T(8,128)S(1)}, u32[]{:S(2)}, u32[]{:S(2)}) %collective-permute-start.29) | collective-permute-done | bytes 65568 | tf_op jit(solution)/shard_map/ppermute | solution.py:210
  95.4 2.3 %collective-permute-start.37 = (f32[128,128]{1,0:T(8,128)S(1)}, f32[128,128]{1,0:T(8,128)S(1)}, u32[]{:S(2)}, u32[]{:S(2)}) collective-permute-start(f32[128,128]{1,0:T(8,128)S(1)} %get-tuple-element.101), channel_id=1, source_target_pairs={{0,8},{1,9},{2,10},{3,11},{4,12},{5,13},{6,14},{7,15},{8,0},{9,1},... | collective-permute-start | bytes 196616 | tf_op jit(solution)/shard_map/ppermute | solution.py:210
  101.3 2.4 %collective-permute-done.38.refs_7_ = f32[128,128]{1,0:T(8,128)S(1)} collective-permute-done((f32[128,128]{1,0:T(8,128)S(1)}, f32[128,128]{1,0:T(8,128)S(1)}, u32[]{:S(2)}, u32[]{:S(2)}) %collective-permute-start.38) | collective-permute-done | bytes 65568 | tf_op jit(solution)/shard_map/ppermute | solution.py:210
  107.7 3.4 %collective-permute-done.49.refs_2_ = f32[4,128,128]{2,1,0:T(8,128)S(1)} collective-permute-done((f32[4,128,128]{2,1,0:T(8,128)S(1)}, f32[4,128,128]{2,1,0:T(8,128)S(1)}, u32[]{:S(2)}, u32[]{:S(2)}) %collective-permute-start.49) | collective-permute-done | bytes 262176 | tf_op jit(solution)/shard_map/ppermute | solution.py:210
  111.1 2.7 %collective-permute-start.31 = (f32[128,128]{1,0:T(8,128)S(1)}, f32[128,128]{1,0:T(8,128)S(1)}, u32[]{:S(2)}, u32[]{:S(2)}) collective-permute-start(f32[128,128]{1,0:T(8,128)S(1)} %get-tuple-element.96), channel_id=1, source_target_pairs={{0,8},{1,9},{2,10},{3,11},{4,12},{5,13},{6,14},{7,15},{8,0},{9,1},... | collective-permute-start | bytes 196616 | tf_op jit(solution)/shard_map/ppermute | solution.py:210
  116.7 2.4 %collective-permute-done.31.refs_2_ = f32[128,128]{1,0:T(8,128)S(1)} collective-permute-done((f32[128,128]{1,0:T(8,128)S(1)}, f32[128,128]{1,0:T(8,128)S(1)}, u32[]{:S(2)}, u32[]{:S(2)}) %collective-permute-start.31) | collective-permute-done | bytes 65568 | tf_op jit(solution)/shard_map/ppermute | solution.py:210
  119.4 2.3 %collective-permute-start.41 = (f32[128,128]{1,0:T(8,128)S(1)}, f32[128,128]{1,0:T(8,128)S(1)}, u32[]{:S(2)}, u32[]{:S(2)}) collective-permute-start(f32[128,128]{1,0:T(8,128)S(1)} %get-tuple-element.106), channel_id=1, source_target_pairs={{0,12},{1,13},{2,14},{3,15},{4,8},{5,9},{6,10},{7,11},{8,4},{9,5},... | collective-permute-start | bytes 196616 | tf_op jit(solution)/shard_map/ppermute | solution.py:210
  124.8 2.3 %collective-permute-start.47 = (f32[128,128]{1,0:T(8,128)S(1)}, f32[128,128]{1,0:T(8,128)S(1)}, u32[]{:S(2)}, u32[]{:S(2)}) collective-permute-start(f32[128,128]{1,0:T(8,128)S(1)} %get-tuple-element.113), channel_id=1, source_target_pairs={{0,12},{1,13},{2,14},{3,15},{4,8},{5,9},{6,10},{7,11},{8,4},{9,5},... | collective-permute-start | bytes 196616 | tf_op jit(solution)/shard_map/ppermute | solution.py:210
  127.1 5.8 %collective-permute-start.52 = (f32[128,128]{1,0:T(8,128)S(1)}, f32[128,128]{1,0:T(8,128)S(1)}, u32[]{:S(2)}, u32[]{:S(2)}) collective-permute-start(f32[128,128]{1,0:T(8,128)S(1)} %get-tuple-element.117), channel_id=1, source_target_pairs={{0,8},{1,9},{2,10},{3,11},{4,12},{5,13},{6,14},{7,15},{8,0},{9,1},... | collective-permute-start | bytes 196616 | tf_op jit(solution)/shard_map/ppermute | solution.py:210
  134.3 2.5 %shard_map.113 = (f32[32,32,128]{2,1,0:T(8,128)S(1)}, f32[32,32,128]{2,1,0:T(8,128)}) custom-call(s32[1]{0:T(128)} %bitcast.me_ref, s32[32,2]{1,0:T(8,128)S(1)} %copy.13.quanta, f32[32,32]{1,0:T(8,128)S(1)} %copy-done.9, f32[128,128]{1,0:T(8,128)S(1)} %copy-done.6, f32[32,32,128]{2,1,0:T(8,128)S(1)} %get-tuple-element.88.prev, ...), custom_call_target="tpu_custom_call" | custom-call | bytes 65536 | tf_op jit(solution)/shard_map/pallas_call | solution.py:185
  136.9 2.1 %collective-permute-done.53.refs_7_ = f32[128,128]{1,0:T(8,128)S(1)} collective-permute-done((f32[128,128]{1,0:T(8,128)S(1)}, f32[128,128]{1,0:T(8,128)S(1)}, u32[]{:S(2)}, u32[]{:S(2)}) %collective-permute-start.53) | collective-permute-done | bytes 65568 | tf_op jit(solution)/shard_map/ppermute | solution.py:210
  (137 shorter events, 74.5 us)
Async XLA Ops:
  13.8 11.4 %collective-permute-start.4 = (f32[4,128,128]{2,1,0:T(8,128)S(1)}, f32[4,128,128]{2,1,0:T(8,128)S(1)}, u32[]{:S(2)}, u32[]{:S(2)}) collective-permute-start(f32[4,128,128]{2,1,0:T(8,128)S(1)} %shard_map.105.refs_0_), channel_id=1, source_target_pairs={{0,2},{1,3},{2,0},{3,1},{4,6},{5,7},{6,4},{7,5},{8,10},{9,11},{10,... | collective-permute-start | bytes 786440 | tf_op jit(solution)/shard_map/ppermute | solution.py:210
  23.8 13.0 %collective-permute-start.16 = (f32[4,128,128]{2,1,0:T(8,128)S(1)}, f32[4,128,128]{2,1,0:T(8,128)S(1)}, u32[]{:S(2)}, u32[]{:S(2)}) collective-permute-start(f32[4,128,128]{2,1,0:T(8,128)S(1)} %shard_map.108.refs_0_), channel_id=1, source_target_pairs={{0,2},{1,3},{2,0},{3,1},{4,6},{5,7},{6,4},{7,5},{8,10},{9,11},{10,... | collective-permute-start | bytes 786440 | tf_op jit(solution)/shard_map/ppermute | solution.py:210
  25.2 23.8 %collective-permute-start.3 = (f32[4,128,128]{2,1,0:T(8,128)S(1)}, f32[4,128,128]{2,1,0:T(8,128)S(1)}, u32[]{:S(2)}, u32[]{:S(2)}) collective-permute-start(f32[4,128,128]{2,1,0:T(8,128)S(1)} %shard_map.105.refs_0_), channel_id=1, source_target_pairs={{0,1},{1,0},{2,3},{3,2},{4,5},{5,4},{6,7},{7,6},{8,9},{9,8},{10,11... | collective-permute-start | bytes 786440 | tf_op jit(solution)/shard_map/ppermute | solution.py:210
  25.2 26.4 %collective-permute-start.5 = (f32[4,128,128]{2,1,0:T(8,128)S(1)}, f32[4,128,128]{2,1,0:T(8,128)S(1)}, u32[]{:S(2)}, u32[]{:S(2)}) collective-permute-start(f32[4,128,128]{2,1,0:T(8,128)S(1)} %collective-permute-done.4.refs_2_), channel_id=1, source_target_pairs={{0,1},{1,0},{2,3},{3,2},{4,5},{5,4},{6,7},{7,6},{8,9},{9,8},{10,11... | collective-permute-start | bytes 786440 | tf_op jit(solution)/shard_map/ppermute | solution.py:210
  36.8 20.9 %collective-permute-start.15 = (f32[4,128,128]{2,1,0:T(8,128)S(1)}, f32[4,128,128]{2,1,0:T(8,128)S(1)}, u32[]{:S(2)}, u32[]{:S(2)}) collective-permute-start(f32[4,128,128]{2,1,0:T(8,128)S(1)} %shard_map.108.refs_0_), channel_id=1, source_target_pairs={{0,1},{1,0},{2,3},{3,2},{4,5},{5,4},{6,7},{7,6},{8,9},{9,8},{10,11... | collective-permute-start | bytes 786440 | tf_op jit(solution)/shard_map/ppermute | solution.py:210
  36.8 20.9 %collective-permute-start.17 = (f32[4,128,128]{2,1,0:T(8,128)S(1)}, f32[4,128,128]{2,1,0:T(8,128)S(1)}, u32[]{:S(2)}, u32[]{:S(2)}) collective-permute-start(f32[4,128,128]{2,1,0:T(8,128)S(1)} %collective-permute-done.16.refs_2_), channel_id=1, source_target_pairs={{0,1},{1,0},{2,3},{3,2},{4,5},{5,4},{6,7},{7,6},{8,9},{9,8},{10,11... | collective-permute-start | bytes 786440 | tf_op jit(solution)/shard_map/ppermute | solution.py:210
  44.2 10.1 %collective-permute-start.18 = (f32[128,128]{1,0:T(8,128)S(1)}, f32[128,128]{1,0:T(8,128)S(1)}, u32[]{:S(2)}, u32[]{:S(2)}) collective-permute-start(f32[128,128]{1,0:T(8,128)S(1)} %get-tuple-element.81), channel_id=1, source_target_pairs={{0,4},{1,5},{2,6},{3,7},{4,0},{5,1},{6,2},{7,3},{8,12},{9,13},{10,... | collective-permute-start | bytes 196616 | tf_op jit(solution)/shard_map/ppermute | solution.py:210
  54.3 16.9 %collective-permute-start.25 = (f32[4,128,128]{2,1,0:T(8,128)S(1)}, f32[4,128,128]{2,1,0:T(8,128)S(1)}, u32[]{:S(2)}, u32[]{:S(2)}) collective-permute-start(f32[4,128,128]{2,1,0:T(8,128)S(1)} %get-tuple-element.89.refs_0_), channel_id=1, source_target_pairs={{0,2},{1,3},{2,0},{3,1},{4,6},{5,7},{6,4},{7,5},{8,10},{9,11},{10,... | collective-permute-start | bytes 786440 | tf_op jit(solution)/shard_map/ppermute | solution.py:210
  58.6 19.1 %collective-permute-start.34 = (f32[4,128,128]{2,1,0:T(8,128)S(1)}, f32[4,128,128]{2,1,0:T(8,128)S(1)}, u32[]{:S(2)}, u32[]{:S(2)}) collective-permute-start(f32[4,128,128]{2,1,0:T(8,128)S(1)} %get-tuple-element.98.refs_0_), channel_id=1, source_target_pairs={{0,2},{1,3},{2,0},{3,1},{4,6},{5,7},{6,4},{7,5},{8,10},{9,11},{10,... | collective-permute-start | bytes 786440 | tf_op jit(solution)/shard_map/ppermute | solution.py:210
  71.2 24.1 %collective-permute-start.24 = (f32[4,128,128]{2,1,0:T(8,128)S(1)}, f32[4,128,128]{2,1,0:T(8,128)S(1)}, u32[]{:S(2)}, u32[]{:S(2)}) collective-permute-start(f32[4,128,128]{2,1,0:T(8,128)S(1)} %get-tuple-element.89.refs_0_), channel_id=1, source_target_pairs={{0,1},{1,0},{2,3},{3,2},{4,5},{5,4},{6,7},{7,6},{8,9},{9,8},{10,11... | collective-permute-start | bytes 786440 | tf_op jit(solution)/shard_map/ppermute | solution.py:210
  71.3 26.4 %collective-permute-start.26 = (f32[4,128,128]{2,1,0:T(8,128)S(1)}, f32[4,128,128]{2,1,0:T(8,128)S(1)}, u32[]{:S(2)}, u32[]{:S(2)}) collective-permute-start(f32[4,128,128]{2,1,0:T(8,128)S(1)} %collective-permute-done.25.refs_2_), channel_id=1, source_target_pairs={{0,1},{1,0},{2,3},{3,2},{4,5},{5,4},{6,7},{7,6},{8,9},{9,8},{10,11... | collective-permute-start | bytes 786440 | tf_op jit(solution)/shard_map/ppermute | solution.py:210
  77.6 26.1 %collective-permute-start.33 = (f32[4,128,128]{2,1,0:T(8,128)S(1)}, f32[4,128,128]{2,1,0:T(8,128)S(1)}, u32[]{:S(2)}, u32[]{:S(2)}) collective-permute-start(f32[4,128,128]{2,1,0:T(8,128)S(1)} %get-tuple-element.98.refs_0_), channel_id=1, source_target_pairs={{0,1},{1,0},{2,3},{3,2},{4,5},{5,4},{6,7},{7,6},{8,9},{9,8},{10,11... | collective-permute-start | bytes 786440 | tf_op jit(solution)/shard_map/ppermute | solution.py:210
  77.7 26.0 %collective-permute-start.35 = (f32[4,128,128]{2,1,0:T(8,128)S(1)}, f32[4,128,128]{2,1,0:T(8,128)S(1)}, u32[]{:S(2)}, u32[]{:S(2)}) collective-permute-start(f32[4,128,128]{2,1,0:T(8,128)S(1)} %collective-permute-done.34.refs_2_), channel_id=1, source_target_pairs={{0,1},{1,0},{2,3},{3,2},{4,5},{5,4},{6,7},{7,6},{8,9},{9,8},{10,11... | collective-permute-start | bytes 786440 | tf_op jit(solution)/shard_map/ppermute | solution.py:210
  107.2 12.2 %collective-permute-start.48 = (f32[4,128,128]{2,1,0:T(8,128)S(1)}, f32[4,128,128]{2,1,0:T(8,128)S(1)}, u32[]{:S(2)}, u32[]{:S(2)}) collective-permute-start(f32[4,128,128]{2,1,0:T(8,128)S(1)} %get-tuple-element.114.refs_0_), channel_id=1, source_target_pairs={{0,1},{1,0},{2,3},{3,2},{4,5},{5,4},{6,7},{7,6},{8,9},{9,8},{10,11... | collective-permute-start | bytes 786440 | tf_op jit(solution)/shard_map/ppermute | solution.py:210
  111.1 10.6 %collective-permute-start.50 = (f32[4,128,128]{2,1,0:T(8,128)S(1)}, f32[4,128,128]{2,1,0:T(8,128)S(1)}, u32[]{:S(2)}, u32[]{:S(2)}) collective-permute-start(f32[4,128,128]{2,1,0:T(8,128)S(1)} %collective-permute-done.49.refs_2_), channel_id=1, source_target_pairs={{0,1},{1,0},{2,3},{3,2},{4,5},{5,4},{6,7},{7,6},{8,9},{9,8},{10,11... | collective-permute-start | bytes 786440 | tf_op jit(solution)/shard_map/ppermute | solution.py:210
  111.1 8.0 %collective-permute-start.31 = (f32[128,128]{1,0:T(8,128)S(1)}, f32[128,128]{1,0:T(8,128)S(1)}, u32[]{:S(2)}, u32[]{:S(2)}) collective-permute-start(f32[128,128]{1,0:T(8,128)S(1)} %get-tuple-element.96), channel_id=1, source_target_pairs={{0,8},{1,9},{2,10},{3,11},{4,12},{5,13},{6,14},{7,15},{8,0},{9,1},... | collective-permute-start | bytes 196616 | tf_op jit(solution)/shard_map/ppermute | solution.py:210
  113.8 9.8 %collective-permute-start.32 = (f32[128,128]{1,0:T(8,128)S(1)}, f32[128,128]{1,0:T(8,128)S(1)}, u32[]{:S(2)}, u32[]{:S(2)}) collective-permute-start(f32[128,128]{1,0:T(8,128)S(1)} %get-tuple-element.97), channel_id=1, source_target_pairs={{0,12},{1,13},{2,14},{3,15},{4,8},{5,9},{6,10},{7,11},{8,4},{9,5},... | collective-permute-start | bytes 196616 | tf_op jit(solution)/shard_map/ppermute | solution.py:210
  116.7 8.1 %collective-permute-start.39 = (f32[128,128]{1,0:T(8,128)S(1)}, f32[128,128]{1,0:T(8,128)S(1)}, u32[]{:S(2)}, u32[]{:S(2)}) collective-permute-start(f32[128,128]{1,0:T(8,128)S(1)} %get-tuple-element.104), channel_id=1, source_target_pairs={{0,4},{1,5},{2,6},{3,7},{4,0},{5,1},{6,2},{7,3},{8,12},{9,13},{10,... | collective-permute-start | bytes 196616 | tf_op jit(solution)/shard_map/ppermute | solution.py:210
  119.1 8.0 %collective-permute-start.40 = (f32[128,128]{1,0:T(8,128)S(1)}, f32[128,128]{1,0:T(8,128)S(1)}, u32[]{:S(2)}, u32[]{:S(2)}) collective-permute-start(f32[128,128]{1,0:T(8,128)S(1)} %get-tuple-element.105), channel_id=1, source_target_pairs={{0,8},{1,9},{2,10},{3,11},{4,12},{5,13},{6,14},{7,15},{8,0},{9,1},... | collective-permute-start | bytes 196616 | tf_op jit(solution)/shard_map/ppermute | solution.py:210
  121.7 11.3 %collective-permute-start.45 = (f32[128,128]{1,0:T(8,128)S(1)}, f32[128,128]{1,0:T(8,128)S(1)}, u32[]{:S(2)}, u32[]{:S(2)}) collective-permute-start(f32[128,128]{1,0:T(8,128)S(1)} %get-tuple-element.111), channel_id=1, source_target_pairs={{0,4},{1,5},{2,6},{3,7},{4,0},{5,1},{6,2},{7,3},{8,12},{9,13},{10,... | collective-permute-start | bytes 196616 | tf_op jit(solution)/shard_map/ppermute | solution.py:210
  123.6 13.3 %collective-permute-start.46 = (f32[128,128]{1,0:T(8,128)S(1)}, f32[128,128]{1,0:T(8,128)S(1)}, u32[]{:S(2)}, u32[]{:S(2)}) collective-permute-start(f32[128,128]{1,0:T(8,128)S(1)} %get-tuple-element.112), channel_id=1, source_target_pairs={{0,8},{1,9},{2,10},{3,11},{4,12},{5,13},{6,14},{7,15},{8,0},{9,1},... | collective-permute-start | bytes 196616 | tf_op jit(solution)/shard_map/ppermute | solution.py:210
  124.8 12.1 %collective-permute-start.47 = (f32[128,128]{1,0:T(8,128)S(1)}, f32[128,128]{1,0:T(8,128)S(1)}, u32[]{:S(2)}, u32[]{:S(2)}) collective-permute-start(f32[128,128]{1,0:T(8,128)S(1)} %get-tuple-element.113), channel_id=1, source_target_pairs={{0,12},{1,13},{2,14},{3,15},{4,8},{5,9},{6,10},{7,11},{8,4},{9,5},... | collective-permute-start | bytes 196616 | tf_op jit(solution)/shard_map/ppermute | solution.py:210
  127.1 9.8 %collective-permute-start.51 = (f32[128,128]{1,0:T(8,128)S(1)}, f32[128,128]{1,0:T(8,128)S(1)}, u32[]{:S(2)}, u32[]{:S(2)}) collective-permute-start(f32[128,128]{1,0:T(8,128)S(1)} %get-tuple-element.116), channel_id=1, source_target_pairs={{0,4},{1,5},{2,6},{3,7},{4,0},{5,1},{6,2},{7,3},{8,12},{9,13},{10,... | collective-permute-start | bytes 196616 | tf_op jit(solution)/shard_map/ppermute | solution.py:210
  127.1 9.7 %collective-permute-start.52 = (f32[128,128]{1,0:T(8,128)S(1)}, f32[128,128]{1,0:T(8,128)S(1)}, u32[]{:S(2)}, u32[]{:S(2)}) collective-permute-start(f32[128,128]{1,0:T(8,128)S(1)} %get-tuple-element.117), channel_id=1, source_target_pairs={{0,8},{1,9},{2,10},{3,11},{4,12},{5,13},{6,14},{7,15},{8,0},{9,1},... | collective-permute-start | bytes 196616 | tf_op jit(solution)/shard_map/ppermute | solution.py:210
  (47 other events, 354.1 us)
where the time goes:
time: 150 us
  starting transfers between devices  67.1 us (45%)
  waiting for transfers between devices  57 us (38%)
  Pallas kernels  16.4 us (11%)
  local copies, waits for them, and re-layouts  8.09 us (5%)
    ppermute x60, starting transfers between devices, swap(): return lax.ppermute(x, 'chan', [(i, i ^ bits) for i in range(nd)])  67.1 us
    ppermute x60, waiting for transfers between devices, swap(): return lax.ppermute(x, 'chan', [(i, i ^ bits) for i in range(nd)])  57 us
    pallas_call x14, Pallas kernels, call(): pl.pallas_call(kernel, out_shape=outs, in_specs=[SM] * len(scalars) + (sp...  16.4 us
    unnamed x23, local copies, waits for them, and re-layouts  8.09 us
  transfers between devices with their start and end apart: 60, of which 25 were waited for; matrix products, arithmetic and copies ran while one was open for 1% of the time, Pallas kernels for 10%

commit v1 on v0

v1 whole, which is shorter than its diff:
```python
import functools

import jax
import jax.numpy as jnp
import numpy as np
from jax import lax
from jax.experimental import pallas as pl
from jax.experimental.pallas import tpu as pltpu
from jax.sharding import PartitionSpec as P

JL_MAX = 40
ITERS = 3
TEAM = 4
F32 = jnp.float32
BF16 = jnp.bfloat16
HP = lax.Precision.HIGHEST
VM = pl.BlockSpec(memory_space=pltpu.VMEM)
SM = pl.BlockSpec(memory_space=pltpu.SMEM)
ANY = pl.BlockSpec(memory_space=pl.ANY)


def place(me_ref):
    return me_ref[0] // TEAM, me_ref[0] % TEAM


def rows_of(spot, s, na):
    return pl.ds(pl.multiple_of((spot ^ s) * na, na), na)


def to_pieces_kernel(na, nc, me_ref, x_ref, *outs):
    spot, _ = place(me_ref)
    for s, out in enumerate(outs):
        for c in range(nc):
            out[pl.ds(c, na, stride=nc), :] = x_ref[c, rows_of(spot, s, na), :]


def pack_kernel(n, me_ref, *refs):
    spot, _ = place(me_ref)
    for s in range(n):
        refs[-1][spot ^ s] = refs[s][...]


def kinetic_kernel(na, nc, n, from_pieces, to_pieces, me_ref, quanta, ks, kr, prev, *refs):
    spot, _ = place(me_ref)
    refs = list(refs)
    take = lambda k: [refs.pop(0) for _ in range(k)]
    pieces = take(n) if from_pieces else ()
    cur = None if from_pieces else take(1)[0]
    u_refs = take(n if to_pieces else 1)
    cur = take(1)[0] if from_pieces else cur
    y_ref = refs.pop(0) if to_pieces else u_refs[0]
    nr, nb = prev.shape[1:]
    kstr = 2.0 * ks[...]
    krad = 2.0 * kr[...]
    stretch = 1.0 + lax.broadcasted_iota(jnp.int32, (nr, nb), 0).astype(F32) / nr
    radius = 1.0 + 3.0 * lax.broadcasted_iota(jnp.int32, (nr, nb), 1).astype(F32) / nb
    rotation = 1.0 / (stretch * stretch)
    orbital = 1.0 / (radius * radius)
    scale = np.float32(0.3 / (JL_MAX * (JL_MAX - 1)))
    group = min(8, nc)
    for start in range(0, nc, group):
        chans = range(start, start + group)
        for s, piece in enumerate(pieces):
            for c in chans:
                cur[c, rows_of(spot, s, na), :] = piece[pl.ds(c, na, stride=nc), :]
        tiles = [cur[c] for c in chans]
        mixed_a = jnp.dot(kstr, jnp.concatenate(tiles, 1), precision=HP, preferred_element_type=F32)
        mixed_b = jnp.dot(jnp.concatenate(tiles, 0), krad, precision=HP, preferred_element_type=F32)
        for i, c in enumerate(chans):
            j = quanta[c, 0].astype(F32)
            l = quanta[c, 1].astype(F32)
            barrier = orbital * (scale * (l * (l + 1.0))) + rotation * (scale * (j * (j + 1.0))) - 0.2
            y = mixed_a[:, i * nb : (i + 1) * nb] + mixed_b[i * nr : (i + 1) * nr]
            y_ref[i if to_pieces else c] = y + barrier * tiles[i] - prev[c]
        if to_pieces:
            for s, u in enumerate(u_refs):
                for i, c in enumerate(chans):
                    u[pl.ds(c, na, stride=nc), :] = y_ref[i, rows_of(spot, s, na), :]


def coupling_kernel(cb, nc, n, me_ref, pat_ref, ang_ref, out_ref, buf, sems):
    _, seat = place(me_ref)
    lam, _, tot = ang_ref.shape

    def row(z):
        return (z * TEAM + seat) * nc

    copies = [
        pltpu.make_async_copy(
            ang_ref.at[m, pl.ds(pl.multiple_of(row(z), nc), nc), :], buf.at[m, z], sems.at[m * n + z]
        )
        for m in range(lam)
        for z in range(n)
    ]
    for copy in copies:
        copy.start()
    lane = lax.broadcasted_iota(jnp.int32, (nc, tot), 1) // cb
    for copy in copies:
        copy.wait()
    for z in range(n):
        factor = jnp.zeros((nc, tot), F32)
        for k in range(tot // cb):
            factor = jnp.where(lane == k, pat_ref[row(z) // cb, k].astype(F32), factor)
        for m in range(lam):
            val = buf[m, z] * factor
            hi = val.astype(BF16)
            out_ref[m, 0, z] = hi
            out_ref[m, 1, z] = (val - hi.astype(F32)).astype(BF16)


def mix_kernel(nc, n, mode, me_ref, coup, pot, *refs):
    spot, seat = place(me_ref)
    sources, refs = refs[:TEAM], list(refs[TEAM:])
    take = lambda k: [refs.pop(0) for _ in range(k)]
    us = take(n) if mode == "next" else ()
    pieces = take(n) if mode != "part" else ()
    tmp = refs.pop(0)
    sq = refs.pop(0) if mode == "next" else None
    xs_hi, xs_lo = refs
    _, rows, nb = sources[0].shape
    na, ch = rows // nc, n * nc
    lam, tot = coup.shape[0], coup.shape[-1]
    step = max(1, na // 2)
    for s, u in enumerate(us):
        tmp[spot ^ s] = u[...]
    total = jnp.zeros((8, nb), F32)
    for k0 in range(0, na, step):
        ks = range(k0, k0 + step)
        for m, src in enumerate(sources):
            for z in range(n):
                x = jnp.concatenate([src[z, k * nc : (k + 1) * nc] for k in ks], 1)
                hi = x.astype(BF16)
                xs_hi[z * TEAM + (seat ^ m)] = hi
                xs_lo[z * TEAM + (seat ^ m)] = (x - hi.astype(F32)).astype(BF16)
        x_hi = xs_hi[...].reshape(tot, step * nb)
        x_lo = xs_lo[...].reshape(tot, step * nb)
        acc = None
        for m in range(lam):
            both = coup[m].reshape(2 * ch, tot)
            p = jnp.dot(both, x_hi, preferred_element_type=F32)
            p = p[:ch] + p[ch:] + jnp.dot(both[:ch], x_lo, preferred_element_type=F32)
            w = jnp.concatenate([pot[m, pl.ds(spot * na + k, 1), :] for k in ks], 1)
            p = p * (2.0 * w)
            acc = p if acc is None else acc + p
        for i, k in enumerate(ks):
            y = acc[:, i * nb : (i + 1) * nb].reshape(n, nc, nb)
            if mode == "next":
                y = y + tmp[:, k * nc : (k + 1) * nc]
                total = total + jnp.sum((y * y).reshape(ch // 8, 8, nb), axis=0)
            tmp[:, k * nc : (k + 1) * nc] = y
    for s, piece in enumerate(pieces):
        piece[...] = tmp[spot ^ s]
    if mode == "next":
        sq[...] = total


def join_kernel(n, me_ref, w_ref, *refs):
    spot, _ = place(me_ref)
    us, pieces, (out, sq) = refs[:n], refs[n:-2], refs[-2:]
    nb = w_ref.shape[-1]
    total = jnp.zeros((8, nb), F32)
    for s in range(n):
        y = w_ref[spot ^ s] + us[s][...]
        out[spot ^ s] = y
        pieces[s][...] = y
        total = total + jnp.sum((y * y).reshape(-1, 8, nb), axis=0)
    sq[...] = total


def last_of(na, nc, u_ref, pieces, spot):
    for s, piece in enumerate(pieces):
        at = rows_of(spot, s, na)
        for c in range(nc):
            yield c, at, u_ref[c, at, :] + piece[pl.ds(c, na, stride=nc), :]


def norm_kernel(na, nc, me_ref, s2_ref, s3_ref, u_ref, *refs):
    spot, _ = place(me_ref)
    nb = u_ref.shape[-1]
    total = jnp.zeros((na, nb), F32)
    for _, _, y in last_of(na, nc, u_ref, refs[:-1], spot):
        total = total + y * y
    tiles = [jnp.sum(t, axis=0, keepdims=True) for t in (s2_ref[...], s3_ref[...], total)]
    refs[-1][...] = jnp.concatenate([*tiles, jnp.zeros((8 - ITERS, nb), F32)], 0)


def finish_kernel(na, nc, me_ref, u_ref, *refs):
    spot, _ = place(me_ref)
    for c, at, y in last_of(na, nc, u_ref, refs[:-1], spot):
        refs[-1][c, at, :] = y


def local(x):
    return pltpu.with_memory_space_constraint(x, pltpu.VMEM)


def call(kernel, outs, scalars, arrays, scratch=(), specs=None):
    return pl.pallas_call(
        kernel,
        out_shape=outs,
        in_specs=[SM] * len(scalars) + (specs or [VM] * len(arrays)),
        out_specs=[VM] * len(outs),
        scratch_shapes=list(scratch),
        compiler_params=pltpu.CompilerParams(vmem_limit_bytes=20 << 20),
        cost_estimate=pl.CostEstimate(flops=0, bytes_accessed=1 << 16, transcendentals=0),
    )(*scalars, *arrays)


def per_device(psi_prev, psi_cur, kin_stretch, kin_radius, potential, angular, pattern, quanta):
    nc, nr, nb = psi_cur.shape
    lam = potential.shape[0]
    nd = lax.axis_size("chan")
    n = nd // TEAM
    na = nr // n
    total_ch = nc * nd
    cb = total_ch // pattern.shape[1]
    me = lax.axis_index("chan").astype(jnp.int32).reshape(1)
    sds = jax.ShapeDtypeStruct

    def swap(x, bits):
        return lax.ppermute(x, "chan", [(i, i ^ bits) for i in range(nd)])

    def across(x, bits):
        return local(swap(x, bits))

    def exchange(pieces):
        return [across(x, s * TEAM) if s else x for s, x in enumerate(pieces)]

    def gather(x, first):
        over = lax.optimization_barrier((swap(x, 2), *first))[0]
        return [x, across(x, 1), local(over), across(over, 1)]

    piece = pltpu.VMEM((na * nc, nb), F32)
    packed = pltpu.VMEM((n, na * nc, nb), F32)
    square = pltpu.VMEM((8, nb), F32)
    on_chip = pltpu.VMEM((nc, nr, nb), F32)
    natural = sds((nc, nr, nb), F32)
    split = pltpu.VMEM((nd, nc, max(1, na // 2) * nb), BF16)

    def kinetic(prev, cur, from_pieces, to_pieces, out=None):
        outs = ([piece] * n if to_pieces else [on_chip]) + ([out] if from_pieces else [])
        scratch = [pltpu.VMEM((min(8, nc), nr, nb), F32)] if to_pieces else []
        kernel = functools.partial(kinetic_kernel, na, nc, n, from_pieces, to_pieces)
        return call(kernel, outs, [me, quanta], [kin_stretch, kin_radius, prev, *cur], scratch)

    def mix(mode, v, beside, u=()):
        outs = [] if mode == "part" else [piece] * n
        outs += [] if mode == "last" else [packed]
        outs += [square] if mode == "next" else []
        scratch = ([packed] if mode == "last" else []) + [split, split]
        return call(
            functools.partial(mix_kernel, nc, n, mode), outs, [me], [coup, potential, *gather(v, beside), *u], scratch
        )

    (coup,) = call(
        functools.partial(coupling_kernel, cb, nc, n),
        [pltpu.VMEM((lam, 2, n, nc, total_ch), BF16)],
        [me, pattern],
        [angular],
        [pltpu.VMEM((lam, n, nc, total_ch), F32), pltpu.SemaphoreType.DMA((lam * n,))],
        [pl.BlockSpec(memory_space=pltpu.HBM)],
    )
    pieces = exchange(call(functools.partial(to_pieces_kernel, na, nc), [piece] * n, [me], [psi_cur]))
    u1 = kinetic(psi_prev, [psi_cur], False, True)
    (v1,) = call(
        functools.partial(pack_kernel, n), [packed], [me], [*pieces, coup, u1[0]], (), [VM] * n + [ANY] * 2
    )
    u1 = exchange(u1)
    *pieces, v2, s2 = mix("next", v1, u1[1:], u1)
    pieces = exchange(pieces)
    *u2, v2_nat = kinetic(psi_cur, pieces, True, True, on_chip)
    (w2,) = mix("part", v2, pieces[1:])
    *pieces, v3, s3 = call(
        functools.partial(join_kernel, n), [piece] * n + [packed, square], [me], [w2, *exchange(u2)]
    )
    pieces = exchange(pieces)
    u3, prev_out = kinetic(v2_nat, pieces, True, False, natural)
    pieces = exchange(mix("last", v3, pieces[1:]))
    (sums,) = call(functools.partial(norm_kernel, na, nc), [sds((8, nb), F32)], [me], [s2, s3, u3, *pieces])
    (cur_out,) = call(functools.partial(finish_kernel, na, nc), [natural], [me], [u3, *pieces])
    bit = 1
    while bit < nd:
        sums = (sums + swap(sums, bit)) + (swap(sums, 2 * bit) + swap(sums, 3 * bit))
        bit *= 4
    norms = jnp.sum(sums[:ITERS], axis=1) / (total_ch * nr * nb)
    return prev_out, cur_out, norms


def solution(mesh):
    return jax.shard_map(
        per_device,
        mesh=mesh,
        in_specs=(
            P(("groups", "chan"), None, None),
            P(("groups", "chan"), None, None),
            P(),
            P(),
            P(),
            P("groups", None, None),
            P("groups", None),
            P(("groups", "chan"), None),
        ),
        out_specs=(
            P(("groups", "chan"), None, None),
            P(("groups", "chan"), None, None),
            P("groups"),
        ),
        check_vma=False,
    )
```

time: 150 us -> 117 us (0.78)
  starting transfers between devices: 67.1 us -> 38.6 us
  local copies, waits for them, and re-layouts: 8.09 us -> 4.39 us
    ppermute x60 -> x33, starting transfers between devices: 67.1 us -> 38.6 us  [swap(): return lax.ppermute(x, 'chan', [(i, i ^ bits) for i in range(nd)])]
    unnamed x23 -> x17, local copies, waits for them, and re-layouts: 8.09 us -> 4.39 us
    ppermute x60 -> x33, waiting for transfers between devices: 57 us -> 56.4 us  [swap(): return lax.ppermute(x, 'chan', [(i, i ^ bits) for i in range(nd)])]
    pallas_call x14 -> x12, Pallas kernels: 16.4 us -> 15.9 us  [call(): pl.pallas_call(kernel, out_shape=outs, in_specs=[SM] * len(scalars) + (sp...]
  transfers between devices with their start and end apart: 60 -> 33, of which waited for: 25 -> 17; matrix products, arithmetic and copies ran while one was open for 1% -> 1% of each run, Pallas kernels for 10% -> 10%
where the time goes in v1:
time: 117 us
  waiting for transfers between devices  56.4 us (48%)
  starting transfers between devices  38.6 us (33%)
  Pallas kernels  15.9 us (14%)
  local copies, waits for them, and re-layouts  4.39 us (4%)
    ppermute x33, waiting for transfers between devices, swap(): return lax.ppermute(x, 'chan', [(i, i ^ bits) for i in range(nd)])  56.4 us
    ppermute x33, starting transfers between devices, swap(): return lax.ppermute(x, 'chan', [(i, i ^ bits) for i in range(nd)])  38.6 us
    pallas_call x12, Pallas kernels, call(): pl.pallas_call(kernel, out_shape=outs, in_specs=[SM] * len(scalars) + (sp...  15.9 us
    unnamed x17, local copies, waits for them, and re-layouts  4.39 us
  transfers between devices with their start and end apart: 33, of which 17 were waited for; matrix products, arithmetic and copies ran while one was open for 1% of the time, Pallas kernels for 10%

profile of v1, /device:TPU:0, one launch (start us, length us, event | category | flops | bytes accessed | tf_op | source)
XLA Modules:
  0.0 116.9 jit_solution(9278362464126457172)
XLA Ops:
  2.0 3.1 %collective-permute-start = (f32[256,128]{1,0:T(8,128)S(1)}, f32[256,128]{1,0:T(8,128)S(1)}, u32[]{:S(2)}, u32[]{:S(2)}) collective-permute-start(f32[256,128]{1,0:T(8,128)S(1)} %get-tuple-element.38), channel_id=1, source_target_pairs={{0,4},{1,5},{2,6},{3,7},{4,0},{5,1},{6,2},{7,3},{8,12},{9,13},{10,... | collective-permute-start | bytes 393224 | tf_op jit(solution)/shard_map/ppermute | solution.py:221
  5.1 2.6 %collective-permute-start.1 = (f32[256,128]{1,0:T(8,128)S(1)}, f32[256,128]{1,0:T(8,128)S(1)}, u32[]{:S(2)}, u32[]{:S(2)}) collective-permute-start(f32[256,128]{1,0:T(8,128)S(1)} %get-tuple-element.39), channel_id=1, source_target_pairs={{0,8},{1,9},{2,10},{3,11},{4,12},{5,13},{6,14},{7,15},{8,0},{9,1},... | collective-permute-start | bytes 393224 | tf_op jit(solution)/shard_map/ppermute | solution.py:221
  8.4 1.9 %copy-done.2 = f32[3,512,512]{2,1,0:T(8,128)S(1)} copy-done((f32[3,512,512]{2,1,0:T(8,128)S(1)}, f32[3,512,512]{2,1,0:T(8,128)}, u32[]{:S(2)}) %copy-start.2) | copy-done | bytes 3145752
  11.0 1.9 %shard_map.103.refs_4_.coup = bf16[3,2,4,32,512]{4,3,2,1,0:T(8,128)(2,1)S(1)} custom-call(s32[1]{0:T(128)} %bitcast.me_ref, s32[8,8]{1,0:T(8,128)S(1)} %copy-done.7, f32[3,512,512]{2,1,0:T(8,128)S(1)} %copy-done.2), custom_call_target="tpu_custom_call" | custom-call | bytes 65536 | tf_op jit(solution)/shard_map/pallas_call | solution.py:198
  13.0 2.2 %shard_map.105 = (f32[256,128]{1,0:T(8,128)S(1)}, f32[256,128]{1,0:T(8,128)S(1)}, f32[256,128]{1,0:T(8,128)S(1)}, f32[256,128]{1,0:T(8,128)S(1)}) custom-call(s32[1]{0:T(128)} %bitcast.me_ref, s32[32,2]{1,0:T(8,128)S(1)} %copy.13.quanta, f32[32,32]{1,0:T(8,128)S(1)} %copy-done.6, f32[128,128]{1,0:T(8,128)S(1)} %copy-done.3, f32[32,32,128]{2,1,0:T(8,128)S(1)} %copy-done.4, ...), custom_call_target="tpu_custom_call" | custom-call | bytes 65536 | tf_op jit(solution)/shard_map/pallas_call | solution.py:198
  15.2 2.9 %collective-permute-done.1.refs_2_ = f32[256,128]{1,0:T(8,128)S(1)} collective-permute-done((f32[256,128]{1,0:T(8,128)S(1)}, f32[256,128]{1,0:T(8,128)S(1)}, u32[]{:S(2)}, u32[]{:S(2)}) %collective-permute-start.1) | collective-permute-done | bytes 131104 | tf_op jit(solution)/shard_map/ppermute | solution.py:221
  19.7 2.0 %collective-permute-start.5 = (f32[256,128]{1,0:T(8,128)S(1)}, f32[256,128]{1,0:T(8,128)S(1)}, u32[]{:S(2)}, u32[]{:S(2)}) collective-permute-start(f32[256,128]{1,0:T(8,128)S(1)} %get-tuple-element.42), channel_id=1, source_target_pairs={{0,4},{1,5},{2,6},{3,7},{4,0},{5,1},{6,2},{7,3},{8,12},{9,13},{10,... | collective-permute-start | bytes 393224 | tf_op jit(solution)/shard_map/ppermute | solution.py:221
  25.8 7.3 %collective-permute-done.6.refs_6_ = f32[256,128]{1,0:T(8,128)S(1)} collective-permute-done((f32[256,128]{1,0:T(8,128)S(1)}, f32[256,128]{1,0:T(8,128)S(1)}, u32[]{:S(2)}, u32[]{:S(2)}) %collective-permute-start.6) | collective-permute-done | bytes 131104 | tf_op jit(solution)/shard_map/ppermute | solution.py:221
  33.1 1.9 %collective-permute-done.8.refs_3_ = f32[4,256,128]{2,1,0:T(8,128)S(1)} collective-permute-done((f32[4,256,128]{2,1,0:T(8,128)S(1)}, f32[4,256,128]{2,1,0:T(8,128)S(1)}, u32[]{:S(2)}, u32[]{:S(2)}) %collective-permute-start.8) | collective-permute-done | bytes 524320 | tf_op jit(solution)/shard_map/ppermute | solution.py:221
  35.0 1.8 %shard_map.107 = (f32[256,128]{1,0:T(8,128)S(1)}, f32[256,128]{1,0:T(8,128)S(1)}, f32[256,128]{1,0:T(8,128)S(1)}, f32[256,128]{1,0:T(8,128)S(1)}, f32[4,256,128]{2,1,0:T(8,128)S(1)}, /*index=5*/f32[8,128]{1,0:T(8,128)S(1)}) custom-call(s32[1]{0:T(128)} %bitcast.me_ref, bf16[3,2,4,32,512]{4,3,2,1,0:T(8,128)(2,1)S(1)} %shard_map.103.refs_4_.coup, ...), custom_call_target="tpu_custom_call" | custom-call | bytes 65536 | tf_op jit(solution)/shard_map/pallas_call | solution.py:198
  37.4 2.0 %collective-permute-start.9 = (f32[256,128]{1,0:T(8,128)S(1)}, f32[256,128]{1,0:T(8,128)S(1)}, u32[]{:S(2)}, u32[]{:S(2)}) collective-permute-start(f32[256,128]{1,0:T(8,128)S(1)} %get-tuple-element.47), channel_id=1, source_target_pairs={{0,4},{1,5},{2,6},{3,7},{4,0},{5,1},{6,2},{7,3},{8,12},{9,13},{10,... | collective-permute-start | bytes 393224 | tf_op jit(solution)/shard_map/ppermute | solution.py:221
  41.8 2.6 %collective-permute-done.9.refs_1_ = f32[256,128]{1,0:T(8,128)S(1)} collective-permute-done((f32[256,128]{1,0:T(8,128)S(1)}, f32[256,128]{1,0:T(8,128)S(1)}, u32[]{:S(2)}, u32[]{:S(2)}) %collective-permute-start.9) | collective-permute-done | bytes 131104 | tf_op jit(solution)/shard_map/ppermute | solution.py:221
  44.4 7.9 %collective-permute-done.10.refs_2_ = f32[256,128]{1,0:T(8,128)S(1)} collective-permute-done((f32[256,128]{1,0:T(8,128)S(1)}, f32[256,128]{1,0:T(8,128)S(1)}, u32[]{:S(2)}, u32[]{:S(2)}) %collective-permute-start.10) | collective-permute-done | bytes 131104 | tf_op jit(solution)/shard_map/ppermute | solution.py:221
  52.3 2.3 %shard_map.108 = (f32[256,128]{1,0:T(8,128)S(1)}, f32[256,128]{1,0:T(8,128)S(1)}, f32[256,128]{1,0:T(8,128)S(1)}, f32[256,128]{1,0:T(8,128)S(1)}, f32[32,32,128]{2,1,0:T(8,128)S(1)}) custom-call(s32[1]{0:T(128)} %bitcast.me_ref, s32[32,2]{1,0:T(8,128)S(1)} %copy.13.quanta, f32[32,32]{1,0:T(8,128)S(1)} %copy-done.6, f32[128,128]{1,0:T(8,128)S(1)} %copy-done.3, ...), custom_call_target="tpu_custom_call" | custom-call | bytes 65536 | tf_op jit(solution)/shard_map/pallas_call | solution.py:198
  54.6 2.0 %collective-permute-start.15 = (f32[256,128]{1,0:T(8,128)S(1)}, f32[256,128]{1,0:T(8,128)S(1)}, u32[]{:S(2)}, u32[]{:S(2)}) collective-permute-start(f32[256,128]{1,0:T(8,128)S(1)} %get-tuple-element.54), channel_id=1, source_target_pairs={{0,4},{1,5},{2,6},{3,7},{4,0},{5,1},{6,2},{7,3},{8,12},{9,13},{10,... | collective-permute-start | bytes 393224 | tf_op jit(solution)/shard_map/ppermute | solution.py:221
  60.8 2.3 %collective-permute-done.15.refs_1_ = f32[256,128]{1,0:T(8,128)S(1)} collective-permute-done((f32[256,128]{1,0:T(8,128)S(1)}, f32[256,128]{1,0:T(8,128)S(1)}, u32[]{:S(2)}, u32[]{:S(2)}) %collective-permute-start.15) | collective-permute-done | bytes 131104 | tf_op jit(solution)/shard_map/ppermute | solution.py:221
  63.0 6.5 %collective-permute-done.16.refs_2_ = f32[256,128]{1,0:T(8,128)S(1)} collective-permute-done((f32[256,128]{1,0:T(8,128)S(1)}, f32[256,128]{1,0:T(8,128)S(1)}, u32[]{:S(2)}, u32[]{:S(2)}) %collective-permute-start.16) | collective-permute-done | bytes 131104 | tf_op jit(solution)/shard_map/ppermute | solution.py:221
  71.2 2.7 %collective-permute-start.18 = (f32[256,128]{1,0:T(8,128)S(1)}, f32[256,128]{1,0:T(8,128)S(1)}, u32[]{:S(2)}, u32[]{:S(2)}) collective-permute-start(f32[256,128]{1,0:T(8,128)S(1)} %get-tuple-element.58), channel_id=1, source_target_pairs={{0,4},{1,5},{2,6},{3,7},{4,0},{5,1},{6,2},{7,3},{8,12},{9,13},{10,... | collective-permute-start | bytes 393224 | tf_op jit(solution)/shard_map/ppermute | solution.py:221
  78.0 8.1 %collective-permute-done.19.refs_2_ = f32[256,128]{1,0:T(8,128)S(1)} collective-permute-done((f32[256,128]{1,0:T(8,128)S(1)}, f32[256,128]{1,0:T(8,128)S(1)}, u32[]{:S(2)}, u32[]{:S(2)}) %collective-permute-start.19) | collective-permute-done | bytes 131104 | tf_op jit(solution)/shard_map/ppermute | solution.py:221
  86.1 1.9 %collective-permute-done.23.refs_3_ = f32[4,256,128]{2,1,0:T(8,128)S(1)} collective-permute-done((f32[4,256,128]{2,1,0:T(8,128)S(1)}, f32[4,256,128]{2,1,0:T(8,128)S(1)}, u32[]{:S(2)}, u32[]{:S(2)}) %collective-permute-start.23) | collective-permute-done | bytes 524320 | tf_op jit(solution)/shard_map/ppermute | solution.py:221
  89.7 2.1 %collective-permute-start.24 = (f32[256,128]{1,0:T(8,128)S(1)}, f32[256,128]{1,0:T(8,128)S(1)}, u32[]{:S(2)}, u32[]{:S(2)}) collective-permute-start(f32[256,128]{1,0:T(8,128)S(1)} %get-tuple-element.66), channel_id=1, source_target_pairs={{0,4},{1,5},{2,6},{3,7},{4,0},{5,1},{6,2},{7,3},{8,12},{9,13},{10,... | collective-permute-start | bytes 393224 | tf_op jit(solution)/shard_map/ppermute | solution.py:221
  94.2 2.5 %shard_map.111 = (f32[32,32,128]{2,1,0:T(8,128)S(1)}, f32[32,32,128]{2,1,0:T(8,128)}) custom-call(s32[1]{0:T(128)} %bitcast.me_ref, s32[32,2]{1,0:T(8,128)S(1)} %copy.13.quanta, f32[32,32]{1,0:T(8,128)S(1)} %copy-done.6, f32[128,128]{1,0:T(8,128)S(1)} %copy-done.3, f32[32,32,128]{2,1,0:T(8,128)S(1)} %get-tuple-element.50.prev, ...), custom_call_target="tpu_custom_call" | custom-call | bytes 65536 | tf_op jit(solution)/shard_map/pallas_call | solution.py:198
  97.4 7.3 %collective-permute-done.25.refs_2_ = f32[256,128]{1,0:T(8,128)S(1)} collective-permute-done((f32[256,128]{1,0:T(8,128)S(1)}, f32[256,128]{1,0:T(8,128)S(1)}, u32[]{:S(2)}, u32[]{:S(2)}) %collective-permute-start.25) | collective-permute-done | bytes 131104 | tf_op jit(solution)/shard_map/ppermute | solution.py:221
  108.8 2.2 %collective-permute-start.32 = (f32[8,128]{1,0:T(8,128)S(1)}, f32[8,128]{1,0:T(8,128)S(1)}, u32[]{:S(2)}, u32[]{:S(2)}) collective-permute-start(f32[8,128]{1,0:T(8,128)S(1)} %add_add_fusion.1), channel_id=1, source_target_pairs={{0,12},{1,13},{2,14},{3,15},{4,8},{5,9},{6,10},{7,11},{8,4},{9,5},... | collective-permute-start | bytes 12296 | tf_op jit(solution)/shard_map/ppermute | solution.py:221
  (75 shorter events, 36.3 us)
Async XLA Ops:
  2.0 13.1 %collective-permute-start = (f32[256,128]{1,0:T(8,128)S(1)}, f32[256,128]{1,0:T(8,128)S(1)}, u32[]{:S(2)}, u32[]{:S(2)}) collective-permute-start(f32[256,128]{1,0:T(8,128)S(1)} %get-tuple-element.38), channel_id=1, source_target_pairs={{0,4},{1,5},{2,6},{3,7},{4,0},{5,1},{6,2},{7,3},{8,12},{9,13},{10,... | collective-permute-start | bytes 393224 | tf_op jit(solution)/shard_map/ppermute | solution.py:221
  5.1 12.9 %collective-permute-start.1 = (f32[256,128]{1,0:T(8,128)S(1)}, f32[256,128]{1,0:T(8,128)S(1)}, u32[]{:S(2)}, u32[]{:S(2)}) collective-permute-start(f32[256,128]{1,0:T(8,128)S(1)} %get-tuple-element.39), channel_id=1, source_target_pairs={{0,8},{1,9},{2,10},{3,11},{4,12},{5,13},{6,14},{7,15},{8,0},{9,1},... | collective-permute-start | bytes 393224 | tf_op jit(solution)/shard_map/ppermute | solution.py:221
  7.7 10.3 %collective-permute-start.2 = (f32[256,128]{1,0:T(8,128)S(1)}, f32[256,128]{1,0:T(8,128)S(1)}, u32[]{:S(2)}, u32[]{:S(2)}) collective-permute-start(f32[256,128]{1,0:T(8,128)S(1)} %get-tuple-element.40), channel_id=1, source_target_pairs={{0,12},{1,13},{2,14},{3,15},{4,8},{5,9},{6,10},{7,11},{8,4},{9,5},... | collective-permute-start | bytes 393224 | tf_op jit(solution)/shard_map/ppermute | solution.py:221
  18.1 15.0 %collective-permute-start.4 = (f32[4,256,128]{2,1,0:T(8,128)S(1)}, f32[4,256,128]{2,1,0:T(8,128)S(1)}, u32[]{:S(2)}, u32[]{:S(2)}) collective-permute-start(f32[4,256,128]{2,1,0:T(8,128)S(1)} %shard_map.106.refs_0_), channel_id=1, source_target_pairs={{0,2},{1,3},{2,0},{3,1},{4,6},{5,7},{6,4},{7,5},{8,10},{9,11},{10,... | collective-permute-start | bytes 1572872 | tf_op jit(solution)/shard_map/ppermute | solution.py:221
  21.6 11.5 %collective-permute-start.6 = (f32[256,128]{1,0:T(8,128)S(1)}, f32[256,128]{1,0:T(8,128)S(1)}, u32[]{:S(2)}, u32[]{:S(2)}) collective-permute-start(f32[256,128]{1,0:T(8,128)S(1)} %get-tuple-element.43), channel_id=1, source_target_pairs={{0,8},{1,9},{2,10},{3,11},{4,12},{5,13},{6,14},{7,15},{8,0},{9,1},... | collective-permute-start | bytes 393224 | tf_op jit(solution)/shard_map/ppermute | solution.py:221
  22.6 10.5 %collective-permute-start.7 = (f32[256,128]{1,0:T(8,128)S(1)}, f32[256,128]{1,0:T(8,128)S(1)}, u32[]{:S(2)}, u32[]{:S(2)}) collective-permute-start(f32[256,128]{1,0:T(8,128)S(1)} %get-tuple-element.44), channel_id=1, source_target_pairs={{0,12},{1,13},{2,14},{3,15},{4,8},{5,9},{6,10},{7,11},{8,4},{9,5},... | collective-permute-start | bytes 393224 | tf_op jit(solution)/shard_map/ppermute | solution.py:221
  24.1 9.0 %collective-permute-start.3 = (f32[4,256,128]{2,1,0:T(8,128)S(1)}, f32[4,256,128]{2,1,0:T(8,128)S(1)}, u32[]{:S(2)}, u32[]{:S(2)}) collective-permute-start(f32[4,256,128]{2,1,0:T(8,128)S(1)} %shard_map.106.refs_0_), channel_id=1, source_target_pairs={{0,1},{1,0},{2,3},{3,2},{4,5},{5,4},{6,7},{7,6},{8,9},{9,8},{10,11... | collective-permute-start | bytes 1572872 | tf_op jit(solution)/shard_map/ppermute | solution.py:221
  36.8 15.5 %collective-permute-start.13 = (f32[4,256,128]{2,1,0:T(8,128)S(1)}, f32[4,256,128]{2,1,0:T(8,128)S(1)}, u32[]{:S(2)}, u32[]{:S(2)}) collective-permute-start(f32[4,256,128]{2,1,0:T(8,128)S(1)} %get-tuple-element.51.refs_0_), channel_id=1, source_target_pairs={{0,2},{1,3},{2,0},{3,1},{4,6},{5,7},{6,4},{7,5},{8,10},{9,11},{10,... | collective-permute-start | bytes 1572872 | tf_op jit(solution)/shard_map/ppermute | solution.py:221
  37.4 7.0 %collective-permute-start.9 = (f32[256,128]{1,0:T(8,128)S(1)}, f32[256,128]{1,0:T(8,128)S(1)}, u32[]{:S(2)}, u32[]{:S(2)}) collective-permute-start(f32[256,128]{1,0:T(8,128)S(1)} %get-tuple-element.47), channel_id=1, source_target_pairs={{0,4},{1,5},{2,6},{3,7},{4,0},{5,1},{6,2},{7,3},{8,12},{9,13},{10,... | collective-permute-start | bytes 393224 | tf_op jit(solution)/shard_map/ppermute | solution.py:221
  39.4 12.9 %collective-permute-start.10 = (f32[256,128]{1,0:T(8,128)S(1)}, f32[256,128]{1,0:T(8,128)S(1)}, u32[]{:S(2)}, u32[]{:S(2)}) collective-permute-start(f32[256,128]{1,0:T(8,128)S(1)} %get-tuple-element.48), channel_id=1, source_target_pairs={{0,8},{1,9},{2,10},{3,11},{4,12},{5,13},{6,14},{7,15},{8,0},{9,1},... | collective-permute-start | bytes 393224 | tf_op jit(solution)/shard_map/ppermute | solution.py:221
  40.3 12.0 %collective-permute-start.11 = (f32[256,128]{1,0:T(8,128)S(1)}, f32[256,128]{1,0:T(8,128)S(1)}, u32[]{:S(2)}, u32[]{:S(2)}) collective-permute-start(f32[256,128]{1,0:T(8,128)S(1)} %get-tuple-element.49), channel_id=1, source_target_pairs={{0,12},{1,13},{2,14},{3,15},{4,8},{5,9},{6,10},{7,11},{8,4},{9,5},... | collective-permute-start | bytes 393224 | tf_op jit(solution)/shard_map/ppermute | solution.py:221
  41.8 17.3 %collective-permute-start.12 = (f32[4,256,128]{2,1,0:T(8,128)S(1)}, f32[4,256,128]{2,1,0:T(8,128)S(1)}, u32[]{:S(2)}, u32[]{:S(2)}) collective-permute-start(f32[4,256,128]{2,1,0:T(8,128)S(1)} %get-tuple-element.51.refs_0_), channel_id=1, source_target_pairs={{0,1},{1,0},{2,3},{3,2},{4,5},{5,4},{6,7},{7,6},{8,9},{9,8},{10,11... | collective-permute-start | bytes 1572872 | tf_op jit(solution)/shard_map/ppermute | solution.py:221
  52.3 6.8 %collective-permute-start.14 = (f32[4,256,128]{2,1,0:T(8,128)S(1)}, f32[4,256,128]{2,1,0:T(8,128)S(1)}, u32[]{:S(2)}, u32[]{:S(2)}) collective-permute-start(f32[4,256,128]{2,1,0:T(8,128)S(1)} %collective-permute-done.13.refs_2_), channel_id=1, source_target_pairs={{0,1},{1,0},{2,3},{3,2},{4,5},{5,4},{6,7},{7,6},{8,9},{9,8},{10,11... | collective-permute-start | bytes 1572872 | tf_op jit(solution)/shard_map/ppermute | solution.py:221
  54.6 8.4 %collective-permute-start.15 = (f32[256,128]{1,0:T(8,128)S(1)}, f32[256,128]{1,0:T(8,128)S(1)}, u32[]{:S(2)}, u32[]{:S(2)}) collective-permute-start(f32[256,128]{1,0:T(8,128)S(1)} %get-tuple-element.54), channel_id=1, source_target_pairs={{0,4},{1,5},{2,6},{3,7},{4,0},{5,1},{6,2},{7,3},{8,12},{9,13},{10,... | collective-permute-start | bytes 393224 | tf_op jit(solution)/shard_map/ppermute | solution.py:221
  56.6 12.9 %collective-permute-start.16 = (f32[256,128]{1,0:T(8,128)S(1)}, f32[256,128]{1,0:T(8,128)S(1)}, u32[]{:S(2)}, u32[]{:S(2)}) collective-permute-start(f32[256,128]{1,0:T(8,128)S(1)} %get-tuple-element.55), channel_id=1, source_target_pairs={{0,8},{1,9},{2,10},{3,11},{4,12},{5,13},{6,14},{7,15},{8,0},{9,1},... | collective-permute-start | bytes 393224 | tf_op jit(solution)/shard_map/ppermute | solution.py:221
  57.6 12.0 %collective-permute-start.17 = (f32[256,128]{1,0:T(8,128)S(1)}, f32[256,128]{1,0:T(8,128)S(1)}, u32[]{:S(2)}, u32[]{:S(2)}) collective-permute-start(f32[256,128]{1,0:T(8,128)S(1)} %get-tuple-element.56), channel_id=1, source_target_pairs={{0,12},{1,13},{2,14},{3,15},{4,8},{5,9},{6,10},{7,11},{8,4},{9,5},... | collective-permute-start | bytes 393224 | tf_op jit(solution)/shard_map/ppermute | solution.py:221
  69.6 16.4 %collective-permute-start.22 = (f32[4,256,128]{2,1,0:T(8,128)S(1)}, f32[4,256,128]{2,1,0:T(8,128)S(1)}, u32[]{:S(2)}, u32[]{:S(2)}) collective-permute-start(f32[4,256,128]{2,1,0:T(8,128)S(1)} %get-tuple-element.63.refs_0_), channel_id=1, source_target_pairs={{0,2},{1,3},{2,0},{3,1},{4,6},{5,7},{6,4},{7,5},{8,10},{9,11},{10,... | collective-permute-start | bytes 1572872 | tf_op jit(solution)/shard_map/ppermute | solution.py:221
  71.2 6.7 %collective-permute-start.18 = (f32[256,128]{1,0:T(8,128)S(1)}, f32[256,128]{1,0:T(8,128)S(1)}, u32[]{:S(2)}, u32[]{:S(2)}) collective-permute-start(f32[256,128]{1,0:T(8,128)S(1)} %get-tuple-element.58), channel_id=1, source_target_pairs={{0,4},{1,5},{2,6},{3,7},{4,0},{5,1},{6,2},{7,3},{8,12},{9,13},{10,... | collective-permute-start | bytes 393224 | tf_op jit(solution)/shard_map/ppermute | solution.py:221
  73.9 12.2 %collective-permute-start.19 = (f32[256,128]{1,0:T(8,128)S(1)}, f32[256,128]{1,0:T(8,128)S(1)}, u32[]{:S(2)}, u32[]{:S(2)}) collective-permute-start(f32[256,128]{1,0:T(8,128)S(1)} %get-tuple-element.59), channel_id=1, source_target_pairs={{0,8},{1,9},{2,10},{3,11},{4,12},{5,13},{6,14},{7,15},{8,0},{9,1},... | collective-permute-start | bytes 393224 | tf_op jit(solution)/shard_map/ppermute | solution.py:221
  74.8 11.3 %collective-permute-start.20 = (f32[256,128]{1,0:T(8,128)S(1)}, f32[256,128]{1,0:T(8,128)S(1)}, u32[]{:S(2)}, u32[]{:S(2)}) collective-permute-start(f32[256,128]{1,0:T(8,128)S(1)} %get-tuple-element.60), channel_id=1, source_target_pairs={{0,12},{1,13},{2,14},{3,15},{4,8},{5,9},{6,10},{7,11},{8,4},{9,5},... | collective-permute-start | bytes 393224 | tf_op jit(solution)/shard_map/ppermute | solution.py:221
  76.3 9.8 %collective-permute-start.21 = (f32[4,256,128]{2,1,0:T(8,128)S(1)}, f32[4,256,128]{2,1,0:T(8,128)S(1)}, u32[]{:S(2)}, u32[]{:S(2)}) collective-permute-start(f32[4,256,128]{2,1,0:T(8,128)S(1)} %get-tuple-element.63.refs_0_), channel_id=1, source_target_pairs={{0,1},{1,0},{2,3},{3,2},{4,5},{5,4},{6,7},{7,6},{8,9},{9,8},{10,11... | collective-permute-start | bytes 1572872 | tf_op jit(solution)/shard_map/ppermute | solution.py:221
  89.7 7.7 %collective-permute-start.24 = (f32[256,128]{1,0:T(8,128)S(1)}, f32[256,128]{1,0:T(8,128)S(1)}, u32[]{:S(2)}, u32[]{:S(2)}) collective-permute-start(f32[256,128]{1,0:T(8,128)S(1)} %get-tuple-element.66), channel_id=1, source_target_pairs={{0,4},{1,5},{2,6},{3,7},{4,0},{5,1},{6,2},{7,3},{8,12},{9,13},{10,... | collective-permute-start | bytes 393224 | tf_op jit(solution)/shard_map/ppermute | solution.py:221
  91.8 12.9 %collective-permute-start.25 = (f32[256,128]{1,0:T(8,128)S(1)}, f32[256,128]{1,0:T(8,128)S(1)}, u32[]{:S(2)}, u32[]{:S(2)}) collective-permute-start(f32[256,128]{1,0:T(8,128)S(1)} %get-tuple-element.67), channel_id=1, source_target_pairs={{0,8},{1,9},{2,10},{3,11},{4,12},{5,13},{6,14},{7,15},{8,0},{9,1},... | collective-permute-start | bytes 393224 | tf_op jit(solution)/shard_map/ppermute | solution.py:221
  92.7 12.0 %collective-permute-start.26 = (f32[256,128]{1,0:T(8,128)S(1)}, f32[256,128]{1,0:T(8,128)S(1)}, u32[]{:S(2)}, u32[]{:S(2)}) collective-permute-start(f32[256,128]{1,0:T(8,128)S(1)} %get-tuple-element.68), channel_id=1, source_target_pairs={{0,12},{1,13},{2,14},{3,15},{4,8},{5,9},{6,10},{7,11},{8,4},{9,5},... | collective-permute-start | bytes 393224 | tf_op jit(solution)/shard_map/ppermute | solution.py:221
  (17 other events, 87.5 us)

commit v2 on v1

v2 whole, which is shorter than its diff:
```python
import functools

import jax
import jax.numpy as jnp
import numpy as np
from jax import lax
from jax.experimental import pallas as pl
from jax.experimental.pallas import tpu as pltpu
from jax.sharding import PartitionSpec as P

JL_MAX = 40
ITERS = 3
TEAM = 4
F32 = jnp.float32
BF16 = jnp.bfloat16
HP = lax.Precision.HIGHEST
VM = pl.BlockSpec(memory_space=pltpu.VMEM)
SM = pl.BlockSpec(memory_space=pltpu.SMEM)
ANY = pl.BlockSpec(memory_space=pl.ANY)


def hop(i, n):
    return i % (n - 1) + 1 if i else 0


def place(me_ref):
    return me_ref[0] // TEAM, me_ref[0] % TEAM


def rows_of(spot, s, n, na):
    return pl.ds(pl.multiple_of((spot ^ hop(s, n)) * na, na), na)


def to_pieces_kernel(na, nc, me_ref, x_ref, *outs):
    spot, _ = place(me_ref)
    for s, out in enumerate(outs):
        for c in range(nc):
            out[pl.ds(c, na, stride=nc), :] = x_ref[c, rows_of(spot, s, len(outs), na), :]


def kinetic_kernel(na, nc, n, n_in, based, n_out, me_ref, quanta, ks, kr, prev, *refs):
    spot, _ = place(me_ref)
    refs = list(refs)
    take = lambda k: [refs.pop(0) for _ in range(k)]
    pieces = take(n_in)
    base = refs.pop(0) if based else None
    cur = None if n_in else refs.pop(0)
    u_refs = take(n_out)
    y_ref = refs.pop(0)
    cur = refs.pop(0) if n_in else cur
    nr, nb = prev.shape[1:]
    kstr = 2.0 * ks[...]
    krad = 2.0 * kr[...]
    stretch = 1.0 + lax.broadcasted_iota(jnp.int32, (nr, nb), 0).astype(F32) / nr
    radius = 1.0 + 3.0 * lax.broadcasted_iota(jnp.int32, (nr, nb), 1).astype(F32) / nb
    rotation = 1.0 / (stretch * stretch)
    orbital = 1.0 / (radius * radius)
    scale = np.float32(0.3 / (JL_MAX * (JL_MAX - 1)))
    group = min(8, nc)
    for start in range(0, nc, group):
        chans = range(start, start + group)
        for s, piece in enumerate(pieces):
            for c in chans:
                at = rows_of(spot, s, n, na)
                x = piece[pl.ds(c, na, stride=nc), :]
                cur[c, at, :] = x + base[c, at, :] if based else x
        tiles = [cur[c] for c in chans]
        mixed_a = jnp.dot(kstr, jnp.concatenate(tiles, 1), precision=HP, preferred_element_type=F32)
        mixed_b = jnp.dot(jnp.concatenate(tiles, 0), krad, precision=HP, preferred_element_type=F32)
        for i, c in enumerate(chans):
            j = quanta[c, 0].astype(F32)
            l = quanta[c, 1].astype(F32)
            barrier = orbital * (scale * (l * (l + 1.0))) + rotation * (scale * (j * (j + 1.0))) - 0.2
            y = mixed_a[:, i * nb : (i + 1) * nb] + mixed_b[i * nr : (i + 1) * nr]
            y_ref[c] = y + barrier * tiles[i] - prev[c]
        for s, u in enumerate(u_refs):
            for c in chans:
                u[pl.ds(c, na, stride=nc), :] = y_ref[c, rows_of(spot, s, n, na), :]


def coupling_kernel(cb, nc, n, me_ref, pat_ref, ang_ref, out_ref, buf, sems):
    spot, seat = place(me_ref)
    lam, _, tot = ang_ref.shape

    def row(s):
        return ((spot ^ hop(s, n)) * TEAM + seat) * nc

    copies = [
        pltpu.make_async_copy(
            ang_ref.at[m, pl.ds(pl.multiple_of(row(z), nc), nc), :], buf.at[m, z], sems.at[m * n + z]
        )
        for m in range(lam)
        for z in range(n)
    ]
    for copy in copies:
        copy.start()
    lane = lax.broadcasted_iota(jnp.int32, (nc, tot), 1) // cb
    for copy in copies:
        copy.wait()
    for z in range(n):
        factor = jnp.zeros((nc, tot), F32)
        for k in range(tot // cb):
            factor = jnp.where(lane == k, pat_ref[row(z) // cb, k].astype(F32), factor)
        for m in range(lam):
            val = buf[m, z] * factor
            hi = val.astype(BF16)
            out_ref[m, 0, z] = hi
            out_ref[m, 1, z] = (val - hi.astype(F32)).astype(BF16)


def mix_kernel(nc, n, n_ref, me_ref, coup, pot, *refs):
    spot, seat = place(me_ref)
    sources, pieces = refs[: TEAM * n_ref], refs[TEAM * n_ref : -2]
    xs_hi, xs_lo = refs[-2:]
    rows, nb = pieces[0].shape
    na, ch = rows // nc, n * nc
    lam, tot = coup.shape[0], coup.shape[-1]
    step = max(1, na // 2)
    for k0 in range(0, na, step):
        ks = range(k0, k0 + step)
        for m in range(TEAM):
            for s in range(n):
                if n_ref == 1:
                    z, src = s, sources[m].at[s]
                else:
                    far = s % (n - 1) > 0
                    z, src = spot ^ hop(s, n), sources[m * 2 + (not far)].at[s - 1 if far else s // (n - 1)]
                x = jnp.concatenate([src[k * nc : (k + 1) * nc] for k in ks], 1)
                hi = x.astype(BF16)
                xs_hi[z * TEAM + (seat ^ m)] = hi
                xs_lo[z * TEAM + (seat ^ m)] = (x - hi.astype(F32)).astype(BF16)
        x_hi = xs_hi[...].reshape(tot, step * nb)
        x_lo = xs_lo[...].reshape(tot, step * nb)
        acc = None
        for m in range(lam):
            both = coup[m].reshape(2 * ch, tot)
            p = jnp.dot(both, x_hi, preferred_element_type=F32)
            p = p[:ch] + p[ch:] + jnp.dot(both[:ch], x_lo, preferred_element_type=F32)
            w = jnp.concatenate([pot[m, pl.ds(spot * na + k, 1), :] for k in ks], 1)
            p = p * (2.0 * w)
            acc = p if acc is None else acc + p
        for s, piece in enumerate(pieces):
            for i, k in enumerate(ks):
                piece[k * nc : (k + 1) * nc] = acc[s * nc : (s + 1) * nc, i * nb : (i + 1) * nb]


def near_far(pieces):
    return [pieces[0], pieces[-1]], pieces[1:-1]


def join_kernel(where, n_add, n_out, n_behind, me_ref, *refs):
    spot, _ = place(me_ref)
    n = len(where)
    terms = [refs[k * n : (k + 1) * n] for k in range(n_add)]
    packed, outs, sq = refs[n_add * n + n_behind], refs[n_add * n + n_behind + 1 :][:n_out], refs[-1]
    total = 0.0
    for i, at in enumerate(where):
        y = sum((t[i][...] for t in terms[1:]), terms[0][i][...])
        packed[i if at is None else spot ^ at] = y
        if n_out:
            outs[i][...] = y
        if n_add > 1:
            total = total + jnp.sum((y * y).reshape(-1, 8, y.shape[1]), axis=0)
    if n_add > 1:
        sq[...] = total


def last_of(na, nc, u_ref, pieces, spot):
    for s, piece in enumerate(pieces):
        at = rows_of(spot, s, len(pieces), na)
        for c in range(nc):
            yield c, at, u_ref[c, at, :] + piece[pl.ds(c, na, stride=nc), :]


def norm_kernel(na, nc, n, me_ref, u_ref, *refs):
    spot, _ = place(me_ref)
    nb = u_ref.shape[-1]
    total = jnp.zeros((na, nb), F32)
    for _, _, y in last_of(na, nc, u_ref, refs[:n], spot):
        total = total + y * y
    squares = [r[...] for r in refs[n:-1]]
    tiles = [jnp.sum(t, axis=0, keepdims=True) for t in (squares[0], sum(squares[2:], squares[1]), total)]
    refs[-1][...] = jnp.concatenate([*tiles, jnp.zeros((8 - ITERS, nb), F32)], 0)


def finish_kernel(na, nc, me_ref, u_ref, *refs):
    spot, _ = place(me_ref)
    for c, at, y in last_of(na, nc, u_ref, refs[:-1], spot):
        refs[-1][c, at, :] = y


def local(x):
    return pltpu.with_memory_space_constraint(x, pltpu.VMEM)


def call(kernel, outs, scalars, arrays, scratch=(), specs=None):
    return pl.pallas_call(
        kernel,
        out_shape=outs,
        in_specs=[SM] * len(scalars) + (specs or [VM] * len(arrays)),
        out_specs=[VM] * len(outs),
        scratch_shapes=list(scratch),
        compiler_params=pltpu.CompilerParams(vmem_limit_bytes=20 << 20),
        cost_estimate=pl.CostEstimate(flops=0, bytes_accessed=1 << 16, transcendentals=0),
    )(*scalars, *arrays)


def per_device(psi_prev, psi_cur, kin_stretch, kin_radius, potential, angular, pattern, quanta):
    nc, nr, nb = psi_cur.shape
    lam = potential.shape[0]
    nd = lax.axis_size("chan")
    n = nd // TEAM
    na = nr // n
    total_ch = nc * nd
    cb = total_ch // pattern.shape[1]
    me = lax.axis_index("chan").astype(jnp.int32).reshape(1)
    sds = jax.ShapeDtypeStruct

    def swap(x, bits):
        return lax.ppermute(x, "chan", [(i, i ^ bits) for i in range(nd)])

    def across(x, bits):
        return local(swap(x, bits))

    def exchange(pieces):
        return [across(x, hop(i, n) * TEAM) if i else x for i, x in enumerate(pieces)]

    def after(x, *others):
        return lax.optimization_barrier((x, *others))[0]

    def gather(x, beside):
        over = local(after(swap(x, 2), *beside))
        return [[y] for y in (x, across(x, 1), over, across(over, 1))]

    def gather_near_far(near, far, *beside):
        over = local(after(swap(near, 2), *beside))
        rows = [[x, across(x, 1), y, across(y, 1)] for x, y in ((far, across(far, 2)), (near, over))]
        return list(zip(*rows))

    piece = pltpu.VMEM((na * nc, nb), F32)
    packed = pltpu.VMEM((n, na * nc, nb), F32)
    square = pltpu.VMEM((8, nb), F32)
    on_chip = pltpu.VMEM((nc, nr, nb), F32)
    natural = sds((nc, nr, nb), F32)
    split = pltpu.VMEM((nd, nc, max(1, na // 2) * nb), BF16)

    def kinetic(prev, cur=(), pieces=(), base=(), n_out=0, out=()):
        kernel = functools.partial(kinetic_kernel, na, nc, n, len(pieces), len(base), n_out)
        arrays = [kin_stretch, kin_radius, prev, *pieces, *base, *cur]
        return call(kernel, [piece] * n_out + [on_chip, *out], [me, quanta], arrays)

    def mix(sources):
        arrays = [coup, potential, *(x for source in sources for x in source)]
        return call(functools.partial(mix_kernel, nc, n, len(sources[0])), [piece] * n, [me], arrays, [split, split])

    def join(terms, where=None, split_too=False, behind=()):
        size = len(terms[0])
        n_out = size if split_too else 0
        outs = [pltpu.VMEM((size, na * nc, nb), F32)] + [piece] * n_out + [square] * (len(terms) > 1)
        specs = [VM] * (size * len(terms)) + [ANY] * len(behind)
        kernel = functools.partial(join_kernel, where or [None] * size, len(terms), n_out, len(behind))
        return call(kernel, outs, [me], [x for t in terms for x in t] + list(behind), (), specs)

    (coup,) = call(
        functools.partial(coupling_kernel, cb, nc, n),
        [pltpu.VMEM((lam, 2, n, nc, total_ch), BF16)],
        [me, pattern],
        [angular],
        [pltpu.VMEM((lam, n, nc, total_ch), F32), pltpu.SemaphoreType.DMA((lam * n,))],
        [pl.BlockSpec(memory_space=pltpu.HBM)],
    )
    v1 = exchange(call(functools.partial(to_pieces_kernel, na, nc), [piece] * n, [me], [psi_cur]))
    *u1, u1_nat = kinetic(psi_prev, [psi_cur], n_out=n)
    near, far = ([*join([part])][0] for part in near_far(v1))
    w1 = mix(gather_near_far(near, far, coup, u1_nat))
    u1 = exchange(u1)
    v2, s2 = join([w1, u1], [hop(i, n) for i in range(n)])
    w1 = exchange(w1)
    *u2, _, v2_nat = kinetic(psi_cur, pieces=w1, base=[u1_nat], n_out=n, out=[on_chip])
    w2 = near_far(mix(gather(v2, w1[1:])))
    u2 = near_far(exchange(u2))
    near, *v3_near, s3 = join([w2[0], u2[0]], split_too=True)
    far, *v3_far, s3_far = join([w2[1], u2[1]], split_too=True, behind=[near])
    v3 = exchange([v3_near[0], *v3_far, v3_near[1]])
    u3, prev_out = kinetic(v2_nat, pieces=v3, out=[natural])
    w3 = exchange(mix(gather_near_far(near, far, v3[1])))
    (sums,) = call(functools.partial(norm_kernel, na, nc, n), [sds((8, nb), F32)], [me], [u3, *w3, s2, s3, s3_far])
    (cur_out,) = call(functools.partial(finish_kernel, na, nc), [natural], [me], [u3, *w3])
    bit = 1
    while bit < nd:
        sums = (sums + swap(sums, bit)) + (swap(sums, 2 * bit) + swap(sums, 3 * bit))
        bit *= 4
    norms = jnp.sum(sums[:ITERS], axis=1) / (total_ch * nr * nb)
    return prev_out, cur_out, norms


def solution(mesh):
    return jax.shard_map(
        per_device,
        mesh=mesh,
        in_specs=(
            P(("groups", "chan"), None, None),
            P(("groups", "chan"), None, None),
            P(),
            P(),
            P(),
            P("groups", None, None),
            P("groups", None),
            P(("groups", "chan"), None),
        ),
        out_specs=(
            P(("groups", "chan"), None, None),
            P(("groups", "chan"), None, None),
            P("groups"),
        ),
        check_vma=False,
    )
```

time: 117 us -> 115 us (0.983)
  waiting for transfers between devices: 56.4 us -> 49.6 us
  starting transfers between devices: 38.6 us -> 42.9 us
    ppermute x33 -> x39, waiting for transfers between devices: 56.4 us -> 49.6 us  [swap(): return lax.ppermute(x, 'chan', [(i, i ^ bits) for i in range(nd)])]
    ppermute x33 -> x39, starting transfers between devices: 38.6 us -> 42.9 us  [swap(): return lax.ppermute(x, 'chan', [(i, i ^ bits) for i in range(nd)])]
    pallas_call x12 -> x15, Pallas kernels: 15.9 us -> 16.6 us  [call(): pl.pallas_call(kernel, out_shape=outs, in_specs=[SM] * len(scalars) + (sp...]
  transfers between devices with their start and end apart: 33 -> 39, of which waited for: 17 -> 15; matrix products, arithmetic and copies ran while one was open for 1% -> 1% of each run, Pallas kernels for 10% -> 14%
where the time goes in v2:
time: 115 us
  waiting for transfers between devices  49.6 us (43%)
  starting transfers between devices  42.9 us (37%)
  Pallas kernels  16.6 us (14%)
  local copies, waits for them, and re-layouts  4.39 us (4%)
    ppermute x39, waiting for transfers between devices, swap(): return lax.ppermute(x, 'chan', [(i, i ^ bits) for i in range(nd)])  49.6 us
    ppermute x39, starting transfers between devices, swap(): return lax.ppermute(x, 'chan', [(i, i ^ bits) for i in range(nd)])  42.9 us
    pallas_call x15, Pallas kernels, call(): pl.pallas_call(kernel, out_shape=outs, in_specs=[SM] * len(scalars) + (sp...  16.6 us
    unnamed x17, local copies, waits for them, and re-layouts  4.39 us
  transfers between devices with their start and end apart: 39, of which 15 were waited for; matrix products, arithmetic and copies ran while one was open for 1% of the time, Pallas kernels for 14%

profile of v2, /device:TPU:0, one launch (start us, length us, event | category | flops | bytes accessed | tf_op | source)
XLA Modules:
  0.0 114.9 jit_solution(2333923750166475238)
XLA Ops:
  2.0 3.1 %collective-permute-start.2 = (f32[256,128]{1,0:T(8,128)S(1)}, f32[256,128]{1,0:T(8,128)S(1)}, u32[]{:S(2)}, u32[]{:S(2)}) collective-permute-start(f32[256,128]{1,0:T(8,128)S(1)} %get-tuple-element.47), channel_id=1, source_target_pairs={{0,4},{1,5},{2,6},{3,7},{4,0},{5,1},{6,2},{7,3},{8,12},{9,13},{10,... | collective-permute-start | bytes 393224 | tf_op jit(solution)/shard_map/ppermute | solution.py:220
  5.1 2.6 %collective-permute-start = (f32[256,128]{1,0:T(8,128)S(1)}, f32[256,128]{1,0:T(8,128)S(1)}, u32[]{:S(2)}, u32[]{:S(2)}) collective-permute-start(f32[256,128]{1,0:T(8,128)S(1)} %get-tuple-element.44), channel_id=1, source_target_pairs={{0,8},{1,9},{2,10},{3,11},{4,12},{5,13},{6,14},{7,15},{8,0},{9,1},... | collective-permute-start | bytes 393224 | tf_op jit(solution)/shard_map/ppermute | solution.py:220
  7.7 2.4 %collective-permute-done.2.refs_1_ = f32[256,128]{1,0:T(8,128)S(1)} collective-permute-done((f32[256,128]{1,0:T(8,128)S(1)}, f32[256,128]{1,0:T(8,128)S(1)}, u32[]{:S(2)}, u32[]{:S(2)}) %collective-permute-start.2) | collective-permute-done | bytes 131104 | tf_op jit(solution)/shard_map/ppermute | solution.py:220
  12.0 6.1 %collective-permute-done.refs_0_ = f32[256,128]{1,0:T(8,128)S(1)} collective-permute-done((f32[256,128]{1,0:T(8,128)S(1)}, f32[256,128]{1,0:T(8,128)S(1)}, u32[]{:S(2)}, u32[]{:S(2)}) %collective-permute-start) | collective-permute-done | bytes 131104 | tf_op jit(solution)/shard_map/ppermute | solution.py:220
  20.9 1.9 %copy-done.2 = f32[3,512,512]{2,1,0:T(8,128)S(1)} copy-done((f32[3,512,512]{2,1,0:T(8,128)S(1)}, f32[3,512,512]{2,1,0:T(8,128)}, u32[]{:S(2)}) %copy-start.2) | copy-done | bytes 3145752
  23.5 1.9 %shard_map.103.coup = bf16[3,2,4,32,512]{4,3,2,1,0:T(8,128)(2,1)S(1)} custom-call(s32[1]{0:T(128)} %bitcast.me_ref, s32[8,8]{1,0:T(8,128)S(1)} %copy-done.7, f32[3,512,512]{2,1,0:T(8,128)S(1)} %copy-done.2), custom_call_target="tpu_custom_call" | custom-call | bytes 65536 | tf_op jit(solution)/shard_map/pallas_call | solution.py:197
  25.4 2.2 %shard_map.107 = (f32[256,128]{1,0:T(8,128)S(1)}, f32[256,128]{1,0:T(8,128)S(1)}, f32[256,128]{1,0:T(8,128)S(1)}, f32[256,128]{1,0:T(8,128)S(1)}, f32[32,32,128]{2,1,0:T(8,128)S(1)}) custom-call(s32[1]{0:T(128)} %bitcast.me_ref, s32[32,2]{1,0:T(8,128)S(1)} %copy.13.quanta, f32[32,32]{1,0:T(8,128)S(1)} %copy-done.6, f32[128,128]{1,0:T(8,128)S(1)} %copy-done.3, ...), custom_call_target="tpu_custom_call" | custom-call | bytes 65536 | tf_op jit(solution)/shard_map/pallas_call | solution.py:197
  28.2 3.0 %collective-permute-start.12 = (f32[256,128]{1,0:T(8,128)S(1)}, f32[256,128]{1,0:T(8,128)S(1)}, u32[]{:S(2)}, u32[]{:S(2)}) collective-permute-start(f32[256,128]{1,0:T(8,128)S(1)} %get-tuple-element.56), channel_id=1, source_target_pairs={{0,8},{1,9},{2,10},{3,11},{4,12},{5,13},{6,14},{7,15},{8,0},{9,1},... | collective-permute-start | bytes 393224 | tf_op jit(solution)/shard_map/ppermute | solution.py:220
  34.2 6.9 %collective-permute-done.12.refs_5_ = f32[256,128]{1,0:T(8,128)S(1)} collective-permute-done((f32[256,128]{1,0:T(8,128)S(1)}, f32[256,128]{1,0:T(8,128)S(1)}, u32[]{:S(2)}, u32[]{:S(2)}) %collective-permute-start.12) | collective-permute-done | bytes 131104 | tf_op jit(solution)/shard_map/ppermute | solution.py:220
  42.6 2.6 %collective-permute-start.9 = (f32[256,128]{1,0:T(8,128)S(1)}, f32[256,128]{1,0:T(8,128)S(1)}, u32[]{:S(2)}, u32[]{:S(2)}) collective-permute-start(f32[256,128]{1,0:T(8,128)S(1)} %get-tuple-element.51.refs_1_), channel_id=1, source_target_pairs={{0,8},{1,9},{2,10},{3,11},{4,12},{5,13},{6,14},{7,15},{8,0},{9,1},... | collective-permute-start | bytes 393224 | tf_op jit(solution)/shard_map/ppermute | solution.py:220
  45.1 1.9 %collective-permute-start.10 = (f32[256,128]{1,0:T(8,128)S(1)}, f32[256,128]{1,0:T(8,128)S(1)}, u32[]{:S(2)}, u32[]{:S(2)}) collective-permute-start(f32[256,128]{1,0:T(8,128)S(1)} %get-tuple-element.52.refs_2_), channel_id=1, source_target_pairs={{0,12},{1,13},{2,14},{3,15},{4,8},{5,9},{6,10},{7,11},{8,4},{9,5},... | collective-permute-start | bytes 393224 | tf_op jit(solution)/shard_map/ppermute | solution.py:220
  47.0 7.8 %collective-permute-done.9.refs_1_ = f32[256,128]{1,0:T(8,128)S(1)} collective-permute-done((f32[256,128]{1,0:T(8,128)S(1)}, f32[256,128]{1,0:T(8,128)S(1)}, u32[]{:S(2)}, u32[]{:S(2)}) %collective-permute-start.9) | collective-permute-done | bytes 131104 | tf_op jit(solution)/shard_map/ppermute | solution.py:220
  55.3 3.0 %shard_map.109 = (f32[256,128]{1,0:T(8,128)S(1)}, f32[256,128]{1,0:T(8,128)S(1)}, f32[256,128]{1,0:T(8,128)S(1)}, f32[256,128]{1,0:T(8,128)S(1)}, f32[32,32,128]{2,1,0:T(8,128)}, /*index=5*/f32[32,32,128]{2,1,0:T(8,128)S(1)}) custom-call(s32[1]{0:T(128)} %bitcast.me_ref, s32[32,2]{1,0:T(8,128)S(1)} %copy.13.quanta, f32[32,32]{1,0:T(8,128)S(1)} %copy-done.6, ...), custom_call_target="tpu_custom_call" | custom-call | bytes 65536 | tf_op jit(solution)/shard_map/pallas_call | solution.py:197
  58.4 2.2 %collective-permute-start.18 = (f32[256,128]{1,0:T(8,128)S(1)}, f32[256,128]{1,0:T(8,128)S(1)}, u32[]{:S(2)}, u32[]{:S(2)}) collective-permute-start(f32[256,128]{1,0:T(8,128)S(1)} %get-tuple-element.64), channel_id=1, source_target_pairs={{0,4},{1,5},{2,6},{3,7},{4,0},{5,1},{6,2},{7,3},{8,12},{9,13},{10,... | collective-permute-start | bytes 393224 | tf_op jit(solution)/shard_map/ppermute | solution.py:220
  60.7 2.2 %collective-permute-start.20 = (f32[256,128]{1,0:T(8,128)S(1)}, f32[256,128]{1,0:T(8,128)S(1)}, u32[]{:S(2)}, u32[]{:S(2)}) collective-permute-start(f32[256,128]{1,0:T(8,128)S(1)} %get-tuple-element.69), channel_id=1, source_target_pairs={{0,12},{1,13},{2,14},{3,15},{4,8},{5,9},{6,10},{7,11},{8,4},{9,5},... | collective-permute-start | bytes 393224 | tf_op jit(solution)/shard_map/ppermute | solution.py:220
  64.6 2.0 %collective-permute-done.18.refs_3_ = f32[256,128]{1,0:T(8,128)S(1)} collective-permute-done((f32[256,128]{1,0:T(8,128)S(1)}, f32[256,128]{1,0:T(8,128)S(1)}, u32[]{:S(2)}, u32[]{:S(2)}) %collective-permute-start.18) | collective-permute-done | bytes 131104 | tf_op jit(solution)/shard_map/ppermute | solution.py:220
  68.1 5.3 %collective-permute-done.19.refs_2_ = f32[256,128]{1,0:T(8,128)S(1)} collective-permute-done((f32[256,128]{1,0:T(8,128)S(1)}, f32[256,128]{1,0:T(8,128)S(1)}, u32[]{:S(2)}, u32[]{:S(2)}) %collective-permute-start.19) | collective-permute-done | bytes 131104 | tf_op jit(solution)/shard_map/ppermute | solution.py:220
  74.3 3.4 %collective-permute-start.21 = (f32[256,128]{1,0:T(8,128)S(1)}, f32[256,128]{1,0:T(8,128)S(1)}, u32[]{:S(2)}, u32[]{:S(2)}) collective-permute-start(f32[256,128]{1,0:T(8,128)S(1)} %get-tuple-element.71), channel_id=1, source_target_pairs={{0,8},{1,9},{2,10},{3,11},{4,12},{5,13},{6,14},{7,15},{8,0},{9,1},... | collective-permute-start | bytes 393224 | tf_op jit(solution)/shard_map/ppermute | solution.py:220
  78.2 5.1 %collective-permute-done.21.refs_1_ = f32[256,128]{1,0:T(8,128)S(1)} collective-permute-done((f32[256,128]{1,0:T(8,128)S(1)}, f32[256,128]{1,0:T(8,128)S(1)}, u32[]{:S(2)}, u32[]{:S(2)}) %collective-permute-start.21) | collective-permute-done | bytes 131104 | tf_op jit(solution)/shard_map/ppermute | solution.py:220
  89.0 1.9 %collective-permute-start.31 = (f32[256,128]{1,0:T(8,128)S(1)}, f32[256,128]{1,0:T(8,128)S(1)}, u32[]{:S(2)}, u32[]{:S(2)}) collective-permute-start(f32[256,128]{1,0:T(8,128)S(1)} %get-tuple-element.80), channel_id=1, source_target_pairs={{0,12},{1,13},{2,14},{3,15},{4,8},{5,9},{6,10},{7,11},{8,4},{9,5},... | collective-permute-start | bytes 393224 | tf_op jit(solution)/shard_map/ppermute | solution.py:220
  91.3 2.0 %collective-permute-done.22.refs_2_ = f32[256,128]{1,0:T(8,128)S(1)} collective-permute-done((f32[256,128]{1,0:T(8,128)S(1)}, f32[256,128]{1,0:T(8,128)S(1)}, u32[]{:S(2)}, u32[]{:S(2)}) %collective-permute-start.22) | collective-permute-done | bytes 131104 | tf_op jit(solution)/shard_map/ppermute | solution.py:220
  93.2 2.5 %shard_map.114 = (f32[32,32,128]{2,1,0:T(8,128)S(1)}, f32[32,32,128]{2,1,0:T(8,128)}) custom-call(s32[1]{0:T(128)} %bitcast.me_ref, s32[32,2]{1,0:T(8,128)S(1)} %copy.13.quanta, f32[32,32]{1,0:T(8,128)S(1)} %copy-done.6, f32[128,128]{1,0:T(8,128)S(1)} %copy-done.3, f32[32,32,128]{2,1,0:T(8,128)S(1)} %get-tuple-element.54.prev, ...), custom_call_target="tpu_custom_call" | custom-call | bytes 65536 | tf_op jit(solution)/shard_map/pallas_call | solution.py:197
  95.7 6.8 %collective-permute-done.30.refs_1_ = f32[256,128]{1,0:T(8,128)S(1)} collective-permute-done((f32[256,128]{1,0:T(8,128)S(1)}, f32[256,128]{1,0:T(8,128)S(1)}, u32[]{:S(2)}, u32[]{:S(2)}) %collective-permute-start.30) | collective-permute-done | bytes 131104 | tf_op jit(solution)/shard_map/ppermute | solution.py:220
  108.4 2.3 %collective-permute-start.37 = (f32[8,128]{1,0:T(8,128)S(1)}, f32[8,128]{1,0:T(8,128)S(1)}, u32[]{:S(2)}, u32[]{:S(2)}) collective-permute-start(f32[8,128]{1,0:T(8,128)S(1)} %add_add_fusion.1), channel_id=1, source_target_pairs={{0,8},{1,9},{2,10},{3,11},{4,12},{5,13},{6,14},{7,15},{8,0},{9,1},... | collective-permute-start | bytes 12296 | tf_op jit(solution)/shard_map/ppermute | solution.py:220
  (90 shorter events, 33.3 us)
Async XLA Ops:
  5.1 12.9 %collective-permute-start = (f32[256,128]{1,0:T(8,128)S(1)}, f32[256,128]{1,0:T(8,128)S(1)}, u32[]{:S(2)}, u32[]{:S(2)}) collective-permute-start(f32[256,128]{1,0:T(8,128)S(1)} %get-tuple-element.44), channel_id=1, source_target_pairs={{0,8},{1,9},{2,10},{3,11},{4,12},{5,13},{6,14},{7,15},{8,0},{9,1},... | collective-permute-start | bytes 393224 | tf_op jit(solution)/shard_map/ppermute | solution.py:220
  7.7 10.3 %collective-permute-start.1 = (f32[256,128]{1,0:T(8,128)S(1)}, f32[256,128]{1,0:T(8,128)S(1)}, u32[]{:S(2)}, u32[]{:S(2)}) collective-permute-start(f32[256,128]{1,0:T(8,128)S(1)} %get-tuple-element.45), channel_id=1, source_target_pairs={{0,12},{1,13},{2,14},{3,15},{4,8},{5,9},{6,10},{7,11},{8,4},{9,5},... | collective-permute-start | bytes 393224 | tf_op jit(solution)/shard_map/ppermute | solution.py:220
  10.2 17.4 %collective-permute-start.6 = (f32[2,256,128]{2,1,0:T(8,128)S(1)}, f32[2,256,128]{2,1,0:T(8,128)S(1)}, u32[]{:S(2)}, u32[]{:S(2)}) collective-permute-start(f32[2,256,128]{2,1,0:T(8,128)S(1)} %shard_map.106.refs_1_), channel_id=1, source_target_pairs={{0,2},{1,3},{2,0},{3,1},{4,6},{5,7},{6,4},{7,5},{8,10},{9,11},{10,... | collective-permute-start | bytes 786440 | tf_op jit(solution)/shard_map/ppermute | solution.py:220
  18.1 9.6 %collective-permute-start.5 = (f32[2,256,128]{2,1,0:T(8,128)S(1)}, f32[2,256,128]{2,1,0:T(8,128)S(1)}, u32[]{:S(2)}, u32[]{:S(2)}) collective-permute-start(f32[2,256,128]{2,1,0:T(8,128)S(1)} %shard_map.105.refs_0_), channel_id=1, source_target_pairs={{0,2},{1,3},{2,0},{3,1},{4,6},{5,7},{6,4},{7,5},{8,10},{9,11},{10,... | collective-permute-start | bytes 786440 | tf_op jit(solution)/shard_map/ppermute | solution.py:220
  19.7 11.5 %collective-permute-start.4 = (f32[2,256,128]{2,1,0:T(8,128)S(1)}, f32[2,256,128]{2,1,0:T(8,128)S(1)}, u32[]{:S(2)}, u32[]{:S(2)}) collective-permute-start(f32[2,256,128]{2,1,0:T(8,128)S(1)} %shard_map.106.refs_1_), channel_id=1, source_target_pairs={{0,1},{1,0},{2,3},{3,2},{4,5},{5,4},{6,7},{7,6},{8,9},{9,8},{10,11... | collective-permute-start | bytes 786440 | tf_op jit(solution)/shard_map/ppermute | solution.py:220
  19.7 12.9 %collective-permute-start.3 = (f32[2,256,128]{2,1,0:T(8,128)S(1)}, f32[2,256,128]{2,1,0:T(8,128)S(1)}, u32[]{:S(2)}, u32[]{:S(2)}) collective-permute-start(f32[2,256,128]{2,1,0:T(8,128)S(1)} %shard_map.105.refs_0_), channel_id=1, source_target_pairs={{0,1},{1,0},{2,3},{3,2},{4,5},{5,4},{6,7},{7,6},{8,9},{9,8},{10,11... | collective-permute-start | bytes 786440 | tf_op jit(solution)/shard_map/ppermute | solution.py:220
  28.2 12.9 %collective-permute-start.12 = (f32[256,128]{1,0:T(8,128)S(1)}, f32[256,128]{1,0:T(8,128)S(1)}, u32[]{:S(2)}, u32[]{:S(2)}) collective-permute-start(f32[256,128]{1,0:T(8,128)S(1)} %get-tuple-element.56), channel_id=1, source_target_pairs={{0,8},{1,9},{2,10},{3,11},{4,12},{5,13},{6,14},{7,15},{8,0},{9,1},... | collective-permute-start | bytes 393224 | tf_op jit(solution)/shard_map/ppermute | solution.py:220
  31.2 10.0 %collective-permute-start.13 = (f32[256,128]{1,0:T(8,128)S(1)}, f32[256,128]{1,0:T(8,128)S(1)}, u32[]{:S(2)}, u32[]{:S(2)}) collective-permute-start(f32[256,128]{1,0:T(8,128)S(1)} %get-tuple-element.57), channel_id=1, source_target_pairs={{0,12},{1,13},{2,14},{3,15},{4,8},{5,9},{6,10},{7,11},{8,4},{9,5},... | collective-permute-start | bytes 393224 | tf_op jit(solution)/shard_map/ppermute | solution.py:220
  32.5 9.4 %collective-permute-start.14 = (f32[256,128]{1,0:T(8,128)S(1)}, f32[256,128]{1,0:T(8,128)S(1)}, u32[]{:S(2)}, u32[]{:S(2)}) collective-permute-start(f32[256,128]{1,0:T(8,128)S(1)} %get-tuple-element.58), channel_id=1, source_target_pairs={{0,4},{1,5},{2,6},{3,7},{4,0},{5,1},{6,2},{7,3},{8,12},{9,13},{10,... | collective-permute-start | bytes 393224 | tf_op jit(solution)/shard_map/ppermute | solution.py:220
  42.0 13.3 %collective-permute-start.16 = (f32[4,256,128]{2,1,0:T(8,128)S(1)}, f32[4,256,128]{2,1,0:T(8,128)S(1)}, u32[]{:S(2)}, u32[]{:S(2)}) collective-permute-start(f32[4,256,128]{2,1,0:T(8,128)S(1)} %get-tuple-element.59.refs_0_), channel_id=1, source_target_pairs={{0,2},{1,3},{2,0},{3,1},{4,6},{5,7},{6,4},{7,5},{8,10},{9,11},{10,... | collective-permute-start | bytes 1572872 | tf_op jit(solution)/shard_map/ppermute | solution.py:220
  42.6 12.2 %collective-permute-start.9 = (f32[256,128]{1,0:T(8,128)S(1)}, f32[256,128]{1,0:T(8,128)S(1)}, u32[]{:S(2)}, u32[]{:S(2)}) collective-permute-start(f32[256,128]{1,0:T(8,128)S(1)} %get-tuple-element.51.refs_1_), channel_id=1, source_target_pairs={{0,8},{1,9},{2,10},{3,11},{4,12},{5,13},{6,14},{7,15},{8,0},{9,1},... | collective-permute-start | bytes 393224 | tf_op jit(solution)/shard_map/ppermute | solution.py:220
  45.1 9.7 %collective-permute-start.10 = (f32[256,128]{1,0:T(8,128)S(1)}, f32[256,128]{1,0:T(8,128)S(1)}, u32[]{:S(2)}, u32[]{:S(2)}) collective-permute-start(f32[256,128]{1,0:T(8,128)S(1)} %get-tuple-element.52.refs_2_), channel_id=1, source_target_pairs={{0,12},{1,13},{2,14},{3,15},{4,8},{5,9},{6,10},{7,11},{8,4},{9,5},... | collective-permute-start | bytes 393224 | tf_op jit(solution)/shard_map/ppermute | solution.py:220
  47.0 8.3 %collective-permute-start.11 = (f32[256,128]{1,0:T(8,128)S(1)}, f32[256,128]{1,0:T(8,128)S(1)}, u32[]{:S(2)}, u32[]{:S(2)}) collective-permute-start(f32[256,128]{1,0:T(8,128)S(1)} %get-tuple-element.53.refs_3_), channel_id=1, source_target_pairs={{0,4},{1,5},{2,6},{3,7},{4,0},{5,1},{6,2},{7,3},{8,12},{9,13},{10,... | collective-permute-start | bytes 393224 | tf_op jit(solution)/shard_map/ppermute | solution.py:220
  47.0 15.9 %collective-permute-start.15 = (f32[4,256,128]{2,1,0:T(8,128)S(1)}, f32[4,256,128]{2,1,0:T(8,128)S(1)}, u32[]{:S(2)}, u32[]{:S(2)}) collective-permute-start(f32[4,256,128]{2,1,0:T(8,128)S(1)} %get-tuple-element.59.refs_0_), channel_id=1, source_target_pairs={{0,1},{1,0},{2,3},{3,2},{4,5},{5,4},{6,7},{7,6},{8,9},{9,8},{10,11... | collective-permute-start | bytes 1572872 | tf_op jit(solution)/shard_map/ppermute | solution.py:220
  60.5 12.9 %collective-permute-start.19 = (f32[256,128]{1,0:T(8,128)S(1)}, f32[256,128]{1,0:T(8,128)S(1)}, u32[]{:S(2)}, u32[]{:S(2)}) collective-permute-start(f32[256,128]{1,0:T(8,128)S(1)} %get-tuple-element.68), channel_id=1, source_target_pairs={{0,8},{1,9},{2,10},{3,11},{4,12},{5,13},{6,14},{7,15},{8,0},{9,1},... | collective-permute-start | bytes 393224 | tf_op jit(solution)/shard_map/ppermute | solution.py:220
  60.7 12.7 %collective-permute-start.20 = (f32[256,128]{1,0:T(8,128)S(1)}, f32[256,128]{1,0:T(8,128)S(1)}, u32[]{:S(2)}, u32[]{:S(2)}) collective-permute-start(f32[256,128]{1,0:T(8,128)S(1)} %get-tuple-element.69), channel_id=1, source_target_pairs={{0,12},{1,13},{2,14},{3,15},{4,8},{5,9},{6,10},{7,11},{8,4},{9,5},... | collective-permute-start | bytes 393224 | tf_op jit(solution)/shard_map/ppermute | solution.py:220
  66.6 16.6 %collective-permute-start.27 = (f32[2,256,128]{2,1,0:T(8,128)S(1)}, f32[2,256,128]{2,1,0:T(8,128)S(1)}, u32[]{:S(2)}, u32[]{:S(2)}) collective-permute-start(f32[2,256,128]{2,1,0:T(8,128)S(1)} %get-tuple-element.70.refs_4_.refs_1_), channel_id=1, source_target_pairs={{0,2},{1,3},{2,0},{3,1},{4,6},{5,7},{6,4},{7,5},{8,10},{9,11},{10,... | collective-permute-start | bytes 786440 | tf_op jit(solution)/shard_map/ppermute | solution.py:220
  73.5 9.8 %collective-permute-start.26 = (f32[2,256,128]{2,1,0:T(8,128)S(1)}, f32[2,256,128]{2,1,0:T(8,128)S(1)}, u32[]{:S(2)}, u32[]{:S(2)}) collective-permute-start(f32[2,256,128]{2,1,0:T(8,128)S(1)} %get-tuple-element.76.refs_0_), channel_id=1, source_target_pairs={{0,2},{1,3},{2,0},{3,1},{4,6},{5,7},{6,4},{7,5},{8,10},{9,11},{10,... | collective-permute-start | bytes 786440 | tf_op jit(solution)/shard_map/ppermute | solution.py:220
  74.3 8.9 %collective-permute-start.21 = (f32[256,128]{1,0:T(8,128)S(1)}, f32[256,128]{1,0:T(8,128)S(1)}, u32[]{:S(2)}, u32[]{:S(2)}) collective-permute-start(f32[256,128]{1,0:T(8,128)S(1)} %get-tuple-element.71), channel_id=1, source_target_pairs={{0,8},{1,9},{2,10},{3,11},{4,12},{5,13},{6,14},{7,15},{8,0},{9,1},... | collective-permute-start | bytes 393224 | tf_op jit(solution)/shard_map/ppermute | solution.py:220
  77.7 8.3 %collective-permute-start.25 = (f32[2,256,128]{2,1,0:T(8,128)S(1)}, f32[2,256,128]{2,1,0:T(8,128)S(1)}, u32[]{:S(2)}, u32[]{:S(2)}) collective-permute-start(f32[2,256,128]{2,1,0:T(8,128)S(1)} %get-tuple-element.70.refs_4_.refs_1_), channel_id=1, source_target_pairs={{0,1},{1,0},{2,3},{3,2},{4,5},{5,4},{6,7},{7,6},{8,9},{9,8},{10,11... | collective-permute-start | bytes 786440 | tf_op jit(solution)/shard_map/ppermute | solution.py:220
  84.4 8.9 %collective-permute-start.22 = (f32[256,128]{1,0:T(8,128)S(1)}, f32[256,128]{1,0:T(8,128)S(1)}, u32[]{:S(2)}, u32[]{:S(2)}) collective-permute-start(f32[256,128]{1,0:T(8,128)S(1)} %get-tuple-element.72), channel_id=1, source_target_pairs={{0,12},{1,13},{2,14},{3,15},{4,8},{5,9},{6,10},{7,11},{8,4},{9,5},... | collective-permute-start | bytes 393224 | tf_op jit(solution)/shard_map/ppermute | solution.py:220
  87.7 14.8 %collective-permute-start.30 = (f32[256,128]{1,0:T(8,128)S(1)}, f32[256,128]{1,0:T(8,128)S(1)}, u32[]{:S(2)}, u32[]{:S(2)}) collective-permute-start(f32[256,128]{1,0:T(8,128)S(1)} %get-tuple-element.79), channel_id=1, source_target_pairs={{0,8},{1,9},{2,10},{3,11},{4,12},{5,13},{6,14},{7,15},{8,0},{9,1},... | collective-permute-start | bytes 393224 | tf_op jit(solution)/shard_map/ppermute | solution.py:220
  89.0 13.5 %collective-permute-start.31 = (f32[256,128]{1,0:T(8,128)S(1)}, f32[256,128]{1,0:T(8,128)S(1)}, u32[]{:S(2)}, u32[]{:S(2)}) collective-permute-start(f32[256,128]{1,0:T(8,128)S(1)} %get-tuple-element.80), channel_id=1, source_target_pairs={{0,12},{1,13},{2,14},{3,15},{4,8},{5,9},{6,10},{7,11},{8,4},{9,5},... | collective-permute-start | bytes 393224 | tf_op jit(solution)/shard_map/ppermute | solution.py:220
  91.0 11.5 %collective-permute-start.32 = (f32[256,128]{1,0:T(8,128)S(1)}, f32[256,128]{1,0:T(8,128)S(1)}, u32[]{:S(2)}, u32[]{:S(2)}) collective-permute-start(f32[256,128]{1,0:T(8,128)S(1)} %get-tuple-element.81), channel_id=1, source_target_pairs={{0,4},{1,5},{2,6},{3,7},{4,0},{5,1},{6,2},{7,3},{8,12},{9,13},{10,... | collective-permute-start | bytes 393224 | tf_op jit(solution)/shard_map/ppermute | solution.py:220
  (23 other events, 205.7 us)

commit v3 on v2

--- a/solution.py
+++ b/solution.py
@@ -49,6 +49,12 @@
     y_ref = refs.pop(0)
     cur = refs.pop(0) if n_in else cur
     nr, nb = prev.shape[1:]
+
+    def placed(some):
+        if len(some) == 1:
+            return [(some[0].at[z], pl.ds(z * na, na)) for z in range(n)]
+        return [(ref, rows_of(spot, s, n, na)) for s, ref in enumerate(some)]
+
     kstr = 2.0 * ks[...]
     krad = 2.0 * kr[...]
     stretch = 1.0 + lax.broadcasted_iota(jnp.int32, (nr, nb), 0).astype(F32) / nr
@@ -59,23 +65,22 @@
     group = min(8, nc)
     for start in range(0, nc, group):
         chans = range(start, start + group)
-        for s, piece in enumerate(pieces):
+        for piece, at in placed(pieces):
             for c in chans:
-                at = rows_of(spot, s, n, na)
                 x = piece[pl.ds(c, na, stride=nc), :]
                 cur[c, at, :] = x + base[c, at, :] if based else x
         tiles = [cur[c] for c in chans]
         mixed_a = jnp.dot(kstr, jnp.concatenate(tiles, 1), precision=HP, preferred_element_type=F32)
         mixed_b = jnp.dot(jnp.concatenate(tiles, 0), krad, precision=HP, preferred_element_type=F32)
         for i, c in enumerate(chans):
-            j = quanta[c, 0].astype(F32)
-            l = quanta[c, 1].astype(F32)
+            j = quanta[0, c].astype(F32)
+            l = quanta[1, c].astype(F32)
             barrier = orbital * (scale * (l * (l + 1.0))) + rotation * (scale * (j * (j + 1.0))) - 0.2
             y = mixed_a[:, i * nb : (i + 1) * nb] + mixed_b[i * nr : (i + 1) * nr]
             y_ref[c] = y + barrier * tiles[i] - prev[c]
-        for s, u in enumerate(u_refs):
+        for u, at in placed(u_refs):
             for c in chans:
-                u[pl.ds(c, na, stride=nc), :] = y_ref[c, rows_of(spot, s, n, na), :]
+                u[pl.ds(c, na, stride=nc), :] = y_ref[c, at, :]
 
 
 def coupling_kernel(cb, nc, n, me_ref, pat_ref, ang_ref, out_ref, buf, sems):
@@ -148,21 +153,38 @@
     return [pieces[0], pieces[-1]], pieces[1:-1]
 
 
-def join_kernel(where, n_add, n_out, n_behind, me_ref, *refs):
-    spot, _ = place(me_ref)
-    n = len(where)
-    terms = [refs[k * n : (k + 1) * n] for k in range(n_add)]
-    packed, outs, sq = refs[n_add * n + n_behind], refs[n_add * n + n_behind + 1 :][:n_out], refs[-1]
+def group_kernel(n, me_ref, *refs):
+    for s in range(n):
+        refs[-1][s] = refs[s][...]
+
+
+def join_kernel(n, me_ref, u_ref, *refs):
+    spot, _ = place(me_ref)
+    out, sq = refs[-2:]
     total = 0.0
-    for i, at in enumerate(where):
-        y = sum((t[i][...] for t in terms[1:]), terms[0][i][...])
-        packed[i if at is None else spot ^ at] = y
-        if n_out:
-            outs[i][...] = y
-        if n_add > 1:
-            total = total + jnp.sum((y * y).reshape(-1, 8, y.shape[1]), axis=0)
-    if n_add > 1:
-        sq[...] = total
+    for s in range(n):
+        at = spot ^ hop(s, n)
+        y = refs[s][...] + u_ref[at]
+        out[at] = y
+        total = total + jnp.sum((y * y).reshape(-1, 8, y.shape[1]), axis=0)
+    sq[...] = total
+
+
+def group_join_kernel(n, n_all, me_ref, *refs):
+    spot, _ = place(me_ref)
+    ws, us, rest = refs[:n], refs[n : 2 * n], refs[2 * n :]
+    near, out, sq = rest[0] if n_all else None, rest[-2 - bool(n_all)], rest[-1 - bool(n_all)]
+    total = 0.0
+    for s in range(n):
+        y = ws[s][...] + us[s][...]
+        out[s] = y
+        if n_all:
+            rest[-1][spot ^ hop(s + 1, n_all)] = y
+        total = total + jnp.sum((y * y).reshape(-1, 8, y.shape[1]), axis=0)
+    if n_all:
+        rest[-1][spot] = near[0]
+        rest[-1][spot ^ hop(n_all - 1, n_all)] = near[1]
+    sq[...] = total
 
 
 def last_of(na, nc, u_ref, pieces, spot):
@@ -225,6 +247,10 @@
     def exchange(pieces):
         return [across(x, hop(i, n) * TEAM) if i else x for i, x in enumerate(pieces)]
 
+    def exchange_all(x):
+        lines = [[spot * TEAM + seat for spot in range(n)] for seat in range(TEAM)]
+        return local(lax.all_to_all(x, "chan", 0, 0, tiled=True, axis_index_groups=lines))
+
     def after(x, *others):
         return lax.optimization_barrier((x, *others))[0]
 
@@ -247,43 +273,48 @@
     def kinetic(prev, cur=(), pieces=(), base=(), n_out=0, out=()):
         kernel = functools.partial(kinetic_kernel, na, nc, n, len(pieces), len(base), n_out)
         arrays = [kin_stretch, kin_radius, prev, *pieces, *base, *cur]
-        return call(kernel, [piece] * n_out + [on_chip, *out], [me, quanta], arrays)
+        outs = [packed] if n_out == 1 else [piece] * n_out
+        return call(kernel, [*outs, on_chip, *out], [me, quanta.T], arrays)
 
     def mix(sources):
         arrays = [coup, potential, *(x for source in sources for x in source)]
         return call(functools.partial(mix_kernel, nc, n, len(sources[0])), [piece] * n, [me], arrays, [split, split])
 
-    def join(terms, where=None, split_too=False, behind=()):
-        size = len(terms[0])
-        n_out = size if split_too else 0
-        outs = [pltpu.VMEM((size, na * nc, nb), F32)] + [piece] * n_out + [square] * (len(terms) > 1)
-        specs = [VM] * (size * len(terms)) + [ANY] * len(behind)
-        kernel = functools.partial(join_kernel, where or [None] * size, len(terms), n_out, len(behind))
-        return call(kernel, outs, [me], [x for t in terms for x in t] + list(behind), (), specs)
+    def group(pieces, behind=()):
+        k = len(pieces)
+        specs = [VM] * k + [ANY] * len(behind)
+        kernel = functools.partial(group_kernel, k)
+        return call(kernel, [pltpu.VMEM((k, na * nc, nb), F32)], [me], [*pieces, *behind], (), specs)[0]
+
+    def group_join(ws, us, near=()):
+        k = len(ws)
+        kernel = functools.partial(group_join_kernel, k, n if near else 0)
+        outs = [pltpu.VMEM((k, na * nc, nb), F32), square] + [packed] * len(near)
+        return call(kernel, outs, [me], [*ws, *us, *near])
 
     (coup,) = call(
         functools.partial(coupling_kernel, cb, nc, n),
         [pltpu.VMEM((lam, 2, n, nc, total_ch), BF16)],
         [me, pattern],
-        [angular],
+        [pltpu.with_memory_space_constraint(angular, pltpu.HBM)],
         [pltpu.VMEM((lam, n, nc, total_ch), F32), pltpu.SemaphoreType.DMA((lam * n,))],
         [pl.BlockSpec(memory_space=pltpu.HBM)],
     )
     v1 = exchange(call(functools.partial(to_pieces_kernel, na, nc), [piece] * n, [me], [psi_cur]))
-    *u1, u1_nat = kinetic(psi_prev, [psi_cur], n_out=n)
-    near, far = ([*join([part])][0] for part in near_far(v1))
-    w1 = mix(gather_near_far(near, far, coup, u1_nat))
-    u1 = exchange(u1)
-    v2, s2 = join([w1, u1], [hop(i, n) for i in range(n)])
-    w1 = exchange(w1)
-    *u2, _, v2_nat = kinetic(psi_cur, pieces=w1, base=[u1_nat], n_out=n, out=[on_chip])
-    w2 = near_far(mix(gather(v2, w1[1:])))
+    u1, u1_nat = kinetic(psi_prev, [psi_cur], n_out=1)
+    u1 = exchange_all(u1)
+    near, far = near_far(v1)
+    w1 = mix(gather_near_far(group(near, [u1_nat]), group(far), coup))
+    w1_c = exchange(w1)
+    v2, s2 = call(functools.partial(join_kernel, n), [packed, square], [me], [u1, *w1])
+    *u2, _, v2_nat = kinetic(psi_cur, pieces=w1_c, base=[u1_nat], n_out=n, out=[on_chip])
+    w2 = near_far(mix(gather(v2, w1_c[1:])))
     u2 = near_far(exchange(u2))
-    near, *v3_near, s3 = join([w2[0], u2[0]], split_too=True)
-    far, *v3_far, s3_far = join([w2[1], u2[1]], split_too=True, behind=[near])
-    v3 = exchange([v3_near[0], *v3_far, v3_near[1]])
-    u3, prev_out = kinetic(v2_nat, pieces=v3, out=[natural])
-    w3 = exchange(mix(gather_near_far(near, far, v3[1])))
+    near, s3 = group_join(w2[0], u2[0])
+    far, s3_far, v3 = group_join(w2[1], u2[1], [near])
+    v3 = exchange_all(v3)
+    u3, prev_out = kinetic(v2_nat, pieces=[v3], out=[natural])
+    w3 = exchange(mix(gather_near_far(near, far)))
     (sums,) = call(functools.partial(norm_kernel, na, nc, n), [sds((8, nb), F32)], [me], [u3, *w3, s2, s3, s3_far])
     (cur_out,) = call(functools.partial(finish_kernel, na, nc), [natural], [me], [u3, *w3])
     bit = 1

time: 115 us -> 130 us (1.13)
  waiting for transfers between devices: 49.6 us -> 60 us
  starting transfers between devices: 42.9 us -> 45 us
    all_to_all x0 -> x2, starting transfers between devices: none -> 11.3 us  [exchange_all(): lax.all_to_all(x, 'chan', 0, 0, tiled=True, axis_index_groups=lines)]
    ppermute x39 -> x33, waiting for transfers between devices: 49.6 us -> 60 us  [swap(): return lax.ppermute(x, 'chan', [(i, i ^ bits) for i in range(nd)])]
    ppermute x39 -> x33, starting transfers between devices: 42.9 us -> 33.8 us  [swap(): return lax.ppermute(x, 'chan', [(i, i ^ bits) for i in range(nd)])]
    unnamed x17 -> x24, local copies, waits for them, and re-layouts: 4.39 us -> 5.39 us
  transfers between devices with their start and end apart: 39 -> 35, of which waited for: 15 -> 17; matrix products, arithmetic and copies ran while one was open for 1% -> 0% of each run, Pallas kernels for 14% -> 10%
where the time goes in v3:
time: 130 us; the launch traced here: 129 us
  waiting for transfers between devices  60 us (46%)
  starting transfers between devices  45 us (35%)
  Pallas kernels  17.6 us (14%)
  local copies, waits for them, and re-layouts  5.39 us (4%)
    ppermute x33, waiting for transfers between devices, swap(): return lax.ppermute(x, 'chan', [(i, i ^ bits) for i in range(nd)])  60 us
    ppermute x33, starting transfers between devices, swap(): return lax.ppermute(x, 'chan', [(i, i ^ bits) for i in range(nd)])  33.8 us
    pallas_call x15, Pallas kernels, call(): pl.pallas_call(kernel, out_shape=outs, in_specs=[SM] * len(scalars) + (sp...  17.6 us
    all_to_all x2, starting transfers between devices, exchange_all(): lax.all_to_all(x, 'chan', 0, 0, tiled=True, axis_index_groups=lines)  11.3 us
    unnamed x24, local copies, waits for them, and re-layouts  5.39 us
  transfers between devices with their start and end apart: 35, of which 17 were waited for; matrix products, arithmetic and copies ran while one was open for 0% of the time, Pallas kernels for 10%

profile of v3, /device:TPU:0, one launch (start us, length us, event | category | flops | bytes accessed | tf_op | source)
XLA Modules:
  0.0 129.5 jit_solution(8780564486250292668)
XLA Ops:
  5.0 2.8 %shard_map.106 = (f32[4,256,128]{2,1,0:T(8,128)}, f32[32,32,128]{2,1,0:T(8,128)S(1)}) custom-call(s32[1]{0:T(128)} %bitcast.me_ref, s32[2,32]{1,0:T(2,128)S(1)} %bitcast.2, f32[32,32]{1,0:T(8,128)S(1)} %copy-done.7, f32[128,128]{1,0:T(8,128)S(1)} %copy-done.3, f32[32,32,128]{2,1,0:T(8,128)S(1)} %copy-done.5, f32[32,32,128]{2,1,0:T(8,128)S(1)} %copy-done), custom_call_target="tpu_custom_call" | custom-call | bytes 65536 | tf_op jit(solution)/shard_map/pallas_call | solution.py:219
  7.8 6.3 %all-to-all-start = ((f32[4,256,128]{2,1,0:T(8,128)}), f32[4,256,128]{2,1,0:T(8,128)S(1)}, u32[]{:S(2)}, u32[]{:S(2)}) async-start(f32[4,256,128]{2,1,0:T(8,128)} %get-tuple-element.48), calls=%async_computation | async-start | bytes 1048576 | tf_op jit(solution)/shard_map/all_to_all | solution.py:252
  15.4 2.1 %collective-permute-start.2 = (f32[256,128]{1,0:T(8,128)S(1)}, f32[256,128]{1,0:T(8,128)S(1)}, u32[]{:S(2)}, u32[]{:S(2)}) collective-permute-start(f32[256,128]{1,0:T(8,128)S(1)} %get-tuple-element.40), channel_id=1, source_target_pairs={{0,4},{1,5},{2,6},{3,7},{4,0},{5,1},{6,2},{7,3},{8,12},{9,13},{10,... | collective-permute-start | bytes 393224 | tf_op jit(solution)/shard_map/ppermute | solution.py:242
  17.5 2.4 %collective-permute-start = (f32[256,128]{1,0:T(8,128)S(1)}, f32[256,128]{1,0:T(8,128)S(1)}, u32[]{:S(2)}, u32[]{:S(2)}) collective-permute-start(f32[256,128]{1,0:T(8,128)S(1)} %get-tuple-element.37), channel_id=1, source_target_pairs={{0,8},{1,9},{2,10},{3,11},{4,12},{5,13},{6,14},{7,15},{8,0},{9,1},... | collective-permute-start | bytes 393224 | tf_op jit(solution)/shard_map/ppermute | solution.py:242
  20.0 6.7 %collective-permute-done.2.refs_1_ = f32[256,128]{1,0:T(8,128)S(1)} collective-permute-done((f32[256,128]{1,0:T(8,128)S(1)}, f32[256,128]{1,0:T(8,128)S(1)}, u32[]{:S(2)}, u32[]{:S(2)}) %collective-permute-start.2) | collective-permute-done | bytes 131104 | tf_op jit(solution)/shard_map/ppermute | solution.py:242
  28.3 9.8 %collective-permute-done.refs_0_ = f32[256,128]{1,0:T(8,128)S(1)} collective-permute-done((f32[256,128]{1,0:T(8,128)S(1)}, f32[256,128]{1,0:T(8,128)S(1)}, u32[]{:S(2)}, u32[]{:S(2)}) %collective-permute-start) | collective-permute-done | bytes 131104 | tf_op jit(solution)/shard_map/ppermute | solution.py:242
  39.7 2.0 %shard_map.103.coup = bf16[3,2,4,32,512]{4,3,2,1,0:T(8,128)(2,1)S(1)} custom-call(s32[1]{0:T(128)} %bitcast.me_ref, s32[8,8]{1,0:T(8,128)S(1)} %copy-done.11, f32[3,512,512]{2,1,0:T(8,128)} %ang_ref.1), custom_call_target="tpu_custom_call" | custom-call | bytes 65536 | tf_op jit(solution)/shard_map/pallas_call | solution.py:219
  42.3 2.3 %collective-permute-done.5.refs_4_ = f32[2,256,128]{2,1,0:T(8,128)S(1)} collective-permute-done((f32[2,256,128]{2,1,0:T(8,128)S(1)}, f32[2,256,128]{2,1,0:T(8,128)S(1)}, u32[]{:S(2)}, u32[]{:S(2)}) %collective-permute-start.5) | collective-permute-done | bytes 262176 | tf_op jit(solution)/shard_map/ppermute | solution.py:242
  46.5 1.7 %shard_map.108 = (f32[256,128]{1,0:T(8,128)S(1)}, f32[256,128]{1,0:T(8,128)S(1)}, f32[256,128]{1,0:T(8,128)S(1)}, f32[256,128]{1,0:T(8,128)S(1)}) custom-call(s32[1]{0:T(128)} %bitcast.me_ref, bf16[3,2,4,32,512]{4,3,2,1,0:T(8,128)(2,1)S(1)} %shard_map.103.coup, f32[3,32,128]{2,1,0:T(8,128)S(1)} %copy-done.6, f32[2,256,128]{2,1,0:T(8,128)S(1)} %shard_map.105.refs_0_, ...), custom_call_target="tpu_custom_call" | custom-call | bytes 65536 | tf_op jit(solution)/shard_map/pallas_call | solution.py:219
  49.8 2.5 %collective-permute-start.9 = (f32[256,128]{1,0:T(8,128)S(1)}, f32[256,128]{1,0:T(8,128)S(1)}, u32[]{:S(2)}, u32[]{:S(2)}) collective-permute-start(f32[256,128]{1,0:T(8,128)S(1)} %get-tuple-element.44.refs_1_), channel_id=1, source_target_pairs={{0,8},{1,9},{2,10},{3,11},{4,12},{5,13},{6,14},{7,15},{8,0},{9,1},... | collective-permute-start | bytes 393224 | tf_op jit(solution)/shard_map/ppermute | solution.py:242
  52.4 3.1 %collective-permute-start.10 = (f32[256,128]{1,0:T(8,128)S(1)}, f32[256,128]{1,0:T(8,128)S(1)}, u32[]{:S(2)}, u32[]{:S(2)}) collective-permute-start(f32[256,128]{1,0:T(8,128)S(1)} %get-tuple-element.45.refs_2_), channel_id=1, source_target_pairs={{0,12},{1,13},{2,14},{3,15},{4,8},{5,9},{6,10},{7,11},{8,4},{9,5},... | collective-permute-start | bytes 393224 | tf_op jit(solution)/shard_map/ppermute | solution.py:242
  55.4 7.3 %collective-permute-done.9.refs_1_ = f32[256,128]{1,0:T(8,128)S(1)} collective-permute-done((f32[256,128]{1,0:T(8,128)S(1)}, f32[256,128]{1,0:T(8,128)S(1)}, u32[]{:S(2)}, u32[]{:S(2)}) %collective-permute-start.9) | collective-permute-done | bytes 131104 | tf_op jit(solution)/shard_map/ppermute | solution.py:242
  63.5 2.8 %shard_map.109 = (f32[256,128]{1,0:T(8,128)S(1)}, f32[256,128]{1,0:T(8,128)S(1)}, f32[256,128]{1,0:T(8,128)S(1)}, f32[256,128]{1,0:T(8,128)S(1)}, f32[32,32,128]{2,1,0:T(8,128)}, /*index=5*/f32[32,32,128]{2,1,0:T(8,128)S(1)}) custom-call(s32[1]{0:T(128)} %bitcast.me_ref, s32[2,32]{1,0:T(2,128)S(1)} %bitcast.3, f32[32,32]{1,0:T(8,128)S(1)} %copy-done.8, ...), custom_call_target="tpu_custom_call" | custom-call | bytes 65536 | tf_op jit(solution)/shard_map/pallas_call | solution.py:219
  66.3 2.0 %collective-permute-start.17 = (f32[256,128]{1,0:T(8,128)S(1)}, f32[256,128]{1,0:T(8,128)S(1)}, u32[]{:S(2)}, u32[]{:S(2)}) collective-permute-start(f32[256,128]{1,0:T(8,128)S(1)} %get-tuple-element.58), channel_id=1, source_target_pairs={{0,4},{1,5},{2,6},{3,7},{4,0},{5,1},{6,2},{7,3},{8,12},{9,13},{10,... | collective-permute-start | bytes 393224 | tf_op jit(solution)/shard_map/ppermute | solution.py:242
  72.5 2.2 %collective-permute-done.17.refs_3_ = f32[256,128]{1,0:T(8,128)S(1)} collective-permute-done((f32[256,128]{1,0:T(8,128)S(1)}, f32[256,128]{1,0:T(8,128)S(1)}, u32[]{:S(2)}, u32[]{:S(2)}) %collective-permute-start.17) | collective-permute-done | bytes 131104 | tf_op jit(solution)/shard_map/ppermute | solution.py:242
  74.8 6.4 %collective-permute-done.15.refs_2_ = f32[256,128]{1,0:T(8,128)S(1)} collective-permute-done((f32[256,128]{1,0:T(8,128)S(1)}, f32[256,128]{1,0:T(8,128)S(1)}, u32[]{:S(2)}, u32[]{:S(2)}) %collective-permute-start.15) | collective-permute-done | bytes 131104 | tf_op jit(solution)/shard_map/ppermute | solution.py:242
  82.1 5.0 %all-to-all-start.1 = ((f32[4,256,128]{2,1,0:T(8,128)}), f32[4,256,128]{2,1,0:T(8,128)S(1)}, u32[]{:S(2)}, u32[]{:S(2)}) async-start(f32[4,256,128]{2,1,0:T(8,128)} %get-tuple-element.60), calls=%async_computation.1 | async-start | bytes 1048576 | tf_op jit(solution)/shard_map/all_to_all | solution.py:252
  89.6 6.7 %collective-permute-done.20.refs_4_ = f32[2,256,128]{2,1,0:T(8,128)S(1)} collective-permute-done((f32[2,256,128]{2,1,0:T(8,128)S(1)}, f32[2,256,128]{2,1,0:T(8,128)S(1)}, u32[]{:S(2)}, u32[]{:S(2)}) %collective-permute-start.20) | collective-permute-done | bytes 262176 | tf_op jit(solution)/shard_map/ppermute | solution.py:242
  96.3 3.7 %collective-permute-done.21.refs_5_ = f32[2,256,128]{2,1,0:T(8,128)S(1)} collective-permute-done((f32[2,256,128]{2,1,0:T(8,128)S(1)}, f32[2,256,128]{2,1,0:T(8,128)S(1)}, u32[]{:S(2)}, u32[]{:S(2)}) %collective-permute-start.21) | collective-permute-done | bytes 262176 | tf_op jit(solution)/shard_map/ppermute | solution.py:242
  103.1 2.8 %collective-permute-start.24 = (f32[256,128]{1,0:T(8,128)S(1)}, f32[256,128]{1,0:T(8,128)S(1)}, u32[]{:S(2)}, u32[]{:S(2)}) collective-permute-start(f32[256,128]{1,0:T(8,128)S(1)} %get-tuple-element.65), channel_id=1, source_target_pairs={{0,8},{1,9},{2,10},{3,11},{4,12},{5,13},{6,14},{7,15},{8,0},{9,1},... | collective-permute-start | bytes 393224 | tf_op jit(solution)/shard_map/ppermute | solution.py:242
  107.3 2.2 %shard_map.114 = (f32[32,32,128]{2,1,0:T(8,128)S(1)}, f32[32,32,128]{2,1,0:T(8,128)}) custom-call(s32[1]{0:T(128)} %bitcast.me_ref, s32[2,32]{1,0:T(2,128)S(1)} %bitcast.4, f32[32,32]{1,0:T(8,128)S(1)} %copy-done.8, f32[128,128]{1,0:T(8,128)S(1)} %copy-done.4, f32[32,32,128]{2,1,0:T(8,128)S(1)} %get-tuple-element.47.prev, ...), custom_call_target="tpu_custom_call" | custom-call | bytes 65536 | tf_op jit(solution)/shard_map/pallas_call | solution.py:219
  109.5 6.6 %collective-permute-done.24.refs_1_ = f32[256,128]{1,0:T(8,128)S(1)} collective-permute-done((f32[256,128]{1,0:T(8,128)S(1)}, f32[256,128]{1,0:T(8,128)S(1)}, u32[]{:S(2)}, u32[]{:S(2)}) %collective-permute-start.24) | collective-permute-done | bytes 131104 | tf_op jit(solution)/shard_map/ppermute | solution.py:242
  120.8 3.5 %collective-permute-start.32 = (f32[8,128]{1,0:T(8,128)S(1)}, f32[8,128]{1,0:T(8,128)S(1)}, u32[]{:S(2)}, u32[]{:S(2)}) collective-permute-start(f32[8,128]{1,0:T(8,128)S(1)} %add_add_fusion.1), channel_id=1, source_target_pairs={{0,12},{1,13},{2,14},{3,15},{4,8},{5,9},{6,10},{7,11},{8,4},{9,5},... | collective-permute-start | bytes 12296 | tf_op jit(solution)/shard_map/ppermute | solution.py:242
  126.6 2.2 %collective-permute-done.31 = f32[8,128]{1,0:T(8,128)S(1)} collective-permute-done((f32[8,128]{1,0:T(8,128)S(1)}, f32[8,128]{1,0:T(8,128)S(1)}, u32[]{:S(2)}, u32[]{:S(2)}) %collective-permute-start.31) | collective-permute-done | bytes 4128 | tf_op jit(solution)/shard_map/ppermute | solution.py:242
  (89 shorter events, 33.8 us)
Async XLA Ops:
  7.8 40.4 %all-to-all-start = ((f32[4,256,128]{2,1,0:T(8,128)}), f32[4,256,128]{2,1,0:T(8,128)S(1)}, u32[]{:S(2)}, u32[]{:S(2)}) async-start(f32[4,256,128]{2,1,0:T(8,128)} %get-tuple-element.48), calls=%async_computation | async-start | bytes 1048576 | tf_op jit(solution)/shard_map/all_to_all | solution.py:252
  15.4 11.2 %collective-permute-start.2 = (f32[256,128]{1,0:T(8,128)S(1)}, f32[256,128]{1,0:T(8,128)S(1)}, u32[]{:S(2)}, u32[]{:S(2)}) collective-permute-start(f32[256,128]{1,0:T(8,128)S(1)} %get-tuple-element.40), channel_id=1, source_target_pairs={{0,4},{1,5},{2,6},{3,7},{4,0},{5,1},{6,2},{7,3},{8,12},{9,13},{10,... | collective-permute-start | bytes 393224 | tf_op jit(solution)/shard_map/ppermute | solution.py:242
  17.5 20.5 %collective-permute-start = (f32[256,128]{1,0:T(8,128)S(1)}, f32[256,128]{1,0:T(8,128)S(1)}, u32[]{:S(2)}, u32[]{:S(2)}) collective-permute-start(f32[256,128]{1,0:T(8,128)S(1)} %get-tuple-element.37), channel_id=1, source_target_pairs={{0,8},{1,9},{2,10},{3,11},{4,12},{5,13},{6,14},{7,15},{8,0},{9,1},... | collective-permute-start | bytes 393224 | tf_op jit(solution)/shard_map/ppermute | solution.py:242
  19.9 18.2 %collective-permute-start.1 = (f32[256,128]{1,0:T(8,128)S(1)}, f32[256,128]{1,0:T(8,128)S(1)}, u32[]{:S(2)}, u32[]{:S(2)}) collective-permute-start(f32[256,128]{1,0:T(8,128)S(1)} %get-tuple-element.38), channel_id=1, source_target_pairs={{0,12},{1,13},{2,14},{3,15},{4,8},{5,9},{6,10},{7,11},{8,4},{9,5},... | collective-permute-start | bytes 393224 | tf_op jit(solution)/shard_map/ppermute | solution.py:242
  26.7 15.6 %collective-permute-start.6 = (f32[2,256,128]{2,1,0:T(8,128)S(1)}, f32[2,256,128]{2,1,0:T(8,128)S(1)}, u32[]{:S(2)}, u32[]{:S(2)}) collective-permute-start(f32[2,256,128]{2,1,0:T(8,128)S(1)} %shard_map.107.refs_1_), channel_id=1, source_target_pairs={{0,2},{1,3},{2,0},{3,1},{4,6},{5,7},{6,4},{7,5},{8,10},{9,11},{10,... | collective-permute-start | bytes 786440 | tf_op jit(solution)/shard_map/ppermute | solution.py:242
  38.1 6.4 %collective-permute-start.5 = (f32[2,256,128]{2,1,0:T(8,128)S(1)}, f32[2,256,128]{2,1,0:T(8,128)S(1)}, u32[]{:S(2)}, u32[]{:S(2)}) collective-permute-start(f32[2,256,128]{2,1,0:T(8,128)S(1)} %shard_map.105.refs_0_), channel_id=1, source_target_pairs={{0,2},{1,3},{2,0},{3,1},{4,6},{5,7},{6,4},{7,5},{8,10},{9,11},{10,... | collective-permute-start | bytes 786440 | tf_op jit(solution)/shard_map/ppermute | solution.py:242
  48.3 15.2 %collective-permute-start.13 = (f32[4,256,128]{2,1,0:T(8,128)S(1)}, f32[4,256,128]{2,1,0:T(8,128)S(1)}, u32[]{:S(2)}, u32[]{:S(2)}) collective-permute-start(f32[4,256,128]{2,1,0:T(8,128)S(1)} %get-tuple-element.49.refs_0_), channel_id=1, source_target_pairs={{0,2},{1,3},{2,0},{3,1},{4,6},{5,7},{6,4},{7,5},{8,10},{9,11},{10,... | collective-permute-start | bytes 1572872 | tf_op jit(solution)/shard_map/ppermute | solution.py:242
  49.8 12.9 %collective-permute-start.9 = (f32[256,128]{1,0:T(8,128)S(1)}, f32[256,128]{1,0:T(8,128)S(1)}, u32[]{:S(2)}, u32[]{:S(2)}) collective-permute-start(f32[256,128]{1,0:T(8,128)S(1)} %get-tuple-element.44.refs_1_), channel_id=1, source_target_pairs={{0,8},{1,9},{2,10},{3,11},{4,12},{5,13},{6,14},{7,15},{8,0},{9,1},... | collective-permute-start | bytes 393224 | tf_op jit(solution)/shard_map/ppermute | solution.py:242
  52.4 10.3 %collective-permute-start.10 = (f32[256,128]{1,0:T(8,128)S(1)}, f32[256,128]{1,0:T(8,128)S(1)}, u32[]{:S(2)}, u32[]{:S(2)}) collective-permute-start(f32[256,128]{1,0:T(8,128)S(1)} %get-tuple-element.45.refs_2_), channel_id=1, source_target_pairs={{0,12},{1,13},{2,14},{3,15},{4,8},{5,9},{6,10},{7,11},{8,4},{9,5},... | collective-permute-start | bytes 393224 | tf_op jit(solution)/shard_map/ppermute | solution.py:242
  55.4 8.1 %collective-permute-start.11 = (f32[256,128]{1,0:T(8,128)S(1)}, f32[256,128]{1,0:T(8,128)S(1)}, u32[]{:S(2)}, u32[]{:S(2)}) collective-permute-start(f32[256,128]{1,0:T(8,128)S(1)} %get-tuple-element.46.refs_3_), channel_id=1, source_target_pairs={{0,4},{1,5},{2,6},{3,7},{4,0},{5,1},{6,2},{7,3},{8,12},{9,13},{10,... | collective-permute-start | bytes 393224 | tf_op jit(solution)/shard_map/ppermute | solution.py:242
  55.4 15.4 %collective-permute-start.12 = (f32[4,256,128]{2,1,0:T(8,128)S(1)}, f32[4,256,128]{2,1,0:T(8,128)S(1)}, u32[]{:S(2)}, u32[]{:S(2)}) collective-permute-start(f32[4,256,128]{2,1,0:T(8,128)S(1)} %get-tuple-element.49.refs_0_), channel_id=1, source_target_pairs={{0,1},{1,0},{2,3},{3,2},{4,5},{5,4},{6,7},{7,6},{8,9},{9,8},{10,11... | collective-permute-start | bytes 1572872 | tf_op jit(solution)/shard_map/ppermute | solution.py:242
  63.5 7.3 %collective-permute-start.14 = (f32[4,256,128]{2,1,0:T(8,128)S(1)}, f32[4,256,128]{2,1,0:T(8,128)S(1)}, u32[]{:S(2)}, u32[]{:S(2)}) collective-permute-start(f32[4,256,128]{2,1,0:T(8,128)S(1)} %collective-permute-done.13.refs_2_), channel_id=1, source_target_pairs={{0,1},{1,0},{2,3},{3,2},{4,5},{5,4},{6,7},{7,6},{8,9},{9,8},{10,11... | collective-permute-start | bytes 1572872 | tf_op jit(solution)/shard_map/ppermute | solution.py:242
  66.3 8.4 %collective-permute-start.17 = (f32[256,128]{1,0:T(8,128)S(1)}, f32[256,128]{1,0:T(8,128)S(1)}, u32[]{:S(2)}, u32[]{:S(2)}) collective-permute-start(f32[256,128]{1,0:T(8,128)S(1)} %get-tuple-element.58), channel_id=1, source_target_pairs={{0,4},{1,5},{2,6},{3,7},{4,0},{5,1},{6,2},{7,3},{8,12},{9,13},{10,... | collective-permute-start | bytes 393224 | tf_op jit(solution)/shard_map/ppermute | solution.py:242
  68.3 12.9 %collective-permute-start.15 = (f32[256,128]{1,0:T(8,128)S(1)}, f32[256,128]{1,0:T(8,128)S(1)}, u32[]{:S(2)}, u32[]{:S(2)}) collective-permute-start(f32[256,128]{1,0:T(8,128)S(1)} %get-tuple-element.53), channel_id=1, source_target_pairs={{0,8},{1,9},{2,10},{3,11},{4,12},{5,13},{6,14},{7,15},{8,0},{9,1},... | collective-permute-start | bytes 393224 | tf_op jit(solution)/shard_map/ppermute | solution.py:242
  69.4 11.8 %collective-permute-start.16 = (f32[256,128]{1,0:T(8,128)S(1)}, f32[256,128]{1,0:T(8,128)S(1)}, u32[]{:S(2)}, u32[]{:S(2)}) collective-permute-start(f32[256,128]{1,0:T(8,128)S(1)} %get-tuple-element.54), channel_id=1, source_target_pairs={{0,12},{1,13},{2,14},{3,15},{4,8},{5,9},{6,10},{7,11},{8,4},{9,5},... | collective-permute-start | bytes 393224 | tf_op jit(solution)/shard_map/ppermute | solution.py:242
  82.1 25.3 %all-to-all-start.1 = ((f32[4,256,128]{2,1,0:T(8,128)}), f32[4,256,128]{2,1,0:T(8,128)S(1)}, u32[]{:S(2)}, u32[]{:S(2)}) async-start(f32[4,256,128]{2,1,0:T(8,128)} %get-tuple-element.60), calls=%async_computation.1 | async-start | bytes 1048576 | tf_op jit(solution)/shard_map/all_to_all | solution.py:252
  87.0 9.2 %collective-permute-start.20 = (f32[2,256,128]{2,1,0:T(8,128)S(1)}, f32[2,256,128]{2,1,0:T(8,128)S(1)}, u32[]{:S(2)}, u32[]{:S(2)}) collective-permute-start(f32[2,256,128]{2,1,0:T(8,128)S(1)} %get-tuple-element.63.refs_0_), channel_id=1, source_target_pairs={{0,2},{1,3},{2,0},{3,1},{4,6},{5,7},{6,4},{7,5},{8,10},{9,11},{10,... | collective-permute-start | bytes 786440 | tf_op jit(solution)/shard_map/ppermute | solution.py:242
  87.5 12.4 %collective-permute-start.21 = (f32[2,256,128]{2,1,0:T(8,128)S(1)}, f32[2,256,128]{2,1,0:T(8,128)S(1)}, u32[]{:S(2)}, u32[]{:S(2)}) collective-permute-start(f32[2,256,128]{2,1,0:T(8,128)S(1)} %get-tuple-element.59.refs_4_.refs_1_), channel_id=1, source_target_pairs={{0,2},{1,3},{2,0},{3,1},{4,6},{5,7},{6,4},{7,5},{8,10},{9,11},{10,... | collective-permute-start | bytes 786440 | tf_op jit(solution)/shard_map/ppermute | solution.py:242
  89.1 10.9 %collective-permute-start.18 = (f32[2,256,128]{2,1,0:T(8,128)S(1)}, f32[2,256,128]{2,1,0:T(8,128)S(1)}, u32[]{:S(2)}, u32[]{:S(2)}) collective-permute-start(f32[2,256,128]{2,1,0:T(8,128)S(1)} %get-tuple-element.63.refs_0_), channel_id=1, source_target_pairs={{0,1},{1,0},{2,3},{3,2},{4,5},{5,4},{6,7},{7,6},{8,9},{9,8},{10,11... | collective-permute-start | bytes 786440 | tf_op jit(solution)/shard_map/ppermute | solution.py:242
  89.1 10.9 %collective-permute-start.19 = (f32[2,256,128]{2,1,0:T(8,128)S(1)}, f32[2,256,128]{2,1,0:T(8,128)S(1)}, u32[]{:S(2)}, u32[]{:S(2)}) collective-permute-start(f32[2,256,128]{2,1,0:T(8,128)S(1)} %get-tuple-element.59.refs_4_.refs_1_), channel_id=1, source_target_pairs={{0,1},{1,0},{2,3},{3,2},{4,5},{5,4},{6,7},{7,6},{8,9},{9,8},{10,11... | collective-permute-start | bytes 786440 | tf_op jit(solution)/shard_map/ppermute | solution.py:242
  103.1 13.0 %collective-permute-start.24 = (f32[256,128]{1,0:T(8,128)S(1)}, f32[256,128]{1,0:T(8,128)S(1)}, u32[]{:S(2)}, u32[]{:S(2)}) collective-permute-start(f32[256,128]{1,0:T(8,128)S(1)} %get-tuple-element.65), channel_id=1, source_target_pairs={{0,8},{1,9},{2,10},{3,11},{4,12},{5,13},{6,14},{7,15},{8,0},{9,1},... | collective-permute-start | bytes 393224 | tf_op jit(solution)/shard_map/ppermute | solution.py:242
  105.9 10.2 %collective-permute-start.25 = (f32[256,128]{1,0:T(8,128)S(1)}, f32[256,128]{1,0:T(8,128)S(1)}, u32[]{:S(2)}, u32[]{:S(2)}) collective-permute-start(f32[256,128]{1,0:T(8,128)S(1)} %get-tuple-element.66), channel_id=1, source_target_pairs={{0,12},{1,13},{2,14},{3,15},{4,8},{5,9},{6,10},{7,11},{8,4},{9,5},... | collective-permute-start | bytes 393224 | tf_op jit(solution)/shard_map/ppermute | solution.py:242
  107.3 9.4 %collective-permute-start.26 = (f32[256,128]{1,0:T(8,128)S(1)}, f32[256,128]{1,0:T(8,128)S(1)}, u32[]{:S(2)}, u32[]{:S(2)}) collective-permute-start(f32[256,128]{1,0:T(8,128)S(1)} %get-tuple-element.67), channel_id=1, source_target_pairs={{0,4},{1,5},{2,6},{3,7},{4,0},{5,1},{6,2},{7,3},{8,12},{9,13},{10,... | collective-permute-start | bytes 393224 | tf_op jit(solution)/shard_map/ppermute | solution.py:242
  120.8 5.8 %collective-permute-start.32 = (f32[8,128]{1,0:T(8,128)S(1)}, f32[8,128]{1,0:T(8,128)S(1)}, u32[]{:S(2)}, u32[]{:S(2)}) collective-permute-start(f32[8,128]{1,0:T(8,128)S(1)} %add_add_fusion.1), channel_id=1, source_target_pairs={{0,12},{1,13},{2,14},{3,15},{4,8},{5,9},{6,10},{7,11},{8,4},{9,5},... | collective-permute-start | bytes 12296 | tf_op jit(solution)/shard_map/ppermute | solution.py:242
  (23 other events, 211.1 us)

commit v4 on v3

--- a/solution.py
+++ b/solution.py
@@ -38,13 +38,14 @@
             out[pl.ds(c, na, stride=nc), :] = x_ref[c, rows_of(spot, s, len(outs), na), :]
 
 
-def kinetic_kernel(na, nc, n, n_in, based, n_out, me_ref, quanta, ks, kr, prev, *refs):
+def kinetic_kernel(na, nc, n, n_in, based, n_out, n_behind, me_ref, quanta, ks, kr, prev, *refs):
     spot, _ = place(me_ref)
     refs = list(refs)
     take = lambda k: [refs.pop(0) for _ in range(k)]
     pieces = take(n_in)
     base = refs.pop(0) if based else None
     cur = None if n_in else refs.pop(0)
+    take(n_behind)
     u_refs = take(n_out)
     y_ref = refs.pop(0)
     cur = refs.pop(0) if n_in else cur
@@ -170,21 +171,22 @@
     sq[...] = total
 
 
-def group_join_kernel(n, n_all, me_ref, *refs):
-    spot, _ = place(me_ref)
-    ws, us, rest = refs[:n], refs[n : 2 * n], refs[2 * n :]
-    near, out, sq = rest[0] if n_all else None, rest[-2 - bool(n_all)], rest[-1 - bool(n_all)]
+def group_join_kernel(n, me_ref, *refs):
+    ws, us, (out, sq) = refs[:n], refs[n : 2 * n], refs[-2:]
     total = 0.0
     for s in range(n):
         y = ws[s][...] + us[s][...]
         out[s] = y
-        if n_all:
-            rest[-1][spot ^ hop(s + 1, n_all)] = y
         total = total + jnp.sum((y * y).reshape(-1, 8, y.shape[1]), axis=0)
-    if n_all:
-        rest[-1][spot] = near[0]
-        rest[-1][spot ^ hop(n_all - 1, n_all)] = near[1]
     sq[...] = total
+
+
+def ungroup_kernel(n, me_ref, near, far, behind_ref, out):
+    spot, _ = place(me_ref)
+    out[spot] = near[0]
+    out[spot ^ hop(n - 1, n)] = near[1]
+    for s in range(1, n - 1):
+        out[spot ^ hop(s, n)] = far[s - 1]
 
 
 def last_of(na, nc, u_ref, pieces, spot):
@@ -215,7 +217,7 @@
     return pltpu.with_memory_space_constraint(x, pltpu.VMEM)
 
 
-def call(kernel, outs, scalars, arrays, scratch=(), specs=None):
+def call(kernel, outs, scalars, arrays, scratch=(), specs=None, flops=0):
     return pl.pallas_call(
         kernel,
         out_shape=outs,
@@ -223,7 +225,7 @@
         out_specs=[VM] * len(outs),
         scratch_shapes=list(scratch),
         compiler_params=pltpu.CompilerParams(vmem_limit_bytes=20 << 20),
-        cost_estimate=pl.CostEstimate(flops=0, bytes_accessed=1 << 16, transcendentals=0),
+        cost_estimate=pl.CostEstimate(flops=flops, bytes_accessed=1 << 16, transcendentals=0),
     )(*scalars, *arrays)
 
 
@@ -258,9 +260,8 @@
         over = local(after(swap(x, 2), *beside))
         return [[y] for y in (x, across(x, 1), over, across(over, 1))]
 
-    def gather_near_far(near, far, *beside):
-        over = local(after(swap(near, 2), *beside))
-        rows = [[x, across(x, 1), y, across(y, 1)] for x, y in ((far, across(far, 2)), (near, over))]
+    def gather_near_far(near, far, near_core, far_core, over):
+        rows = [[x, y, z, across(z, 1)] for x, y, z in ((far, far_core, across(far, 2)), (near, near_core, over))]
         return list(zip(*rows))
 
     piece = pltpu.VMEM((na * nc, nb), F32)
@@ -270,15 +271,17 @@
     natural = sds((nc, nr, nb), F32)
     split = pltpu.VMEM((nd, nc, max(1, na // 2) * nb), BF16)
 
-    def kinetic(prev, cur=(), pieces=(), base=(), n_out=0, out=()):
-        kernel = functools.partial(kinetic_kernel, na, nc, n, len(pieces), len(base), n_out)
+    def kinetic(prev, cur=(), pieces=(), base=(), n_out=0, out=(), behind=()):
+        kernel = functools.partial(kinetic_kernel, na, nc, n, len(pieces), len(base), n_out, len(behind))
         arrays = [kin_stretch, kin_radius, prev, *pieces, *base, *cur]
         outs = [packed] if n_out == 1 else [piece] * n_out
-        return call(kernel, [*outs, on_chip, *out], [me, quanta.T], arrays)
-
-    def mix(sources):
+        specs = [VM] * len(arrays) + [ANY] * len(behind)
+        return call(kernel, [*outs, on_chip, *out], [me, quanta.T], arrays + list(behind), (), specs)
+
+    def mix(sources, flops=0):
         arrays = [coup, potential, *(x for source in sources for x in source)]
-        return call(functools.partial(mix_kernel, nc, n, len(sources[0])), [piece] * n, [me], arrays, [split, split])
+        kernel = functools.partial(mix_kernel, nc, n, len(sources[0]))
+        return call(kernel, [piece] * n, [me], arrays, [split, split], flops=flops)
 
     def group(pieces, behind=()):
         k = len(pieces)
@@ -286,11 +289,11 @@
         kernel = functools.partial(group_kernel, k)
         return call(kernel, [pltpu.VMEM((k, na * nc, nb), F32)], [me], [*pieces, *behind], (), specs)[0]
 
-    def group_join(ws, us, near=()):
+    def group_join(ws, us, behind=()):
         k = len(ws)
-        kernel = functools.partial(group_join_kernel, k, n if near else 0)
-        outs = [pltpu.VMEM((k, na * nc, nb), F32), square] + [packed] * len(near)
-        return call(kernel, outs, [me], [*ws, *us, *near])
+        outs = [pltpu.VMEM((k, na * nc, nb), F32), square]
+        specs = [VM] * (2 * k) + [ANY] * len(behind)
+        return call(functools.partial(group_join_kernel, k), outs, [me], [*ws, *us, *behind], (), specs)
 
     (coup,) = call(
         functools.partial(coupling_kernel, cb, nc, n),
@@ -299,22 +302,28 @@
         [pltpu.with_memory_space_constraint(angular, pltpu.HBM)],
         [pltpu.VMEM((lam, n, nc, total_ch), F32), pltpu.SemaphoreType.DMA((lam * n,))],
         [pl.BlockSpec(memory_space=pltpu.HBM)],
+        flops=5000000000,
     )
     v1 = exchange(call(functools.partial(to_pieces_kernel, na, nc), [piece] * n, [me], [psi_cur]))
+    near, far = near_far(v1)
+    near = group(near)
     u1, u1_nat = kinetic(psi_prev, [psi_cur], n_out=1)
     u1 = exchange_all(u1)
-    near, far = near_far(v1)
-    w1 = mix(gather_near_far(group(near, [u1_nat]), group(far), coup))
+    far = group(far, [u1_nat])
+    w1 = mix(gather_near_far(near, far, across(near, 1), across(far, 1), local(after(swap(near, 2), coup))), 0)
     w1_c = exchange(w1)
     v2, s2 = call(functools.partial(join_kernel, n), [packed, square], [me], [u1, *w1])
     *u2, _, v2_nat = kinetic(psi_cur, pieces=w1_c, base=[u1_nat], n_out=n, out=[on_chip])
     w2 = near_far(mix(gather(v2, w1_c[1:])))
     u2 = near_far(exchange(u2))
     near, s3 = group_join(w2[0], u2[0])
-    far, s3_far, v3 = group_join(w2[1], u2[1], [near])
+    near_core, near_over = across(near, 1), across(near, 2)
+    far, s3_far = group_join(w2[1], u2[1], [near])
+    far_core = across(far, 1)
+    (v3,) = call(functools.partial(ungroup_kernel, n), [packed], [me], [near, far, far_core], (), [VM, VM, ANY])
     v3 = exchange_all(v3)
     u3, prev_out = kinetic(v2_nat, pieces=[v3], out=[natural])
-    w3 = exchange(mix(gather_near_far(near, far)))
+    w3 = exchange(mix(gather_near_far(near, far, near_core, far_core, near_over), 2500000000))
     (sums,) = call(functools.partial(norm_kernel, na, nc, n), [sds((8, nb), F32)], [me], [u3, *w3, s2, s3, s3_far])
     (cur_out,) = call(functools.partial(finish_kernel, na, nc), [natural], [me], [u3, *w3])
     bit = 1

time: 130 us -> 115 us (0.88)
  waiting for transfers between devices: 60 us -> 45.4 us
  Pallas kernels: 17.6 us -> 19.2 us
    ppermute x33, waiting for transfers between devices: 60 us -> 45.4 us  [swap(): return lax.ppermute(x, 'chan', [(i, i ^ bits) for i in range(nd)])]
    pallas_call x15 -> x16, Pallas kernels: 17.6 us -> 19.2 us  [call(): pl.pallas_call(kernel, out_shape=outs, in_specs=[SM] * len(scalars) + (sp...]
    unnamed x24 -> x22, local copies, waits for them, and re-layouts: 5.39 us -> 4.35 us
  transfers between devices with their start and end apart: 35 -> 35, of which waited for: 17 -> 17; matrix products, arithmetic and copies ran while one was open for 0% -> 0% of each run, Pallas kernels for 10% -> 16%
where the time goes in v4:
time: 115 us; the launch traced here: 114 us
  waiting for transfers between devices  45.4 us (39%)
  starting transfers between devices  44.1 us (38%)
  Pallas kernels  19.2 us (17%)
  local copies, waits for them, and re-layouts  4.35 us (4%)
    ppermute x33, waiting for transfers between devices, swap(): return lax.ppermute(x, 'chan', [(i, i ^ bits) for i in range(nd)])  45.4 us
    ppermute x33, starting transfers between devices, swap(): return lax.ppermute(x, 'chan', [(i, i ^ bits) for i in range(nd)])  33.3 us
    pallas_call x16, Pallas kernels, call(): pl.pallas_call(kernel, out_shape=outs, in_specs=[SM] * len(scalars) + (sp...  19.2 us
    all_to_all x2, starting transfers between devices, exchange_all(): lax.all_to_all(x, 'chan', 0, 0, tiled=True, axis_index_groups=lines)  10.8 us
    unnamed x22, local copies, waits for them, and re-layouts  4.35 us
  transfers between devices with their start and end apart: 35, of which 17 were waited for; matrix products, arithmetic and copies ran while one was open for 0% of the time, Pallas kernels for 16%

profile of v4, /device:TPU:0, one launch (start us, length us, event | category | flops | bytes accessed | tf_op | source)
XLA Modules:
  0.0 114.5 jit_solution(9628216819421630534)
XLA Ops:
  2.0 3.1 %collective-permute-start.2 = (f32[256,128]{1,0:T(8,128)S(1)}, f32[256,128]{1,0:T(8,128)S(1)}, u32[]{:S(2)}, u32[]{:S(2)}) collective-permute-start(f32[256,128]{1,0:T(8,128)S(1)} %get-tuple-element.40), channel_id=1, source_target_pairs={{0,4},{1,5},{2,6},{3,7},{4,0},{5,1},{6,2},{7,3},{8,12},{9,13},{10,... | collective-permute-start | bytes 393224 | tf_op jit(solution)/shard_map/ppermute | solution.py:244
  5.1 2.6 %collective-permute-start = (f32[256,128]{1,0:T(8,128)S(1)}, f32[256,128]{1,0:T(8,128)S(1)}, u32[]{:S(2)}, u32[]{:S(2)}) collective-permute-start(f32[256,128]{1,0:T(8,128)S(1)} %get-tuple-element.36), channel_id=1, source_target_pairs={{0,8},{1,9},{2,10},{3,11},{4,12},{5,13},{6,14},{7,15},{8,0},{9,1},... | collective-permute-start | bytes 393224 | tf_op jit(solution)/shard_map/ppermute | solution.py:244
  11.0 2.8 %shard_map.105 = (f32[4,256,128]{2,1,0:T(8,128)}, f32[32,32,128]{2,1,0:T(8,128)S(1)}) custom-call(s32[1]{0:T(128)} %bitcast.me_ref, s32[2,32]{1,0:T(2,128)S(1)} %bitcast.2, f32[32,32]{1,0:T(8,128)S(1)} %copy-done.6, f32[128,128]{1,0:T(8,128)S(1)} %copy-done.2, f32[32,32,128]{2,1,0:T(8,128)S(1)} %copy-done.4, f32[32,32,128]{2,1,0:T(8,128)S(1)} %copy-done), custom_call_target="tpu_custom_call" | custom-call | bytes 65536 | tf_op jit(solution)/shard_map/pallas_call | solution.py:221
  13.7 5.1 %all-to-all-start = ((f32[4,256,128]{2,1,0:T(8,128)}), f32[4,256,128]{2,1,0:T(8,128)S(1)}, u32[]{:S(2)}, u32[]{:S(2)}) async-start(f32[4,256,128]{2,1,0:T(8,128)} %get-tuple-element.47), calls=%async_computation | async-start | bytes 1048576 | tf_op jit(solution)/shard_map/all_to_all | solution.py:254
  21.1 2.0 %shard_map.103.coup = bf16[3,2,4,32,512]{4,3,2,1,0:T(8,128)(2,1)S(1)} custom-call(s32[1]{0:T(128)} %bitcast.me_ref, s32[8,8]{1,0:T(8,128)S(1)} %copy-done.10, f32[3,512,512]{2,1,0:T(8,128)} %ang_ref.1), custom_call_target="tpu_custom_call" | custom-call | flops 5000000000 | bytes 65536 | tf_op jit(solution)/shard_map/pallas_call | solution.py:221
  23.7 4.5 %collective-permute-done.6.refs_5_ = f32[2,256,128]{2,1,0:T(8,128)S(1)} collective-permute-done((f32[2,256,128]{2,1,0:T(8,128)S(1)}, f32[2,256,128]{2,1,0:T(8,128)S(1)}, u32[]{:S(2)}, u32[]{:S(2)}) %collective-permute-start.6) | collective-permute-done | bytes 262176 | tf_op jit(solution)/shard_map/ppermute | solution.py:244
  28.2 3.3 %collective-permute-done.5.refs_4_ = f32[2,256,128]{2,1,0:T(8,128)S(1)} collective-permute-done((f32[2,256,128]{2,1,0:T(8,128)S(1)}, f32[2,256,128]{2,1,0:T(8,128)S(1)}, u32[]{:S(2)}, u32[]{:S(2)}) %collective-permute-start.5) | collective-permute-done | bytes 262176 | tf_op jit(solution)/shard_map/ppermute | solution.py:244
  33.0 1.7 %shard_map.108 = (f32[256,128]{1,0:T(8,128)S(1)}, f32[256,128]{1,0:T(8,128)S(1)}, f32[256,128]{1,0:T(8,128)S(1)}, f32[256,128]{1,0:T(8,128)S(1)}) custom-call(s32[1]{0:T(128)} %bitcast.me_ref, bf16[3,2,4,32,512]{4,3,2,1,0:T(8,128)(2,1)S(1)} %shard_map.103.coup, f32[3,32,128]{2,1,0:T(8,128)S(1)} %copy-done.5, f32[2,256,128]{2,1,0:T(8,128)S(1)} %shard_map.106.refs_0_, ...), custom_call_target="tpu_custom_call" | custom-call | bytes 65536 | tf_op jit(solution)/shard_map/pallas_call | solution.py:221
  36.4 2.6 %collective-permute-start.9 = (f32[256,128]{1,0:T(8,128)S(1)}, f32[256,128]{1,0:T(8,128)S(1)}, u32[]{:S(2)}, u32[]{:S(2)}) collective-permute-start(f32[256,128]{1,0:T(8,128)S(1)} %get-tuple-element.43.refs_1_), channel_id=1, source_target_pairs={{0,8},{1,9},{2,10},{3,11},{4,12},{5,13},{6,14},{7,15},{8,0},{9,1},... | collective-permute-start | bytes 393224 | tf_op jit(solution)/shard_map/ppermute | solution.py:244
  40.5 8.8 %collective-permute-done.9.refs_1_ = f32[256,128]{1,0:T(8,128)S(1)} collective-permute-done((f32[256,128]{1,0:T(8,128)S(1)}, f32[256,128]{1,0:T(8,128)S(1)}, u32[]{:S(2)}, u32[]{:S(2)}) %collective-permute-start.9) | collective-permute-done | bytes 131104 | tf_op jit(solution)/shard_map/ppermute | solution.py:244
  49.6 2.8 %shard_map.109 = (f32[256,128]{1,0:T(8,128)S(1)}, f32[256,128]{1,0:T(8,128)S(1)}, f32[256,128]{1,0:T(8,128)S(1)}, f32[256,128]{1,0:T(8,128)S(1)}, f32[32,32,128]{2,1,0:T(8,128)}, /*index=5*/f32[32,32,128]{2,1,0:T(8,128)S(1)}) custom-call(s32[1]{0:T(128)} %bitcast.me_ref, s32[2,32]{1,0:T(2,128)S(1)} %bitcast.3, f32[32,32]{1,0:T(8,128)S(1)} %copy-done.7, ...), custom_call_target="tpu_custom_call" | custom-call | bytes 65536 | tf_op jit(solution)/shard_map/pallas_call | solution.py:221
  52.4 2.2 %collective-permute-start.15 = (f32[256,128]{1,0:T(8,128)S(1)}, f32[256,128]{1,0:T(8,128)S(1)}, u32[]{:S(2)}, u32[]{:S(2)}) collective-permute-start(f32[256,128]{1,0:T(8,128)S(1)} %get-tuple-element.53), channel_id=1, source_target_pairs={{0,4},{1,5},{2,6},{3,7},{4,0},{5,1},{6,2},{7,3},{8,12},{9,13},{10,... | collective-permute-start | bytes 393224 | tf_op jit(solution)/shard_map/ppermute | solution.py:244
  54.6 1.9 %collective-permute-start.16 = (f32[256,128]{1,0:T(8,128)S(1)}, f32[256,128]{1,0:T(8,128)S(1)}, u32[]{:S(2)}, u32[]{:S(2)}) collective-permute-start(f32[256,128]{1,0:T(8,128)S(1)} %get-tuple-element.57), channel_id=1, source_target_pairs={{0,8},{1,9},{2,10},{3,11},{4,12},{5,13},{6,14},{7,15},{8,0},{9,1},... | collective-permute-start | bytes 393224 | tf_op jit(solution)/shard_map/ppermute | solution.py:244
  58.0 1.6 %shard_map.111 = (f32[256,128]{1,0:T(8,128)S(1)}, f32[256,128]{1,0:T(8,128)S(1)}, f32[256,128]{1,0:T(8,128)S(1)}, f32[256,128]{1,0:T(8,128)S(1)}) custom-call(s32[1]{0:T(128)} %bitcast.me_ref, bf16[3,2,4,32,512]{4,3,2,1,0:T(8,128)(2,1)S(1)} %shard_map.103.coup, f32[3,32,128]{2,1,0:T(8,128)S(1)} %copy-done.5, f32[4,256,128]{2,1,0:T(8,128)S(1)} %get-tuple-element.48.refs_0_, ...), custom_call_target="tpu_custom_call" | custom-call | bytes 65536 | tf_op jit(solution)/shard_map/pallas_call | solution.py:221
  59.7 1.7 %collective-permute-done.15.refs_3_ = f32[256,128]{1,0:T(8,128)S(1)} collective-permute-done((f32[256,128]{1,0:T(8,128)S(1)}, f32[256,128]{1,0:T(8,128)S(1)}, u32[]{:S(2)}, u32[]{:S(2)}) %collective-permute-start.15) | collective-permute-done | bytes 131104 | tf_op jit(solution)/shard_map/ppermute | solution.py:244
  62.0 5.6 %collective-permute-done.17.refs_3_ = f32[256,128]{1,0:T(8,128)S(1)} collective-permute-done((f32[256,128]{1,0:T(8,128)S(1)}, f32[256,128]{1,0:T(8,128)S(1)}, u32[]{:S(2)}, u32[]{:S(2)}) %collective-permute-start.17) | collective-permute-done | bytes 131104 | tf_op jit(solution)/shard_map/ppermute | solution.py:244
  70.6 5.7 %all-to-all-start.1 = ((f32[4,256,128]{2,1,0:T(8,128)}), f32[4,256,128]{2,1,0:T(8,128)S(1)}, u32[]{:S(2)}, u32[]{:S(2)}) async-start(f32[4,256,128]{2,1,0:T(8,128)} %shard_map.114), calls=%async_computation.1 | async-start | bytes 1048576 | tf_op jit(solution)/shard_map/all_to_all | solution.py:254
  76.9 5.3 %collective-permute-done.21.refs_5_ = f32[2,256,128]{2,1,0:T(8,128)} collective-permute-done((f32[2,256,128]{2,1,0:T(8,128)S(1)}, f32[2,256,128]{2,1,0:T(8,128)}, u32[]{:S(2)}, u32[]{:S(2)}) %collective-permute-start.21) | collective-permute-done | bytes 262176 | tf_op jit(solution)/shard_map/ppermute | solution.py:244
  82.2 1.7 %collective-permute-done.23.refs_7_ = f32[2,256,128]{2,1,0:T(8,128)S(1)} collective-permute-done((f32[2,256,128]{2,1,0:T(8,128)}, f32[2,256,128]{2,1,0:T(8,128)S(1)}, u32[]{:S(2)}, u32[]{:S(2)}) %collective-permute-start.23) | collective-permute-done | bytes 262176 | tf_op jit(solution)/shard_map/ppermute | solution.py:244
  83.9 3.2 %shard_map.116 = (f32[256,128]{1,0:T(8,128)S(1)}, f32[256,128]{1,0:T(8,128)}, f32[256,128]{1,0:T(8,128)S(1)}, f32[256,128]{1,0:T(8,128)S(1)}) custom-call(s32[1]{0:T(128)} %bitcast.me_ref, bf16[3,2,4,32,512]{4,3,2,1,0:T(8,128)(2,1)S(1)} %shard_map.103.coup, f32[3,32,128]{2,1,0:T(8,128)S(1)} %copy-done.5, f32[2,256,128]{2,1,0:T(8,128)S(1)} %get-tuple-element.59.far.refs_0_, ...), custom_call_target="tpu_custom_call" | custom-call | flops 2500000000 | bytes 65536 | tf_op jit(solution)/shard_map/pallas_call | solution.py:221
  87.1 4.4 %collective-permute-start.24 = (f32[256,128]{1,0:T(8,128)}, f32[256,128]{1,0:T(8,128)S(1)}, u32[]{:S(2)}, u32[]{:S(2)}) collective-permute-start(f32[256,128]{1,0:T(8,128)} %get-tuple-element.63), channel_id=1, source_target_pairs={{0,8},{1,9},{2,10},{3,11},{4,12},{5,13},{6,14},{7,15},{8,0},{9,1},... | collective-permute-start | bytes 393224 | tf_op jit(solution)/shard_map/ppermute | solution.py:244
  92.1 2.2 %shard_map.115 = (f32[32,32,128]{2,1,0:T(8,128)S(1)}, f32[32,32,128]{2,1,0:T(8,128)}) custom-call(s32[1]{0:T(128)} %bitcast.me_ref, s32[2,32]{1,0:T(2,128)S(1)} %bitcast.4, f32[32,32]{1,0:T(8,128)S(1)} %copy-done.7, f32[128,128]{1,0:T(8,128)S(1)} %copy-done.3, f32[32,32,128]{2,1,0:T(8,128)S(1)} %get-tuple-element.46.prev, ...), custom_call_target="tpu_custom_call" | custom-call | bytes 65536 | tf_op jit(solution)/shard_map/pallas_call | solution.py:221
  94.3 7.2 %collective-permute-done.24.refs_1_ = f32[256,128]{1,0:T(8,128)S(1)} collective-permute-done((f32[256,128]{1,0:T(8,128)}, f32[256,128]{1,0:T(8,128)S(1)}, u32[]{:S(2)}, u32[]{:S(2)}) %collective-permute-start.24) | collective-permute-done | bytes 131104 | tf_op jit(solution)/shard_map/ppermute | solution.py:244
  107.9 2.3 %collective-permute-start.31 = (f32[8,128]{1,0:T(8,128)S(1)}, f32[8,128]{1,0:T(8,128)S(1)}, u32[]{:S(2)}, u32[]{:S(2)}) collective-permute-start(f32[8,128]{1,0:T(8,128)S(1)} %add_add_fusion.1), channel_id=1, source_target_pairs={{0,8},{1,9},{2,10},{3,11},{4,12},{5,13},{6,14},{7,15},{8,0},{9,1},... | collective-permute-start | bytes 12296 | tf_op jit(solution)/shard_map/ppermute | solution.py:244
  (88 shorter events, 29.2 us)
Async XLA Ops:
  2.0 16.8 %collective-permute-start.2 = (f32[256,128]{1,0:T(8,128)S(1)}, f32[256,128]{1,0:T(8,128)S(1)}, u32[]{:S(2)}, u32[]{:S(2)}) collective-permute-start(f32[256,128]{1,0:T(8,128)S(1)} %get-tuple-element.40), channel_id=1, source_target_pairs={{0,4},{1,5},{2,6},{3,7},{4,0},{5,1},{6,2},{7,3},{8,12},{9,13},{10,... | collective-permute-start | bytes 393224 | tf_op jit(solution)/shard_map/ppermute | solution.py:244
  5.1 15.4 %collective-permute-start = (f32[256,128]{1,0:T(8,128)S(1)}, f32[256,128]{1,0:T(8,128)S(1)}, u32[]{:S(2)}, u32[]{:S(2)}) collective-permute-start(f32[256,128]{1,0:T(8,128)S(1)} %get-tuple-element.36), channel_id=1, source_target_pairs={{0,8},{1,9},{2,10},{3,11},{4,12},{5,13},{6,14},{7,15},{8,0},{9,1},... | collective-permute-start | bytes 393224 | tf_op jit(solution)/shard_map/ppermute | solution.py:244
  7.7 12.8 %collective-permute-start.1 = (f32[256,128]{1,0:T(8,128)S(1)}, f32[256,128]{1,0:T(8,128)S(1)}, u32[]{:S(2)}, u32[]{:S(2)}) collective-permute-start(f32[256,128]{1,0:T(8,128)S(1)} %get-tuple-element.37), channel_id=1, source_target_pairs={{0,12},{1,13},{2,14},{3,15},{4,8},{5,9},{6,10},{7,11},{8,4},{9,5},... | collective-permute-start | bytes 393224 | tf_op jit(solution)/shard_map/ppermute | solution.py:244
  13.7 20.9 %all-to-all-start = ((f32[4,256,128]{2,1,0:T(8,128)}), f32[4,256,128]{2,1,0:T(8,128)S(1)}, u32[]{:S(2)}, u32[]{:S(2)}) async-start(f32[4,256,128]{2,1,0:T(8,128)} %get-tuple-element.47), calls=%async_computation | async-start | bytes 1048576 | tf_op jit(solution)/shard_map/all_to_all | solution.py:254
  18.9 9.3 %collective-permute-start.6 = (f32[2,256,128]{2,1,0:T(8,128)S(1)}, f32[2,256,128]{2,1,0:T(8,128)S(1)}, u32[]{:S(2)}, u32[]{:S(2)}) collective-permute-start(f32[2,256,128]{2,1,0:T(8,128)S(1)} %shard_map.107.refs_1_), channel_id=1, source_target_pairs={{0,2},{1,3},{2,0},{3,1},{4,6},{5,7},{6,4},{7,5},{8,10},{9,11},{10,... | collective-permute-start | bytes 786440 | tf_op jit(solution)/shard_map/ppermute | solution.py:244
  20.5 11.0 %collective-permute-start.5 = (f32[2,256,128]{2,1,0:T(8,128)S(1)}, f32[2,256,128]{2,1,0:T(8,128)S(1)}, u32[]{:S(2)}, u32[]{:S(2)}) collective-permute-start(f32[2,256,128]{2,1,0:T(8,128)S(1)} %shard_map.106.refs_0_), channel_id=1, source_target_pairs={{0,2},{1,3},{2,0},{3,1},{4,6},{5,7},{6,4},{7,5},{8,10},{9,11},{10,... | collective-permute-start | bytes 786440 | tf_op jit(solution)/shard_map/ppermute | solution.py:244
  23.1 8.4 %collective-permute-start.4 = (f32[2,256,128]{2,1,0:T(8,128)S(1)}, f32[2,256,128]{2,1,0:T(8,128)S(1)}, u32[]{:S(2)}, u32[]{:S(2)}) collective-permute-start(f32[2,256,128]{2,1,0:T(8,128)S(1)} %shard_map.107.refs_1_), channel_id=1, source_target_pairs={{0,1},{1,0},{2,3},{3,2},{4,5},{5,4},{6,7},{7,6},{8,9},{9,8},{10,11... | collective-permute-start | bytes 786440 | tf_op jit(solution)/shard_map/ppermute | solution.py:244
  23.2 8.3 %collective-permute-start.3 = (f32[2,256,128]{2,1,0:T(8,128)S(1)}, f32[2,256,128]{2,1,0:T(8,128)S(1)}, u32[]{:S(2)}, u32[]{:S(2)}) collective-permute-start(f32[2,256,128]{2,1,0:T(8,128)S(1)} %shard_map.106.refs_0_), channel_id=1, source_target_pairs={{0,1},{1,0},{2,3},{3,2},{4,5},{5,4},{6,7},{7,6},{8,9},{9,8},{10,11... | collective-permute-start | bytes 786440 | tf_op jit(solution)/shard_map/ppermute | solution.py:244
  34.8 14.7 %collective-permute-start.13 = (f32[4,256,128]{2,1,0:T(8,128)S(1)}, f32[4,256,128]{2,1,0:T(8,128)S(1)}, u32[]{:S(2)}, u32[]{:S(2)}) collective-permute-start(f32[4,256,128]{2,1,0:T(8,128)S(1)} %get-tuple-element.48.refs_0_), channel_id=1, source_target_pairs={{0,2},{1,3},{2,0},{3,1},{4,6},{5,7},{6,4},{7,5},{8,10},{9,11},{10,... | collective-permute-start | bytes 1572872 | tf_op jit(solution)/shard_map/ppermute | solution.py:244
  36.4 12.9 %collective-permute-start.9 = (f32[256,128]{1,0:T(8,128)S(1)}, f32[256,128]{1,0:T(8,128)S(1)}, u32[]{:S(2)}, u32[]{:S(2)}) collective-permute-start(f32[256,128]{1,0:T(8,128)S(1)} %get-tuple-element.43.refs_1_), channel_id=1, source_target_pairs={{0,8},{1,9},{2,10},{3,11},{4,12},{5,13},{6,14},{7,15},{8,0},{9,1},... | collective-permute-start | bytes 393224 | tf_op jit(solution)/shard_map/ppermute | solution.py:244
  39.0 10.3 %collective-permute-start.10 = (f32[256,128]{1,0:T(8,128)S(1)}, f32[256,128]{1,0:T(8,128)S(1)}, u32[]{:S(2)}, u32[]{:S(2)}) collective-permute-start(f32[256,128]{1,0:T(8,128)S(1)} %get-tuple-element.44.refs_2_), channel_id=1, source_target_pairs={{0,12},{1,13},{2,14},{3,15},{4,8},{5,9},{6,10},{7,11},{8,4},{9,5},... | collective-permute-start | bytes 393224 | tf_op jit(solution)/shard_map/ppermute | solution.py:244
  40.5 9.0 %collective-permute-start.11 = (f32[256,128]{1,0:T(8,128)S(1)}, f32[256,128]{1,0:T(8,128)S(1)}, u32[]{:S(2)}, u32[]{:S(2)}) collective-permute-start(f32[256,128]{1,0:T(8,128)S(1)} %get-tuple-element.45.refs_3_), channel_id=1, source_target_pairs={{0,4},{1,5},{2,6},{3,7},{4,0},{5,1},{6,2},{7,3},{8,12},{9,13},{10,... | collective-permute-start | bytes 393224 | tf_op jit(solution)/shard_map/ppermute | solution.py:244
  40.5 17.5 %collective-permute-start.12 = (f32[4,256,128]{2,1,0:T(8,128)S(1)}, f32[4,256,128]{2,1,0:T(8,128)S(1)}, u32[]{:S(2)}, u32[]{:S(2)}) collective-permute-start(f32[4,256,128]{2,1,0:T(8,128)S(1)} %get-tuple-element.48.refs_0_), channel_id=1, source_target_pairs={{0,1},{1,0},{2,3},{3,2},{4,5},{5,4},{6,7},{7,6},{8,9},{9,8},{10,11... | collective-permute-start | bytes 1572872 | tf_op jit(solution)/shard_map/ppermute | solution.py:244
  49.5 8.5 %collective-permute-start.14 = (f32[4,256,128]{2,1,0:T(8,128)S(1)}, f32[4,256,128]{2,1,0:T(8,128)S(1)}, u32[]{:S(2)}, u32[]{:S(2)}) collective-permute-start(f32[4,256,128]{2,1,0:T(8,128)S(1)} %collective-permute-done.13.refs_2_), channel_id=1, source_target_pairs={{0,1},{1,0},{2,3},{3,2},{4,5},{5,4},{6,7},{7,6},{8,9},{9,8},{10,11... | collective-permute-start | bytes 1572872 | tf_op jit(solution)/shard_map/ppermute | solution.py:244
  52.4 9.0 %collective-permute-start.15 = (f32[256,128]{1,0:T(8,128)S(1)}, f32[256,128]{1,0:T(8,128)S(1)}, u32[]{:S(2)}, u32[]{:S(2)}) collective-permute-start(f32[256,128]{1,0:T(8,128)S(1)} %get-tuple-element.53), channel_id=1, source_target_pairs={{0,4},{1,5},{2,6},{3,7},{4,0},{5,1},{6,2},{7,3},{8,12},{9,13},{10,... | collective-permute-start | bytes 393224 | tf_op jit(solution)/shard_map/ppermute | solution.py:244
  54.6 7.4 %collective-permute-start.16 = (f32[256,128]{1,0:T(8,128)S(1)}, f32[256,128]{1,0:T(8,128)S(1)}, u32[]{:S(2)}, u32[]{:S(2)}) collective-permute-start(f32[256,128]{1,0:T(8,128)S(1)} %get-tuple-element.57), channel_id=1, source_target_pairs={{0,8},{1,9},{2,10},{3,11},{4,12},{5,13},{6,14},{7,15},{8,0},{9,1},... | collective-permute-start | bytes 393224 | tf_op jit(solution)/shard_map/ppermute | solution.py:244
  56.5 11.0 %collective-permute-start.17 = (f32[256,128]{1,0:T(8,128)S(1)}, f32[256,128]{1,0:T(8,128)S(1)}, u32[]{:S(2)}, u32[]{:S(2)}) collective-permute-start(f32[256,128]{1,0:T(8,128)S(1)} %get-tuple-element.58), channel_id=1, source_target_pairs={{0,12},{1,13},{2,14},{3,15},{4,8},{5,9},{6,10},{7,11},{8,4},{9,5},... | collective-permute-start | bytes 393224 | tf_op jit(solution)/shard_map/ppermute | solution.py:244
  67.7 9.2 %collective-permute-start.20 = (f32[2,256,128]{2,1,0:T(8,128)S(1)}, f32[2,256,128]{2,1,0:T(8,128)S(1)}, u32[]{:S(2)}, u32[]{:S(2)}) collective-permute-start(f32[2,256,128]{2,1,0:T(8,128)S(1)} %get-tuple-element.59.far.refs_0_), channel_id=1, source_target_pairs={{0,2},{1,3},{2,0},{3,1},{4,6},{5,7},{6,4},{7,5},{8,10},{9,11},{10,... | collective-permute-start | bytes 786440 | tf_op jit(solution)/shard_map/ppermute | solution.py:244
  68.3 13.9 %collective-permute-start.21 = (f32[2,256,128]{2,1,0:T(8,128)S(1)}, f32[2,256,128]{2,1,0:T(8,128)}, u32[]{:S(2)}, u32[]{:S(2)}) collective-permute-start(f32[2,256,128]{2,1,0:T(8,128)S(1)} %get-tuple-element.54.refs_4_.near.refs_1_), channel_id=1, source_target_pairs={{0,2},{1,3},{2,0},{3,1},{4,6},{5,7},{6,4},{7,5},{8,10},{9,11},{10,... | collective-permute-start | bytes 786440 | tf_op jit(solution)/shard_map/ppermute | solution.py:244
  70.6 21.5 %all-to-all-start.1 = ((f32[4,256,128]{2,1,0:T(8,128)}), f32[4,256,128]{2,1,0:T(8,128)S(1)}, u32[]{:S(2)}, u32[]{:S(2)}) async-start(f32[4,256,128]{2,1,0:T(8,128)} %shard_map.114), calls=%async_computation.1 | async-start | bytes 1048576 | tf_op jit(solution)/shard_map/all_to_all | solution.py:254
  76.3 5.8 %collective-permute-start.19 = (f32[2,256,128]{2,1,0:T(8,128)S(1)}, f32[2,256,128]{2,1,0:T(8,128)S(1)}, u32[]{:S(2)}, u32[]{:S(2)}) collective-permute-start(f32[2,256,128]{2,1,0:T(8,128)S(1)} %get-tuple-element.54.refs_4_.near.refs_1_), channel_id=1, source_target_pairs={{0,1},{1,0},{2,3},{3,2},{4,5},{5,4},{6,7},{7,6},{8,9},{9,8},{10,11... | collective-permute-start | bytes 786440 | tf_op jit(solution)/shard_map/ppermute | solution.py:244
  87.1 14.4 %collective-permute-start.24 = (f32[256,128]{1,0:T(8,128)}, f32[256,128]{1,0:T(8,128)S(1)}, u32[]{:S(2)}, u32[]{:S(2)}) collective-permute-start(f32[256,128]{1,0:T(8,128)} %get-tuple-element.63), channel_id=1, source_target_pairs={{0,8},{1,9},{2,10},{3,11},{4,12},{5,13},{6,14},{7,15},{8,0},{9,1},... | collective-permute-start | bytes 393224 | tf_op jit(solution)/shard_map/ppermute | solution.py:244
  91.6 10.0 %collective-permute-start.25 = (f32[256,128]{1,0:T(8,128)S(1)}, f32[256,128]{1,0:T(8,128)S(1)}, u32[]{:S(2)}, u32[]{:S(2)}) collective-permute-start(f32[256,128]{1,0:T(8,128)S(1)} %get-tuple-element.64), channel_id=1, source_target_pairs={{0,12},{1,13},{2,14},{3,15},{4,8},{5,9},{6,10},{7,11},{8,4},{9,5},... | collective-permute-start | bytes 393224 | tf_op jit(solution)/shard_map/ppermute | solution.py:244
  92.0 10.3 %collective-permute-start.26 = (f32[256,128]{1,0:T(8,128)S(1)}, f32[256,128]{1,0:T(8,128)S(1)}, u32[]{:S(2)}, u32[]{:S(2)}) collective-permute-start(f32[256,128]{1,0:T(8,128)S(1)} %get-tuple-element.65), channel_id=1, source_target_pairs={{0,4},{1,5},{2,6},{3,7},{4,0},{5,1},{6,2},{7,3},{8,12},{9,13},{10,... | collective-permute-start | bytes 393224 | tf_op jit(solution)/shard_map/ppermute | solution.py:244
  (22 other events, 180.7 us)

commit v5 on v4

--- a/solution.py
+++ b/solution.py
@@ -279,7 +279,7 @@
         return call(kernel, [*outs, on_chip, *out], [me, quanta.T], arrays + list(behind), (), specs)
 
     def mix(sources, flops=0):
-        arrays = [coup, potential, *(x for source in sources for x in source)]
+        arrays = [local(coup), local(potential), *(x for source in sources for x in source)]
         kernel = functools.partial(mix_kernel, nc, n, len(sources[0]))
         return call(kernel, [piece] * n, [me], arrays, [split, split], flops=flops)
 
@@ -302,26 +302,27 @@
         [pltpu.with_memory_space_constraint(angular, pltpu.HBM)],
         [pltpu.VMEM((lam, n, nc, total_ch), F32), pltpu.SemaphoreType.DMA((lam * n,))],
         [pl.BlockSpec(memory_space=pltpu.HBM)],
-        flops=5000000000,
+        flops=0,
     )
     v1 = exchange(call(functools.partial(to_pieces_kernel, na, nc), [piece] * n, [me], [psi_cur]))
     near, far = near_far(v1)
     near = group(near)
+    near_core, near_over = across(near, 1), across(near, 2)
     u1, u1_nat = kinetic(psi_prev, [psi_cur], n_out=1)
-    u1 = exchange_all(u1)
-    far = group(far, [u1_nat])
-    w1 = mix(gather_near_far(near, far, across(near, 1), across(far, 1), local(after(swap(near, 2), coup))), 0)
+    u1 = exchange_all(after(u1, near_over))
+    far = group(far, [coup, u1_nat])
+    w1 = mix(gather_near_far(near, far, near_core, across(far, 1), near_over), 5000000000)
     w1_c = exchange(w1)
     v2, s2 = call(functools.partial(join_kernel, n), [packed, square], [me], [u1, *w1])
     *u2, _, v2_nat = kinetic(psi_cur, pieces=w1_c, base=[u1_nat], n_out=n, out=[on_chip])
-    w2 = near_far(mix(gather(v2, w1_c[1:])))
+    w2 = near_far(mix(gather(v2, w1_c[1:]), 0))
     u2 = near_far(exchange(u2))
     near, s3 = group_join(w2[0], u2[0])
     near_core, near_over = across(near, 1), across(near, 2)
     far, s3_far = group_join(w2[1], u2[1], [near])
     far_core = across(far, 1)
     (v3,) = call(functools.partial(ungroup_kernel, n), [packed], [me], [near, far, far_core], (), [VM, VM, ANY])
-    v3 = exchange_all(v3)
+    v3 = exchange_all(after(v3, near_over))
     u3, prev_out = kinetic(v2_nat, pieces=[v3], out=[natural])
     w3 = exchange(mix(gather_near_far(near, far, near_core, far_core, near_over), 2500000000))
     (sums,) = call(functools.partial(norm_kernel, na, nc, n), [sds((8, nb), F32)], [me], [u3, *w3, s2, s3, s3_far])

time: 115 us -> 116 us (level)
  waiting for transfers between devices: 45.4 us -> 49.8 us
  starting transfers between devices: 44.1 us -> 41.8 us
  local copies, waits for them, and re-layouts: 4.35 us -> 2.7 us
    all_to_all x2, waiting for transfers between devices: 0.01 us -> 16.7 us  [exchange_all(): lax.all_to_all(x, 'chan', 0, 0, tiled=True, axis_index_groups=lines)]
    ppermute x33, waiting for transfers between devices: 45.4 us -> 33.1 us  [swap(): return lax.ppermute(x, 'chan', [(i, i ^ bits) for i in range(nd)])]
    unnamed x22 -> x20, local copies, waits for them, and re-layouts: 4.35 us -> 2.7 us
    all_to_all x2, starting transfers between devices: 10.8 us -> 9.2 us  [exchange_all(): lax.all_to_all(x, 'chan', 0, 0, tiled=True, axis_index_groups=lines)]
  transfers between devices with their start and end apart: 35 -> 35, of which waited for: 17 -> 24; matrix products, arithmetic and copies ran while one was open for 0% -> 0% of each run, Pallas kernels for 16% -> 17%
where the time goes in v5:
time: 116 us
  waiting for transfers between devices  49.8 us (43%)
  starting transfers between devices  41.8 us (36%)
  Pallas kernels  20.1 us (17%)
  local copies, waits for them, and re-layouts  2.7 us (2%)
    ppermute x33, waiting for transfers between devices, swap(): return lax.ppermute(x, 'chan', [(i, i ^ bits) for i in range(nd)])  33.1 us
    ppermute x33, starting transfers between devices, swap(): return lax.ppermute(x, 'chan', [(i, i ^ bits) for i in range(nd)])  32.6 us
    pallas_call x16, Pallas kernels, call(): pl.pallas_call(kernel, out_shape=outs, in_specs=[SM] * len(scalars) + (sp...  20.1 us
    all_to_all x2, waiting for transfers between devices, exchange_all(): lax.all_to_all(x, 'chan', 0, 0, tiled=True, axis_index_groups=lines)  16.7 us
    all_to_all x2, starting transfers between devices, exchange_all(): lax.all_to_all(x, 'chan', 0, 0, tiled=True, axis_index_groups=lines)  9.2 us
    unnamed x20, local copies, waits for them, and re-layouts  2.7 us
  transfers between devices with their start and end apart: 35, of which 24 were waited for; matrix products, arithmetic and copies ran while one was open for 0% of the time, Pallas kernels for 17%

profile of v5, /device:TPU:0, one launch (start us, length us, event | category | flops | bytes accessed | tf_op | source)
XLA Modules:
  0.0 115.9 jit_solution(2450249944161865544)
XLA Ops:
  2.0 3.1 %collective-permute-start.2 = (f32[256,128]{1,0:T(8,128)S(1)}, f32[256,128]{1,0:T(8,128)S(1)}, u32[]{:S(2)}, u32[]{:S(2)}) collective-permute-start(f32[256,128]{1,0:T(8,128)S(1)} %get-tuple-element.41), channel_id=1, source_target_pairs={{0,4},{1,5},{2,6},{3,7},{4,0},{5,1},{6,2},{7,3},{8,12},{9,13},{10,... | collective-permute-start | bytes 393224 | tf_op jit(solution)/shard_map/ppermute | solution.py:244
  5.1 2.6 %collective-permute-start = (f32[256,128]{1,0:T(8,128)S(1)}, f32[256,128]{1,0:T(8,128)S(1)}, u32[]{:S(2)}, u32[]{:S(2)}) collective-permute-start(f32[256,128]{1,0:T(8,128)S(1)} %get-tuple-element.37), channel_id=1, source_target_pairs={{0,8},{1,9},{2,10},{3,11},{4,12},{5,13},{6,14},{7,15},{8,0},{9,1},... | collective-permute-start | bytes 393224 | tf_op jit(solution)/shard_map/ppermute | solution.py:244
  7.7 2.4 %collective-permute-done.2.refs_1_ = f32[256,128]{1,0:T(8,128)S(1)} collective-permute-done((f32[256,128]{1,0:T(8,128)S(1)}, f32[256,128]{1,0:T(8,128)S(1)}, u32[]{:S(2)}, u32[]{:S(2)}) %collective-permute-start.2) | collective-permute-done | bytes 131104 | tf_op jit(solution)/shard_map/ppermute | solution.py:244
  10.2 1.8 %collective-permute-start.6 = (f32[2,256,128]{2,1,0:T(8,128)S(1)}, f32[2,256,128]{2,1,0:T(8,128)S(1)}, u32[]{:S(2)}, u32[]{:S(2)}) collective-permute-start(f32[2,256,128]{2,1,0:T(8,128)S(1)} %shard_map.107.refs_1_), channel_id=1, source_target_pairs={{0,2},{1,3},{2,0},{3,1},{4,6},{5,7},{6,4},{7,5},{8,10},{9,11},{10,... | collective-permute-start | bytes 786440 | tf_op jit(solution)/shard_map/ppermute | solution.py:244
  12.7 2.0 %shard_map.103.refs_2_.coup = bf16[3,2,4,32,512]{4,3,2,1,0:T(8,128)(2,1)S(1)} custom-call(s32[1]{0:T(128)} %bitcast.me_ref, s32[8,8]{1,0:T(8,128)S(1)} %copy-done.7, f32[3,512,512]{2,1,0:T(8,128)} %ang_ref.1), custom_call_target="tpu_custom_call" | custom-call | bytes 65536 | tf_op jit(solution)/shard_map/pallas_call | solution.py:221
  14.7 2.8 %shard_map.105 = (f32[4,256,128]{2,1,0:T(8,128)}, f32[32,32,128]{2,1,0:T(8,128)S(1)}) custom-call(s32[1]{0:T(128)} %bitcast.me_ref, s32[2,32]{1,0:T(2,128)S(1)} %bitcast.2, f32[32,32]{1,0:T(8,128)S(1)} %copy-done.4, f32[128,128]{1,0:T(8,128)S(1)} %copy-done.2, f32[32,32,128]{2,1,0:T(8,128)S(1)} %copy-done.3, f32[32,32,128]{2,1,0:T(8,128)S(1)} %copy-done.1), custom_call_target="tpu_custom_call" | custom-call | bytes 65536 | tf_op jit(solution)/shard_map/pallas_call | solution.py:221
  19.7 4.2 %all-to-all-start = ((f32[4,256,128]{2,1,0:T(8,128)}), f32[4,256,128]{2,1,0:T(8,128)S(1)}, u32[]{:S(2)}, u32[]{:S(2)}) async-start(f32[4,256,128]{2,1,0:T(8,128)} %get-tuple-element.48), calls=%async_computation | async-start | bytes 1048576 | tf_op jit(solution)/shard_map/all_to_all | solution.py:254
  27.7 2.6 %shard_map.108 = (f32[256,128]{1,0:T(8,128)S(1)}, f32[256,128]{1,0:T(8,128)S(1)}, f32[256,128]{1,0:T(8,128)S(1)}, f32[256,128]{1,0:T(8,128)S(1)}) custom-call(s32[1]{0:T(128)} %bitcast.me_ref, bf16[3,2,4,32,512]{4,3,2,1,0:T(8,128)(2,1)S(1)} %shard_map.103.refs_2_.coup, f32[3,32,128]{2,1,0:T(8,128)S(1)} %copy-done.5, f32[2,256,128]{2,1,0:T(8,128)S(1)} %shard_map.106.refs_0_, ...), custom_call_target="tpu_custom_call" | custom-call | flops 5000000000 | bytes 65536 | tf_op jit(solution)/shard_map/pallas_call | solution.py:221
  30.3 6.8 %all-to-all-done.u_ref = f32[4,256,128]{2,1,0:T(8,128)S(1)} async-done(((f32[4,256,128]{2,1,0:T(8,128)}), f32[4,256,128]{2,1,0:T(8,128)S(1)}, u32[]{:S(2)}, u32[]{:S(2)}) %all-to-all-start) | async-done | bytes 524320 | tf_op jit(solution)/shard_map/all_to_all | solution.py:254
  39.3 2.0 %collective-permute-start.11 = (f32[256,128]{1,0:T(8,128)S(1)}, f32[256,128]{1,0:T(8,128)S(1)}, u32[]{:S(2)}, u32[]{:S(2)}) collective-permute-start(f32[256,128]{1,0:T(8,128)S(1)} %get-tuple-element.45.refs_3_), channel_id=1, source_target_pairs={{0,4},{1,5},{2,6},{3,7},{4,0},{5,1},{6,2},{7,3},{8,12},{9,13},{10,... | collective-permute-start | bytes 393224 | tf_op jit(solution)/shard_map/ppermute | solution.py:244
  41.3 6.5 %collective-permute-done.9.refs_1_ = f32[256,128]{1,0:T(8,128)S(1)} collective-permute-done((f32[256,128]{1,0:T(8,128)S(1)}, f32[256,128]{1,0:T(8,128)S(1)}, u32[]{:S(2)}, u32[]{:S(2)}) %collective-permute-start.9) | collective-permute-done | bytes 131104 | tf_op jit(solution)/shard_map/ppermute | solution.py:244
  48.2 1.7 %collective-permute-done.13.refs_2_ = f32[4,256,128]{2,1,0:T(8,128)S(1)} collective-permute-done((f32[4,256,128]{2,1,0:T(8,128)S(1)}, f32[4,256,128]{2,1,0:T(8,128)S(1)}, u32[]{:S(2)}, u32[]{:S(2)}) %collective-permute-start.13) | collective-permute-done | bytes 524320 | tf_op jit(solution)/shard_map/ppermute | solution.py:244
  50.0 2.8 %shard_map.109 = (f32[256,128]{1,0:T(8,128)S(1)}, f32[256,128]{1,0:T(8,128)S(1)}, f32[256,128]{1,0:T(8,128)S(1)}, f32[256,128]{1,0:T(8,128)S(1)}, f32[32,32,128]{2,1,0:T(8,128)}, /*index=5*/f32[32,32,128]{2,1,0:T(8,128)S(1)}) custom-call(s32[1]{0:T(128)} %bitcast.me_ref, s32[2,32]{1,0:T(2,128)S(1)} %bitcast.3, f32[32,32]{1,0:T(8,128)S(1)} %copy-done.4, ...), custom_call_target="tpu_custom_call" | custom-call | bytes 65536 | tf_op jit(solution)/shard_map/pallas_call | solution.py:221
  54.3 2.8 %collective-permute-start.17 = (f32[256,128]{1,0:T(8,128)S(1)}, f32[256,128]{1,0:T(8,128)S(1)}, u32[]{:S(2)}, u32[]{:S(2)}) collective-permute-start(f32[256,128]{1,0:T(8,128)S(1)} %get-tuple-element.59), channel_id=1, source_target_pairs={{0,12},{1,13},{2,14},{3,15},{4,8},{5,9},{6,10},{7,11},{8,4},{9,5},... | collective-permute-start | bytes 393224 | tf_op jit(solution)/shard_map/ppermute | solution.py:244
  58.8 2.3 %collective-permute-done.15.refs_3_ = f32[256,128]{1,0:T(8,128)S(1)} collective-permute-done((f32[256,128]{1,0:T(8,128)S(1)}, f32[256,128]{1,0:T(8,128)S(1)}, u32[]{:S(2)}, u32[]{:S(2)}) %collective-permute-start.15) | collective-permute-done | bytes 131104 | tf_op jit(solution)/shard_map/ppermute | solution.py:244
  61.1 4.7 %collective-permute-done.16.refs_2_ = f32[256,128]{1,0:T(8,128)S(1)} collective-permute-done((f32[256,128]{1,0:T(8,128)S(1)}, f32[256,128]{1,0:T(8,128)S(1)}, u32[]{:S(2)}, u32[]{:S(2)}) %collective-permute-start.16) | collective-permute-done | bytes 131104 | tf_op jit(solution)/shard_map/ppermute | solution.py:244
  68.9 6.2 %collective-permute-done.19.refs_5_ = f32[2,256,128]{2,1,0:T(8,128)S(1)} collective-permute-done((f32[2,256,128]{2,1,0:T(8,128)S(1)}, f32[2,256,128]{2,1,0:T(8,128)S(1)}, u32[]{:S(2)}, u32[]{:S(2)}) %collective-permute-start.19) | collective-permute-done | bytes 262176 | tf_op jit(solution)/shard_map/ppermute | solution.py:244
  75.2 5.0 %all-to-all-start.1 = ((f32[4,256,128]{2,1,0:T(8,128)}), f32[4,256,128]{2,1,0:T(8,128)S(1)}, u32[]{:S(2)}, u32[]{:S(2)}) async-start(f32[4,256,128]{2,1,0:T(8,128)} %shard_map.114), calls=%async_computation.1 | async-start | bytes 1048576 | tf_op jit(solution)/shard_map/all_to_all | solution.py:254
  82.4 3.2 %shard_map.116 = (f32[256,128]{1,0:T(8,128)S(1)}, f32[256,128]{1,0:T(8,128)}, f32[256,128]{1,0:T(8,128)S(1)}, f32[256,128]{1,0:T(8,128)S(1)}) custom-call(s32[1]{0:T(128)} %bitcast.me_ref, bf16[3,2,4,32,512]{4,3,2,1,0:T(8,128)(2,1)S(1)} %shard_map.103.refs_2_.coup, f32[3,32,128]{2,1,0:T(8,128)S(1)} %copy-done.5, ...), custom_call_target="tpu_custom_call" | custom-call | flops 2500000000 | bytes 65536 | tf_op jit(solution)/shard_map/pallas_call | solution.py:221
  85.6 3.8 %collective-permute-start.24 = (f32[256,128]{1,0:T(8,128)}, f32[256,128]{1,0:T(8,128)S(1)}, u32[]{:S(2)}, u32[]{:S(2)}) collective-permute-start(f32[256,128]{1,0:T(8,128)} %get-tuple-element.65), channel_id=1, source_target_pairs={{0,8},{1,9},{2,10},{3,11},{4,12},{5,13},{6,14},{7,15},{8,0},{9,1},... | collective-permute-start | bytes 393224 | tf_op jit(solution)/shard_map/ppermute | solution.py:244
  90.9 9.9 %all-to-all-done.1.refs_0_ = f32[4,256,128]{2,1,0:T(8,128)S(1)} async-done(((f32[4,256,128]{2,1,0:T(8,128)}), f32[4,256,128]{2,1,0:T(8,128)S(1)}, u32[]{:S(2)}, u32[]{:S(2)}) %all-to-all-start.1) | async-done | bytes 524320 | tf_op jit(solution)/shard_map/all_to_all | solution.py:254
  100.8 2.2 %shard_map.115 = (f32[32,32,128]{2,1,0:T(8,128)S(1)}, f32[32,32,128]{2,1,0:T(8,128)}) custom-call(s32[1]{0:T(128)} %bitcast.me_ref, s32[2,32]{1,0:T(2,128)S(1)} %bitcast.4, f32[32,32]{1,0:T(8,128)S(1)} %copy-done.4, f32[128,128]{1,0:T(8,128)S(1)} %copy-done.2, f32[32,32,128]{2,1,0:T(8,128)S(1)} %get-tuple-element.46.prev, ...), custom_call_target="tpu_custom_call" | custom-call | bytes 65536 | tf_op jit(solution)/shard_map/pallas_call | solution.py:221
  107.6 1.9 %collective-permute-start.32 = (f32[8,128]{1,0:T(8,128)S(1)}, f32[8,128]{1,0:T(8,128)S(1)}, u32[]{:S(2)}, u32[]{:S(2)}) collective-permute-start(f32[8,128]{1,0:T(8,128)S(1)} %add_add_fusion.1), channel_id=1, source_target_pairs={{0,12},{1,13},{2,14},{3,15},{4,8},{5,9},{6,10},{7,11},{8,4},{9,5},... | collective-permute-start | bytes 12296 | tf_op jit(solution)/shard_map/ppermute | solution.py:244
  109.5 2.1 %collective-permute-start.31 = (f32[8,128]{1,0:T(8,128)S(1)}, f32[8,128]{1,0:T(8,128)S(1)}, u32[]{:S(2)}, u32[]{:S(2)}) collective-permute-start(f32[8,128]{1,0:T(8,128)S(1)} %add_add_fusion.1), channel_id=1, source_target_pairs={{0,8},{1,9},{2,10},{3,11},{4,12},{5,13},{6,14},{7,15},{8,0},{9,1},... | collective-permute-start | bytes 12296 | tf_op jit(solution)/shard_map/ppermute | solution.py:244
  (86 shorter events, 29.5 us)
Async XLA Ops:
  2.0 8.1 %collective-permute-start.2 = (f32[256,128]{1,0:T(8,128)S(1)}, f32[256,128]{1,0:T(8,128)S(1)}, u32[]{:S(2)}, u32[]{:S(2)}) collective-permute-start(f32[256,128]{1,0:T(8,128)S(1)} %get-tuple-element.41), channel_id=1, source_target_pairs={{0,4},{1,5},{2,6},{3,7},{4,0},{5,1},{6,2},{7,3},{8,12},{9,13},{10,... | collective-permute-start | bytes 393224 | tf_op jit(solution)/shard_map/ppermute | solution.py:244
  5.1 12.9 %collective-permute-start = (f32[256,128]{1,0:T(8,128)S(1)}, f32[256,128]{1,0:T(8,128)S(1)}, u32[]{:S(2)}, u32[]{:S(2)}) collective-permute-start(f32[256,128]{1,0:T(8,128)S(1)} %get-tuple-element.37), channel_id=1, source_target_pairs={{0,8},{1,9},{2,10},{3,11},{4,12},{5,13},{6,14},{7,15},{8,0},{9,1},... | collective-permute-start | bytes 393224 | tf_op jit(solution)/shard_map/ppermute | solution.py:244
  7.7 10.3 %collective-permute-start.1 = (f32[256,128]{1,0:T(8,128)S(1)}, f32[256,128]{1,0:T(8,128)S(1)}, u32[]{:S(2)}, u32[]{:S(2)}) collective-permute-start(f32[256,128]{1,0:T(8,128)S(1)} %get-tuple-element.38), channel_id=1, source_target_pairs={{0,12},{1,13},{2,14},{3,15},{4,8},{5,9},{6,10},{7,11},{8,4},{9,5},... | collective-permute-start | bytes 393224 | tf_op jit(solution)/shard_map/ppermute | solution.py:244
  10.2 9.5 %collective-permute-start.6 = (f32[2,256,128]{2,1,0:T(8,128)S(1)}, f32[2,256,128]{2,1,0:T(8,128)S(1)}, u32[]{:S(2)}, u32[]{:S(2)}) collective-permute-start(f32[2,256,128]{2,1,0:T(8,128)S(1)} %shard_map.107.refs_1_), channel_id=1, source_target_pairs={{0,2},{1,3},{2,0},{3,1},{4,6},{5,7},{6,4},{7,5},{8,10},{9,11},{10,... | collective-permute-start | bytes 786440 | tf_op jit(solution)/shard_map/ppermute | solution.py:244
  18.1 6.5 %collective-permute-start.5 = (f32[2,256,128]{2,1,0:T(8,128)S(1)}, f32[2,256,128]{2,1,0:T(8,128)}, u32[]{:S(2)}, u32[]{:S(2)}) collective-permute-start(f32[2,256,128]{2,1,0:T(8,128)S(1)} %shard_map.106.refs_0_), channel_id=1, source_target_pairs={{0,2},{1,3},{2,0},{3,1},{4,6},{5,7},{6,4},{7,5},{8,10},{9,11},{10,... | collective-permute-start | bytes 786440 | tf_op jit(solution)/shard_map/ppermute | solution.py:244
  19.7 17.5 %all-to-all-start = ((f32[4,256,128]{2,1,0:T(8,128)}), f32[4,256,128]{2,1,0:T(8,128)S(1)}, u32[]{:S(2)}, u32[]{:S(2)}) async-start(f32[4,256,128]{2,1,0:T(8,128)} %get-tuple-element.48), calls=%async_computation | async-start | bytes 1048576 | tf_op jit(solution)/shard_map/all_to_all | solution.py:254
  37.3 12.7 %collective-permute-start.13 = (f32[4,256,128]{2,1,0:T(8,128)S(1)}, f32[4,256,128]{2,1,0:T(8,128)S(1)}, u32[]{:S(2)}, u32[]{:S(2)}) collective-permute-start(f32[4,256,128]{2,1,0:T(8,128)S(1)} %get-tuple-element.49.refs_0_), channel_id=1, source_target_pairs={{0,2},{1,3},{2,0},{3,1},{4,6},{5,7},{6,4},{7,5},{8,10},{9,11},{10,... | collective-permute-start | bytes 1572872 | tf_op jit(solution)/shard_map/ppermute | solution.py:244
  37.8 10.0 %collective-permute-start.9 = (f32[256,128]{1,0:T(8,128)S(1)}, f32[256,128]{1,0:T(8,128)S(1)}, u32[]{:S(2)}, u32[]{:S(2)}) collective-permute-start(f32[256,128]{1,0:T(8,128)S(1)} %get-tuple-element.43.refs_1_), channel_id=1, source_target_pairs={{0,8},{1,9},{2,10},{3,11},{4,12},{5,13},{6,14},{7,15},{8,0},{9,1},... | collective-permute-start | bytes 393224 | tf_op jit(solution)/shard_map/ppermute | solution.py:244
  37.8 10.0 %collective-permute-start.10 = (f32[256,128]{1,0:T(8,128)S(1)}, f32[256,128]{1,0:T(8,128)S(1)}, u32[]{:S(2)}, u32[]{:S(2)}) collective-permute-start(f32[256,128]{1,0:T(8,128)S(1)} %get-tuple-element.44.refs_2_), channel_id=1, source_target_pairs={{0,12},{1,13},{2,14},{3,15},{4,8},{5,9},{6,10},{7,11},{8,4},{9,5},... | collective-permute-start | bytes 393224 | tf_op jit(solution)/shard_map/ppermute | solution.py:244
  39.3 8.9 %collective-permute-start.11 = (f32[256,128]{1,0:T(8,128)S(1)}, f32[256,128]{1,0:T(8,128)S(1)}, u32[]{:S(2)}, u32[]{:S(2)}) collective-permute-start(f32[256,128]{1,0:T(8,128)S(1)} %get-tuple-element.45.refs_3_), channel_id=1, source_target_pairs={{0,4},{1,5},{2,6},{3,7},{4,0},{5,1},{6,2},{7,3},{8,12},{9,13},{10,... | collective-permute-start | bytes 393224 | tf_op jit(solution)/shard_map/ppermute | solution.py:244
  41.3 15.8 %collective-permute-start.12 = (f32[4,256,128]{2,1,0:T(8,128)S(1)}, f32[4,256,128]{2,1,0:T(8,128)S(1)}, u32[]{:S(2)}, u32[]{:S(2)}) collective-permute-start(f32[4,256,128]{2,1,0:T(8,128)S(1)} %get-tuple-element.49.refs_0_), channel_id=1, source_target_pairs={{0,1},{1,0},{2,3},{3,2},{4,5},{5,4},{6,7},{7,6},{8,9},{9,8},{10,11... | collective-permute-start | bytes 1572872 | tf_op jit(solution)/shard_map/ppermute | solution.py:244
  50.0 7.2 %collective-permute-start.14 = (f32[4,256,128]{2,1,0:T(8,128)S(1)}, f32[4,256,128]{2,1,0:T(8,128)S(1)}, u32[]{:S(2)}, u32[]{:S(2)}) collective-permute-start(f32[4,256,128]{2,1,0:T(8,128)S(1)} %collective-permute-done.13.refs_2_), channel_id=1, source_target_pairs={{0,1},{1,0},{2,3},{3,2},{4,5},{5,4},{6,7},{7,6},{8,9},{9,8},{10,11... | collective-permute-start | bytes 1572872 | tf_op jit(solution)/shard_map/ppermute | solution.py:244
  52.8 8.3 %collective-permute-start.15 = (f32[256,128]{1,0:T(8,128)S(1)}, f32[256,128]{1,0:T(8,128)S(1)}, u32[]{:S(2)}, u32[]{:S(2)}) collective-permute-start(f32[256,128]{1,0:T(8,128)S(1)} %get-tuple-element.54), channel_id=1, source_target_pairs={{0,4},{1,5},{2,6},{3,7},{4,0},{5,1},{6,2},{7,3},{8,12},{9,13},{10,... | collective-permute-start | bytes 393224 | tf_op jit(solution)/shard_map/ppermute | solution.py:244
  53.0 12.9 %collective-permute-start.16 = (f32[256,128]{1,0:T(8,128)S(1)}, f32[256,128]{1,0:T(8,128)S(1)}, u32[]{:S(2)}, u32[]{:S(2)}) collective-permute-start(f32[256,128]{1,0:T(8,128)S(1)} %get-tuple-element.58), channel_id=1, source_target_pairs={{0,8},{1,9},{2,10},{3,11},{4,12},{5,13},{6,14},{7,15},{8,0},{9,1},... | collective-permute-start | bytes 393224 | tf_op jit(solution)/shard_map/ppermute | solution.py:244
  54.3 11.5 %collective-permute-start.17 = (f32[256,128]{1,0:T(8,128)S(1)}, f32[256,128]{1,0:T(8,128)S(1)}, u32[]{:S(2)}, u32[]{:S(2)}) collective-permute-start(f32[256,128]{1,0:T(8,128)S(1)} %get-tuple-element.59), channel_id=1, source_target_pairs={{0,12},{1,13},{2,14},{3,15},{4,8},{5,9},{6,10},{7,11},{8,4},{9,5},... | collective-permute-start | bytes 393224 | tf_op jit(solution)/shard_map/ppermute | solution.py:244
  66.0 9.2 %collective-permute-start.19 = (f32[2,256,128]{2,1,0:T(8,128)S(1)}, f32[2,256,128]{2,1,0:T(8,128)S(1)}, u32[]{:S(2)}, u32[]{:S(2)}) collective-permute-start(f32[2,256,128]{2,1,0:T(8,128)S(1)} %get-tuple-element.55.refs_4_.near.refs_1_), channel_id=1, source_target_pairs={{0,2},{1,3},{2,0},{3,1},{4,6},{5,7},{6,4},{7,5},{8,10},{9,11},{10,... | collective-permute-start | bytes 786440 | tf_op jit(solution)/shard_map/ppermute | solution.py:244
  67.7 12.8 %collective-permute-start.21 = (f32[2,256,128]{2,1,0:T(8,128)S(1)}, f32[2,256,128]{2,1,0:T(8,128)}, u32[]{:S(2)}, u32[]{:S(2)}) collective-permute-start(f32[2,256,128]{2,1,0:T(8,128)S(1)} %get-tuple-element.60.far.refs_0_), channel_id=1, source_target_pairs={{0,2},{1,3},{2,0},{3,1},{4,6},{5,7},{6,4},{7,5},{8,10},{9,11},{10,... | collective-permute-start | bytes 786440 | tf_op jit(solution)/shard_map/ppermute | solution.py:244
  75.2 25.6 %all-to-all-start.1 = ((f32[4,256,128]{2,1,0:T(8,128)}), f32[4,256,128]{2,1,0:T(8,128)S(1)}, u32[]{:S(2)}, u32[]{:S(2)}) async-start(f32[4,256,128]{2,1,0:T(8,128)} %shard_map.114), calls=%async_computation.1 | async-start | bytes 1048576 | tf_op jit(solution)/shard_map/all_to_all | solution.py:254
  85.6 17.9 %collective-permute-start.24 = (f32[256,128]{1,0:T(8,128)}, f32[256,128]{1,0:T(8,128)S(1)}, u32[]{:S(2)}, u32[]{:S(2)}) collective-permute-start(f32[256,128]{1,0:T(8,128)} %get-tuple-element.65), channel_id=1, source_target_pairs={{0,8},{1,9},{2,10},{3,11},{4,12},{5,13},{6,14},{7,15},{8,0},{9,1},... | collective-permute-start | bytes 393224 | tf_op jit(solution)/shard_map/ppermute | solution.py:244
  89.4 14.1 %collective-permute-start.25 = (f32[256,128]{1,0:T(8,128)S(1)}, f32[256,128]{1,0:T(8,128)S(1)}, u32[]{:S(2)}, u32[]{:S(2)}) collective-permute-start(f32[256,128]{1,0:T(8,128)S(1)} %get-tuple-element.66), channel_id=1, source_target_pairs={{0,12},{1,13},{2,14},{3,15},{4,8},{5,9},{6,10},{7,11},{8,4},{9,5},... | collective-permute-start | bytes 393224 | tf_op jit(solution)/shard_map/ppermute | solution.py:244
  90.9 12.7 %collective-permute-start.26 = (f32[256,128]{1,0:T(8,128)S(1)}, f32[256,128]{1,0:T(8,128)S(1)}, u32[]{:S(2)}, u32[]{:S(2)}) collective-permute-start(f32[256,128]{1,0:T(8,128)S(1)} %get-tuple-element.67), channel_id=1, source_target_pairs={{0,4},{1,5},{2,6},{3,7},{4,0},{5,1},{6,2},{7,3},{8,12},{9,13},{10,... | collective-permute-start | bytes 393224 | tf_op jit(solution)/shard_map/ppermute | solution.py:244
  104.0 3.7 %collective-permute-start.28 = (f32[8,128]{1,0:T(8,128)S(1)}, f32[8,128]{1,0:T(8,128)S(1)}, u32[]{:S(2)}, u32[]{:S(2)}) collective-permute-start(f32[8,128]{1,0:T(8,128)S(1)} %shard_map.118), channel_id=1, source_target_pairs={{0,2},{1,3},{2,0},{3,1},{4,6},{5,7},{6,4},{7,5},{8,10},{9,11},{10,... | collective-permute-start | bytes 12296 | tf_op jit(solution)/shard_map/ppermute | solution.py:244
  107.6 5.6 %collective-permute-start.32 = (f32[8,128]{1,0:T(8,128)S(1)}, f32[8,128]{1,0:T(8,128)S(1)}, u32[]{:S(2)}, u32[]{:S(2)}) collective-permute-start(f32[8,128]{1,0:T(8,128)S(1)} %add_add_fusion.1), channel_id=1, source_target_pairs={{0,12},{1,13},{2,14},{3,15},{4,8},{5,9},{6,10},{7,11},{8,4},{9,5},... | collective-permute-start | bytes 12296 | tf_op jit(solution)/shard_map/ppermute | solution.py:244
  109.5 4.5 %collective-permute-start.31 = (f32[8,128]{1,0:T(8,128)S(1)}, f32[8,128]{1,0:T(8,128)S(1)}, u32[]{:S(2)}, u32[]{:S(2)}) collective-permute-start(f32[8,128]{1,0:T(8,128)S(1)} %add_add_fusion.1), channel_id=1, source_target_pairs={{0,8},{1,9},{2,10},{3,11},{4,12},{5,13},{6,14},{7,15},{8,0},{9,1},... | collective-permute-start | bytes 12296 | tf_op jit(solution)/shard_map/ppermute | solution.py:244
  (21 other events, 116.2 us)

commit v6 on v5

--- a/solution.py
+++ b/solution.py
@@ -172,21 +172,14 @@
 
 
 def group_join_kernel(n, me_ref, *refs):
-    ws, us, (out, sq) = refs[:n], refs[n : 2 * n], refs[-2:]
+    ws, us, outs, (out, sq) = refs[:n], refs[n : 2 * n], refs[-2 - n : -2], refs[-2:]
     total = 0.0
     for s in range(n):
         y = ws[s][...] + us[s][...]
         out[s] = y
+        outs[s][...] = y
         total = total + jnp.sum((y * y).reshape(-1, 8, y.shape[1]), axis=0)
     sq[...] = total
-
-
-def ungroup_kernel(n, me_ref, near, far, behind_ref, out):
-    spot, _ = place(me_ref)
-    out[spot] = near[0]
-    out[spot ^ hop(n - 1, n)] = near[1]
-    for s in range(1, n - 1):
-        out[spot ^ hop(s, n)] = far[s - 1]
 
 
 def last_of(na, nc, u_ref, pieces, spot):
@@ -291,7 +284,7 @@
 
     def group_join(ws, us, behind=()):
         k = len(ws)
-        outs = [pltpu.VMEM((k, na * nc, nb), F32), square]
+        outs = [piece] * k + [pltpu.VMEM((k, na * nc, nb), F32), square]
         specs = [VM] * (2 * k) + [ANY] * len(behind)
         return call(functools.partial(group_join_kernel, k), outs, [me], [*ws, *us, *behind], (), specs)
 
@@ -317,14 +310,12 @@
     *u2, _, v2_nat = kinetic(psi_cur, pieces=w1_c, base=[u1_nat], n_out=n, out=[on_chip])
     w2 = near_far(mix(gather(v2, w1_c[1:]), 0))
     u2 = near_far(exchange(u2))
-    near, s3 = group_join(w2[0], u2[0])
-    near_core, near_over = across(near, 1), across(near, 2)
-    far, s3_far = group_join(w2[1], u2[1], [near])
-    far_core = across(far, 1)
-    (v3,) = call(functools.partial(ungroup_kernel, n), [packed], [me], [near, far, far_core], (), [VM, VM, ANY])
-    v3 = exchange_all(after(v3, near_over))
-    u3, prev_out = kinetic(v2_nat, pieces=[v3], out=[natural])
-    w3 = exchange(mix(gather_near_far(near, far, near_core, far_core, near_over), 2500000000))
+    *v3_near, near, s3 = group_join(w2[0], u2[0])
+    *v3_far, far, s3_far = group_join(w2[1], u2[1], [near])
+    v3 = exchange([v3_near[0], *v3_far, v3_near[1]])
+    u3, prev_out = kinetic(v2_nat, pieces=v3, out=[natural])
+    near_over = local(after(swap(near, 2), v3[1]))
+    w3 = exchange(mix(gather_near_far(near, far, across(near, 1), across(far, 1), near_over), 0))
     (sums,) = call(functools.partial(norm_kernel, na, nc, n), [sds((8, nb), F32)], [me], [u3, *w3, s2, s3, s3_far])
     (cur_out,) = call(functools.partial(finish_kernel, na, nc), [natural], [me], [u3, *w3])
     bit = 1

time: 116 us -> 109 us (0.940)
  waiting for transfers between devices: 49.8 us -> 45.3 us
  Pallas kernels: 20.1 us -> 17.8 us
    all_to_all x2 -> x1, waiting for transfers between devices: 16.7 us -> 6.82 us  [exchange_all(): lax.all_to_all(x, 'chan', 0, 0, tiled=True, axis_index_groups=lines)]
    ppermute x33 -> x36, waiting for transfers between devices: 33.1 us -> 38.5 us  [swap(): return lax.ppermute(x, 'chan', [(i, i ^ bits) for i in range(nd)])]
    all_to_all x2 -> x1, starting transfers between devices: 9.2 us -> 4.24 us  [exchange_all(): lax.all_to_all(x, 'chan', 0, 0, tiled=True, axis_index_groups=lines)]
    ppermute x33 -> x36, starting transfers between devices: 32.6 us -> 37 us  [swap(): return lax.ppermute(x, 'chan', [(i, i ^ bits) for i in range(nd)])]
    pallas_call x16 -> x15, Pallas kernels: 20.1 us -> 17.8 us  [call(): pl.pallas_call(kernel, out_shape=outs, in_specs=[SM] * len(scalars) + (sp...]
  transfers between devices with their start and end apart: 35 -> 37, of which waited for: 24 -> 20; matrix products, arithmetic and copies ran while one was open for 0% -> 0% of each run, Pallas kernels for 17% -> 16%
where the time goes in v6:
time: 109 us; the launch traced here: 108 us
  waiting for transfers between devices  45.3 us (42%)
  starting transfers between devices  41.2 us (38%)
  Pallas kernels  17.8 us (16%)
  local copies, waits for them, and re-layouts  2.7 us (2%)
    ppermute x36, waiting for transfers between devices, swap(): return lax.ppermute(x, 'chan', [(i, i ^ bits) for i in range(nd)])  38.5 us
    ppermute x36, starting transfers between devices, swap(): return lax.ppermute(x, 'chan', [(i, i ^ bits) for i in range(nd)])  37 us
    pallas_call x15, Pallas kernels, call(): pl.pallas_call(kernel, out_shape=outs, in_specs=[SM] * len(scalars) + (sp...  17.8 us
    all_to_all x1, waiting for transfers between devices, exchange_all(): lax.all_to_all(x, 'chan', 0, 0, tiled=True, axis_index_groups=lines)  6.82 us
    all_to_all x1, starting transfers between devices, exchange_all(): lax.all_to_all(x, 'chan', 0, 0, tiled=True, axis_index_groups=lines)  4.24 us
    unnamed x20, local copies, waits for them, and re-layouts  2.7 us
  transfers between devices with their start and end apart: 37, of which 20 were waited for; matrix products, arithmetic and copies ran while one was open for 0% of the time, Pallas kernels for 16%

profile of v6, /device:TPU:0, one launch (start us, length us, event | category | flops | bytes accessed | tf_op | source)
XLA Modules:
  0.0 108.5 jit_solution(8421415543942519015)
XLA Ops:
  2.0 3.1 %collective-permute-start.2 = (f32[256,128]{1,0:T(8,128)S(1)}, f32[256,128]{1,0:T(8,128)S(1)}, u32[]{:S(2)}, u32[]{:S(2)}) collective-permute-start(f32[256,128]{1,0:T(8,128)S(1)} %get-tuple-element.45), channel_id=1, source_target_pairs={{0,4},{1,5},{2,6},{3,7},{4,0},{5,1},{6,2},{7,3},{8,12},{9,13},{10,... | collective-permute-start | bytes 393224 | tf_op jit(solution)/shard_map/ppermute | solution.py:237
  5.1 2.6 %collective-permute-start = (f32[256,128]{1,0:T(8,128)S(1)}, f32[256,128]{1,0:T(8,128)S(1)}, u32[]{:S(2)}, u32[]{:S(2)}) collective-permute-start(f32[256,128]{1,0:T(8,128)S(1)} %get-tuple-element.41), channel_id=1, source_target_pairs={{0,8},{1,9},{2,10},{3,11},{4,12},{5,13},{6,14},{7,15},{8,0},{9,1},... | collective-permute-start | bytes 393224 | tf_op jit(solution)/shard_map/ppermute | solution.py:237
  7.7 2.4 %collective-permute-done.2.refs_1_ = f32[256,128]{1,0:T(8,128)S(1)} collective-permute-done((f32[256,128]{1,0:T(8,128)S(1)}, f32[256,128]{1,0:T(8,128)S(1)}, u32[]{:S(2)}, u32[]{:S(2)}) %collective-permute-start.2) | collective-permute-done | bytes 131104 | tf_op jit(solution)/shard_map/ppermute | solution.py:237
  10.2 1.8 %collective-permute-start.6 = (f32[2,256,128]{2,1,0:T(8,128)S(1)}, f32[2,256,128]{2,1,0:T(8,128)S(1)}, u32[]{:S(2)}, u32[]{:S(2)}) collective-permute-start(f32[2,256,128]{2,1,0:T(8,128)S(1)} %shard_map.107.refs_1_), channel_id=1, source_target_pairs={{0,2},{1,3},{2,0},{3,1},{4,6},{5,7},{6,4},{7,5},{8,10},{9,11},{10,... | collective-permute-start | bytes 786440 | tf_op jit(solution)/shard_map/ppermute | solution.py:237
  12.7 2.0 %shard_map.103.refs_2_.coup = bf16[3,2,4,32,512]{4,3,2,1,0:T(8,128)(2,1)S(1)} custom-call(s32[1]{0:T(128)} %bitcast.me_ref, s32[8,8]{1,0:T(8,128)S(1)} %copy-done.7, f32[3,512,512]{2,1,0:T(8,128)} %ang_ref.1), custom_call_target="tpu_custom_call" | custom-call | bytes 65536 | tf_op jit(solution)/shard_map/pallas_call | solution.py:214
  14.7 2.8 %shard_map.105 = (f32[4,256,128]{2,1,0:T(8,128)}, f32[32,32,128]{2,1,0:T(8,128)S(1)}) custom-call(s32[1]{0:T(128)} %bitcast.me_ref, s32[2,32]{1,0:T(2,128)S(1)} %bitcast.2, f32[32,32]{1,0:T(8,128)S(1)} %copy-done.5, f32[128,128]{1,0:T(8,128)S(1)} %copy-done.2, f32[32,32,128]{2,1,0:T(8,128)S(1)} %copy-done.3, f32[32,32,128]{2,1,0:T(8,128)S(1)} %copy-done.1), custom_call_target="tpu_custom_call" | custom-call | bytes 65536 | tf_op jit(solution)/shard_map/pallas_call | solution.py:214
  19.7 4.2 %all-to-all-start = ((f32[4,256,128]{2,1,0:T(8,128)}), f32[4,256,128]{2,1,0:T(8,128)S(1)}, u32[]{:S(2)}, u32[]{:S(2)}) async-start(f32[4,256,128]{2,1,0:T(8,128)} %get-tuple-element.52), calls=%async_computation | async-start | bytes 1048576 | tf_op jit(solution)/shard_map/all_to_all | solution.py:247
  27.7 2.6 %shard_map.108 = (f32[256,128]{1,0:T(8,128)S(1)}, f32[256,128]{1,0:T(8,128)S(1)}, f32[256,128]{1,0:T(8,128)S(1)}, f32[256,128]{1,0:T(8,128)S(1)}) custom-call(s32[1]{0:T(128)} %bitcast.me_ref, bf16[3,2,4,32,512]{4,3,2,1,0:T(8,128)(2,1)S(1)} %shard_map.103.refs_2_.coup, f32[3,32,128]{2,1,0:T(8,128)S(1)} %copy-done.4, f32[2,256,128]{2,1,0:T(8,128)S(1)} %shard_map.106.refs_0_, ...), custom_call_target="tpu_custom_call" | custom-call | flops 5000000000 | bytes 65536 | tf_op jit(solution)/shard_map/pallas_call | solution.py:214
  30.3 6.8 %all-to-all-done.u_ref = f32[4,256,128]{2,1,0:T(8,128)S(1)} async-done(((f32[4,256,128]{2,1,0:T(8,128)}), f32[4,256,128]{2,1,0:T(8,128)S(1)}, u32[]{:S(2)}, u32[]{:S(2)}) %all-to-all-start) | async-done | bytes 524320 | tf_op jit(solution)/shard_map/all_to_all | solution.py:247
  39.3 2.0 %collective-permute-start.11 = (f32[256,128]{1,0:T(8,128)S(1)}, f32[256,128]{1,0:T(8,128)S(1)}, u32[]{:S(2)}, u32[]{:S(2)}) collective-permute-start(f32[256,128]{1,0:T(8,128)S(1)} %get-tuple-element.49.refs_3_), channel_id=1, source_target_pairs={{0,4},{1,5},{2,6},{3,7},{4,0},{5,1},{6,2},{7,3},{8,12},{9,13},{10,... | collective-permute-start | bytes 393224 | tf_op jit(solution)/shard_map/ppermute | solution.py:237
  41.3 6.5 %collective-permute-done.9.refs_1_ = f32[256,128]{1,0:T(8,128)S(1)} collective-permute-done((f32[256,128]{1,0:T(8,128)S(1)}, f32[256,128]{1,0:T(8,128)S(1)}, u32[]{:S(2)}, u32[]{:S(2)}) %collective-permute-start.9) | collective-permute-done | bytes 131104 | tf_op jit(solution)/shard_map/ppermute | solution.py:237
  50.0 2.8 %shard_map.109 = (f32[256,128]{1,0:T(8,128)S(1)}, f32[256,128]{1,0:T(8,128)S(1)}, f32[256,128]{1,0:T(8,128)S(1)}, f32[256,128]{1,0:T(8,128)S(1)}, f32[32,32,128]{2,1,0:T(8,128)}, /*index=5*/f32[32,32,128]{2,1,0:T(8,128)S(1)}) custom-call(s32[1]{0:T(128)} %bitcast.me_ref, s32[2,32]{1,0:T(2,128)S(1)} %bitcast.3, f32[32,32]{1,0:T(8,128)S(1)} %copy-done.5, ...), custom_call_target="tpu_custom_call" | custom-call | bytes 65536 | tf_op jit(solution)/shard_map/pallas_call | solution.py:214
  54.3 2.8 %collective-permute-start.17 = (f32[256,128]{1,0:T(8,128)S(1)}, f32[256,128]{1,0:T(8,128)S(1)}, u32[]{:S(2)}, u32[]{:S(2)}) collective-permute-start(f32[256,128]{1,0:T(8,128)S(1)} %get-tuple-element.63), channel_id=1, source_target_pairs={{0,12},{1,13},{2,14},{3,15},{4,8},{5,9},{6,10},{7,11},{8,4},{9,5},... | collective-permute-start | bytes 393224 | tf_op jit(solution)/shard_map/ppermute | solution.py:237
  58.8 2.3 %collective-permute-done.15.refs_3_ = f32[256,128]{1,0:T(8,128)S(1)} collective-permute-done((f32[256,128]{1,0:T(8,128)S(1)}, f32[256,128]{1,0:T(8,128)S(1)}, u32[]{:S(2)}, u32[]{:S(2)}) %collective-permute-start.15) | collective-permute-done | bytes 131104 | tf_op jit(solution)/shard_map/ppermute | solution.py:237
  61.6 4.3 %collective-permute-done.16.refs_2_ = f32[256,128]{1,0:T(8,128)S(1)} collective-permute-done((f32[256,128]{1,0:T(8,128)S(1)}, f32[256,128]{1,0:T(8,128)S(1)}, u32[]{:S(2)}, u32[]{:S(2)}) %collective-permute-start.16) | collective-permute-done | bytes 131104 | tf_op jit(solution)/shard_map/ppermute | solution.py:237
  67.6 3.6 %collective-permute-start.18 = (f32[256,128]{1,0:T(8,128)S(1)}, f32[256,128]{1,0:T(8,128)S(1)}, u32[]{:S(2)}, u32[]{:S(2)}) collective-permute-start(f32[256,128]{1,0:T(8,128)S(1)} %get-tuple-element.65), channel_id=1, source_target_pairs={{0,8},{1,9},{2,10},{3,11},{4,12},{5,13},{6,14},{7,15},{8,0},{9,1},... | collective-permute-start | bytes 393224 | tf_op jit(solution)/shard_map/ppermute | solution.py:237
  71.7 5.1 %collective-permute-done.18.refs_1_ = f32[256,128]{1,0:T(8,128)S(1)} collective-permute-done((f32[256,128]{1,0:T(8,128)S(1)}, f32[256,128]{1,0:T(8,128)S(1)}, u32[]{:S(2)}, u32[]{:S(2)}) %collective-permute-start.18) | collective-permute-done | bytes 131104 | tf_op jit(solution)/shard_map/ppermute | solution.py:237
  77.3 1.9 %collective-permute-start.19 = (f32[256,128]{1,0:T(8,128)S(1)}, f32[256,128]{1,0:T(8,128)S(1)}, u32[]{:S(2)}, u32[]{:S(2)}) collective-permute-start(f32[256,128]{1,0:T(8,128)S(1)} %get-tuple-element.66), channel_id=1, source_target_pairs={{0,12},{1,13},{2,14},{3,15},{4,8},{5,9},{6,10},{7,11},{8,4},{9,5},... | collective-permute-start | bytes 393224 | tf_op jit(solution)/shard_map/ppermute | solution.py:237
  82.6 1.9 %collective-permute-start.28 = (f32[256,128]{1,0:T(8,128)S(1)}, f32[256,128]{1,0:T(8,128)S(1)}, u32[]{:S(2)}, u32[]{:S(2)}) collective-permute-start(f32[256,128]{1,0:T(8,128)S(1)} %get-tuple-element.74), channel_id=1, source_target_pairs={{0,12},{1,13},{2,14},{3,15},{4,8},{5,9},{6,10},{7,11},{8,4},{9,5},... | collective-permute-start | bytes 393224 | tf_op jit(solution)/shard_map/ppermute | solution.py:237
  84.5 1.9 %collective-permute-done.19.refs_2_ = f32[256,128]{1,0:T(8,128)S(1)} collective-permute-done((f32[256,128]{1,0:T(8,128)S(1)}, f32[256,128]{1,0:T(8,128)S(1)}, u32[]{:S(2)}, u32[]{:S(2)}) %collective-permute-start.19) | collective-permute-done | bytes 131104 | tf_op jit(solution)/shard_map/ppermute | solution.py:237
  86.5 2.2 %shard_map.114 = (f32[32,32,128]{2,1,0:T(8,128)S(1)}, f32[32,32,128]{2,1,0:T(8,128)}) custom-call(s32[1]{0:T(128)} %bitcast.me_ref, s32[2,32]{1,0:T(2,128)S(1)} %bitcast.4, f32[32,32]{1,0:T(8,128)S(1)} %copy-done.5, f32[128,128]{1,0:T(8,128)S(1)} %copy-done.2, f32[32,32,128]{2,1,0:T(8,128)S(1)} %get-tuple-element.50.prev, ...), custom_call_target="tpu_custom_call" | custom-call | bytes 65536 | tf_op jit(solution)/shard_map/pallas_call | solution.py:214
  88.7 7.4 %collective-permute-done.27.refs_1_ = f32[256,128]{1,0:T(8,128)S(1)} collective-permute-done((f32[256,128]{1,0:T(8,128)S(1)}, f32[256,128]{1,0:T(8,128)S(1)}, u32[]{:S(2)}, u32[]{:S(2)}) %collective-permute-start.27) | collective-permute-done | bytes 131104 | tf_op jit(solution)/shard_map/ppermute | solution.py:237
  100.2 1.9 %collective-permute-start.35 = (f32[8,128]{1,0:T(8,128)S(1)}, f32[8,128]{1,0:T(8,128)S(1)}, u32[]{:S(2)}, u32[]{:S(2)}) collective-permute-start(f32[8,128]{1,0:T(8,128)S(1)} %add_add_fusion.1), channel_id=1, source_target_pairs={{0,12},{1,13},{2,14},{3,15},{4,8},{5,9},{6,10},{7,11},{8,4},{9,5},... | collective-permute-start | bytes 12296 | tf_op jit(solution)/shard_map/ppermute | solution.py:237
  102.1 2.1 %collective-permute-start.34 = (f32[8,128]{1,0:T(8,128)S(1)}, f32[8,128]{1,0:T(8,128)S(1)}, u32[]{:S(2)}, u32[]{:S(2)}) collective-permute-start(f32[8,128]{1,0:T(8,128)S(1)} %add_add_fusion.1), channel_id=1, source_target_pairs={{0,8},{1,9},{2,10},{3,11},{4,12},{5,13},{6,14},{7,15},{8,0},{9,1},... | collective-permute-start | bytes 12296 | tf_op jit(solution)/shard_map/ppermute | solution.py:237
  (89 shorter events, 30.5 us)
Async XLA Ops:
  2.0 8.1 %collective-permute-start.2 = (f32[256,128]{1,0:T(8,128)S(1)}, f32[256,128]{1,0:T(8,128)S(1)}, u32[]{:S(2)}, u32[]{:S(2)}) collective-permute-start(f32[256,128]{1,0:T(8,128)S(1)} %get-tuple-element.45), channel_id=1, source_target_pairs={{0,4},{1,5},{2,6},{3,7},{4,0},{5,1},{6,2},{7,3},{8,12},{9,13},{10,... | collective-permute-start | bytes 393224 | tf_op jit(solution)/shard_map/ppermute | solution.py:237
  5.1 12.9 %collective-permute-start = (f32[256,128]{1,0:T(8,128)S(1)}, f32[256,128]{1,0:T(8,128)S(1)}, u32[]{:S(2)}, u32[]{:S(2)}) collective-permute-start(f32[256,128]{1,0:T(8,128)S(1)} %get-tuple-element.41), channel_id=1, source_target_pairs={{0,8},{1,9},{2,10},{3,11},{4,12},{5,13},{6,14},{7,15},{8,0},{9,1},... | collective-permute-start | bytes 393224 | tf_op jit(solution)/shard_map/ppermute | solution.py:237
  7.7 10.3 %collective-permute-start.1 = (f32[256,128]{1,0:T(8,128)S(1)}, f32[256,128]{1,0:T(8,128)S(1)}, u32[]{:S(2)}, u32[]{:S(2)}) collective-permute-start(f32[256,128]{1,0:T(8,128)S(1)} %get-tuple-element.42), channel_id=1, source_target_pairs={{0,12},{1,13},{2,14},{3,15},{4,8},{5,9},{6,10},{7,11},{8,4},{9,5},... | collective-permute-start | bytes 393224 | tf_op jit(solution)/shard_map/ppermute | solution.py:237
  10.2 9.5 %collective-permute-start.6 = (f32[2,256,128]{2,1,0:T(8,128)S(1)}, f32[2,256,128]{2,1,0:T(8,128)S(1)}, u32[]{:S(2)}, u32[]{:S(2)}) collective-permute-start(f32[2,256,128]{2,1,0:T(8,128)S(1)} %shard_map.107.refs_1_), channel_id=1, source_target_pairs={{0,2},{1,3},{2,0},{3,1},{4,6},{5,7},{6,4},{7,5},{8,10},{9,11},{10,... | collective-permute-start | bytes 786440 | tf_op jit(solution)/shard_map/ppermute | solution.py:237
  18.1 6.5 %collective-permute-start.5 = (f32[2,256,128]{2,1,0:T(8,128)S(1)}, f32[2,256,128]{2,1,0:T(8,128)}, u32[]{:S(2)}, u32[]{:S(2)}) collective-permute-start(f32[2,256,128]{2,1,0:T(8,128)S(1)} %shard_map.106.refs_0_), channel_id=1, source_target_pairs={{0,2},{1,3},{2,0},{3,1},{4,6},{5,7},{6,4},{7,5},{8,10},{9,11},{10,... | collective-permute-start | bytes 786440 | tf_op jit(solution)/shard_map/ppermute | solution.py:237
  19.7 17.5 %all-to-all-start = ((f32[4,256,128]{2,1,0:T(8,128)}), f32[4,256,128]{2,1,0:T(8,128)S(1)}, u32[]{:S(2)}, u32[]{:S(2)}) async-start(f32[4,256,128]{2,1,0:T(8,128)} %get-tuple-element.52), calls=%async_computation | async-start | bytes 1048576 | tf_op jit(solution)/shard_map/all_to_all | solution.py:247
  37.3 12.7 %collective-permute-start.13 = (f32[4,256,128]{2,1,0:T(8,128)S(1)}, f32[4,256,128]{2,1,0:T(8,128)S(1)}, u32[]{:S(2)}, u32[]{:S(2)}) collective-permute-start(f32[4,256,128]{2,1,0:T(8,128)S(1)} %get-tuple-element.53.refs_0_), channel_id=1, source_target_pairs={{0,2},{1,3},{2,0},{3,1},{4,6},{5,7},{6,4},{7,5},{8,10},{9,11},{10,... | collective-permute-start | bytes 1572872 | tf_op jit(solution)/shard_map/ppermute | solution.py:237
  37.8 10.0 %collective-permute-start.9 = (f32[256,128]{1,0:T(8,128)S(1)}, f32[256,128]{1,0:T(8,128)S(1)}, u32[]{:S(2)}, u32[]{:S(2)}) collective-permute-start(f32[256,128]{1,0:T(8,128)S(1)} %get-tuple-element.47.refs_1_), channel_id=1, source_target_pairs={{0,8},{1,9},{2,10},{3,11},{4,12},{5,13},{6,14},{7,15},{8,0},{9,1},... | collective-permute-start | bytes 393224 | tf_op jit(solution)/shard_map/ppermute | solution.py:237
  37.8 10.0 %collective-permute-start.10 = (f32[256,128]{1,0:T(8,128)S(1)}, f32[256,128]{1,0:T(8,128)S(1)}, u32[]{:S(2)}, u32[]{:S(2)}) collective-permute-start(f32[256,128]{1,0:T(8,128)S(1)} %get-tuple-element.48.refs_2_), channel_id=1, source_target_pairs={{0,12},{1,13},{2,14},{3,15},{4,8},{5,9},{6,10},{7,11},{8,4},{9,5},... | collective-permute-start | bytes 393224 | tf_op jit(solution)/shard_map/ppermute | solution.py:237
  39.3 8.9 %collective-permute-start.11 = (f32[256,128]{1,0:T(8,128)S(1)}, f32[256,128]{1,0:T(8,128)S(1)}, u32[]{:S(2)}, u32[]{:S(2)}) collective-permute-start(f32[256,128]{1,0:T(8,128)S(1)} %get-tuple-element.49.refs_3_), channel_id=1, source_target_pairs={{0,4},{1,5},{2,6},{3,7},{4,0},{5,1},{6,2},{7,3},{8,12},{9,13},{10,... | collective-permute-start | bytes 393224 | tf_op jit(solution)/shard_map/ppermute | solution.py:237
  41.3 15.8 %collective-permute-start.12 = (f32[4,256,128]{2,1,0:T(8,128)S(1)}, f32[4,256,128]{2,1,0:T(8,128)S(1)}, u32[]{:S(2)}, u32[]{:S(2)}) collective-permute-start(f32[4,256,128]{2,1,0:T(8,128)S(1)} %get-tuple-element.53.refs_0_), channel_id=1, source_target_pairs={{0,1},{1,0},{2,3},{3,2},{4,5},{5,4},{6,7},{7,6},{8,9},{9,8},{10,11... | collective-permute-start | bytes 1572872 | tf_op jit(solution)/shard_map/ppermute | solution.py:237
  50.0 7.2 %collective-permute-start.14 = (f32[4,256,128]{2,1,0:T(8,128)S(1)}, f32[4,256,128]{2,1,0:T(8,128)S(1)}, u32[]{:S(2)}, u32[]{:S(2)}) collective-permute-start(f32[4,256,128]{2,1,0:T(8,128)S(1)} %collective-permute-done.13.refs_2_), channel_id=1, source_target_pairs={{0,1},{1,0},{2,3},{3,2},{4,5},{5,4},{6,7},{7,6},{8,9},{9,8},{10,11... | collective-permute-start | bytes 1572872 | tf_op jit(solution)/shard_map/ppermute | solution.py:237
  52.8 8.3 %collective-permute-start.15 = (f32[256,128]{1,0:T(8,128)S(1)}, f32[256,128]{1,0:T(8,128)S(1)}, u32[]{:S(2)}, u32[]{:S(2)}) collective-permute-start(f32[256,128]{1,0:T(8,128)S(1)} %get-tuple-element.58), channel_id=1, source_target_pairs={{0,4},{1,5},{2,6},{3,7},{4,0},{5,1},{6,2},{7,3},{8,12},{9,13},{10,... | collective-permute-start | bytes 393224 | tf_op jit(solution)/shard_map/ppermute | solution.py:237
  53.0 12.9 %collective-permute-start.16 = (f32[256,128]{1,0:T(8,128)S(1)}, f32[256,128]{1,0:T(8,128)S(1)}, u32[]{:S(2)}, u32[]{:S(2)}) collective-permute-start(f32[256,128]{1,0:T(8,128)S(1)} %get-tuple-element.62), channel_id=1, source_target_pairs={{0,8},{1,9},{2,10},{3,11},{4,12},{5,13},{6,14},{7,15},{8,0},{9,1},... | collective-permute-start | bytes 393224 | tf_op jit(solution)/shard_map/ppermute | solution.py:237
  54.3 11.5 %collective-permute-start.17 = (f32[256,128]{1,0:T(8,128)S(1)}, f32[256,128]{1,0:T(8,128)S(1)}, u32[]{:S(2)}, u32[]{:S(2)}) collective-permute-start(f32[256,128]{1,0:T(8,128)S(1)} %get-tuple-element.63), channel_id=1, source_target_pairs={{0,12},{1,13},{2,14},{3,15},{4,8},{5,9},{6,10},{7,11},{8,4},{9,5},... | collective-permute-start | bytes 393224 | tf_op jit(solution)/shard_map/ppermute | solution.py:237
  61.1 15.7 %collective-permute-start.24 = (f32[2,256,128]{2,1,0:T(8,128)S(1)}, f32[2,256,128]{2,1,0:T(8,128)S(1)}, u32[]{:S(2)}, u32[]{:S(2)}) collective-permute-start(f32[2,256,128]{2,1,0:T(8,128)S(1)} %get-tuple-element.64.refs_4_.refs_1_), channel_id=1, source_target_pairs={{0,2},{1,3},{2,0},{3,1},{4,6},{5,7},{6,4},{7,5},{8,10},{9,11},{10,... | collective-permute-start | bytes 786440 | tf_op jit(solution)/shard_map/ppermute | solution.py:237
  65.9 10.9 %collective-permute-start.23 = (f32[2,256,128]{2,1,0:T(8,128)S(1)}, f32[2,256,128]{2,1,0:T(8,128)S(1)}, u32[]{:S(2)}, u32[]{:S(2)}) collective-permute-start(f32[2,256,128]{2,1,0:T(8,128)S(1)} %get-tuple-element.70.refs_0_), channel_id=1, source_target_pairs={{0,2},{1,3},{2,0},{3,1},{4,6},{5,7},{6,4},{7,5},{8,10},{9,11},{10,... | collective-permute-start | bytes 786440 | tf_op jit(solution)/shard_map/ppermute | solution.py:237
  67.6 9.2 %collective-permute-start.18 = (f32[256,128]{1,0:T(8,128)S(1)}, f32[256,128]{1,0:T(8,128)S(1)}, u32[]{:S(2)}, u32[]{:S(2)}) collective-permute-start(f32[256,128]{1,0:T(8,128)S(1)} %get-tuple-element.65), channel_id=1, source_target_pairs={{0,8},{1,9},{2,10},{3,11},{4,12},{5,13},{6,14},{7,15},{8,0},{9,1},... | collective-permute-start | bytes 393224 | tf_op jit(solution)/shard_map/ppermute | solution.py:237
  71.2 8.0 %collective-permute-start.22 = (f32[2,256,128]{2,1,0:T(8,128)S(1)}, f32[2,256,128]{2,1,0:T(8,128)S(1)}, u32[]{:S(2)}, u32[]{:S(2)}) collective-permute-start(f32[2,256,128]{2,1,0:T(8,128)S(1)} %get-tuple-element.64.refs_4_.refs_1_), channel_id=1, source_target_pairs={{0,1},{1,0},{2,3},{3,2},{4,5},{5,4},{6,7},{7,6},{8,9},{9,8},{10,11... | collective-permute-start | bytes 786440 | tf_op jit(solution)/shard_map/ppermute | solution.py:237
  77.3 7.2 %collective-permute-start.20 = (f32[256,128]{1,0:T(8,128)S(1)}, f32[256,128]{1,0:T(8,128)S(1)}, u32[]{:S(2)}, u32[]{:S(2)}) collective-permute-start(f32[256,128]{1,0:T(8,128)S(1)} %get-tuple-element.67), channel_id=1, source_target_pairs={{0,4},{1,5},{2,6},{3,7},{4,0},{5,1},{6,2},{7,3},{8,12},{9,13},{10,... | collective-permute-start | bytes 393224 | tf_op jit(solution)/shard_map/ppermute | solution.py:237
  77.3 9.1 %collective-permute-start.19 = (f32[256,128]{1,0:T(8,128)S(1)}, f32[256,128]{1,0:T(8,128)S(1)}, u32[]{:S(2)}, u32[]{:S(2)}) collective-permute-start(f32[256,128]{1,0:T(8,128)S(1)} %get-tuple-element.66), channel_id=1, source_target_pairs={{0,12},{1,13},{2,14},{3,15},{4,8},{5,9},{6,10},{7,11},{8,4},{9,5},... | collective-permute-start | bytes 393224 | tf_op jit(solution)/shard_map/ppermute | solution.py:237
  80.9 15.1 %collective-permute-start.27 = (f32[256,128]{1,0:T(8,128)S(1)}, f32[256,128]{1,0:T(8,128)S(1)}, u32[]{:S(2)}, u32[]{:S(2)}) collective-permute-start(f32[256,128]{1,0:T(8,128)S(1)} %get-tuple-element.73), channel_id=1, source_target_pairs={{0,8},{1,9},{2,10},{3,11},{4,12},{5,13},{6,14},{7,15},{8,0},{9,1},... | collective-permute-start | bytes 393224 | tf_op jit(solution)/shard_map/ppermute | solution.py:237
  82.6 13.5 %collective-permute-start.28 = (f32[256,128]{1,0:T(8,128)S(1)}, f32[256,128]{1,0:T(8,128)S(1)}, u32[]{:S(2)}, u32[]{:S(2)}) collective-permute-start(f32[256,128]{1,0:T(8,128)S(1)} %get-tuple-element.74), channel_id=1, source_target_pairs={{0,12},{1,13},{2,14},{3,15},{4,8},{5,9},{6,10},{7,11},{8,4},{9,5},... | collective-permute-start | bytes 393224 | tf_op jit(solution)/shard_map/ppermute | solution.py:237
  84.5 11.6 %collective-permute-start.29 = (f32[256,128]{1,0:T(8,128)S(1)}, f32[256,128]{1,0:T(8,128)S(1)}, u32[]{:S(2)}, u32[]{:S(2)}) collective-permute-start(f32[256,128]{1,0:T(8,128)S(1)} %get-tuple-element.75), channel_id=1, source_target_pairs={{0,4},{1,5},{2,6},{3,7},{4,0},{5,1},{6,2},{7,3},{8,12},{9,13},{10,... | collective-permute-start | bytes 393224 | tf_op jit(solution)/shard_map/ppermute | solution.py:237
  (23 other events, 135.2 us)

commit v7 on v6

--- a/solution.py
+++ b/solution.py
@@ -159,6 +159,10 @@
         refs[-1][s] = refs[s][...]
 
 
+def held_kernel(me_ref, x_ref, behind_ref, out_ref):
+    out_ref[...] = x_ref[...]
+
+
 def join_kernel(n, me_ref, u_ref, *refs):
     spot, _ = place(me_ref)
     out, sq = refs[-2:]
@@ -302,7 +306,7 @@
     near = group(near)
     near_core, near_over = across(near, 1), across(near, 2)
     u1, u1_nat = kinetic(psi_prev, [psi_cur], n_out=1)
-    u1 = exchange_all(after(u1, near_over))
+    u1 = exchange_all(call(held_kernel, [packed], [me], [u1, near_over], (), [VM, ANY])[0])
     far = group(far, [coup, u1_nat])
     w1 = mix(gather_near_far(near, far, near_core, across(far, 1), near_over), 5000000000)
     w1_c = exchange(w1)

time: 109 us -> 111 us (1.018)
  local copies, waits for them, and re-layouts: 2.7 us -> 4.85 us
    unnamed x20 -> x24, local copies, waits for them, and re-layouts: 2.7 us -> 4.85 us
    pallas_call x15 -> x16, Pallas kernels: 17.8 us -> 17.6 us  [call(): pl.pallas_call(kernel, out_shape=outs, in_specs=[SM] * len(scalars) + (sp...]
  transfers between devices with their start and end apart: 37 -> 37, of which waited for: 20 -> 19; matrix products, arithmetic and copies ran while one was open for 0% -> 0% of each run, Pallas kernels for 16% -> 15%
where the time goes in v7:
time: 111 us
  waiting for transfers between devices  45.8 us (41%)
  starting transfers between devices  41.4 us (37%)
  Pallas kernels  17.6 us (16%)
  local copies, waits for them, and re-layouts  4.85 us (4%)
    ppermute x36, waiting for transfers between devices, swap(): return lax.ppermute(x, 'chan', [(i, i ^ bits) for i in range(nd)])  39.3 us
    ppermute x36, starting transfers between devices, swap(): return lax.ppermute(x, 'chan', [(i, i ^ bits) for i in range(nd)])  37.2 us
    pallas_call x16, Pallas kernels, call(): pl.pallas_call(kernel, out_shape=outs, in_specs=[SM] * len(scalars) + (sp...  17.6 us
    all_to_all x1, waiting for transfers between devices, exchange_all(): lax.all_to_all(x, 'chan', 0, 0, tiled=True, axis_index_groups=lines)  6.52 us
    unnamed x24, local copies, waits for them, and re-layouts  4.85 us
    all_to_all x1, starting transfers between devices, exchange_all(): lax.all_to_all(x, 'chan', 0, 0, tiled=True, axis_index_groups=lines)  4.24 us
  transfers between devices with their start and end apart: 37, of which 19 were waited for; matrix products, arithmetic and copies ran while one was open for 0% of the time, Pallas kernels for 15%

profile of v7, /device:TPU:0, one launch (start us, length us, event | category | flops | bytes accessed | tf_op | source)
XLA Modules:
  0.0 111.1 jit_solution(5616894293000486135)
XLA Ops:
  2.0 3.1 %collective-permute-start.2 = (f32[256,128]{1,0:T(8,128)S(1)}, f32[256,128]{1,0:T(8,128)S(1)}, u32[]{:S(2)}, u32[]{:S(2)}) collective-permute-start(f32[256,128]{1,0:T(8,128)S(1)} %get-tuple-element.44), channel_id=1, source_target_pairs={{0,4},{1,5},{2,6},{3,7},{4,0},{5,1},{6,2},{7,3},{8,12},{9,13},{10,... | collective-permute-start | bytes 393224 | tf_op jit(solution)/shard_map/ppermute | solution.py:241
  5.1 2.6 %collective-permute-start = (f32[256,128]{1,0:T(8,128)S(1)}, f32[256,128]{1,0:T(8,128)S(1)}, u32[]{:S(2)}, u32[]{:S(2)}) collective-permute-start(f32[256,128]{1,0:T(8,128)S(1)} %get-tuple-element.40), channel_id=1, source_target_pairs={{0,8},{1,9},{2,10},{3,11},{4,12},{5,13},{6,14},{7,15},{8,0},{9,1},... | collective-permute-start | bytes 393224 | tf_op jit(solution)/shard_map/ppermute | solution.py:241
  7.7 2.4 %collective-permute-done.2.refs_1_ = f32[256,128]{1,0:T(8,128)S(1)} collective-permute-done((f32[256,128]{1,0:T(8,128)S(1)}, f32[256,128]{1,0:T(8,128)S(1)}, u32[]{:S(2)}, u32[]{:S(2)}) %collective-permute-start.2) | collective-permute-done | bytes 131104 | tf_op jit(solution)/shard_map/ppermute | solution.py:241
  10.2 1.8 %collective-permute-start.6 = (f32[2,256,128]{2,1,0:T(8,128)S(1)}, f32[2,256,128]{2,1,0:T(8,128)S(1)}, u32[]{:S(2)}, u32[]{:S(2)}) collective-permute-start(f32[2,256,128]{2,1,0:T(8,128)S(1)} %shard_map.107.refs_1_), channel_id=1, source_target_pairs={{0,2},{1,3},{2,0},{3,1},{4,6},{5,7},{6,4},{7,5},{8,10},{9,11},{10,... | collective-permute-start | bytes 786440 | tf_op jit(solution)/shard_map/ppermute | solution.py:241
  12.7 2.0 %shard_map.103.refs_2_.coup = bf16[3,2,4,32,512]{4,3,2,1,0:T(8,128)(2,1)S(1)} custom-call(s32[1]{0:T(128)} %bitcast.me_ref, s32[8,8]{1,0:T(8,128)S(1)} %copy-done.11, f32[3,512,512]{2,1,0:T(8,128)} %ang_ref.1), custom_call_target="tpu_custom_call" | custom-call | bytes 65536 | tf_op jit(solution)/shard_map/pallas_call | solution.py:218
  14.7 2.0 %shard_map.105 = (f32[4,256,128]{2,1,0:T(8,128)S(1)}, f32[32,32,128]{2,1,0:T(8,128)S(1)}) custom-call(s32[1]{0:T(128)} %bitcast.me_ref, s32[2,32]{1,0:T(2,128)S(1)} %bitcast.2, f32[32,32]{1,0:T(8,128)S(1)} %copy-done.5, f32[128,128]{1,0:T(8,128)S(1)} %copy-done.2, f32[32,32,128]{2,1,0:T(8,128)S(1)} %copy-done.3, f32[32,32,128]{2,1,0:T(8,128)S(1)} %copy-done.1), custom_call_target="tpu_custom_call" | custom-call | bytes 65536 | tf_op jit(solution)/shard_map/pallas_call | solution.py:218
  20.5 4.2 %all-to-all-start = ((f32[4,256,128]{2,1,0:T(8,128)}), f32[4,256,128]{2,1,0:T(8,128)S(1)}, u32[]{:S(2)}, u32[]{:S(2)}) async-start(f32[4,256,128]{2,1,0:T(8,128)} %shard_map.110), calls=%async_computation | async-start | bytes 1048576 | tf_op jit(solution)/shard_map/all_to_all | solution.py:251
  27.6 2.6 %shard_map.108 = (f32[256,128]{1,0:T(8,128)S(1)}, f32[256,128]{1,0:T(8,128)S(1)}, f32[256,128]{1,0:T(8,128)S(1)}, f32[256,128]{1,0:T(8,128)S(1)}) custom-call(s32[1]{0:T(128)} %bitcast.me_ref, bf16[3,2,4,32,512]{4,3,2,1,0:T(8,128)(2,1)S(1)} %shard_map.103.refs_2_.coup, f32[3,32,128]{2,1,0:T(8,128)S(1)} %copy-done.4, f32[2,256,128]{2,1,0:T(8,128)S(1)} %shard_map.106.refs_0_, ...), custom_call_target="tpu_custom_call" | custom-call | flops 5000000000 | bytes 65536 | tf_op jit(solution)/shard_map/pallas_call | solution.py:218
  31.5 6.5 %all-to-all-done.u_ref = f32[4,256,128]{2,1,0:T(8,128)S(1)} async-done(((f32[4,256,128]{2,1,0:T(8,128)}), f32[4,256,128]{2,1,0:T(8,128)S(1)}, u32[]{:S(2)}, u32[]{:S(2)}) %all-to-all-start) | async-done | bytes 524320 | tf_op jit(solution)/shard_map/all_to_all | solution.py:251
  42.0 2.0 %collective-permute-start.11 = (f32[256,128]{1,0:T(8,128)S(1)}, f32[256,128]{1,0:T(8,128)S(1)}, u32[]{:S(2)}, u32[]{:S(2)}) collective-permute-start(f32[256,128]{1,0:T(8,128)S(1)} %get-tuple-element.48.refs_3_), channel_id=1, source_target_pairs={{0,4},{1,5},{2,6},{3,7},{4,0},{5,1},{6,2},{7,3},{8,12},{9,13},{10,... | collective-permute-start | bytes 393224 | tf_op jit(solution)/shard_map/ppermute | solution.py:241
  44.0 6.5 %collective-permute-done.9.refs_1_ = f32[256,128]{1,0:T(8,128)S(1)} collective-permute-done((f32[256,128]{1,0:T(8,128)S(1)}, f32[256,128]{1,0:T(8,128)S(1)}, u32[]{:S(2)}, u32[]{:S(2)}) %collective-permute-start.9) | collective-permute-done | bytes 131104 | tf_op jit(solution)/shard_map/ppermute | solution.py:241
  52.6 2.8 %shard_map.109 = (f32[256,128]{1,0:T(8,128)S(1)}, f32[256,128]{1,0:T(8,128)S(1)}, f32[256,128]{1,0:T(8,128)S(1)}, f32[256,128]{1,0:T(8,128)S(1)}, f32[32,32,128]{2,1,0:T(8,128)}, /*index=5*/f32[32,32,128]{2,1,0:T(8,128)S(1)}) custom-call(s32[1]{0:T(128)} %bitcast.me_ref, s32[2,32]{1,0:T(2,128)S(1)} %bitcast.3, f32[32,32]{1,0:T(8,128)S(1)} %copy-done.5, ...), custom_call_target="tpu_custom_call" | custom-call | bytes 65536 | tf_op jit(solution)/shard_map/pallas_call | solution.py:218
  56.9 2.8 %collective-permute-start.17 = (f32[256,128]{1,0:T(8,128)S(1)}, f32[256,128]{1,0:T(8,128)S(1)}, u32[]{:S(2)}, u32[]{:S(2)}) collective-permute-start(f32[256,128]{1,0:T(8,128)S(1)} %get-tuple-element.61), channel_id=1, source_target_pairs={{0,12},{1,13},{2,14},{3,15},{4,8},{5,9},{6,10},{7,11},{8,4},{9,5},... | collective-permute-start | bytes 393224 | tf_op jit(solution)/shard_map/ppermute | solution.py:241
  61.4 2.3 %collective-permute-done.15.refs_3_ = f32[256,128]{1,0:T(8,128)S(1)} collective-permute-done((f32[256,128]{1,0:T(8,128)S(1)}, f32[256,128]{1,0:T(8,128)S(1)}, u32[]{:S(2)}, u32[]{:S(2)}) %collective-permute-start.15) | collective-permute-done | bytes 131104 | tf_op jit(solution)/shard_map/ppermute | solution.py:241
  64.2 4.3 %collective-permute-done.16.refs_2_ = f32[256,128]{1,0:T(8,128)S(1)} collective-permute-done((f32[256,128]{1,0:T(8,128)S(1)}, f32[256,128]{1,0:T(8,128)S(1)}, u32[]{:S(2)}, u32[]{:S(2)}) %collective-permute-start.16) | collective-permute-done | bytes 131104 | tf_op jit(solution)/shard_map/ppermute | solution.py:241
  70.2 3.6 %collective-permute-start.18 = (f32[256,128]{1,0:T(8,128)S(1)}, f32[256,128]{1,0:T(8,128)S(1)}, u32[]{:S(2)}, u32[]{:S(2)}) collective-permute-start(f32[256,128]{1,0:T(8,128)S(1)} %get-tuple-element.63), channel_id=1, source_target_pairs={{0,8},{1,9},{2,10},{3,11},{4,12},{5,13},{6,14},{7,15},{8,0},{9,1},... | collective-permute-start | bytes 393224 | tf_op jit(solution)/shard_map/ppermute | solution.py:241
  74.3 5.1 %collective-permute-done.18.refs_1_ = f32[256,128]{1,0:T(8,128)S(1)} collective-permute-done((f32[256,128]{1,0:T(8,128)S(1)}, f32[256,128]{1,0:T(8,128)S(1)}, u32[]{:S(2)}, u32[]{:S(2)}) %collective-permute-start.18) | collective-permute-done | bytes 131104 | tf_op jit(solution)/shard_map/ppermute | solution.py:241
  79.9 1.9 %collective-permute-start.19 = (f32[256,128]{1,0:T(8,128)S(1)}, f32[256,128]{1,0:T(8,128)S(1)}, u32[]{:S(2)}, u32[]{:S(2)}) collective-permute-start(f32[256,128]{1,0:T(8,128)S(1)} %get-tuple-element.64), channel_id=1, source_target_pairs={{0,12},{1,13},{2,14},{3,15},{4,8},{5,9},{6,10},{7,11},{8,4},{9,5},... | collective-permute-start | bytes 393224 | tf_op jit(solution)/shard_map/ppermute | solution.py:241
  85.1 1.9 %collective-permute-start.28 = (f32[256,128]{1,0:T(8,128)S(1)}, f32[256,128]{1,0:T(8,128)S(1)}, u32[]{:S(2)}, u32[]{:S(2)}) collective-permute-start(f32[256,128]{1,0:T(8,128)S(1)} %get-tuple-element.72), channel_id=1, source_target_pairs={{0,12},{1,13},{2,14},{3,15},{4,8},{5,9},{6,10},{7,11},{8,4},{9,5},... | collective-permute-start | bytes 393224 | tf_op jit(solution)/shard_map/ppermute | solution.py:241
  87.1 2.0 %collective-permute-done.19.refs_2_ = f32[256,128]{1,0:T(8,128)S(1)} collective-permute-done((f32[256,128]{1,0:T(8,128)S(1)}, f32[256,128]{1,0:T(8,128)S(1)}, u32[]{:S(2)}, u32[]{:S(2)}) %collective-permute-start.19) | collective-permute-done | bytes 131104 | tf_op jit(solution)/shard_map/ppermute | solution.py:241
  89.1 2.2 %shard_map.115 = (f32[32,32,128]{2,1,0:T(8,128)S(1)}, f32[32,32,128]{2,1,0:T(8,128)}) custom-call(s32[1]{0:T(128)} %bitcast.me_ref, s32[2,32]{1,0:T(2,128)S(1)} %bitcast.4, f32[32,32]{1,0:T(8,128)S(1)} %copy-done.5, f32[128,128]{1,0:T(8,128)S(1)} %copy-done.2, f32[32,32,128]{2,1,0:T(8,128)S(1)} %get-tuple-element.49.prev, ...), custom_call_target="tpu_custom_call" | custom-call | bytes 65536 | tf_op jit(solution)/shard_map/pallas_call | solution.py:218
  91.3 7.4 %collective-permute-done.27.refs_1_ = f32[256,128]{1,0:T(8,128)S(1)} collective-permute-done((f32[256,128]{1,0:T(8,128)S(1)}, f32[256,128]{1,0:T(8,128)S(1)}, u32[]{:S(2)}, u32[]{:S(2)}) %collective-permute-start.27) | collective-permute-done | bytes 131104 | tf_op jit(solution)/shard_map/ppermute | solution.py:241
  102.8 1.9 %collective-permute-start.35 = (f32[8,128]{1,0:T(8,128)S(1)}, f32[8,128]{1,0:T(8,128)S(1)}, u32[]{:S(2)}, u32[]{:S(2)}) collective-permute-start(f32[8,128]{1,0:T(8,128)S(1)} %add_add_fusion.1), channel_id=1, source_target_pairs={{0,12},{1,13},{2,14},{3,15},{4,8},{5,9},{6,10},{7,11},{8,4},{9,5},... | collective-permute-start | bytes 12296 | tf_op jit(solution)/shard_map/ppermute | solution.py:241
  104.8 2.1 %collective-permute-start.34 = (f32[8,128]{1,0:T(8,128)S(1)}, f32[8,128]{1,0:T(8,128)S(1)}, u32[]{:S(2)}, u32[]{:S(2)}) collective-permute-start(f32[8,128]{1,0:T(8,128)S(1)} %add_add_fusion.1), channel_id=1, source_target_pairs={{0,8},{1,9},{2,10},{3,11},{4,12},{5,13},{6,14},{7,15},{8,0},{9,1},... | collective-permute-start | bytes 12296 | tf_op jit(solution)/shard_map/ppermute | solution.py:241
  (94 shorter events, 34.1 us)
Async XLA Ops:
  2.0 8.1 %collective-permute-start.2 = (f32[256,128]{1,0:T(8,128)S(1)}, f32[256,128]{1,0:T(8,128)S(1)}, u32[]{:S(2)}, u32[]{:S(2)}) collective-permute-start(f32[256,128]{1,0:T(8,128)S(1)} %get-tuple-element.44), channel_id=1, source_target_pairs={{0,4},{1,5},{2,6},{3,7},{4,0},{5,1},{6,2},{7,3},{8,12},{9,13},{10,... | collective-permute-start | bytes 393224 | tf_op jit(solution)/shard_map/ppermute | solution.py:241
  5.1 12.9 %collective-permute-start = (f32[256,128]{1,0:T(8,128)S(1)}, f32[256,128]{1,0:T(8,128)S(1)}, u32[]{:S(2)}, u32[]{:S(2)}) collective-permute-start(f32[256,128]{1,0:T(8,128)S(1)} %get-tuple-element.40), channel_id=1, source_target_pairs={{0,8},{1,9},{2,10},{3,11},{4,12},{5,13},{6,14},{7,15},{8,0},{9,1},... | collective-permute-start | bytes 393224 | tf_op jit(solution)/shard_map/ppermute | solution.py:241
  7.7 10.3 %collective-permute-start.1 = (f32[256,128]{1,0:T(8,128)S(1)}, f32[256,128]{1,0:T(8,128)S(1)}, u32[]{:S(2)}, u32[]{:S(2)}) collective-permute-start(f32[256,128]{1,0:T(8,128)S(1)} %get-tuple-element.41), channel_id=1, source_target_pairs={{0,12},{1,13},{2,14},{3,15},{4,8},{5,9},{6,10},{7,11},{8,4},{9,5},... | collective-permute-start | bytes 393224 | tf_op jit(solution)/shard_map/ppermute | solution.py:241
  10.2 9.5 %collective-permute-start.6 = (f32[2,256,128]{2,1,0:T(8,128)S(1)}, f32[2,256,128]{2,1,0:T(8,128)S(1)}, u32[]{:S(2)}, u32[]{:S(2)}) collective-permute-start(f32[2,256,128]{2,1,0:T(8,128)S(1)} %shard_map.107.refs_1_), channel_id=1, source_target_pairs={{0,2},{1,3},{2,0},{3,1},{4,6},{5,7},{6,4},{7,5},{8,10},{9,11},{10,... | collective-permute-start | bytes 786440 | tf_op jit(solution)/shard_map/ppermute | solution.py:241
  18.1 7.2 %collective-permute-start.5 = (f32[2,256,128]{2,1,0:T(8,128)S(1)}, f32[2,256,128]{2,1,0:T(8,128)}, u32[]{:S(2)}, u32[]{:S(2)}) collective-permute-start(f32[2,256,128]{2,1,0:T(8,128)S(1)} %shard_map.106.refs_0_), channel_id=1, source_target_pairs={{0,2},{1,3},{2,0},{3,1},{4,6},{5,7},{6,4},{7,5},{8,10},{9,11},{10,... | collective-permute-start | bytes 786440 | tf_op jit(solution)/shard_map/ppermute | solution.py:241
  20.5 17.5 %all-to-all-start = ((f32[4,256,128]{2,1,0:T(8,128)}), f32[4,256,128]{2,1,0:T(8,128)S(1)}, u32[]{:S(2)}, u32[]{:S(2)}) async-start(f32[4,256,128]{2,1,0:T(8,128)} %shard_map.110), calls=%async_computation | async-start | bytes 1048576 | tf_op jit(solution)/shard_map/all_to_all | solution.py:251
  39.9 12.7 %collective-permute-start.13 = (f32[4,256,128]{2,1,0:T(8,128)S(1)}, f32[4,256,128]{2,1,0:T(8,128)S(1)}, u32[]{:S(2)}, u32[]{:S(2)}) collective-permute-start(f32[4,256,128]{2,1,0:T(8,128)S(1)} %get-tuple-element.51.refs_0_), channel_id=1, source_target_pairs={{0,2},{1,3},{2,0},{3,1},{4,6},{5,7},{6,4},{7,5},{8,10},{9,11},{10,... | collective-permute-start | bytes 1572872 | tf_op jit(solution)/shard_map/ppermute | solution.py:241
  40.5 10.0 %collective-permute-start.9 = (f32[256,128]{1,0:T(8,128)S(1)}, f32[256,128]{1,0:T(8,128)S(1)}, u32[]{:S(2)}, u32[]{:S(2)}) collective-permute-start(f32[256,128]{1,0:T(8,128)S(1)} %copy-done.9), channel_id=1, source_target_pairs={{0,8},{1,9},{2,10},{3,11},{4,12},{5,13},{6,14},{7,15},{8,0},{9,1},... | collective-permute-start | bytes 393224 | tf_op jit(solution)/shard_map/ppermute | solution.py:241
  40.5 10.0 %collective-permute-start.10 = (f32[256,128]{1,0:T(8,128)S(1)}, f32[256,128]{1,0:T(8,128)S(1)}, u32[]{:S(2)}, u32[]{:S(2)}) collective-permute-start(f32[256,128]{1,0:T(8,128)S(1)} %copy-done.7), channel_id=1, source_target_pairs={{0,12},{1,13},{2,14},{3,15},{4,8},{5,9},{6,10},{7,11},{8,4},{9,5},... | collective-permute-start | bytes 393224 | tf_op jit(solution)/shard_map/ppermute | solution.py:241
  42.0 8.9 %collective-permute-start.11 = (f32[256,128]{1,0:T(8,128)S(1)}, f32[256,128]{1,0:T(8,128)S(1)}, u32[]{:S(2)}, u32[]{:S(2)}) collective-permute-start(f32[256,128]{1,0:T(8,128)S(1)} %get-tuple-element.48.refs_3_), channel_id=1, source_target_pairs={{0,4},{1,5},{2,6},{3,7},{4,0},{5,1},{6,2},{7,3},{8,12},{9,13},{10,... | collective-permute-start | bytes 393224 | tf_op jit(solution)/shard_map/ppermute | solution.py:241
  44.0 15.8 %collective-permute-start.12 = (f32[4,256,128]{2,1,0:T(8,128)S(1)}, f32[4,256,128]{2,1,0:T(8,128)S(1)}, u32[]{:S(2)}, u32[]{:S(2)}) collective-permute-start(f32[4,256,128]{2,1,0:T(8,128)S(1)} %get-tuple-element.51.refs_0_), channel_id=1, source_target_pairs={{0,1},{1,0},{2,3},{3,2},{4,5},{5,4},{6,7},{7,6},{8,9},{9,8},{10,11... | collective-permute-start | bytes 1572872 | tf_op jit(solution)/shard_map/ppermute | solution.py:241
  52.6 7.2 %collective-permute-start.14 = (f32[4,256,128]{2,1,0:T(8,128)S(1)}, f32[4,256,128]{2,1,0:T(8,128)S(1)}, u32[]{:S(2)}, u32[]{:S(2)}) collective-permute-start(f32[4,256,128]{2,1,0:T(8,128)S(1)} %collective-permute-done.13.refs_2_), channel_id=1, source_target_pairs={{0,1},{1,0},{2,3},{3,2},{4,5},{5,4},{6,7},{7,6},{8,9},{9,8},{10,11... | collective-permute-start | bytes 1572872 | tf_op jit(solution)/shard_map/ppermute | solution.py:241
  55.4 8.3 %collective-permute-start.15 = (f32[256,128]{1,0:T(8,128)S(1)}, f32[256,128]{1,0:T(8,128)S(1)}, u32[]{:S(2)}, u32[]{:S(2)}) collective-permute-start(f32[256,128]{1,0:T(8,128)S(1)} %get-tuple-element.56), channel_id=1, source_target_pairs={{0,4},{1,5},{2,6},{3,7},{4,0},{5,1},{6,2},{7,3},{8,12},{9,13},{10,... | collective-permute-start | bytes 393224 | tf_op jit(solution)/shard_map/ppermute | solution.py:241
  55.6 12.9 %collective-permute-start.16 = (f32[256,128]{1,0:T(8,128)S(1)}, f32[256,128]{1,0:T(8,128)S(1)}, u32[]{:S(2)}, u32[]{:S(2)}) collective-permute-start(f32[256,128]{1,0:T(8,128)S(1)} %get-tuple-element.60), channel_id=1, source_target_pairs={{0,8},{1,9},{2,10},{3,11},{4,12},{5,13},{6,14},{7,15},{8,0},{9,1},... | collective-permute-start | bytes 393224 | tf_op jit(solution)/shard_map/ppermute | solution.py:241
  56.9 11.5 %collective-permute-start.17 = (f32[256,128]{1,0:T(8,128)S(1)}, f32[256,128]{1,0:T(8,128)S(1)}, u32[]{:S(2)}, u32[]{:S(2)}) collective-permute-start(f32[256,128]{1,0:T(8,128)S(1)} %get-tuple-element.61), channel_id=1, source_target_pairs={{0,12},{1,13},{2,14},{3,15},{4,8},{5,9},{6,10},{7,11},{8,4},{9,5},... | collective-permute-start | bytes 393224 | tf_op jit(solution)/shard_map/ppermute | solution.py:241
  63.8 15.7 %collective-permute-start.24 = (f32[2,256,128]{2,1,0:T(8,128)S(1)}, f32[2,256,128]{2,1,0:T(8,128)S(1)}, u32[]{:S(2)}, u32[]{:S(2)}) collective-permute-start(f32[2,256,128]{2,1,0:T(8,128)S(1)} %get-tuple-element.62.refs_4_.refs_1_), channel_id=1, source_target_pairs={{0,2},{1,3},{2,0},{3,1},{4,6},{5,7},{6,4},{7,5},{8,10},{9,11},{10,... | collective-permute-start | bytes 786440 | tf_op jit(solution)/shard_map/ppermute | solution.py:241
  68.5 10.9 %collective-permute-start.23 = (f32[2,256,128]{2,1,0:T(8,128)S(1)}, f32[2,256,128]{2,1,0:T(8,128)S(1)}, u32[]{:S(2)}, u32[]{:S(2)}) collective-permute-start(f32[2,256,128]{2,1,0:T(8,128)S(1)} %get-tuple-element.68.refs_0_), channel_id=1, source_target_pairs={{0,2},{1,3},{2,0},{3,1},{4,6},{5,7},{6,4},{7,5},{8,10},{9,11},{10,... | collective-permute-start | bytes 786440 | tf_op jit(solution)/shard_map/ppermute | solution.py:241
  70.2 9.2 %collective-permute-start.18 = (f32[256,128]{1,0:T(8,128)S(1)}, f32[256,128]{1,0:T(8,128)S(1)}, u32[]{:S(2)}, u32[]{:S(2)}) collective-permute-start(f32[256,128]{1,0:T(8,128)S(1)} %get-tuple-element.63), channel_id=1, source_target_pairs={{0,8},{1,9},{2,10},{3,11},{4,12},{5,13},{6,14},{7,15},{8,0},{9,1},... | collective-permute-start | bytes 393224 | tf_op jit(solution)/shard_map/ppermute | solution.py:241
  73.8 8.0 %collective-permute-start.22 = (f32[2,256,128]{2,1,0:T(8,128)S(1)}, f32[2,256,128]{2,1,0:T(8,128)S(1)}, u32[]{:S(2)}, u32[]{:S(2)}) collective-permute-start(f32[2,256,128]{2,1,0:T(8,128)S(1)} %get-tuple-element.62.refs_4_.refs_1_), channel_id=1, source_target_pairs={{0,1},{1,0},{2,3},{3,2},{4,5},{5,4},{6,7},{7,6},{8,9},{9,8},{10,11... | collective-permute-start | bytes 786440 | tf_op jit(solution)/shard_map/ppermute | solution.py:241
  79.9 7.1 %collective-permute-start.20 = (f32[256,128]{1,0:T(8,128)S(1)}, f32[256,128]{1,0:T(8,128)S(1)}, u32[]{:S(2)}, u32[]{:S(2)}) collective-permute-start(f32[256,128]{1,0:T(8,128)S(1)} %get-tuple-element.65), channel_id=1, source_target_pairs={{0,4},{1,5},{2,6},{3,7},{4,0},{5,1},{6,2},{7,3},{8,12},{9,13},{10,... | collective-permute-start | bytes 393224 | tf_op jit(solution)/shard_map/ppermute | solution.py:241
  79.9 9.1 %collective-permute-start.19 = (f32[256,128]{1,0:T(8,128)S(1)}, f32[256,128]{1,0:T(8,128)S(1)}, u32[]{:S(2)}, u32[]{:S(2)}) collective-permute-start(f32[256,128]{1,0:T(8,128)S(1)} %get-tuple-element.64), channel_id=1, source_target_pairs={{0,12},{1,13},{2,14},{3,15},{4,8},{5,9},{6,10},{7,11},{8,4},{9,5},... | collective-permute-start | bytes 393224 | tf_op jit(solution)/shard_map/ppermute | solution.py:241
  83.5 15.2 %collective-permute-start.27 = (f32[256,128]{1,0:T(8,128)S(1)}, f32[256,128]{1,0:T(8,128)S(1)}, u32[]{:S(2)}, u32[]{:S(2)}) collective-permute-start(f32[256,128]{1,0:T(8,128)S(1)} %get-tuple-element.71), channel_id=1, source_target_pairs={{0,8},{1,9},{2,10},{3,11},{4,12},{5,13},{6,14},{7,15},{8,0},{9,1},... | collective-permute-start | bytes 393224 | tf_op jit(solution)/shard_map/ppermute | solution.py:241
  85.1 13.6 %collective-permute-start.28 = (f32[256,128]{1,0:T(8,128)S(1)}, f32[256,128]{1,0:T(8,128)S(1)}, u32[]{:S(2)}, u32[]{:S(2)}) collective-permute-start(f32[256,128]{1,0:T(8,128)S(1)} %get-tuple-element.72), channel_id=1, source_target_pairs={{0,12},{1,13},{2,14},{3,15},{4,8},{5,9},{6,10},{7,11},{8,4},{9,5},... | collective-permute-start | bytes 393224 | tf_op jit(solution)/shard_map/ppermute | solution.py:241
  87.0 11.7 %collective-permute-start.29 = (f32[256,128]{1,0:T(8,128)S(1)}, f32[256,128]{1,0:T(8,128)S(1)}, u32[]{:S(2)}, u32[]{:S(2)}) collective-permute-start(f32[256,128]{1,0:T(8,128)S(1)} %get-tuple-element.73), channel_id=1, source_target_pairs={{0,4},{1,5},{2,6},{3,7},{4,0},{5,1},{6,2},{7,3},{8,12},{9,13},{10,... | collective-permute-start | bytes 393224 | tf_op jit(solution)/shard_map/ppermute | solution.py:241
  (25 other events, 126.9 us)

commit v8 on v6

--- a/solution.py
+++ b/solution.py
@@ -13,7 +13,6 @@
 TEAM = 4
 F32 = jnp.float32
 BF16 = jnp.bfloat16
-HP = lax.Precision.HIGHEST
 VM = pl.BlockSpec(memory_space=pltpu.VMEM)
 SM = pl.BlockSpec(memory_space=pltpu.SMEM)
 ANY = pl.BlockSpec(memory_space=pl.ANY)
@@ -29,6 +28,15 @@
 
 def rows_of(spot, s, n, na):
     return pl.ds(pl.multiple_of((spot ^ hop(s, n)) * na, na), na)
+
+
+def halves(x):
+    hi = x.astype(BF16)
+    return hi, (x - hi.astype(F32)).astype(BF16)
+
+
+def product(a, b):
+    return sum(jnp.dot(a[i], b[j], preferred_element_type=F32) for i, j in ((0, 1), (1, 0), (0, 0)))
 
 
 def to_pieces_kernel(na, nc, me_ref, x_ref, *outs):
@@ -56,8 +64,8 @@
             return [(some[0].at[z], pl.ds(z * na, na)) for z in range(n)]
         return [(ref, rows_of(spot, s, n, na)) for s, ref in enumerate(some)]
 
-    kstr = 2.0 * ks[...]
-    krad = 2.0 * kr[...]
+    kstr = halves(2.0 * ks[...])
+    krad = halves(2.0 * kr[...])
     stretch = 1.0 + lax.broadcasted_iota(jnp.int32, (nr, nb), 0).astype(F32) / nr
     radius = 1.0 + 3.0 * lax.broadcasted_iota(jnp.int32, (nr, nb), 1).astype(F32) / nb
     rotation = 1.0 / (stretch * stretch)
@@ -71,8 +79,8 @@
                 x = piece[pl.ds(c, na, stride=nc), :]
                 cur[c, at, :] = x + base[c, at, :] if based else x
         tiles = [cur[c] for c in chans]
-        mixed_a = jnp.dot(kstr, jnp.concatenate(tiles, 1), precision=HP, preferred_element_type=F32)
-        mixed_b = jnp.dot(jnp.concatenate(tiles, 0), krad, precision=HP, preferred_element_type=F32)
+        mixed_a = product(kstr, halves(jnp.concatenate(tiles, 1)))
+        mixed_b = product(halves(jnp.concatenate(tiles, 0)), krad)
         for i, c in enumerate(chans):
             j = quanta[0, c].astype(F32)
             l = quanta[1, c].astype(F32)
@@ -318,10 +326,11 @@
     w3 = exchange(mix(gather_near_far(near, far, across(near, 1), across(far, 1), near_over), 0))
     (sums,) = call(functools.partial(norm_kernel, na, nc, n), [sds((8, nb), F32)], [me], [u3, *w3, s2, s3, s3_far])
     (cur_out,) = call(functools.partial(finish_kernel, na, nc), [natural], [me], [u3, *w3])
-    bit = 1
+    sums = (sums + swap(sums, 1)) + (swap(sums, 2) + swap(sums, 3))
+    bit = TEAM
     while bit < nd:
-        sums = (sums + swap(sums, bit)) + (swap(sums, 2 * bit) + swap(sums, 3 * bit))
-        bit *= 4
+        sums = sums + swap(sums, bit)
+        bit *= 2
     norms = jnp.sum(sums[:ITERS], axis=1) / (total_ch * nr * nb)
     return prev_out, cur_out, norms
 

time: 109 us -> 109 us (level)
  waiting for transfers between devices: 45.3 us -> 46.6 us
  Pallas kernels: 17.8 us -> 16.5 us
    pallas_call x15, Pallas kernels: 17.8 us -> 16.5 us  [call(): pl.pallas_call(kernel, out_shape=outs, in_specs=[SM] * len(scalars) + (sp...]
    ppermute x36 -> x35, waiting for transfers between devices: 38.5 us -> 39.8 us  [swap(): return lax.ppermute(x, 'chan', [(i, i ^ bits) for i in range(nd)])]
    ppermute x36 -> x35, starting transfers between devices: 37 us -> 37.5 us  [swap(): return lax.ppermute(x, 'chan', [(i, i ^ bits) for i in range(nd)])]
  transfers between devices with their start and end apart: 37 -> 36, of which waited for: 20 -> 20; matrix products, arithmetic and copies ran while one was open for 0% -> 0% of each run, Pallas kernels for 16% -> 14%
where the time goes in v8:
time: 109 us
  waiting for transfers between devices  46.6 us (43%)
  starting transfers between devices  41.8 us (38%)
  Pallas kernels  16.5 us (15%)
  local copies, waits for them, and re-layouts  2.7 us (2%)
    ppermute x35, waiting for transfers between devices, swap(): return lax.ppermute(x, 'chan', [(i, i ^ bits) for i in range(nd)])  39.8 us
    ppermute x35, starting transfers between devices, swap(): return lax.ppermute(x, 'chan', [(i, i ^ bits) for i in range(nd)])  37.5 us
    pallas_call x15, Pallas kernels, call(): pl.pallas_call(kernel, out_shape=outs, in_specs=[SM] * len(scalars) + (sp...  16.5 us
    all_to_all x1, waiting for transfers between devices, exchange_all(): lax.all_to_all(x, 'chan', 0, 0, tiled=True, axis_index_groups=lines)  6.82 us
    all_to_all x1, starting transfers between devices, exchange_all(): lax.all_to_all(x, 'chan', 0, 0, tiled=True, axis_index_groups=lines)  4.24 us
    unnamed x20, local copies, waits for them, and re-layouts  2.7 us
  transfers between devices with their start and end apart: 36, of which 20 were waited for; matrix products, arithmetic and copies ran while one was open for 0% of the time, Pallas kernels for 14%

profile of v8, /device:TPU:0, one launch (start us, length us, event | category | flops | bytes accessed | tf_op | source)
XLA Modules:
  0.0 109.0 jit_solution(16328920099873161971)
XLA Ops:
  2.0 3.1 %collective-permute-start.2 = (f32[256,128]{1,0:T(8,128)S(1)}, f32[256,128]{1,0:T(8,128)S(1)}, u32[]{:S(2)}, u32[]{:S(2)}) collective-permute-start(f32[256,128]{1,0:T(8,128)S(1)} %get-tuple-element.45), channel_id=1, source_target_pairs={{0,4},{1,5},{2,6},{3,7},{4,0},{5,1},{6,2},{7,3},{8,12},{9,13},{10,... | collective-permute-start | bytes 393224 | tf_op jit(solution)/shard_map/ppermute | solution.py:245
  5.1 2.6 %collective-permute-start = (f32[256,128]{1,0:T(8,128)S(1)}, f32[256,128]{1,0:T(8,128)S(1)}, u32[]{:S(2)}, u32[]{:S(2)}) collective-permute-start(f32[256,128]{1,0:T(8,128)S(1)} %get-tuple-element.41), channel_id=1, source_target_pairs={{0,8},{1,9},{2,10},{3,11},{4,12},{5,13},{6,14},{7,15},{8,0},{9,1},... | collective-permute-start | bytes 393224 | tf_op jit(solution)/shard_map/ppermute | solution.py:245
  7.7 2.4 %collective-permute-done.2.refs_1_ = f32[256,128]{1,0:T(8,128)S(1)} collective-permute-done((f32[256,128]{1,0:T(8,128)S(1)}, f32[256,128]{1,0:T(8,128)S(1)}, u32[]{:S(2)}, u32[]{:S(2)}) %collective-permute-start.2) | collective-permute-done | bytes 131104 | tf_op jit(solution)/shard_map/ppermute | solution.py:245
  10.2 1.8 %collective-permute-start.6 = (f32[2,256,128]{2,1,0:T(8,128)S(1)}, f32[2,256,128]{2,1,0:T(8,128)S(1)}, u32[]{:S(2)}, u32[]{:S(2)}) collective-permute-start(f32[2,256,128]{2,1,0:T(8,128)S(1)} %shard_map.107.refs_1_), channel_id=1, source_target_pairs={{0,2},{1,3},{2,0},{3,1},{4,6},{5,7},{6,4},{7,5},{8,10},{9,11},{10,... | collective-permute-start | bytes 786440 | tf_op jit(solution)/shard_map/ppermute | solution.py:245
  12.7 2.0 %shard_map.103.refs_2_.coup = bf16[3,2,4,32,512]{4,3,2,1,0:T(8,128)(2,1)S(1)} custom-call(s32[1]{0:T(128)} %bitcast.me_ref, s32[8,8]{1,0:T(8,128)S(1)} %copy-done.7, f32[3,512,512]{2,1,0:T(8,128)} %ang_ref.1), custom_call_target="tpu_custom_call" | custom-call | bytes 65536 | tf_op jit(solution)/shard_map/pallas_call | solution.py:222
  14.7 2.3 %shard_map.105 = (f32[4,256,128]{2,1,0:T(8,128)}, f32[32,32,128]{2,1,0:T(8,128)S(1)}) custom-call(s32[1]{0:T(128)} %bitcast.me_ref, s32[2,32]{1,0:T(2,128)S(1)} %bitcast.2, f32[32,32]{1,0:T(8,128)S(1)} %copy-done.5, f32[128,128]{1,0:T(8,128)S(1)} %copy-done.2, f32[32,32,128]{2,1,0:T(8,128)S(1)} %copy-done.3, f32[32,32,128]{2,1,0:T(8,128)S(1)} %copy-done.1), custom_call_target="tpu_custom_call" | custom-call | bytes 65536 | tf_op jit(solution)/shard_map/pallas_call | solution.py:222
  19.7 4.2 %all-to-all-start = ((f32[4,256,128]{2,1,0:T(8,128)}), f32[4,256,128]{2,1,0:T(8,128)S(1)}, u32[]{:S(2)}, u32[]{:S(2)}) async-start(f32[4,256,128]{2,1,0:T(8,128)} %get-tuple-element.52), calls=%async_computation | async-start | bytes 1048576 | tf_op jit(solution)/shard_map/all_to_all | solution.py:255
  27.7 2.6 %shard_map.108 = (f32[256,128]{1,0:T(8,128)S(1)}, f32[256,128]{1,0:T(8,128)S(1)}, f32[256,128]{1,0:T(8,128)S(1)}, f32[256,128]{1,0:T(8,128)S(1)}) custom-call(s32[1]{0:T(128)} %bitcast.me_ref, bf16[3,2,4,32,512]{4,3,2,1,0:T(8,128)(2,1)S(1)} %shard_map.103.refs_2_.coup, f32[3,32,128]{2,1,0:T(8,128)S(1)} %copy-done.4, f32[2,256,128]{2,1,0:T(8,128)S(1)} %shard_map.106.refs_0_, ...), custom_call_target="tpu_custom_call" | custom-call | flops 5000000000 | bytes 65536 | tf_op jit(solution)/shard_map/pallas_call | solution.py:222
  30.3 6.8 %all-to-all-done.u_ref = f32[4,256,128]{2,1,0:T(8,128)S(1)} async-done(((f32[4,256,128]{2,1,0:T(8,128)}), f32[4,256,128]{2,1,0:T(8,128)S(1)}, u32[]{:S(2)}, u32[]{:S(2)}) %all-to-all-start) | async-done | bytes 524320 | tf_op jit(solution)/shard_map/all_to_all | solution.py:255
  39.3 2.0 %collective-permute-start.11 = (f32[256,128]{1,0:T(8,128)S(1)}, f32[256,128]{1,0:T(8,128)S(1)}, u32[]{:S(2)}, u32[]{:S(2)}) collective-permute-start(f32[256,128]{1,0:T(8,128)S(1)} %get-tuple-element.49.refs_3_), channel_id=1, source_target_pairs={{0,4},{1,5},{2,6},{3,7},{4,0},{5,1},{6,2},{7,3},{8,12},{9,13},{10,... | collective-permute-start | bytes 393224 | tf_op jit(solution)/shard_map/ppermute | solution.py:245
  41.3 6.6 %collective-permute-done.9.refs_1_ = f32[256,128]{1,0:T(8,128)S(1)} collective-permute-done((f32[256,128]{1,0:T(8,128)S(1)}, f32[256,128]{1,0:T(8,128)S(1)}, u32[]{:S(2)}, u32[]{:S(2)}) %collective-permute-start.9) | collective-permute-done | bytes 131104 | tf_op jit(solution)/shard_map/ppermute | solution.py:245
  50.0 2.3 %shard_map.109 = (f32[256,128]{1,0:T(8,128)S(1)}, f32[256,128]{1,0:T(8,128)S(1)}, f32[256,128]{1,0:T(8,128)S(1)}, f32[256,128]{1,0:T(8,128)S(1)}, f32[32,32,128]{2,1,0:T(8,128)}, /*index=5*/f32[32,32,128]{2,1,0:T(8,128)S(1)}) custom-call(s32[1]{0:T(128)} %bitcast.me_ref, s32[2,32]{1,0:T(2,128)S(1)} %bitcast.3, f32[32,32]{1,0:T(8,128)S(1)} %copy-done.5, ...), custom_call_target="tpu_custom_call" | custom-call | bytes 65536 | tf_op jit(solution)/shard_map/pallas_call | solution.py:222
  53.8 2.8 %collective-permute-start.17 = (f32[256,128]{1,0:T(8,128)S(1)}, f32[256,128]{1,0:T(8,128)S(1)}, u32[]{:S(2)}, u32[]{:S(2)}) collective-permute-start(f32[256,128]{1,0:T(8,128)S(1)} %get-tuple-element.63), channel_id=1, source_target_pairs={{0,12},{1,13},{2,14},{3,15},{4,8},{5,9},{6,10},{7,11},{8,4},{9,5},... | collective-permute-start | bytes 393224 | tf_op jit(solution)/shard_map/ppermute | solution.py:245
  58.3 2.2 %collective-permute-done.15.refs_3_ = f32[256,128]{1,0:T(8,128)S(1)} collective-permute-done((f32[256,128]{1,0:T(8,128)S(1)}, f32[256,128]{1,0:T(8,128)S(1)}, u32[]{:S(2)}, u32[]{:S(2)}) %collective-permute-start.15) | collective-permute-done | bytes 131104 | tf_op jit(solution)/shard_map/ppermute | solution.py:245
  61.1 4.3 %collective-permute-done.16.refs_2_ = f32[256,128]{1,0:T(8,128)S(1)} collective-permute-done((f32[256,128]{1,0:T(8,128)S(1)}, f32[256,128]{1,0:T(8,128)S(1)}, u32[]{:S(2)}, u32[]{:S(2)}) %collective-permute-start.16) | collective-permute-done | bytes 131104 | tf_op jit(solution)/shard_map/ppermute | solution.py:245
  67.1 3.6 %collective-permute-start.18 = (f32[256,128]{1,0:T(8,128)S(1)}, f32[256,128]{1,0:T(8,128)S(1)}, u32[]{:S(2)}, u32[]{:S(2)}) collective-permute-start(f32[256,128]{1,0:T(8,128)S(1)} %get-tuple-element.65), channel_id=1, source_target_pairs={{0,8},{1,9},{2,10},{3,11},{4,12},{5,13},{6,14},{7,15},{8,0},{9,1},... | collective-permute-start | bytes 393224 | tf_op jit(solution)/shard_map/ppermute | solution.py:245
  71.2 5.1 %collective-permute-done.18.refs_1_ = f32[256,128]{1,0:T(8,128)S(1)} collective-permute-done((f32[256,128]{1,0:T(8,128)S(1)}, f32[256,128]{1,0:T(8,128)S(1)}, u32[]{:S(2)}, u32[]{:S(2)}) %collective-permute-start.18) | collective-permute-done | bytes 131104 | tf_op jit(solution)/shard_map/ppermute | solution.py:245
  76.8 1.9 %collective-permute-start.19 = (f32[256,128]{1,0:T(8,128)S(1)}, f32[256,128]{1,0:T(8,128)S(1)}, u32[]{:S(2)}, u32[]{:S(2)}) collective-permute-start(f32[256,128]{1,0:T(8,128)S(1)} %get-tuple-element.66), channel_id=1, source_target_pairs={{0,12},{1,13},{2,14},{3,15},{4,8},{5,9},{6,10},{7,11},{8,4},{9,5},... | collective-permute-start | bytes 393224 | tf_op jit(solution)/shard_map/ppermute | solution.py:245
  82.1 1.9 %collective-permute-start.28 = (f32[256,128]{1,0:T(8,128)S(1)}, f32[256,128]{1,0:T(8,128)S(1)}, u32[]{:S(2)}, u32[]{:S(2)}) collective-permute-start(f32[256,128]{1,0:T(8,128)S(1)} %get-tuple-element.74), channel_id=1, source_target_pairs={{0,12},{1,13},{2,14},{3,15},{4,8},{5,9},{6,10},{7,11},{8,4},{9,5},... | collective-permute-start | bytes 393224 | tf_op jit(solution)/shard_map/ppermute | solution.py:245
  84.0 1.9 %collective-permute-done.19.refs_2_ = f32[256,128]{1,0:T(8,128)S(1)} collective-permute-done((f32[256,128]{1,0:T(8,128)S(1)}, f32[256,128]{1,0:T(8,128)S(1)}, u32[]{:S(2)}, u32[]{:S(2)}) %collective-permute-start.19) | collective-permute-done | bytes 131104 | tf_op jit(solution)/shard_map/ppermute | solution.py:245
  86.0 1.9 %shard_map.114 = (f32[32,32,128]{2,1,0:T(8,128)S(1)}, f32[32,32,128]{2,1,0:T(8,128)}) custom-call(s32[1]{0:T(128)} %bitcast.me_ref, s32[2,32]{1,0:T(2,128)S(1)} %bitcast.4, f32[32,32]{1,0:T(8,128)S(1)} %copy-done.5, f32[128,128]{1,0:T(8,128)S(1)} %copy-done.2, f32[32,32,128]{2,1,0:T(8,128)S(1)} %get-tuple-element.50.prev, ...), custom_call_target="tpu_custom_call" | custom-call | bytes 65536 | tf_op jit(solution)/shard_map/pallas_call | solution.py:222
  87.9 7.7 %collective-permute-done.27.refs_1_ = f32[256,128]{1,0:T(8,128)S(1)} collective-permute-done((f32[256,128]{1,0:T(8,128)S(1)}, f32[256,128]{1,0:T(8,128)S(1)}, u32[]{:S(2)}, u32[]{:S(2)}) %collective-permute-start.27) | collective-permute-done | bytes 131104 | tf_op jit(solution)/shard_map/ppermute | solution.py:245
  99.7 2.5 %collective-permute-start.33 = (f32[8,128]{1,0:T(8,128)S(1)}, f32[8,128]{1,0:T(8,128)S(1)}, u32[]{:S(2)}, u32[]{:S(2)}) collective-permute-start(f32[8,128]{1,0:T(8,128)S(1)} %add_add_fusion), channel_id=1, source_target_pairs={{0,4},{1,5},{2,6},{3,7},{4,0},{5,1},{6,2},{7,3},{8,12},{9,13},{10,... | collective-permute-start | bytes 12296 | tf_op jit(solution)/shard_map/ppermute | solution.py:245
  103.9 2.4 %collective-permute-start.34 = (f32[8,128]{1,0:T(8,128)S(1)}, f32[8,128]{1,0:T(8,128)S(1)}, u32[]{:S(2)}, u32[]{:S(2)}) collective-permute-start(f32[8,128]{1,0:T(8,128)S(1)} %add.18), channel_id=1, source_target_pairs={{0,8},{1,9},{2,10},{3,11},{4,12},{5,13},{6,14},{7,15},{8,0},{9,1},... | collective-permute-start | bytes 12296 | tf_op jit(solution)/shard_map/ppermute | solution.py:245
  (88 shorter events, 31.0 us)
Async XLA Ops:
  2.0 8.1 %collective-permute-start.2 = (f32[256,128]{1,0:T(8,128)S(1)}, f32[256,128]{1,0:T(8,128)S(1)}, u32[]{:S(2)}, u32[]{:S(2)}) collective-permute-start(f32[256,128]{1,0:T(8,128)S(1)} %get-tuple-element.45), channel_id=1, source_target_pairs={{0,4},{1,5},{2,6},{3,7},{4,0},{5,1},{6,2},{7,3},{8,12},{9,13},{10,... | collective-permute-start | bytes 393224 | tf_op jit(solution)/shard_map/ppermute | solution.py:245
  5.1 12.9 %collective-permute-start = (f32[256,128]{1,0:T(8,128)S(1)}, f32[256,128]{1,0:T(8,128)S(1)}, u32[]{:S(2)}, u32[]{:S(2)}) collective-permute-start(f32[256,128]{1,0:T(8,128)S(1)} %get-tuple-element.41), channel_id=1, source_target_pairs={{0,8},{1,9},{2,10},{3,11},{4,12},{5,13},{6,14},{7,15},{8,0},{9,1},... | collective-permute-start | bytes 393224 | tf_op jit(solution)/shard_map/ppermute | solution.py:245
  7.7 10.3 %collective-permute-start.1 = (f32[256,128]{1,0:T(8,128)S(1)}, f32[256,128]{1,0:T(8,128)S(1)}, u32[]{:S(2)}, u32[]{:S(2)}) collective-permute-start(f32[256,128]{1,0:T(8,128)S(1)} %get-tuple-element.42), channel_id=1, source_target_pairs={{0,12},{1,13},{2,14},{3,15},{4,8},{5,9},{6,10},{7,11},{8,4},{9,5},... | collective-permute-start | bytes 393224 | tf_op jit(solution)/shard_map/ppermute | solution.py:245
  10.2 9.5 %collective-permute-start.6 = (f32[2,256,128]{2,1,0:T(8,128)S(1)}, f32[2,256,128]{2,1,0:T(8,128)S(1)}, u32[]{:S(2)}, u32[]{:S(2)}) collective-permute-start(f32[2,256,128]{2,1,0:T(8,128)S(1)} %shard_map.107.refs_1_), channel_id=1, source_target_pairs={{0,2},{1,3},{2,0},{3,1},{4,6},{5,7},{6,4},{7,5},{8,10},{9,11},{10,... | collective-permute-start | bytes 786440 | tf_op jit(solution)/shard_map/ppermute | solution.py:245
  18.1 6.5 %collective-permute-start.5 = (f32[2,256,128]{2,1,0:T(8,128)S(1)}, f32[2,256,128]{2,1,0:T(8,128)}, u32[]{:S(2)}, u32[]{:S(2)}) collective-permute-start(f32[2,256,128]{2,1,0:T(8,128)S(1)} %shard_map.106.refs_0_), channel_id=1, source_target_pairs={{0,2},{1,3},{2,0},{3,1},{4,6},{5,7},{6,4},{7,5},{8,10},{9,11},{10,... | collective-permute-start | bytes 786440 | tf_op jit(solution)/shard_map/ppermute | solution.py:245
  19.7 17.5 %all-to-all-start = ((f32[4,256,128]{2,1,0:T(8,128)}), f32[4,256,128]{2,1,0:T(8,128)S(1)}, u32[]{:S(2)}, u32[]{:S(2)}) async-start(f32[4,256,128]{2,1,0:T(8,128)} %get-tuple-element.52), calls=%async_computation | async-start | bytes 1048576 | tf_op jit(solution)/shard_map/all_to_all | solution.py:255
  37.3 12.7 %collective-permute-start.13 = (f32[4,256,128]{2,1,0:T(8,128)S(1)}, f32[4,256,128]{2,1,0:T(8,128)S(1)}, u32[]{:S(2)}, u32[]{:S(2)}) collective-permute-start(f32[4,256,128]{2,1,0:T(8,128)S(1)} %get-tuple-element.53.refs_0_), channel_id=1, source_target_pairs={{0,2},{1,3},{2,0},{3,1},{4,6},{5,7},{6,4},{7,5},{8,10},{9,11},{10,... | collective-permute-start | bytes 1572872 | tf_op jit(solution)/shard_map/ppermute | solution.py:245
  37.8 10.1 %collective-permute-start.9 = (f32[256,128]{1,0:T(8,128)S(1)}, f32[256,128]{1,0:T(8,128)S(1)}, u32[]{:S(2)}, u32[]{:S(2)}) collective-permute-start(f32[256,128]{1,0:T(8,128)S(1)} %get-tuple-element.47.refs_1_), channel_id=1, source_target_pairs={{0,8},{1,9},{2,10},{3,11},{4,12},{5,13},{6,14},{7,15},{8,0},{9,1},... | collective-permute-start | bytes 393224 | tf_op jit(solution)/shard_map/ppermute | solution.py:245
  37.8 10.1 %collective-permute-start.10 = (f32[256,128]{1,0:T(8,128)S(1)}, f32[256,128]{1,0:T(8,128)S(1)}, u32[]{:S(2)}, u32[]{:S(2)}) collective-permute-start(f32[256,128]{1,0:T(8,128)S(1)} %get-tuple-element.48.refs_2_), channel_id=1, source_target_pairs={{0,12},{1,13},{2,14},{3,15},{4,8},{5,9},{6,10},{7,11},{8,4},{9,5},... | collective-permute-start | bytes 393224 | tf_op jit(solution)/shard_map/ppermute | solution.py:245
  39.3 9.0 %collective-permute-start.11 = (f32[256,128]{1,0:T(8,128)S(1)}, f32[256,128]{1,0:T(8,128)S(1)}, u32[]{:S(2)}, u32[]{:S(2)}) collective-permute-start(f32[256,128]{1,0:T(8,128)S(1)} %get-tuple-element.49.refs_3_), channel_id=1, source_target_pairs={{0,4},{1,5},{2,6},{3,7},{4,0},{5,1},{6,2},{7,3},{8,12},{9,13},{10,... | collective-permute-start | bytes 393224 | tf_op jit(solution)/shard_map/ppermute | solution.py:245
  41.3 15.3 %collective-permute-start.12 = (f32[4,256,128]{2,1,0:T(8,128)S(1)}, f32[4,256,128]{2,1,0:T(8,128)S(1)}, u32[]{:S(2)}, u32[]{:S(2)}) collective-permute-start(f32[4,256,128]{2,1,0:T(8,128)S(1)} %get-tuple-element.53.refs_0_), channel_id=1, source_target_pairs={{0,1},{1,0},{2,3},{3,2},{4,5},{5,4},{6,7},{7,6},{8,9},{9,8},{10,11... | collective-permute-start | bytes 1572872 | tf_op jit(solution)/shard_map/ppermute | solution.py:245
  50.0 6.7 %collective-permute-start.14 = (f32[4,256,128]{2,1,0:T(8,128)S(1)}, f32[4,256,128]{2,1,0:T(8,128)S(1)}, u32[]{:S(2)}, u32[]{:S(2)}) collective-permute-start(f32[4,256,128]{2,1,0:T(8,128)S(1)} %collective-permute-done.13.refs_2_), channel_id=1, source_target_pairs={{0,1},{1,0},{2,3},{3,2},{4,5},{5,4},{6,7},{7,6},{8,9},{9,8},{10,11... | collective-permute-start | bytes 1572872 | tf_op jit(solution)/shard_map/ppermute | solution.py:245
  52.2 8.3 %collective-permute-start.15 = (f32[256,128]{1,0:T(8,128)S(1)}, f32[256,128]{1,0:T(8,128)S(1)}, u32[]{:S(2)}, u32[]{:S(2)}) collective-permute-start(f32[256,128]{1,0:T(8,128)S(1)} %get-tuple-element.58), channel_id=1, source_target_pairs={{0,4},{1,5},{2,6},{3,7},{4,0},{5,1},{6,2},{7,3},{8,12},{9,13},{10,... | collective-permute-start | bytes 393224 | tf_op jit(solution)/shard_map/ppermute | solution.py:245
  52.6 12.9 %collective-permute-start.16 = (f32[256,128]{1,0:T(8,128)S(1)}, f32[256,128]{1,0:T(8,128)S(1)}, u32[]{:S(2)}, u32[]{:S(2)}) collective-permute-start(f32[256,128]{1,0:T(8,128)S(1)} %get-tuple-element.62), channel_id=1, source_target_pairs={{0,8},{1,9},{2,10},{3,11},{4,12},{5,13},{6,14},{7,15},{8,0},{9,1},... | collective-permute-start | bytes 393224 | tf_op jit(solution)/shard_map/ppermute | solution.py:245
  53.8 11.6 %collective-permute-start.17 = (f32[256,128]{1,0:T(8,128)S(1)}, f32[256,128]{1,0:T(8,128)S(1)}, u32[]{:S(2)}, u32[]{:S(2)}) collective-permute-start(f32[256,128]{1,0:T(8,128)S(1)} %get-tuple-element.63), channel_id=1, source_target_pairs={{0,12},{1,13},{2,14},{3,15},{4,8},{5,9},{6,10},{7,11},{8,4},{9,5},... | collective-permute-start | bytes 393224 | tf_op jit(solution)/shard_map/ppermute | solution.py:245
  60.6 15.7 %collective-permute-start.24 = (f32[2,256,128]{2,1,0:T(8,128)S(1)}, f32[2,256,128]{2,1,0:T(8,128)S(1)}, u32[]{:S(2)}, u32[]{:S(2)}) collective-permute-start(f32[2,256,128]{2,1,0:T(8,128)S(1)} %get-tuple-element.64.refs_4_.refs_1_), channel_id=1, source_target_pairs={{0,2},{1,3},{2,0},{3,1},{4,6},{5,7},{6,4},{7,5},{8,10},{9,11},{10,... | collective-permute-start | bytes 786440 | tf_op jit(solution)/shard_map/ppermute | solution.py:245
  65.5 10.8 %collective-permute-start.23 = (f32[2,256,128]{2,1,0:T(8,128)S(1)}, f32[2,256,128]{2,1,0:T(8,128)S(1)}, u32[]{:S(2)}, u32[]{:S(2)}) collective-permute-start(f32[2,256,128]{2,1,0:T(8,128)S(1)} %get-tuple-element.70.refs_0_), channel_id=1, source_target_pairs={{0,2},{1,3},{2,0},{3,1},{4,6},{5,7},{6,4},{7,5},{8,10},{9,11},{10,... | collective-permute-start | bytes 786440 | tf_op jit(solution)/shard_map/ppermute | solution.py:245
  67.1 9.2 %collective-permute-start.18 = (f32[256,128]{1,0:T(8,128)S(1)}, f32[256,128]{1,0:T(8,128)S(1)}, u32[]{:S(2)}, u32[]{:S(2)}) collective-permute-start(f32[256,128]{1,0:T(8,128)S(1)} %get-tuple-element.65), channel_id=1, source_target_pairs={{0,8},{1,9},{2,10},{3,11},{4,12},{5,13},{6,14},{7,15},{8,0},{9,1},... | collective-permute-start | bytes 393224 | tf_op jit(solution)/shard_map/ppermute | solution.py:245
  70.7 8.1 %collective-permute-start.22 = (f32[2,256,128]{2,1,0:T(8,128)S(1)}, f32[2,256,128]{2,1,0:T(8,128)S(1)}, u32[]{:S(2)}, u32[]{:S(2)}) collective-permute-start(f32[2,256,128]{2,1,0:T(8,128)S(1)} %get-tuple-element.64.refs_4_.refs_1_), channel_id=1, source_target_pairs={{0,1},{1,0},{2,3},{3,2},{4,5},{5,4},{6,7},{7,6},{8,9},{9,8},{10,11... | collective-permute-start | bytes 786440 | tf_op jit(solution)/shard_map/ppermute | solution.py:245
  76.8 7.2 %collective-permute-start.20 = (f32[256,128]{1,0:T(8,128)S(1)}, f32[256,128]{1,0:T(8,128)S(1)}, u32[]{:S(2)}, u32[]{:S(2)}) collective-permute-start(f32[256,128]{1,0:T(8,128)S(1)} %get-tuple-element.67), channel_id=1, source_target_pairs={{0,4},{1,5},{2,6},{3,7},{4,0},{5,1},{6,2},{7,3},{8,12},{9,13},{10,... | collective-permute-start | bytes 393224 | tf_op jit(solution)/shard_map/ppermute | solution.py:245
  76.8 9.1 %collective-permute-start.19 = (f32[256,128]{1,0:T(8,128)S(1)}, f32[256,128]{1,0:T(8,128)S(1)}, u32[]{:S(2)}, u32[]{:S(2)}) collective-permute-start(f32[256,128]{1,0:T(8,128)S(1)} %get-tuple-element.66), channel_id=1, source_target_pairs={{0,12},{1,13},{2,14},{3,15},{4,8},{5,9},{6,10},{7,11},{8,4},{9,5},... | collective-permute-start | bytes 393224 | tf_op jit(solution)/shard_map/ppermute | solution.py:245
  80.5 15.1 %collective-permute-start.27 = (f32[256,128]{1,0:T(8,128)S(1)}, f32[256,128]{1,0:T(8,128)S(1)}, u32[]{:S(2)}, u32[]{:S(2)}) collective-permute-start(f32[256,128]{1,0:T(8,128)S(1)} %get-tuple-element.73), channel_id=1, source_target_pairs={{0,8},{1,9},{2,10},{3,11},{4,12},{5,13},{6,14},{7,15},{8,0},{9,1},... | collective-permute-start | bytes 393224 | tf_op jit(solution)/shard_map/ppermute | solution.py:245
  82.1 13.5 %collective-permute-start.28 = (f32[256,128]{1,0:T(8,128)S(1)}, f32[256,128]{1,0:T(8,128)S(1)}, u32[]{:S(2)}, u32[]{:S(2)}) collective-permute-start(f32[256,128]{1,0:T(8,128)S(1)} %get-tuple-element.74), channel_id=1, source_target_pairs={{0,12},{1,13},{2,14},{3,15},{4,8},{5,9},{6,10},{7,11},{8,4},{9,5},... | collective-permute-start | bytes 393224 | tf_op jit(solution)/shard_map/ppermute | solution.py:245
  84.0 11.6 %collective-permute-start.29 = (f32[256,128]{1,0:T(8,128)S(1)}, f32[256,128]{1,0:T(8,128)S(1)}, u32[]{:S(2)}, u32[]{:S(2)}) collective-permute-start(f32[256,128]{1,0:T(8,128)S(1)} %get-tuple-element.75), channel_id=1, source_target_pairs={{0,4},{1,5},{2,6},{3,7},{4,0},{5,1},{6,2},{7,3},{8,12},{9,13},{10,... | collective-permute-start | bytes 393224 | tf_op jit(solution)/shard_map/ppermute | solution.py:245
  (22 other events, 130.1 us)

commit v9 on v8

--- a/solution.py
+++ b/solution.py
@@ -326,11 +326,10 @@
     w3 = exchange(mix(gather_near_far(near, far, across(near, 1), across(far, 1), near_over), 0))
     (sums,) = call(functools.partial(norm_kernel, na, nc, n), [sds((8, nb), F32)], [me], [u3, *w3, s2, s3, s3_far])
     (cur_out,) = call(functools.partial(finish_kernel, na, nc), [natural], [me], [u3, *w3])
-    sums = (sums + swap(sums, 1)) + (swap(sums, 2) + swap(sums, 3))
-    bit = TEAM
+    bit = 1
     while bit < nd:
-        sums = sums + swap(sums, bit)
-        bit *= 2
+        sums = (sums + swap(sums, bit)) + (swap(sums, 2 * bit) + swap(sums, 3 * bit))
+        bit *= 4
     norms = jnp.sum(sums[:ITERS], axis=1) / (total_ch * nr * nb)
     return prev_out, cur_out, norms
 

time: 109 us -> 108 us (level)
    ppermute x35 -> x36, starting transfers between devices: 37.5 us -> 37 us  [swap(): return lax.ppermute(x, 'chan', [(i, i ^ bits) for i in range(nd)])]
    ppermute x35 -> x36, waiting for transfers between devices: 39.8 us -> 39.3 us  [swap(): return lax.ppermute(x, 'chan', [(i, i ^ bits) for i in range(nd)])]
  transfers between devices with their start and end apart: 36 -> 37, of which waited for: 20 -> 20; matrix products, arithmetic and copies ran while one was open for 0% -> 0% of each run, Pallas kernels for 14% -> 15%
where the time goes in v9:
time: 108 us
  waiting for transfers between devices  46.1 us (43%)
  starting transfers between devices  41.2 us (38%)
  Pallas kernels  16.5 us (15%)
  local copies, waits for them, and re-layouts  2.7 us (2%)
    ppermute x36, waiting for transfers between devices, swap(): return lax.ppermute(x, 'chan', [(i, i ^ bits) for i in range(nd)])  39.3 us
    ppermute x36, starting transfers between devices, swap(): return lax.ppermute(x, 'chan', [(i, i ^ bits) for i in range(nd)])  37 us
    pallas_call x15, Pallas kernels, call(): pl.pallas_call(kernel, out_shape=outs, in_specs=[SM] * len(scalars) + (sp...  16.5 us
    all_to_all x1, waiting for transfers between devices, exchange_all(): lax.all_to_all(x, 'chan', 0, 0, tiled=True, axis_index_groups=lines)  6.82 us
    all_to_all x1, starting transfers between devices, exchange_all(): lax.all_to_all(x, 'chan', 0, 0, tiled=True, axis_index_groups=lines)  4.24 us
    unnamed x20, local copies, waits for them, and re-layouts  2.7 us
  transfers between devices with their start and end apart: 37, of which 20 were waited for; matrix products, arithmetic and copies ran while one was open for 0% of the time, Pallas kernels for 15%

profile of v9, /device:TPU:0, one launch (start us, length us, event | category | flops | bytes accessed | tf_op | source)
XLA Modules:
  0.0 108.0 jit_solution(6812783429673995606)
XLA Ops:
  2.0 3.1 %collective-permute-start.2 = (f32[256,128]{1,0:T(8,128)S(1)}, f32[256,128]{1,0:T(8,128)S(1)}, u32[]{:S(2)}, u32[]{:S(2)}) collective-permute-start(f32[256,128]{1,0:T(8,128)S(1)} %get-tuple-element.45), channel_id=1, source_target_pairs={{0,4},{1,5},{2,6},{3,7},{4,0},{5,1},{6,2},{7,3},{8,12},{9,13},{10,... | collective-permute-start | bytes 393224 | tf_op jit(solution)/shard_map/ppermute | solution.py:245
  5.1 2.6 %collective-permute-start = (f32[256,128]{1,0:T(8,128)S(1)}, f32[256,128]{1,0:T(8,128)S(1)}, u32[]{:S(2)}, u32[]{:S(2)}) collective-permute-start(f32[256,128]{1,0:T(8,128)S(1)} %get-tuple-element.41), channel_id=1, source_target_pairs={{0,8},{1,9},{2,10},{3,11},{4,12},{5,13},{6,14},{7,15},{8,0},{9,1},... | collective-permute-start | bytes 393224 | tf_op jit(solution)/shard_map/ppermute | solution.py:245
  7.7 2.4 %collective-permute-done.2.refs_1_ = f32[256,128]{1,0:T(8,128)S(1)} collective-permute-done((f32[256,128]{1,0:T(8,128)S(1)}, f32[256,128]{1,0:T(8,128)S(1)}, u32[]{:S(2)}, u32[]{:S(2)}) %collective-permute-start.2) | collective-permute-done | bytes 131104 | tf_op jit(solution)/shard_map/ppermute | solution.py:245
  10.2 1.8 %collective-permute-start.6 = (f32[2,256,128]{2,1,0:T(8,128)S(1)}, f32[2,256,128]{2,1,0:T(8,128)S(1)}, u32[]{:S(2)}, u32[]{:S(2)}) collective-permute-start(f32[2,256,128]{2,1,0:T(8,128)S(1)} %shard_map.107.refs_1_), channel_id=1, source_target_pairs={{0,2},{1,3},{2,0},{3,1},{4,6},{5,7},{6,4},{7,5},{8,10},{9,11},{10,... | collective-permute-start | bytes 786440 | tf_op jit(solution)/shard_map/ppermute | solution.py:245
  12.7 2.0 %shard_map.103.refs_2_.coup = bf16[3,2,4,32,512]{4,3,2,1,0:T(8,128)(2,1)S(1)} custom-call(s32[1]{0:T(128)} %bitcast.me_ref, s32[8,8]{1,0:T(8,128)S(1)} %copy-done.7, f32[3,512,512]{2,1,0:T(8,128)} %ang_ref.1), custom_call_target="tpu_custom_call" | custom-call | bytes 65536 | tf_op jit(solution)/shard_map/pallas_call | solution.py:222
  14.7 2.3 %shard_map.105 = (f32[4,256,128]{2,1,0:T(8,128)}, f32[32,32,128]{2,1,0:T(8,128)S(1)}) custom-call(s32[1]{0:T(128)} %bitcast.me_ref, s32[2,32]{1,0:T(2,128)S(1)} %bitcast.2, f32[32,32]{1,0:T(8,128)S(1)} %copy-done.5, f32[128,128]{1,0:T(8,128)S(1)} %copy-done.2, f32[32,32,128]{2,1,0:T(8,128)S(1)} %copy-done.3, f32[32,32,128]{2,1,0:T(8,128)S(1)} %copy-done.1), custom_call_target="tpu_custom_call" | custom-call | bytes 65536 | tf_op jit(solution)/shard_map/pallas_call | solution.py:222
  19.7 4.2 %all-to-all-start = ((f32[4,256,128]{2,1,0:T(8,128)}), f32[4,256,128]{2,1,0:T(8,128)S(1)}, u32[]{:S(2)}, u32[]{:S(2)}) async-start(f32[4,256,128]{2,1,0:T(8,128)} %get-tuple-element.52), calls=%async_computation | async-start | bytes 1048576 | tf_op jit(solution)/shard_map/all_to_all | solution.py:255
  27.7 2.6 %shard_map.108 = (f32[256,128]{1,0:T(8,128)S(1)}, f32[256,128]{1,0:T(8,128)S(1)}, f32[256,128]{1,0:T(8,128)S(1)}, f32[256,128]{1,0:T(8,128)S(1)}) custom-call(s32[1]{0:T(128)} %bitcast.me_ref, bf16[3,2,4,32,512]{4,3,2,1,0:T(8,128)(2,1)S(1)} %shard_map.103.refs_2_.coup, f32[3,32,128]{2,1,0:T(8,128)S(1)} %copy-done.4, f32[2,256,128]{2,1,0:T(8,128)S(1)} %shard_map.106.refs_0_, ...), custom_call_target="tpu_custom_call" | custom-call | flops 5000000000 | bytes 65536 | tf_op jit(solution)/shard_map/pallas_call | solution.py:222
  30.3 6.8 %all-to-all-done.u_ref = f32[4,256,128]{2,1,0:T(8,128)S(1)} async-done(((f32[4,256,128]{2,1,0:T(8,128)}), f32[4,256,128]{2,1,0:T(8,128)S(1)}, u32[]{:S(2)}, u32[]{:S(2)}) %all-to-all-start) | async-done | bytes 524320 | tf_op jit(solution)/shard_map/all_to_all | solution.py:255
  39.3 2.0 %collective-permute-start.11 = (f32[256,128]{1,0:T(8,128)S(1)}, f32[256,128]{1,0:T(8,128)S(1)}, u32[]{:S(2)}, u32[]{:S(2)}) collective-permute-start(f32[256,128]{1,0:T(8,128)S(1)} %get-tuple-element.49.refs_3_), channel_id=1, source_target_pairs={{0,4},{1,5},{2,6},{3,7},{4,0},{5,1},{6,2},{7,3},{8,12},{9,13},{10,... | collective-permute-start | bytes 393224 | tf_op jit(solution)/shard_map/ppermute | solution.py:245
  41.3 6.6 %collective-permute-done.9.refs_1_ = f32[256,128]{1,0:T(8,128)S(1)} collective-permute-done((f32[256,128]{1,0:T(8,128)S(1)}, f32[256,128]{1,0:T(8,128)S(1)}, u32[]{:S(2)}, u32[]{:S(2)}) %collective-permute-start.9) | collective-permute-done | bytes 131104 | tf_op jit(solution)/shard_map/ppermute | solution.py:245
  50.0 2.3 %shard_map.109 = (f32[256,128]{1,0:T(8,128)S(1)}, f32[256,128]{1,0:T(8,128)S(1)}, f32[256,128]{1,0:T(8,128)S(1)}, f32[256,128]{1,0:T(8,128)S(1)}, f32[32,32,128]{2,1,0:T(8,128)}, /*index=5*/f32[32,32,128]{2,1,0:T(8,128)S(1)}) custom-call(s32[1]{0:T(128)} %bitcast.me_ref, s32[2,32]{1,0:T(2,128)S(1)} %bitcast.3, f32[32,32]{1,0:T(8,128)S(1)} %copy-done.5, ...), custom_call_target="tpu_custom_call" | custom-call | bytes 65536 | tf_op jit(solution)/shard_map/pallas_call | solution.py:222
  53.8 2.8 %collective-permute-start.17 = (f32[256,128]{1,0:T(8,128)S(1)}, f32[256,128]{1,0:T(8,128)S(1)}, u32[]{:S(2)}, u32[]{:S(2)}) collective-permute-start(f32[256,128]{1,0:T(8,128)S(1)} %get-tuple-element.63), channel_id=1, source_target_pairs={{0,12},{1,13},{2,14},{3,15},{4,8},{5,9},{6,10},{7,11},{8,4},{9,5},... | collective-permute-start | bytes 393224 | tf_op jit(solution)/shard_map/ppermute | solution.py:245
  58.3 2.2 %collective-permute-done.15.refs_3_ = f32[256,128]{1,0:T(8,128)S(1)} collective-permute-done((f32[256,128]{1,0:T(8,128)S(1)}, f32[256,128]{1,0:T(8,128)S(1)}, u32[]{:S(2)}, u32[]{:S(2)}) %collective-permute-start.15) | collective-permute-done | bytes 131104 | tf_op jit(solution)/shard_map/ppermute | solution.py:245
  61.1 4.3 %collective-permute-done.16.refs_2_ = f32[256,128]{1,0:T(8,128)S(1)} collective-permute-done((f32[256,128]{1,0:T(8,128)S(1)}, f32[256,128]{1,0:T(8,128)S(1)}, u32[]{:S(2)}, u32[]{:S(2)}) %collective-permute-start.16) | collective-permute-done | bytes 131104 | tf_op jit(solution)/shard_map/ppermute | solution.py:245
  67.1 3.6 %collective-permute-start.18 = (f32[256,128]{1,0:T(8,128)S(1)}, f32[256,128]{1,0:T(8,128)S(1)}, u32[]{:S(2)}, u32[]{:S(2)}) collective-permute-start(f32[256,128]{1,0:T(8,128)S(1)} %get-tuple-element.65), channel_id=1, source_target_pairs={{0,8},{1,9},{2,10},{3,11},{4,12},{5,13},{6,14},{7,15},{8,0},{9,1},... | collective-permute-start | bytes 393224 | tf_op jit(solution)/shard_map/ppermute | solution.py:245
  71.2 5.1 %collective-permute-done.18.refs_1_ = f32[256,128]{1,0:T(8,128)S(1)} collective-permute-done((f32[256,128]{1,0:T(8,128)S(1)}, f32[256,128]{1,0:T(8,128)S(1)}, u32[]{:S(2)}, u32[]{:S(2)}) %collective-permute-start.18) | collective-permute-done | bytes 131104 | tf_op jit(solution)/shard_map/ppermute | solution.py:245
  76.8 1.9 %collective-permute-start.19 = (f32[256,128]{1,0:T(8,128)S(1)}, f32[256,128]{1,0:T(8,128)S(1)}, u32[]{:S(2)}, u32[]{:S(2)}) collective-permute-start(f32[256,128]{1,0:T(8,128)S(1)} %get-tuple-element.66), channel_id=1, source_target_pairs={{0,12},{1,13},{2,14},{3,15},{4,8},{5,9},{6,10},{7,11},{8,4},{9,5},... | collective-permute-start | bytes 393224 | tf_op jit(solution)/shard_map/ppermute | solution.py:245
  82.1 1.9 %collective-permute-start.28 = (f32[256,128]{1,0:T(8,128)S(1)}, f32[256,128]{1,0:T(8,128)S(1)}, u32[]{:S(2)}, u32[]{:S(2)}) collective-permute-start(f32[256,128]{1,0:T(8,128)S(1)} %get-tuple-element.74), channel_id=1, source_target_pairs={{0,12},{1,13},{2,14},{3,15},{4,8},{5,9},{6,10},{7,11},{8,4},{9,5},... | collective-permute-start | bytes 393224 | tf_op jit(solution)/shard_map/ppermute | solution.py:245
  84.0 1.9 %collective-permute-done.19.refs_2_ = f32[256,128]{1,0:T(8,128)S(1)} collective-permute-done((f32[256,128]{1,0:T(8,128)S(1)}, f32[256,128]{1,0:T(8,128)S(1)}, u32[]{:S(2)}, u32[]{:S(2)}) %collective-permute-start.19) | collective-permute-done | bytes 131104 | tf_op jit(solution)/shard_map/ppermute | solution.py:245
  86.0 1.9 %shard_map.114 = (f32[32,32,128]{2,1,0:T(8,128)S(1)}, f32[32,32,128]{2,1,0:T(8,128)}) custom-call(s32[1]{0:T(128)} %bitcast.me_ref, s32[2,32]{1,0:T(2,128)S(1)} %bitcast.4, f32[32,32]{1,0:T(8,128)S(1)} %copy-done.5, f32[128,128]{1,0:T(8,128)S(1)} %copy-done.2, f32[32,32,128]{2,1,0:T(8,128)S(1)} %get-tuple-element.50.prev, ...), custom_call_target="tpu_custom_call" | custom-call | bytes 65536 | tf_op jit(solution)/shard_map/pallas_call | solution.py:222
  87.9 7.7 %collective-permute-done.27.refs_1_ = f32[256,128]{1,0:T(8,128)S(1)} collective-permute-done((f32[256,128]{1,0:T(8,128)S(1)}, f32[256,128]{1,0:T(8,128)S(1)}, u32[]{:S(2)}, u32[]{:S(2)}) %collective-permute-start.27) | collective-permute-done | bytes 131104 | tf_op jit(solution)/shard_map/ppermute | solution.py:245
  99.7 1.9 %collective-permute-start.35 = (f32[8,128]{1,0:T(8,128)S(1)}, f32[8,128]{1,0:T(8,128)S(1)}, u32[]{:S(2)}, u32[]{:S(2)}) collective-permute-start(f32[8,128]{1,0:T(8,128)S(1)} %add_add_fusion.1), channel_id=1, source_target_pairs={{0,12},{1,13},{2,14},{3,15},{4,8},{5,9},{6,10},{7,11},{8,4},{9,5},... | collective-permute-start | bytes 12296 | tf_op jit(solution)/shard_map/ppermute | solution.py:245
  101.6 2.1 %collective-permute-start.34 = (f32[8,128]{1,0:T(8,128)S(1)}, f32[8,128]{1,0:T(8,128)S(1)}, u32[]{:S(2)}, u32[]{:S(2)}) collective-permute-start(f32[8,128]{1,0:T(8,128)S(1)} %add_add_fusion.1), channel_id=1, source_target_pairs={{0,8},{1,9},{2,10},{3,11},{4,12},{5,13},{6,14},{7,15},{8,0},{9,1},... | collective-permute-start | bytes 12296 | tf_op jit(solution)/shard_map/ppermute | solution.py:245
  (89 shorter events, 31.0 us)
Async XLA Ops:
  2.0 8.1 %collective-permute-start.2 = (f32[256,128]{1,0:T(8,128)S(1)}, f32[256,128]{1,0:T(8,128)S(1)}, u32[]{:S(2)}, u32[]{:S(2)}) collective-permute-start(f32[256,128]{1,0:T(8,128)S(1)} %get-tuple-element.45), channel_id=1, source_target_pairs={{0,4},{1,5},{2,6},{3,7},{4,0},{5,1},{6,2},{7,3},{8,12},{9,13},{10,... | collective-permute-start | bytes 393224 | tf_op jit(solution)/shard_map/ppermute | solution.py:245
  5.1 12.9 %collective-permute-start = (f32[256,128]{1,0:T(8,128)S(1)}, f32[256,128]{1,0:T(8,128)S(1)}, u32[]{:S(2)}, u32[]{:S(2)}) collective-permute-start(f32[256,128]{1,0:T(8,128)S(1)} %get-tuple-element.41), channel_id=1, source_target_pairs={{0,8},{1,9},{2,10},{3,11},{4,12},{5,13},{6,14},{7,15},{8,0},{9,1},... | collective-permute-start | bytes 393224 | tf_op jit(solution)/shard_map/ppermute | solution.py:245
  7.7 10.3 %collective-permute-start.1 = (f32[256,128]{1,0:T(8,128)S(1)}, f32[256,128]{1,0:T(8,128)S(1)}, u32[]{:S(2)}, u32[]{:S(2)}) collective-permute-start(f32[256,128]{1,0:T(8,128)S(1)} %get-tuple-element.42), channel_id=1, source_target_pairs={{0,12},{1,13},{2,14},{3,15},{4,8},{5,9},{6,10},{7,11},{8,4},{9,5},... | collective-permute-start | bytes 393224 | tf_op jit(solution)/shard_map/ppermute | solution.py:245
  10.2 9.5 %collective-permute-start.6 = (f32[2,256,128]{2,1,0:T(8,128)S(1)}, f32[2,256,128]{2,1,0:T(8,128)S(1)}, u32[]{:S(2)}, u32[]{:S(2)}) collective-permute-start(f32[2,256,128]{2,1,0:T(8,128)S(1)} %shard_map.107.refs_1_), channel_id=1, source_target_pairs={{0,2},{1,3},{2,0},{3,1},{4,6},{5,7},{6,4},{7,5},{8,10},{9,11},{10,... | collective-permute-start | bytes 786440 | tf_op jit(solution)/shard_map/ppermute | solution.py:245
  18.1 6.5 %collective-permute-start.5 = (f32[2,256,128]{2,1,0:T(8,128)S(1)}, f32[2,256,128]{2,1,0:T(8,128)}, u32[]{:S(2)}, u32[]{:S(2)}) collective-permute-start(f32[2,256,128]{2,1,0:T(8,128)S(1)} %shard_map.106.refs_0_), channel_id=1, source_target_pairs={{0,2},{1,3},{2,0},{3,1},{4,6},{5,7},{6,4},{7,5},{8,10},{9,11},{10,... | collective-permute-start | bytes 786440 | tf_op jit(solution)/shard_map/ppermute | solution.py:245
  19.7 17.5 %all-to-all-start = ((f32[4,256,128]{2,1,0:T(8,128)}), f32[4,256,128]{2,1,0:T(8,128)S(1)}, u32[]{:S(2)}, u32[]{:S(2)}) async-start(f32[4,256,128]{2,1,0:T(8,128)} %get-tuple-element.52), calls=%async_computation | async-start | bytes 1048576 | tf_op jit(solution)/shard_map/all_to_all | solution.py:255
  37.3 12.7 %collective-permute-start.13 = (f32[4,256,128]{2,1,0:T(8,128)S(1)}, f32[4,256,128]{2,1,0:T(8,128)S(1)}, u32[]{:S(2)}, u32[]{:S(2)}) collective-permute-start(f32[4,256,128]{2,1,0:T(8,128)S(1)} %get-tuple-element.53.refs_0_), channel_id=1, source_target_pairs={{0,2},{1,3},{2,0},{3,1},{4,6},{5,7},{6,4},{7,5},{8,10},{9,11},{10,... | collective-permute-start | bytes 1572872 | tf_op jit(solution)/shard_map/ppermute | solution.py:245
  37.8 10.1 %collective-permute-start.9 = (f32[256,128]{1,0:T(8,128)S(1)}, f32[256,128]{1,0:T(8,128)S(1)}, u32[]{:S(2)}, u32[]{:S(2)}) collective-permute-start(f32[256,128]{1,0:T(8,128)S(1)} %get-tuple-element.47.refs_1_), channel_id=1, source_target_pairs={{0,8},{1,9},{2,10},{3,11},{4,12},{5,13},{6,14},{7,15},{8,0},{9,1},... | collective-permute-start | bytes 393224 | tf_op jit(solution)/shard_map/ppermute | solution.py:245
  37.8 10.1 %collective-permute-start.10 = (f32[256,128]{1,0:T(8,128)S(1)}, f32[256,128]{1,0:T(8,128)S(1)}, u32[]{:S(2)}, u32[]{:S(2)}) collective-permute-start(f32[256,128]{1,0:T(8,128)S(1)} %get-tuple-element.48.refs_2_), channel_id=1, source_target_pairs={{0,12},{1,13},{2,14},{3,15},{4,8},{5,9},{6,10},{7,11},{8,4},{9,5},... | collective-permute-start | bytes 393224 | tf_op jit(solution)/shard_map/ppermute | solution.py:245
  39.3 9.0 %collective-permute-start.11 = (f32[256,128]{1,0:T(8,128)S(1)}, f32[256,128]{1,0:T(8,128)S(1)}, u32[]{:S(2)}, u32[]{:S(2)}) collective-permute-start(f32[256,128]{1,0:T(8,128)S(1)} %get-tuple-element.49.refs_3_), channel_id=1, source_target_pairs={{0,4},{1,5},{2,6},{3,7},{4,0},{5,1},{6,2},{7,3},{8,12},{9,13},{10,... | collective-permute-start | bytes 393224 | tf_op jit(solution)/shard_map/ppermute | solution.py:245
  41.3 15.3 %collective-permute-start.12 = (f32[4,256,128]{2,1,0:T(8,128)S(1)}, f32[4,256,128]{2,1,0:T(8,128)S(1)}, u32[]{:S(2)}, u32[]{:S(2)}) collective-permute-start(f32[4,256,128]{2,1,0:T(8,128)S(1)} %get-tuple-element.53.refs_0_), channel_id=1, source_target_pairs={{0,1},{1,0},{2,3},{3,2},{4,5},{5,4},{6,7},{7,6},{8,9},{9,8},{10,11... | collective-permute-start | bytes 1572872 | tf_op jit(solution)/shard_map/ppermute | solution.py:245
  50.0 6.7 %collective-permute-start.14 = (f32[4,256,128]{2,1,0:T(8,128)S(1)}, f32[4,256,128]{2,1,0:T(8,128)S(1)}, u32[]{:S(2)}, u32[]{:S(2)}) collective-permute-start(f32[4,256,128]{2,1,0:T(8,128)S(1)} %collective-permute-done.13.refs_2_), channel_id=1, source_target_pairs={{0,1},{1,0},{2,3},{3,2},{4,5},{5,4},{6,7},{7,6},{8,9},{9,8},{10,11... | collective-permute-start | bytes 1572872 | tf_op jit(solution)/shard_map/ppermute | solution.py:245
  52.2 8.3 %collective-permute-start.15 = (f32[256,128]{1,0:T(8,128)S(1)}, f32[256,128]{1,0:T(8,128)S(1)}, u32[]{:S(2)}, u32[]{:S(2)}) collective-permute-start(f32[256,128]{1,0:T(8,128)S(1)} %get-tuple-element.58), channel_id=1, source_target_pairs={{0,4},{1,5},{2,6},{3,7},{4,0},{5,1},{6,2},{7,3},{8,12},{9,13},{10,... | collective-permute-start | bytes 393224 | tf_op jit(solution)/shard_map/ppermute | solution.py:245
  52.6 12.9 %collective-permute-start.16 = (f32[256,128]{1,0:T(8,128)S(1)}, f32[256,128]{1,0:T(8,128)S(1)}, u32[]{:S(2)}, u32[]{:S(2)}) collective-permute-start(f32[256,128]{1,0:T(8,128)S(1)} %get-tuple-element.62), channel_id=1, source_target_pairs={{0,8},{1,9},{2,10},{3,11},{4,12},{5,13},{6,14},{7,15},{8,0},{9,1},... | collective-permute-start | bytes 393224 | tf_op jit(solution)/shard_map/ppermute | solution.py:245
  53.8 11.6 %collective-permute-start.17 = (f32[256,128]{1,0:T(8,128)S(1)}, f32[256,128]{1,0:T(8,128)S(1)}, u32[]{:S(2)}, u32[]{:S(2)}) collective-permute-start(f32[256,128]{1,0:T(8,128)S(1)} %get-tuple-element.63), channel_id=1, source_target_pairs={{0,12},{1,13},{2,14},{3,15},{4,8},{5,9},{6,10},{7,11},{8,4},{9,5},... | collective-permute-start | bytes 393224 | tf_op jit(solution)/shard_map/ppermute | solution.py:245
  60.6 15.7 %collective-permute-start.24 = (f32[2,256,128]{2,1,0:T(8,128)S(1)}, f32[2,256,128]{2,1,0:T(8,128)S(1)}, u32[]{:S(2)}, u32[]{:S(2)}) collective-permute-start(f32[2,256,128]{2,1,0:T(8,128)S(1)} %get-tuple-element.64.refs_4_.refs_1_), channel_id=1, source_target_pairs={{0,2},{1,3},{2,0},{3,1},{4,6},{5,7},{6,4},{7,5},{8,10},{9,11},{10,... | collective-permute-start | bytes 786440 | tf_op jit(solution)/shard_map/ppermute | solution.py:245
  65.5 10.8 %collective-permute-start.23 = (f32[2,256,128]{2,1,0:T(8,128)S(1)}, f32[2,256,128]{2,1,0:T(8,128)S(1)}, u32[]{:S(2)}, u32[]{:S(2)}) collective-permute-start(f32[2,256,128]{2,1,0:T(8,128)S(1)} %get-tuple-element.70.refs_0_), channel_id=1, source_target_pairs={{0,2},{1,3},{2,0},{3,1},{4,6},{5,7},{6,4},{7,5},{8,10},{9,11},{10,... | collective-permute-start | bytes 786440 | tf_op jit(solution)/shard_map/ppermute | solution.py:245
  67.1 9.2 %collective-permute-start.18 = (f32[256,128]{1,0:T(8,128)S(1)}, f32[256,128]{1,0:T(8,128)S(1)}, u32[]{:S(2)}, u32[]{:S(2)}) collective-permute-start(f32[256,128]{1,0:T(8,128)S(1)} %get-tuple-element.65), channel_id=1, source_target_pairs={{0,8},{1,9},{2,10},{3,11},{4,12},{5,13},{6,14},{7,15},{8,0},{9,1},... | collective-permute-start | bytes 393224 | tf_op jit(solution)/shard_map/ppermute | solution.py:245
  70.7 8.1 %collective-permute-start.22 = (f32[2,256,128]{2,1,0:T(8,128)S(1)}, f32[2,256,128]{2,1,0:T(8,128)S(1)}, u32[]{:S(2)}, u32[]{:S(2)}) collective-permute-start(f32[2,256,128]{2,1,0:T(8,128)S(1)} %get-tuple-element.64.refs_4_.refs_1_), channel_id=1, source_target_pairs={{0,1},{1,0},{2,3},{3,2},{4,5},{5,4},{6,7},{7,6},{8,9},{9,8},{10,11... | collective-permute-start | bytes 786440 | tf_op jit(solution)/shard_map/ppermute | solution.py:245
  76.8 7.2 %collective-permute-start.20 = (f32[256,128]{1,0:T(8,128)S(1)}, f32[256,128]{1,0:T(8,128)S(1)}, u32[]{:S(2)}, u32[]{:S(2)}) collective-permute-start(f32[256,128]{1,0:T(8,128)S(1)} %get-tuple-element.67), channel_id=1, source_target_pairs={{0,4},{1,5},{2,6},{3,7},{4,0},{5,1},{6,2},{7,3},{8,12},{9,13},{10,... | collective-permute-start | bytes 393224 | tf_op jit(solution)/shard_map/ppermute | solution.py:245
  76.8 9.1 %collective-permute-start.19 = (f32[256,128]{1,0:T(8,128)S(1)}, f32[256,128]{1,0:T(8,128)S(1)}, u32[]{:S(2)}, u32[]{:S(2)}) collective-permute-start(f32[256,128]{1,0:T(8,128)S(1)} %get-tuple-element.66), channel_id=1, source_target_pairs={{0,12},{1,13},{2,14},{3,15},{4,8},{5,9},{6,10},{7,11},{8,4},{9,5},... | collective-permute-start | bytes 393224 | tf_op jit(solution)/shard_map/ppermute | solution.py:245
  80.5 15.1 %collective-permute-start.27 = (f32[256,128]{1,0:T(8,128)S(1)}, f32[256,128]{1,0:T(8,128)S(1)}, u32[]{:S(2)}, u32[]{:S(2)}) collective-permute-start(f32[256,128]{1,0:T(8,128)S(1)} %get-tuple-element.73), channel_id=1, source_target_pairs={{0,8},{1,9},{2,10},{3,11},{4,12},{5,13},{6,14},{7,15},{8,0},{9,1},... | collective-permute-start | bytes 393224 | tf_op jit(solution)/shard_map/ppermute | solution.py:245
  82.1 13.5 %collective-permute-start.28 = (f32[256,128]{1,0:T(8,128)S(1)}, f32[256,128]{1,0:T(8,128)S(1)}, u32[]{:S(2)}, u32[]{:S(2)}) collective-permute-start(f32[256,128]{1,0:T(8,128)S(1)} %get-tuple-element.74), channel_id=1, source_target_pairs={{0,12},{1,13},{2,14},{3,15},{4,8},{5,9},{6,10},{7,11},{8,4},{9,5},... | collective-permute-start | bytes 393224 | tf_op jit(solution)/shard_map/ppermute | solution.py:245
  84.0 11.6 %collective-permute-start.29 = (f32[256,128]{1,0:T(8,128)S(1)}, f32[256,128]{1,0:T(8,128)S(1)}, u32[]{:S(2)}, u32[]{:S(2)}) collective-permute-start(f32[256,128]{1,0:T(8,128)S(1)} %get-tuple-element.75), channel_id=1, source_target_pairs={{0,4},{1,5},{2,6},{3,7},{4,0},{5,1},{6,2},{7,3},{8,12},{9,13},{10,... | collective-permute-start | bytes 393224 | tf_op jit(solution)/shard_map/ppermute | solution.py:245
  (23 other events, 135.2 us)

commit v10 on v9

--- a/solution.py
+++ b/solution.py
@@ -71,7 +71,7 @@
     rotation = 1.0 / (stretch * stretch)
     orbital = 1.0 / (radius * radius)
     scale = np.float32(0.3 / (JL_MAX * (JL_MAX - 1)))
-    group = min(8, nc)
+    group = min(16, nc)
     for start in range(0, nc, group):
         chans = range(start, start + group)
         for piece, at in placed(pieces):

time: 108 us -> 108 us (level)
  no operation moved by 1% of the time
where the time goes in v10:
time: 108 us
  waiting for transfers between devices  45.9 us (42%)
  starting transfers between devices  41.2 us (38%)
  Pallas kernels  16.7 us (15%)
  local copies, waits for them, and re-layouts  2.7 us (2%)
    ppermute x36, waiting for transfers between devices, swap(): return lax.ppermute(x, 'chan', [(i, i ^ bits) for i in range(nd)])  39.1 us
    ppermute x36, starting transfers between devices, swap(): return lax.ppermute(x, 'chan', [(i, i ^ bits) for i in range(nd)])  37 us
    pallas_call x15, Pallas kernels, call(): pl.pallas_call(kernel, out_shape=outs, in_specs=[SM] * len(scalars) + (sp...  16.7 us
    all_to_all x1, waiting for transfers between devices, exchange_all(): lax.all_to_all(x, 'chan', 0, 0, tiled=True, axis_index_groups=lines)  6.82 us
    all_to_all x1, starting transfers between devices, exchange_all(): lax.all_to_all(x, 'chan', 0, 0, tiled=True, axis_index_groups=lines)  4.24 us
    unnamed x20, local copies, waits for them, and re-layouts  2.7 us
  transfers between devices with their start and end apart: 37, of which 20 were waited for; matrix products, arithmetic and copies ran while one was open for 0% of the time, Pallas kernels for 15%

profile of v10, /device:TPU:0, one launch (start us, length us, event | category | flops | bytes accessed | tf_op | source)
XLA Modules:
  0.0 108.0 jit_solution(1332989694339091248)
XLA Ops:
  2.0 3.1 %collective-permute-start.2 = (f32[256,128]{1,0:T(8,128)S(1)}, f32[256,128]{1,0:T(8,128)S(1)}, u32[]{:S(2)}, u32[]{:S(2)}) collective-permute-start(f32[256,128]{1,0:T(8,128)S(1)} %get-tuple-element.45), channel_id=1, source_target_pairs={{0,4},{1,5},{2,6},{3,7},{4,0},{5,1},{6,2},{7,3},{8,12},{9,13},{10,... | collective-permute-start | bytes 393224 | tf_op jit(solution)/shard_map/ppermute | solution.py:245
  5.1 2.6 %collective-permute-start = (f32[256,128]{1,0:T(8,128)S(1)}, f32[256,128]{1,0:T(8,128)S(1)}, u32[]{:S(2)}, u32[]{:S(2)}) collective-permute-start(f32[256,128]{1,0:T(8,128)S(1)} %get-tuple-element.41), channel_id=1, source_target_pairs={{0,8},{1,9},{2,10},{3,11},{4,12},{5,13},{6,14},{7,15},{8,0},{9,1},... | collective-permute-start | bytes 393224 | tf_op jit(solution)/shard_map/ppermute | solution.py:245
  7.7 2.4 %collective-permute-done.2.refs_1_ = f32[256,128]{1,0:T(8,128)S(1)} collective-permute-done((f32[256,128]{1,0:T(8,128)S(1)}, f32[256,128]{1,0:T(8,128)S(1)}, u32[]{:S(2)}, u32[]{:S(2)}) %collective-permute-start.2) | collective-permute-done | bytes 131104 | tf_op jit(solution)/shard_map/ppermute | solution.py:245
  10.2 1.8 %collective-permute-start.6 = (f32[2,256,128]{2,1,0:T(8,128)S(1)}, f32[2,256,128]{2,1,0:T(8,128)S(1)}, u32[]{:S(2)}, u32[]{:S(2)}) collective-permute-start(f32[2,256,128]{2,1,0:T(8,128)S(1)} %shard_map.107.refs_1_), channel_id=1, source_target_pairs={{0,2},{1,3},{2,0},{3,1},{4,6},{5,7},{6,4},{7,5},{8,10},{9,11},{10,... | collective-permute-start | bytes 786440 | tf_op jit(solution)/shard_map/ppermute | solution.py:245
  12.7 2.0 %shard_map.103.refs_2_.coup = bf16[3,2,4,32,512]{4,3,2,1,0:T(8,128)(2,1)S(1)} custom-call(s32[1]{0:T(128)} %bitcast.me_ref, s32[8,8]{1,0:T(8,128)S(1)} %copy-done.7, f32[3,512,512]{2,1,0:T(8,128)} %ang_ref.1), custom_call_target="tpu_custom_call" | custom-call | bytes 65536 | tf_op jit(solution)/shard_map/pallas_call | solution.py:222
  14.7 2.3 %shard_map.105 = (f32[4,256,128]{2,1,0:T(8,128)}, f32[32,32,128]{2,1,0:T(8,128)S(1)}) custom-call(s32[1]{0:T(128)} %bitcast.me_ref, s32[2,32]{1,0:T(2,128)S(1)} %bitcast.2, f32[32,32]{1,0:T(8,128)S(1)} %copy-done.5, f32[128,128]{1,0:T(8,128)S(1)} %copy-done.2, f32[32,32,128]{2,1,0:T(8,128)S(1)} %copy-done.3, f32[32,32,128]{2,1,0:T(8,128)S(1)} %copy-done.1), custom_call_target="tpu_custom_call" | custom-call | bytes 65536 | tf_op jit(solution)/shard_map/pallas_call | solution.py:222
  19.7 4.2 %all-to-all-start = ((f32[4,256,128]{2,1,0:T(8,128)}), f32[4,256,128]{2,1,0:T(8,128)S(1)}, u32[]{:S(2)}, u32[]{:S(2)}) async-start(f32[4,256,128]{2,1,0:T(8,128)} %get-tuple-element.52), calls=%async_computation | async-start | bytes 1048576 | tf_op jit(solution)/shard_map/all_to_all | solution.py:255
  27.7 2.6 %shard_map.108 = (f32[256,128]{1,0:T(8,128)S(1)}, f32[256,128]{1,0:T(8,128)S(1)}, f32[256,128]{1,0:T(8,128)S(1)}, f32[256,128]{1,0:T(8,128)S(1)}) custom-call(s32[1]{0:T(128)} %bitcast.me_ref, bf16[3,2,4,32,512]{4,3,2,1,0:T(8,128)(2,1)S(1)} %shard_map.103.refs_2_.coup, f32[3,32,128]{2,1,0:T(8,128)S(1)} %copy-done.4, f32[2,256,128]{2,1,0:T(8,128)S(1)} %shard_map.106.refs_0_, ...), custom_call_target="tpu_custom_call" | custom-call | flops 5000000000 | bytes 65536 | tf_op jit(solution)/shard_map/pallas_call | solution.py:222
  30.3 6.8 %all-to-all-done.u_ref = f32[4,256,128]{2,1,0:T(8,128)S(1)} async-done(((f32[4,256,128]{2,1,0:T(8,128)}), f32[4,256,128]{2,1,0:T(8,128)S(1)}, u32[]{:S(2)}, u32[]{:S(2)}) %all-to-all-start) | async-done | bytes 524320 | tf_op jit(solution)/shard_map/all_to_all | solution.py:255
  39.3 2.0 %collective-permute-start.11 = (f32[256,128]{1,0:T(8,128)S(1)}, f32[256,128]{1,0:T(8,128)S(1)}, u32[]{:S(2)}, u32[]{:S(2)}) collective-permute-start(f32[256,128]{1,0:T(8,128)S(1)} %get-tuple-element.49.refs_3_), channel_id=1, source_target_pairs={{0,4},{1,5},{2,6},{3,7},{4,0},{5,1},{6,2},{7,3},{8,12},{9,13},{10,... | collective-permute-start | bytes 393224 | tf_op jit(solution)/shard_map/ppermute | solution.py:245
  41.3 6.6 %collective-permute-done.9.refs_1_ = f32[256,128]{1,0:T(8,128)S(1)} collective-permute-done((f32[256,128]{1,0:T(8,128)S(1)}, f32[256,128]{1,0:T(8,128)S(1)}, u32[]{:S(2)}, u32[]{:S(2)}) %collective-permute-start.9) | collective-permute-done | bytes 131104 | tf_op jit(solution)/shard_map/ppermute | solution.py:245
  50.0 2.4 %shard_map.109 = (f32[256,128]{1,0:T(8,128)S(1)}, f32[256,128]{1,0:T(8,128)S(1)}, f32[256,128]{1,0:T(8,128)S(1)}, f32[256,128]{1,0:T(8,128)S(1)}, f32[32,32,128]{2,1,0:T(8,128)}, /*index=5*/f32[32,32,128]{2,1,0:T(8,128)S(1)}) custom-call(s32[1]{0:T(128)} %bitcast.me_ref, s32[2,32]{1,0:T(2,128)S(1)} %bitcast.3, f32[32,32]{1,0:T(8,128)S(1)} %copy-done.5, ...), custom_call_target="tpu_custom_call" | custom-call | bytes 65536 | tf_op jit(solution)/shard_map/pallas_call | solution.py:222
  53.9 2.8 %collective-permute-start.17 = (f32[256,128]{1,0:T(8,128)S(1)}, f32[256,128]{1,0:T(8,128)S(1)}, u32[]{:S(2)}, u32[]{:S(2)}) collective-permute-start(f32[256,128]{1,0:T(8,128)S(1)} %get-tuple-element.63), channel_id=1, source_target_pairs={{0,12},{1,13},{2,14},{3,15},{4,8},{5,9},{6,10},{7,11},{8,4},{9,5},... | collective-permute-start | bytes 393224 | tf_op jit(solution)/shard_map/ppermute | solution.py:245
  58.4 2.2 %collective-permute-done.15.refs_3_ = f32[256,128]{1,0:T(8,128)S(1)} collective-permute-done((f32[256,128]{1,0:T(8,128)S(1)}, f32[256,128]{1,0:T(8,128)S(1)}, u32[]{:S(2)}, u32[]{:S(2)}) %collective-permute-start.15) | collective-permute-done | bytes 131104 | tf_op jit(solution)/shard_map/ppermute | solution.py:245
  61.2 4.3 %collective-permute-done.16.refs_2_ = f32[256,128]{1,0:T(8,128)S(1)} collective-permute-done((f32[256,128]{1,0:T(8,128)S(1)}, f32[256,128]{1,0:T(8,128)S(1)}, u32[]{:S(2)}, u32[]{:S(2)}) %collective-permute-start.16) | collective-permute-done | bytes 131104 | tf_op jit(solution)/shard_map/ppermute | solution.py:245
  67.2 3.6 %collective-permute-start.18 = (f32[256,128]{1,0:T(8,128)S(1)}, f32[256,128]{1,0:T(8,128)S(1)}, u32[]{:S(2)}, u32[]{:S(2)}) collective-permute-start(f32[256,128]{1,0:T(8,128)S(1)} %get-tuple-element.65), channel_id=1, source_target_pairs={{0,8},{1,9},{2,10},{3,11},{4,12},{5,13},{6,14},{7,15},{8,0},{9,1},... | collective-permute-start | bytes 393224 | tf_op jit(solution)/shard_map/ppermute | solution.py:245
  71.3 5.1 %collective-permute-done.18.refs_1_ = f32[256,128]{1,0:T(8,128)S(1)} collective-permute-done((f32[256,128]{1,0:T(8,128)S(1)}, f32[256,128]{1,0:T(8,128)S(1)}, u32[]{:S(2)}, u32[]{:S(2)}) %collective-permute-start.18) | collective-permute-done | bytes 131104 | tf_op jit(solution)/shard_map/ppermute | solution.py:245
  76.9 2.0 %collective-permute-start.19 = (f32[256,128]{1,0:T(8,128)S(1)}, f32[256,128]{1,0:T(8,128)S(1)}, u32[]{:S(2)}, u32[]{:S(2)}) collective-permute-start(f32[256,128]{1,0:T(8,128)S(1)} %get-tuple-element.66), channel_id=1, source_target_pairs={{0,12},{1,13},{2,14},{3,15},{4,8},{5,9},{6,10},{7,11},{8,4},{9,5},... | collective-permute-start | bytes 393224 | tf_op jit(solution)/shard_map/ppermute | solution.py:245
  82.1 1.9 %collective-permute-start.28 = (f32[256,128]{1,0:T(8,128)S(1)}, f32[256,128]{1,0:T(8,128)S(1)}, u32[]{:S(2)}, u32[]{:S(2)}) collective-permute-start(f32[256,128]{1,0:T(8,128)S(1)} %get-tuple-element.74), channel_id=1, source_target_pairs={{0,12},{1,13},{2,14},{3,15},{4,8},{5,9},{6,10},{7,11},{8,4},{9,5},... | collective-permute-start | bytes 393224 | tf_op jit(solution)/shard_map/ppermute | solution.py:245
  84.1 1.9 %collective-permute-done.19.refs_2_ = f32[256,128]{1,0:T(8,128)S(1)} collective-permute-done((f32[256,128]{1,0:T(8,128)S(1)}, f32[256,128]{1,0:T(8,128)S(1)}, u32[]{:S(2)}, u32[]{:S(2)}) %collective-permute-start.19) | collective-permute-done | bytes 131104 | tf_op jit(solution)/shard_map/ppermute | solution.py:245
  86.0 2.1 %shard_map.114 = (f32[32,32,128]{2,1,0:T(8,128)S(1)}, f32[32,32,128]{2,1,0:T(8,128)}) custom-call(s32[1]{0:T(128)} %bitcast.me_ref, s32[2,32]{1,0:T(2,128)S(1)} %bitcast.4, f32[32,32]{1,0:T(8,128)S(1)} %copy-done.5, f32[128,128]{1,0:T(8,128)S(1)} %copy-done.2, f32[32,32,128]{2,1,0:T(8,128)S(1)} %get-tuple-element.50.prev, ...), custom_call_target="tpu_custom_call" | custom-call | bytes 65536 | tf_op jit(solution)/shard_map/pallas_call | solution.py:222
  88.1 7.5 %collective-permute-done.27.refs_1_ = f32[256,128]{1,0:T(8,128)S(1)} collective-permute-done((f32[256,128]{1,0:T(8,128)S(1)}, f32[256,128]{1,0:T(8,128)S(1)}, u32[]{:S(2)}, u32[]{:S(2)}) %collective-permute-start.27) | collective-permute-done | bytes 131104 | tf_op jit(solution)/shard_map/ppermute | solution.py:245
  99.8 1.9 %collective-permute-start.35 = (f32[8,128]{1,0:T(8,128)S(1)}, f32[8,128]{1,0:T(8,128)S(1)}, u32[]{:S(2)}, u32[]{:S(2)}) collective-permute-start(f32[8,128]{1,0:T(8,128)S(1)} %add_add_fusion.1), channel_id=1, source_target_pairs={{0,12},{1,13},{2,14},{3,15},{4,8},{5,9},{6,10},{7,11},{8,4},{9,5},... | collective-permute-start | bytes 12296 | tf_op jit(solution)/shard_map/ppermute | solution.py:245
  101.7 2.1 %collective-permute-start.34 = (f32[8,128]{1,0:T(8,128)S(1)}, f32[8,128]{1,0:T(8,128)S(1)}, u32[]{:S(2)}, u32[]{:S(2)}) collective-permute-start(f32[8,128]{1,0:T(8,128)S(1)} %add_add_fusion.1), channel_id=1, source_target_pairs={{0,8},{1,9},{2,10},{3,11},{4,12},{5,13},{6,14},{7,15},{8,0},{9,1},... | collective-permute-start | bytes 12296 | tf_op jit(solution)/shard_map/ppermute | solution.py:245
  (89 shorter events, 30.9 us)
Async XLA Ops:
  2.0 8.1 %collective-permute-start.2 = (f32[256,128]{1,0:T(8,128)S(1)}, f32[256,128]{1,0:T(8,128)S(1)}, u32[]{:S(2)}, u32[]{:S(2)}) collective-permute-start(f32[256,128]{1,0:T(8,128)S(1)} %get-tuple-element.45), channel_id=1, source_target_pairs={{0,4},{1,5},{2,6},{3,7},{4,0},{5,1},{6,2},{7,3},{8,12},{9,13},{10,... | collective-permute-start | bytes 393224 | tf_op jit(solution)/shard_map/ppermute | solution.py:245
  5.1 12.9 %collective-permute-start = (f32[256,128]{1,0:T(8,128)S(1)}, f32[256,128]{1,0:T(8,128)S(1)}, u32[]{:S(2)}, u32[]{:S(2)}) collective-permute-start(f32[256,128]{1,0:T(8,128)S(1)} %get-tuple-element.41), channel_id=1, source_target_pairs={{0,8},{1,9},{2,10},{3,11},{4,12},{5,13},{6,14},{7,15},{8,0},{9,1},... | collective-permute-start | bytes 393224 | tf_op jit(solution)/shard_map/ppermute | solution.py:245
  7.7 10.3 %collective-permute-start.1 = (f32[256,128]{1,0:T(8,128)S(1)}, f32[256,128]{1,0:T(8,128)S(1)}, u32[]{:S(2)}, u32[]{:S(2)}) collective-permute-start(f32[256,128]{1,0:T(8,128)S(1)} %get-tuple-element.42), channel_id=1, source_target_pairs={{0,12},{1,13},{2,14},{3,15},{4,8},{5,9},{6,10},{7,11},{8,4},{9,5},... | collective-permute-start | bytes 393224 | tf_op jit(solution)/shard_map/ppermute | solution.py:245
  10.2 9.5 %collective-permute-start.6 = (f32[2,256,128]{2,1,0:T(8,128)S(1)}, f32[2,256,128]{2,1,0:T(8,128)S(1)}, u32[]{:S(2)}, u32[]{:S(2)}) collective-permute-start(f32[2,256,128]{2,1,0:T(8,128)S(1)} %shard_map.107.refs_1_), channel_id=1, source_target_pairs={{0,2},{1,3},{2,0},{3,1},{4,6},{5,7},{6,4},{7,5},{8,10},{9,11},{10,... | collective-permute-start | bytes 786440 | tf_op jit(solution)/shard_map/ppermute | solution.py:245
  18.1 6.5 %collective-permute-start.5 = (f32[2,256,128]{2,1,0:T(8,128)S(1)}, f32[2,256,128]{2,1,0:T(8,128)}, u32[]{:S(2)}, u32[]{:S(2)}) collective-permute-start(f32[2,256,128]{2,1,0:T(8,128)S(1)} %shard_map.106.refs_0_), channel_id=1, source_target_pairs={{0,2},{1,3},{2,0},{3,1},{4,6},{5,7},{6,4},{7,5},{8,10},{9,11},{10,... | collective-permute-start | bytes 786440 | tf_op jit(solution)/shard_map/ppermute | solution.py:245
  19.7 17.5 %all-to-all-start = ((f32[4,256,128]{2,1,0:T(8,128)}), f32[4,256,128]{2,1,0:T(8,128)S(1)}, u32[]{:S(2)}, u32[]{:S(2)}) async-start(f32[4,256,128]{2,1,0:T(8,128)} %get-tuple-element.52), calls=%async_computation | async-start | bytes 1048576 | tf_op jit(solution)/shard_map/all_to_all | solution.py:255
  37.3 12.7 %collective-permute-start.13 = (f32[4,256,128]{2,1,0:T(8,128)S(1)}, f32[4,256,128]{2,1,0:T(8,128)S(1)}, u32[]{:S(2)}, u32[]{:S(2)}) collective-permute-start(f32[4,256,128]{2,1,0:T(8,128)S(1)} %get-tuple-element.53.refs_0_), channel_id=1, source_target_pairs={{0,2},{1,3},{2,0},{3,1},{4,6},{5,7},{6,4},{7,5},{8,10},{9,11},{10,... | collective-permute-start | bytes 1572872 | tf_op jit(solution)/shard_map/ppermute | solution.py:245
  37.8 10.1 %collective-permute-start.9 = (f32[256,128]{1,0:T(8,128)S(1)}, f32[256,128]{1,0:T(8,128)S(1)}, u32[]{:S(2)}, u32[]{:S(2)}) collective-permute-start(f32[256,128]{1,0:T(8,128)S(1)} %get-tuple-element.47.refs_1_), channel_id=1, source_target_pairs={{0,8},{1,9},{2,10},{3,11},{4,12},{5,13},{6,14},{7,15},{8,0},{9,1},... | collective-permute-start | bytes 393224 | tf_op jit(solution)/shard_map/ppermute | solution.py:245
  37.8 10.1 %collective-permute-start.10 = (f32[256,128]{1,0:T(8,128)S(1)}, f32[256,128]{1,0:T(8,128)S(1)}, u32[]{:S(2)}, u32[]{:S(2)}) collective-permute-start(f32[256,128]{1,0:T(8,128)S(1)} %get-tuple-element.48.refs_2_), channel_id=1, source_target_pairs={{0,12},{1,13},{2,14},{3,15},{4,8},{5,9},{6,10},{7,11},{8,4},{9,5},... | collective-permute-start | bytes 393224 | tf_op jit(solution)/shard_map/ppermute | solution.py:245
  39.3 9.0 %collective-permute-start.11 = (f32[256,128]{1,0:T(8,128)S(1)}, f32[256,128]{1,0:T(8,128)S(1)}, u32[]{:S(2)}, u32[]{:S(2)}) collective-permute-start(f32[256,128]{1,0:T(8,128)S(1)} %get-tuple-element.49.refs_3_), channel_id=1, source_target_pairs={{0,4},{1,5},{2,6},{3,7},{4,0},{5,1},{6,2},{7,3},{8,12},{9,13},{10,... | collective-permute-start | bytes 393224 | tf_op jit(solution)/shard_map/ppermute | solution.py:245
  41.3 15.4 %collective-permute-start.12 = (f32[4,256,128]{2,1,0:T(8,128)S(1)}, f32[4,256,128]{2,1,0:T(8,128)S(1)}, u32[]{:S(2)}, u32[]{:S(2)}) collective-permute-start(f32[4,256,128]{2,1,0:T(8,128)S(1)} %get-tuple-element.53.refs_0_), channel_id=1, source_target_pairs={{0,1},{1,0},{2,3},{3,2},{4,5},{5,4},{6,7},{7,6},{8,9},{9,8},{10,11... | collective-permute-start | bytes 1572872 | tf_op jit(solution)/shard_map/ppermute | solution.py:245
  50.0 6.8 %collective-permute-start.14 = (f32[4,256,128]{2,1,0:T(8,128)S(1)}, f32[4,256,128]{2,1,0:T(8,128)S(1)}, u32[]{:S(2)}, u32[]{:S(2)}) collective-permute-start(f32[4,256,128]{2,1,0:T(8,128)S(1)} %collective-permute-done.13.refs_2_), channel_id=1, source_target_pairs={{0,1},{1,0},{2,3},{3,2},{4,5},{5,4},{6,7},{7,6},{8,9},{9,8},{10,11... | collective-permute-start | bytes 1572872 | tf_op jit(solution)/shard_map/ppermute | solution.py:245
  52.3 8.3 %collective-permute-start.15 = (f32[256,128]{1,0:T(8,128)S(1)}, f32[256,128]{1,0:T(8,128)S(1)}, u32[]{:S(2)}, u32[]{:S(2)}) collective-permute-start(f32[256,128]{1,0:T(8,128)S(1)} %get-tuple-element.58), channel_id=1, source_target_pairs={{0,4},{1,5},{2,6},{3,7},{4,0},{5,1},{6,2},{7,3},{8,12},{9,13},{10,... | collective-permute-start | bytes 393224 | tf_op jit(solution)/shard_map/ppermute | solution.py:245
  52.6 12.9 %collective-permute-start.16 = (f32[256,128]{1,0:T(8,128)S(1)}, f32[256,128]{1,0:T(8,128)S(1)}, u32[]{:S(2)}, u32[]{:S(2)}) collective-permute-start(f32[256,128]{1,0:T(8,128)S(1)} %get-tuple-element.62), channel_id=1, source_target_pairs={{0,8},{1,9},{2,10},{3,11},{4,12},{5,13},{6,14},{7,15},{8,0},{9,1},... | collective-permute-start | bytes 393224 | tf_op jit(solution)/shard_map/ppermute | solution.py:245
  53.9 11.6 %collective-permute-start.17 = (f32[256,128]{1,0:T(8,128)S(1)}, f32[256,128]{1,0:T(8,128)S(1)}, u32[]{:S(2)}, u32[]{:S(2)}) collective-permute-start(f32[256,128]{1,0:T(8,128)S(1)} %get-tuple-element.63), channel_id=1, source_target_pairs={{0,12},{1,13},{2,14},{3,15},{4,8},{5,9},{6,10},{7,11},{8,4},{9,5},... | collective-permute-start | bytes 393224 | tf_op jit(solution)/shard_map/ppermute | solution.py:245
  60.7 15.7 %collective-permute-start.24 = (f32[2,256,128]{2,1,0:T(8,128)S(1)}, f32[2,256,128]{2,1,0:T(8,128)S(1)}, u32[]{:S(2)}, u32[]{:S(2)}) collective-permute-start(f32[2,256,128]{2,1,0:T(8,128)S(1)} %get-tuple-element.64.refs_4_.refs_1_), channel_id=1, source_target_pairs={{0,2},{1,3},{2,0},{3,1},{4,6},{5,7},{6,4},{7,5},{8,10},{9,11},{10,... | collective-permute-start | bytes 786440 | tf_op jit(solution)/shard_map/ppermute | solution.py:245
  65.6 10.8 %collective-permute-start.23 = (f32[2,256,128]{2,1,0:T(8,128)S(1)}, f32[2,256,128]{2,1,0:T(8,128)S(1)}, u32[]{:S(2)}, u32[]{:S(2)}) collective-permute-start(f32[2,256,128]{2,1,0:T(8,128)S(1)} %get-tuple-element.70.refs_0_), channel_id=1, source_target_pairs={{0,2},{1,3},{2,0},{3,1},{4,6},{5,7},{6,4},{7,5},{8,10},{9,11},{10,... | collective-permute-start | bytes 786440 | tf_op jit(solution)/shard_map/ppermute | solution.py:245
  67.2 9.2 %collective-permute-start.18 = (f32[256,128]{1,0:T(8,128)S(1)}, f32[256,128]{1,0:T(8,128)S(1)}, u32[]{:S(2)}, u32[]{:S(2)}) collective-permute-start(f32[256,128]{1,0:T(8,128)S(1)} %get-tuple-element.65), channel_id=1, source_target_pairs={{0,8},{1,9},{2,10},{3,11},{4,12},{5,13},{6,14},{7,15},{8,0},{9,1},... | collective-permute-start | bytes 393224 | tf_op jit(solution)/shard_map/ppermute | solution.py:245
  70.8 8.1 %collective-permute-start.22 = (f32[2,256,128]{2,1,0:T(8,128)S(1)}, f32[2,256,128]{2,1,0:T(8,128)S(1)}, u32[]{:S(2)}, u32[]{:S(2)}) collective-permute-start(f32[2,256,128]{2,1,0:T(8,128)S(1)} %get-tuple-element.64.refs_4_.refs_1_), channel_id=1, source_target_pairs={{0,1},{1,0},{2,3},{3,2},{4,5},{5,4},{6,7},{7,6},{8,9},{9,8},{10,11... | collective-permute-start | bytes 786440 | tf_op jit(solution)/shard_map/ppermute | solution.py:245
  76.9 7.2 %collective-permute-start.20 = (f32[256,128]{1,0:T(8,128)S(1)}, f32[256,128]{1,0:T(8,128)S(1)}, u32[]{:S(2)}, u32[]{:S(2)}) collective-permute-start(f32[256,128]{1,0:T(8,128)S(1)} %get-tuple-element.67), channel_id=1, source_target_pairs={{0,4},{1,5},{2,6},{3,7},{4,0},{5,1},{6,2},{7,3},{8,12},{9,13},{10,... | collective-permute-start | bytes 393224 | tf_op jit(solution)/shard_map/ppermute | solution.py:245
  76.9 9.2 %collective-permute-start.19 = (f32[256,128]{1,0:T(8,128)S(1)}, f32[256,128]{1,0:T(8,128)S(1)}, u32[]{:S(2)}, u32[]{:S(2)}) collective-permute-start(f32[256,128]{1,0:T(8,128)S(1)} %get-tuple-element.66), channel_id=1, source_target_pairs={{0,12},{1,13},{2,14},{3,15},{4,8},{5,9},{6,10},{7,11},{8,4},{9,5},... | collective-permute-start | bytes 393224 | tf_op jit(solution)/shard_map/ppermute | solution.py:245
  80.5 15.1 %collective-permute-start.27 = (f32[256,128]{1,0:T(8,128)S(1)}, f32[256,128]{1,0:T(8,128)S(1)}, u32[]{:S(2)}, u32[]{:S(2)}) collective-permute-start(f32[256,128]{1,0:T(8,128)S(1)} %get-tuple-element.73), channel_id=1, source_target_pairs={{0,8},{1,9},{2,10},{3,11},{4,12},{5,13},{6,14},{7,15},{8,0},{9,1},... | collective-permute-start | bytes 393224 | tf_op jit(solution)/shard_map/ppermute | solution.py:245
  82.1 13.5 %collective-permute-start.28 = (f32[256,128]{1,0:T(8,128)S(1)}, f32[256,128]{1,0:T(8,128)S(1)}, u32[]{:S(2)}, u32[]{:S(2)}) collective-permute-start(f32[256,128]{1,0:T(8,128)S(1)} %get-tuple-element.74), channel_id=1, source_target_pairs={{0,12},{1,13},{2,14},{3,15},{4,8},{5,9},{6,10},{7,11},{8,4},{9,5},... | collective-permute-start | bytes 393224 | tf_op jit(solution)/shard_map/ppermute | solution.py:245
  84.0 11.6 %collective-permute-start.29 = (f32[256,128]{1,0:T(8,128)S(1)}, f32[256,128]{1,0:T(8,128)S(1)}, u32[]{:S(2)}, u32[]{:S(2)}) collective-permute-start(f32[256,128]{1,0:T(8,128)S(1)} %get-tuple-element.75), channel_id=1, source_target_pairs={{0,4},{1,5},{2,6},{3,7},{4,0},{5,1},{6,2},{7,3},{8,12},{9,13},{10,... | collective-permute-start | bytes 393224 | tf_op jit(solution)/shard_map/ppermute | solution.py:245
  (23 other events, 135.2 us)
